TPU v7x, 32 devices: a whole 2x2x4 slice. The times are simulated.
32 devices in a mesh: dp: 8 (over y, x, core), head: 4 (over z).
Axes of the slice: x: 2, y: 2, z: 4, core: 2. Of those that a mesh axis runs over, the one named last changes fastest.
Arguments:
- source_ids: int32 [32, 384], P('dp'), may hold values from 0 to 32127
- target_ids: int32 [32, 128], P('dp'), may hold values from 0 to 32127
- source_lens: int32 [32], P('dp'), may hold values from 96 to 384
- target_lens: int32 [32], P('dp'), may hold values from 0 to 128, as said below
- kl_mask: int32 [32, 128], P('dp'), may hold values 0 or 1
- teacher: bfloat16 [4096, 32128], P('dp', 'head'), may hold values from -10 to 32
- embed: float32 [32128, 512], P('head', 'dp'), may hold values from -12 to 12
- attn_in: float32 [3, 3, 512, 512], P(None, None, 'dp', 'head'), may hold values from -0.25 to 0.25
- attn_out: float32 [3, 512, 512], P(None, 'head', 'dp'), may hold values from -3 to 3
- ff_in: float32 [2, 512, 2048], P(None, 'dp', 'head'), may hold values from -0.25 to 0.25
- ff_out: float32 [2, 2048, 512], P(None, 'head', 'dp'), may hold values from -0.125 to 0.125
- gains: float32 [7, 512], P(None, 'dp'), may hold values from 0.5 to 1.5
- moment_embed: float32 [32128, 512], P('head', 'dp'), may hold values from -1.1920929e-07 to 1.1920929e-07
- moment_attn_in: float32 [3, 3, 512, 512], P(None, None, 'dp', 'head'), may hold values from -2.861023e-06 to 2.861023e-06
- moment_attn_out: float32 [3, 512, 512], P(None, 'head', 'dp'), may hold values from -2.861023e-06 to 2.861023e-06
- moment_ff_in: float32 [2, 512, 2048], P(None, 'dp', 'head'), may hold values from -2.861023e-06 to 2.861023e-06
- moment_ff_out: float32 [2, 2048, 512], P(None, 'head', 'dp'), may hold values from -2.861023e-06 to 2.861023e-06
- moment_gains: float32 [7, 512], P(None, 'dp'), may hold values from -1.335144e-05 to 1.335144e-05
- second_embed: float32 [32128, 512], P('head', 'dp'), may hold values from 6.304335e-17 to 2.521734e-16
- second_attn_in: float32 [3, 3, 512, 512], P(None, None, 'dp', 'head'), may hold values from 1.681156e-14 to 6.724624e-14
- second_attn_out: float32 [3, 512, 512], P(None, 'head', 'dp'), may hold values from 1.681156e-14 to 6.724624e-14
- second_ff_in: float32 [2, 512, 2048], P(None, 'dp', 'head'), may hold values from 1.681156e-14 to 6.724624e-14
- second_ff_out: float32 [2, 2048, 512], P(None, 'head', 'dp'), may hold values from 1.681156e-14 to 6.724624e-14
- second_gains: float32 [7, 512], P(None, 'dp'), may hold values from 4.20289e-13 to 1.681156e-12
Outputs:
- total_loss: float32 [1], replicated
- grad_norm: float32 [1], replicated
- new_embed: float32 [32128, 512], P('head', 'dp')
- new_attn_in: float32 [3, 3, 512, 512], P(None, None, 'dp', 'head')
- new_attn_out: float32 [3, 512, 512], P(None, 'head', 'dp')
- new_ff_in: float32 [2, 512, 2048], P(None, 'dp', 'head')
- new_ff_out: float32 [2, 2048, 512], P(None, 'head', 'dp')
- new_gains: float32 [7, 512], P(None, 'dp')
- new_moment_embed: float32 [32128, 512], P('head', 'dp')
- new_moment_attn_in: float32 [3, 3, 512, 512], P(None, None, 'dp', 'head')
- new_moment_attn_out: float32 [3, 512, 512], P(None, 'head', 'dp')
- new_moment_ff_in: float32 [2, 512, 2048], P(None, 'dp', 'head')
- new_moment_ff_out: float32 [2, 2048, 512], P(None, 'head', 'dp')
- new_moment_gains: float32 [7, 512], P(None, 'dp')
- new_second_embed: float32 [32128, 512], P('head', 'dp')
- new_second_attn_in: float32 [3, 3, 512, 512], P(None, None, 'dp', 'head')
- new_second_attn_out: float32 [3, 512, 512], P(None, 'head', 'dp')
- new_second_ff_in: float32 [2, 512, 2048], P(None, 'dp', 'head')
- new_second_ff_out: float32 [2, 2048, 512], P(None, 'head', 'dp')
- new_second_gains: float32 [7, 512], P(None, 'dp')
Inputs may be any that keep to these rules, and one draw needn't show every extreme that they name: `target_lens`: some sequences have no target tokens.
All inputs are finite; a program needn't handle non-finite values. No bound on the sum of `kl_mask` on one device may be relied on, other than what follows from the above.
Results may differ from a plain program's by a relative error of at most 0.012.
Values may be sent and summed in bfloat16 or wider, within the bound.
No kernel may reach another device: no remote copies, remote signals or barrier semaphores. Data moves between devices by JAX's collectives and lax.ppermute only.
A program may use at most 256 MiB of HBM per device.

v0:
```python
import jax
import jax.numpy as jnp
from jax import lax
from jax.sharding import PartitionSpec as P

D = 512
DH = 64
STEP_NUM = 10


NORM_EPS = 1e-06
SOFTEN_FACTOR = 2.0
DIVERGENCE_SCALE = 1.0
CLIP_NORM = 0.02
BETA_ONE = 0.9
BETA_TWO = 0.999
ADAM_EPS = 1e-08
WEIGHT_DECAY = 0.01
LEARN_RATE = 0.3
MATRIX_AXES = ((0, 1), (2, 3), (1, 2), (1, 2), (1, 2), (1,))
SHARD_DIMS = (1, 2, 2, 1, 2, 1)


def head_sum(parts):
    return lax.psum(parts, "head")


def head_back(parts):
    return lax.psum(parts, "head")


def normed(inputs, gain_row):
    return (
        inputs * lax.rsqrt(jnp.mean(inputs * inputs, -1, keepdims=True) + NORM_EPS) * gain_row
    ).astype(jnp.bfloat16)


def norm_back(inputs, gain_row, upstream):
    factor = lax.rsqrt(jnp.mean(inputs * inputs, -1, keepdims=True) + NORM_EPS)
    scaled = upstream * gain_row
    inner = jnp.mean(scaled * inputs, -1, keepdims=True)
    return (
        factor * (scaled - inputs * factor * factor * inner),
        jnp.sum(upstream * inputs * factor, axis=(0, 1)),
    )


def project(inputs, weight_matrix):
    return jnp.einsum("bld,dh->blh", inputs, weight_matrix, preferred_element_type=jnp.float32)


def split_heads(array):
    return array.reshape(array.shape[0], array.shape[1], -1, DH)


def merge_heads(array):
    return array.reshape(array.shape[0], array.shape[1], -1)


def attn_probs(query, keys_all, allowed):
    scores = jnp.einsum(
        "bqhe,bkhe->bhqk", query, keys_all, preferred_element_type=jnp.float32
    ) * DH ** (-0.5)
    return jax.nn.softmax(jnp.where(allowed[:, None], scores, -1000000000.0), -1)


def attend_fwd(query_in, source, weights_in, weight_out, allowed):
    query = split_heads(project(query_in, weights_in[0]).astype(jnp.bfloat16))
    keys_all = split_heads(project(source, weights_in[1]).astype(jnp.bfloat16))
    values = split_heads(project(source, weights_in[2]).astype(jnp.bfloat16))
    probs = attn_probs(query, keys_all, allowed)
    mixed = merge_heads(
        jnp.einsum(
            "bhqk,bkhe->bqhe",
            probs.astype(jnp.bfloat16),
            values,
            preferred_element_type=jnp.float32,
        ).astype(jnp.bfloat16)
    )
    return (
        jnp.einsum("blh,hd->bld", mixed, weight_out, preferred_element_type=jnp.float32),
        (query, keys_all, values, mixed),
    )


def attend_back(upstream, query_in, source, weights_in, weight_out, allowed, kept):
    query, keys_all, values, mixed = kept
    up_low = upstream.astype(jnp.bfloat16)
    grad_out = jnp.einsum("blh,bld->hd", mixed, up_low, preferred_element_type=jnp.float32)
    grad_mixed = split_heads(
        jnp.einsum("bld,hd->blh", up_low, weight_out, preferred_element_type=jnp.float32).astype(
            jnp.bfloat16
        )
    )
    probs = attn_probs(query, keys_all, allowed)
    grad_probs = jnp.einsum(
        "bqhe,bkhe->bhqk", grad_mixed, values, preferred_element_type=jnp.float32
    )
    grad_scores = (probs * (grad_probs - jnp.sum(grad_probs * probs, -1, keepdims=True))).astype(
        jnp.bfloat16
    )
    grad_query = merge_heads(
        (
            jnp.einsum("bhqk,bkhe->bqhe", grad_scores, keys_all, preferred_element_type=jnp.float32)
            * DH ** (-0.5)
        ).astype(jnp.bfloat16)
    )
    grad_keys = merge_heads(
        (
            jnp.einsum("bhqk,bqhe->bkhe", grad_scores, query, preferred_element_type=jnp.float32)
            * DH ** (-0.5)
        ).astype(jnp.bfloat16)
    )
    grad_values = merge_heads(
        jnp.einsum(
            "bhqk,bqhe->bkhe",
            probs.astype(jnp.bfloat16),
            grad_mixed,
            preferred_element_type=jnp.float32,
        ).astype(jnp.bfloat16)
    )
    grad_in = jnp.stack(
        [
            jnp.einsum("bld,blh->dh", query_in, grad_query, preferred_element_type=jnp.float32),
            jnp.einsum("bld,blh->dh", source, grad_keys, preferred_element_type=jnp.float32),
            jnp.einsum("bld,blh->dh", source, grad_values, preferred_element_type=jnp.float32),
        ]
    )
    back_query = jnp.einsum(
        "blh,dh->bld", grad_query, weights_in[0], preferred_element_type=jnp.float32
    )
    back_source = jnp.einsum(
        "blh,dh->bld", grad_keys, weights_in[1], preferred_element_type=jnp.float32
    )
    back_source = back_source + jnp.einsum(
        "blh,dh->bld", grad_values, weights_in[2], preferred_element_type=jnp.float32
    )
    return (back_query, back_source, grad_in, grad_out)


def feed_fwd(inputs, weight_up, weight_down):
    hidden = jax.nn.relu(project(inputs, weight_up)).astype(jnp.bfloat16)
    return (
        jnp.einsum("blf,fd->bld", hidden, weight_down, preferred_element_type=jnp.float32),
        hidden,
    )


def feed_back(upstream, inputs, weight_up, weight_down, hidden):
    up_low = upstream.astype(jnp.bfloat16)
    grad_down = jnp.einsum("blf,bld->fd", hidden, up_low, preferred_element_type=jnp.float32)
    grad_hidden = jnp.einsum("bld,fd->blf", up_low, weight_down, preferred_element_type=jnp.float32)
    grad_pre = jnp.where(hidden > 0, grad_hidden, 0.0).astype(jnp.bfloat16)
    grad_up = jnp.einsum("bld,blf->df", inputs, grad_pre, preferred_element_type=jnp.float32)
    back_in = jnp.einsum("blf,df->bld", grad_pre, weight_up, preferred_element_type=jnp.float32)
    return (back_in, grad_up, grad_down)


def body(
    source_ids,
    target_ids,
    source_lens,
    target_lens,
    kl_mask,
    teacher,
    embed,
    attn_in,
    attn_out,
    ff_in,
    ff_out,
    gains,
    moment_embed,
    moment_attn_in,
    moment_attn_out,
    moment_ff_in,
    moment_ff_out,
    moment_gains,
    second_embed,
    second_attn_in,
    second_attn_out,
    second_ff_in,
    second_ff_out,
    second_gains,
):
    masters = (embed, attn_in, attn_out, ff_in, ff_out, gains)
    moments = (
        moment_embed,
        moment_attn_in,
        moment_attn_out,
        moment_ff_in,
        moment_ff_out,
        moment_gains,
    )
    seconds = (
        second_embed,
        second_attn_in,
        second_attn_out,
        second_ff_in,
        second_ff_out,
        second_gains,
    )
    table, w_in, w_out, w_up, w_down, gain_low = (
        lax.all_gather(embed.astype(jnp.bfloat16), "dp", axis=1, tiled=True),
        lax.all_gather(attn_in.astype(jnp.bfloat16), "dp", axis=2, tiled=True),
        lax.all_gather(attn_out.astype(jnp.bfloat16), "dp", axis=2, tiled=True),
        lax.all_gather(ff_in.astype(jnp.bfloat16), "dp", axis=1, tiled=True),
        lax.all_gather(ff_out.astype(jnp.bfloat16), "dp", axis=2, tiled=True),
        lax.all_gather(gains.astype(jnp.bfloat16), "dp", axis=1, tiled=True),
    )
    gain = gain_low.astype(jnp.float32)
    head_pos = lax.axis_index("head")
    lead = (head_pos == 0).astype(jnp.float32)
    vocab_local = table.shape[0]
    vocab_start = head_pos * vocab_local
    batch_size, source_len = source_ids.shape
    target_len = target_ids.shape[1]
    token_count = batch_size * target_len
    dec_ids = jnp.concatenate([jnp.zeros((batch_size, 1), jnp.int32), target_ids[:, :-1]], 1)
    src_local = source_ids - vocab_start
    src_inside = (src_local >= 0) & (src_local < vocab_local)
    dec_local = dec_ids - vocab_start
    dec_inside = (dec_local >= 0) & (dec_local < vocab_local)

    def lookup(local, inside):
        return (
            jnp.take(table, jnp.clip(local, 0, vocab_local - 1), axis=0).astype(jnp.float32)
            * inside[..., None]
        )

    def spread(local, inside, grad):
        slots = jnp.where(inside, local, vocab_local).reshape(-1)
        return (
            jnp.zeros((vocab_local, grad.shape[-1]), jnp.float32)
            .at[slots]
            .add(grad.reshape(-1, grad.shape[-1]), mode="drop")
        )

    src_keys = jnp.arange(source_len)[None, :] < source_lens[:, None]
    enc_allowed = jnp.broadcast_to(src_keys[:, None, :], (batch_size, source_len, source_len))
    cross_allowed = jnp.broadcast_to(src_keys[:, None, :], (batch_size, target_len, source_len))
    causal = jnp.broadcast_to(
        (jnp.arange(target_len)[:, None] >= jnp.arange(target_len)[None, :])[None],
        (batch_size, target_len, target_len),
    )
    enc_embed, dec_embed = head_sum((lookup(src_local, src_inside), lookup(dec_local, dec_inside)))
    norm_a = normed(enc_embed, gain[0])
    branch, kept_enc = attend_fwd(norm_a, norm_a, w_in[0], w_out[0], enc_allowed)
    enc_mid = enc_embed + head_sum(branch)
    norm_b = normed(enc_mid, gain[1])
    branch, hidden_enc = feed_fwd(norm_b, w_up[0], w_down[0])
    enc_last = enc_mid + head_sum(branch)
    encoded = normed(enc_last, gain[2])
    norm_c = normed(dec_embed, gain[3])
    branch, kept_self = attend_fwd(norm_c, norm_c, w_in[1], w_out[1], causal)
    dec_one = dec_embed + head_sum(branch)
    norm_d = normed(dec_one, gain[4])
    branch, kept_cross = attend_fwd(norm_d, encoded, w_in[2], w_out[2], cross_allowed)
    dec_two = dec_one + head_sum(branch)
    norm_e = normed(dec_two, gain[5])
    branch, hidden_dec = feed_fwd(norm_e, w_up[1], w_down[1])
    dec_three = dec_two + head_sum(branch)
    head_gain = gain[6] * D ** (-0.5)
    final = normed(dec_three, head_gain).reshape(token_count, -1)
    student_logits = jnp.einsum("td,vd->tv", final, table, preferred_element_type=jnp.float32)
    real_count = jnp.maximum(lax.psum(jnp.sum((target_lens > 0).astype(jnp.float32)), "dp"), 1.0)
    valid = (jnp.arange(target_len)[None, :] < target_lens[:, None]).astype(jnp.float32)
    token_weight = (
        valid / (jnp.maximum(target_lens, 1).astype(jnp.float32)[:, None] * real_count)
    ).reshape(token_count)
    divergence_mask = kl_mask.astype(jnp.float32).reshape(token_count)
    labels = target_ids.reshape(token_count)
    teacher_full = teacher.astype(jnp.float32)
    peak_student, peak_teacher = lax.pmax(
        (jnp.max(student_logits, -1), jnp.max(teacher_full, -1)), "head"
    )
    shifted = student_logits - peak_student[:, None]
    teacher_exp = jnp.exp((teacher_full - peak_teacher[:, None]) / SOFTEN_FACTOR)
    local_hit = ((labels - vocab_start)[:, None] == jnp.arange(vocab_local)[None, :]).astype(
        jnp.float32
    )
    sum_one, sum_half, sum_teacher, sum_cross, label_logprob = lax.psum(
        (
            jnp.sum(jnp.exp(shifted), -1),
            jnp.sum(jnp.exp(shifted / SOFTEN_FACTOR), -1),
            jnp.sum(teacher_exp, -1),
            jnp.sum(teacher_exp * (teacher_full - student_logits), -1) / SOFTEN_FACTOR,
            jnp.sum(local_hit * student_logits, -1),
        ),
        "head",
    )
    lse_one = peak_student + jnp.log(sum_one)
    lse_half = peak_student / SOFTEN_FACTOR + jnp.log(sum_half)
    lse_teacher = peak_teacher / SOFTEN_FACTOR + jnp.log(sum_teacher)
    cross_entropy = lse_one - label_logprob
    divergence_value = sum_cross / sum_teacher - lse_teacher + lse_half
    loss_part = lead * jnp.sum(
        token_weight
        * (
            cross_entropy
            + DIVERGENCE_SCALE * SOFTEN_FACTOR * SOFTEN_FACTOR * divergence_value * divergence_mask
        )
    )
    grad_logits = (
        token_weight[:, None]
        * (
            jnp.exp(student_logits - lse_one[:, None])
            - local_hit
            + DIVERGENCE_SCALE
            * SOFTEN_FACTOR
            * (
                jnp.exp(student_logits / SOFTEN_FACTOR - lse_half[:, None])
                - jnp.exp(teacher_full / SOFTEN_FACTOR - lse_teacher[:, None])
            )
            * divergence_mask[:, None]
        )
    ).astype(jnp.bfloat16)
    grad_table = jnp.einsum("tv,td->vd", grad_logits, final, preferred_element_type=jnp.float32)
    grad_final = head_back(
        jnp.einsum("tv,vd->td", grad_logits, table, preferred_element_type=jnp.float32)
    ).reshape(batch_size, target_len, -1)
    grad_three, gain_six = norm_back(dec_three, head_gain, grad_final)
    back_in, up_dec, down_dec = feed_back(grad_three, norm_e, w_up[1], w_down[1], hidden_dec)
    grad_norm_in, gain_five = norm_back(dec_two, gain[5], head_back(back_in))
    grad_two = grad_three + grad_norm_in
    back_query, back_source, in_cross, out_cross = attend_back(
        grad_two, norm_d, encoded, w_in[2], w_out[2], cross_allowed, kept_cross
    )
    grad_query_in, grad_encoded = head_back((back_query, back_source))
    grad_norm_in, gain_four = norm_back(dec_one, gain[4], grad_query_in)
    grad_one = grad_two + grad_norm_in
    back_query, back_source, in_self, out_self = attend_back(
        grad_one, norm_c, norm_c, w_in[1], w_out[1], causal, kept_self
    )
    grad_norm_in, gain_three = norm_back(dec_embed, gain[3], head_back(back_query + back_source))
    grad_dec_embed = grad_one + grad_norm_in
    grad_last, gain_two = norm_back(enc_last, gain[2], grad_encoded)
    back_in, up_enc, down_enc = feed_back(grad_last, norm_b, w_up[0], w_down[0], hidden_enc)
    grad_norm_in, gain_one = norm_back(enc_mid, gain[1], head_back(back_in))
    grad_mid = grad_last + grad_norm_in
    back_query, back_source, in_enc, out_enc = attend_back(
        grad_mid, norm_a, norm_a, w_in[0], w_out[0], enc_allowed, kept_enc
    )
    grad_norm_in, gain_zero = norm_back(enc_embed, gain[0], head_back(back_query + back_source))
    grad_enc_embed = grad_mid + grad_norm_in
    grad_table = (
        grad_table
        + spread(src_local, src_inside, grad_enc_embed)
        + spread(dec_local, dec_inside, grad_dec_embed)
    )
    grad_attn_in = jnp.stack([in_enc, in_self, in_cross])
    grad_attn_out = jnp.stack([out_enc, out_self, out_cross])
    grad_up = jnp.stack([up_enc, up_dec])
    grad_down = jnp.stack([down_enc, down_dec])
    grad_gain = jnp.stack(
        [gain_zero, gain_one, gain_two, gain_three, gain_four, gain_five, gain_six * D ** (-0.5)]
    )
    summed = lax.psum(
        (grad_table, grad_attn_in, grad_attn_out, grad_up, grad_down, grad_gain), "dp"
    )
    dp_pos = lax.axis_index("dp")
    shards = [
        lax.dynamic_slice_in_dim(
            summed[position],
            dp_pos * masters[position].shape[SHARD_DIMS[position]],
            masters[position].shape[SHARD_DIMS[position]],
            SHARD_DIMS[position],
        )
        for position in range(6)
    ]

    def matrix_squares(arrays):
        return [
            jnp.sum(arrays[position] * arrays[position], axis=MATRIX_AXES[position])
            * (lead if position == 5 else 1.0)
            for position in range(6)
        ]

    weight_sq = matrix_squares(masters)
    grad_sq = matrix_squares(shards)
    totals = lax.psum(
        (
            weight_sq[0],
            weight_sq[1],
            weight_sq[2],
            weight_sq[3],
            weight_sq[4],
            weight_sq[5],
            grad_sq[0],
            grad_sq[1],
            grad_sq[2],
            grad_sq[3],
            grad_sq[4],
            grad_sq[5],
            loss_part,
        ),
        ("dp", "head"),
    )
    grad_norm = jnp.sqrt(sum((jnp.sum(item) for item in totals[6:12])))
    clip_scale = jnp.minimum(1.0, CLIP_NORM / grad_norm)
    bias_one = 1.0 - BETA_ONE**STEP_NUM
    bias_two = 1.0 - BETA_TWO**STEP_NUM
    updates, fresh_m, fresh_v = ([], [], [])
    for position in range(6):
        grad_now = shards[position] * clip_scale
        moment_new = BETA_ONE * moments[position] + (1 - BETA_ONE) * grad_now
        second_new = BETA_TWO * seconds[position] + (1 - BETA_TWO) * grad_now * grad_now
        update = (
            moment_new / bias_one / (jnp.sqrt(second_new / bias_two) + ADAM_EPS)
            + WEIGHT_DECAY * masters[position]
        )
        updates.append(update)
        fresh_m.append(moment_new)
        fresh_v.append(second_new)
    update_sq = matrix_squares(updates)
    update_tot = lax.psum(
        (update_sq[0], update_sq[1], update_sq[2], update_sq[3], update_sq[4], update_sq[5]),
        ("dp", "head"),
    )
    fresh_w = [
        masters[position]
        - LEARN_RATE
        * jnp.expand_dims(
            jnp.sqrt(totals[position]) / (jnp.sqrt(update_tot[position]) + 1e-06),
            MATRIX_AXES[position],
        )
        * updates[position]
        for position in range(6)
    ]
    return (
        totals[12].reshape(1),
        grad_norm.reshape(1),
        fresh_w[0],
        fresh_w[1],
        fresh_w[2],
        fresh_w[3],
        fresh_w[4],
        fresh_w[5],
        fresh_m[0],
        fresh_m[1],
        fresh_m[2],
        fresh_m[3],
        fresh_m[4],
        fresh_m[5],
        fresh_v[0],
        fresh_v[1],
        fresh_v[2],
        fresh_v[3],
        fresh_v[4],
        fresh_v[5],
    )


def solution(mesh):
    return jax.shard_map(
        body,
        mesh=mesh,
        in_specs=(
            P("dp", None),
            P("dp", None),
            P("dp"),
            P("dp"),
            P("dp", None),
            P("dp", "head"),
            P("head", "dp"),
            P(None, None, "dp", "head"),
            P(None, "head", "dp"),
            P(None, "dp", "head"),
            P(None, "head", "dp"),
            P(None, "dp"),
            P("head", "dp"),
            P(None, None, "dp", "head"),
            P(None, "head", "dp"),
            P(None, "dp", "head"),
            P(None, "head", "dp"),
            P(None, "dp"),
            P("head", "dp"),
            P(None, None, "dp", "head"),
            P(None, "head", "dp"),
            P(None, "dp", "head"),
            P(None, "head", "dp"),
            P(None, "dp"),
        ),
        out_specs=(
            P(),
            P(),
            P("head", "dp"),
            P(None, None, "dp", "head"),
            P(None, "head", "dp"),
            P(None, "dp", "head"),
            P(None, "head", "dp"),
            P(None, "dp"),
            P("head", "dp"),
            P(None, None, "dp", "head"),
            P(None, "head", "dp"),
            P(None, "dp", "head"),
            P(None, "head", "dp"),
            P(None, "dp"),
            P("head", "dp"),
            P(None, None, "dp", "head"),
            P(None, "head", "dp"),
            P(None, "dp", "head"),
            P(None, "head", "dp"),
            P(None, "dp"),
        ),
        check_vma=False,
    )
```

profile of v0, /device:TPU:0, one launch (start us, length us, event | category | flops | bytes accessed | tf_op | source)
XLA Modules:
  0.0 1910.2 jit_solution(4673176603682217238)
XLA Ops:
  7.2 2.7 convert_element_type.245
  10.0 57.0 %all-gather.6.cloned.1.call-done = bf16[8032,512]{0,1:T(8,128)(2,1)} async-done(((bf16[8032,64]{0,1:T(8,128)(2,1)}), bf16[8032,512]{0,1:T(8,128)(2,1)}) %all-gather.6.cloned.1.call-update) | async-done | bytes 8224784 | tf_op jit(solution)/shard_map/all_gather | solution.py:203
  67.1 11.7 copy.454
  78.8 9.3 gather_fusion.1
  92.7 8.9 all-gather
  102.9 8.6 all_gather.21
  111.6 6.4 gather_fusion
  119.2 92.2 %all-reduce.22.cloned.1.call-done = f32[4,384,512]{2,1,0:T(8,128)} async-done(((f32[4,384,512]{2,1,0:T(8,128)}), f32[4,384,512]{2,1,0:T(8,128)}) %all-reduce.22.cloned.1.call-update) | async-done | bytes 3145744 | tf_op jit(solution)/shard_map/psum | solution.py:25
  215.8 21.2 %all-gather.8.cloned.1.call-done = bf16[3,3,512,128]{3,2,1,0:T(8,128)(2,1)} async-done(((bf16[3,3,64,128]{3,2,1,0:T(8,128)(2,1)}), bf16[3,3,512,128]{3,2,1,0:T(8,128)(2,1)}) %all-gather.8.cloned.1.call-update) | async-done | bytes 1179664 | tf_op jit(solution)/shard_map/all_gather | solution.py:204
  237.0 3.0 convolution_convert_fusion.4
  240.0 2.8 convolution_convert_fusion.3
  245.1 5.1 fusion.106
  250.2 3.0 convolution_convert_fusion.8
  259.1 3.7 all-gather.12.cloned.1.call-done
  262.8 4.3 fusion.105
  267.1 3.5 copy.607
  270.6 150.5 %all-reduce.42.cloned.1.call-done = (f32[4,128,512]{2,1,0:T(8,128)}, f32[4,384,512]{2,1,0:T(8,128)}) async-done(((f32[4,128,512]{2,1,0:T(8,128)}, f32[4,384,512]{2,1,0:T(8,128)}), (f32[4,128,512]{2,1,0:T(8,128)}, f32[4,384,512]{2,1,0:T(8,128)})) %all-reduce.42.cloned.1.call-update) | async-done | bytes 4194320 | tf_op jit(solution)/shard_map/psum | solution.py:25
  421.0 3.9 multiply_reduce_fusion.8
  431.1 2.7 fusion.107
  438.3 7.8 all-gather.10.cloned.1.call-done
  446.1 4.1 fusion.39
  451.3 2.8 fusion.48
  454.1 155.4 %all-reduce.40.cloned.1.call-done = (f32[4,128,512]{2,1,0:T(8,128)}, f32[4,384,512]{2,1,0:T(8,128)}) async-done(((f32[4,128,512]{2,1,0:T(8,128)}, f32[4,384,512]{2,1,0:T(8,128)}), (f32[4,128,512]{2,1,0:T(8,128)}, f32[4,384,512]{2,1,0:T(8,128)})) %all-reduce.40.cloned.1.call-update) | async-done | bytes 4194320 | tf_op jit(solution)/shard_map/psum | solution.py:25
  609.5 3.4 multiply_reduce_fusion.7
  614.6 2.4 convolution_convert_fusion.1
  619.0 3.4 fusion.108
  629.2 3.5 copy.612
  632.7 47.4 %all-reduce.24.cloned.1.call-done = f32[4,128,512]{2,1,0:T(8,128)} async-done(((f32[4,128,512]{2,1,0:T(8,128)}), f32[4,128,512]{2,1,0:T(8,128)}) %all-reduce.24.cloned.1.call-update) | async-done | bytes 1048592 | tf_op jit(solution)/shard_map/psum | solution.py:25
  688.5 15.0 psum.315
  703.5 5.1 reduce_max.66
  713.0 25.5 %all-reduce.26.cloned.1.call-done = f32[4,128,512]{2,1,0:T(8,128)} async-done(((f32[4,128,512]{2,1,0:T(8,128)}), f32[4,128,512]{2,1,0:T(8,128)}) %all-reduce.26.cloned.1.call-update) | async-done | bytes 1048592 | tf_op jit(solution)/shard_map/psum | solution.py:25
  742.2 14.1 fusion.109
  756.3 10.9 all-reduce.9
  767.2 14.7 select_reduce_fusion
  782.5 17.0 all-reduce.4
  800.9 14.1 fusion.14
  815.0 11.0 fusion.111
  827.8 48.6 %all-reduce.28.cloned.1.call-done = f32[4,128,512]{2,1,0:T(8,128)} async-done(((f32[4,128,512]{2,1,0:T(8,128)}), f32[4,128,512]{2,1,0:T(8,128)}) %all-reduce.28.cloned.1.call-update) | async-done | bytes 1048592 | tf_op jit(solution)/shard_map/psum | solution.py:29
  876.4 2.5 multiply_reduce_fusion.14
  884.8 51.3 %all-reduce.30.cloned.1.call-done = f32[4,128,512]{2,1,0:T(8,128)} async-done(((f32[4,128,512]{2,1,0:T(8,128)}), f32[4,128,512]{2,1,0:T(8,128)}) %all-reduce.30.cloned.1.call-update) | async-done | bytes 1048592 | tf_op jit(solution)/shard_map/psum | solution.py:29
  936.1 2.5 multiply_reduce_fusion.15
  946.7 3.2 convolution_add_fusion
  955.0 115.6 %all-reduce.32.cloned.1.call-done = f32[4,384,512]{2,1,0:T(8,128)} async-done(((f32[4,384,512]{2,1,0:T(8,128)}), f32[4,384,512]{2,1,0:T(8,128)}) %all-reduce.32.cloned.1.call-update) | async-done | bytes 3145744 | tf_op jit(solution)/shard_map/psum | solution.py:29
  1070.6 4.3 multiply_reduce_fusion.1
  1078.9 2.7 fusion.52
  1083.6 14.4 fusion.110
  1103.7 132.4 %all-reduce.38.cloned.1.call-done = (f32[4,128,512]{2,1,0:T(8,128)}, f32[4,384,512]{2,1,0:T(8,128)}) async-done(((f32[4,128,512]{2,1,0:T(8,128)}, f32[4,384,512]{2,1,0:T(8,128)}), (f32[4,128,512]{2,1,0:T(8,128)}, f32[4,384,512]{2,1,0:T(8,128)})) %all-reduce.38.cloned.1.call-update) | async-done | bytes 4194320 | tf_op jit(solution)/shard_map/psum | solution.py:29
  1236.1 4.3 multiply_reduce_fusion.2
  1240.8 2.7 multiply_add_fusion.1
  1270.9 2.7 convolution_bitcast_fusion.1
  1286.8 133.7 %all-reduce.36.cloned.1.call-done = (f32[4,128,512]{2,1,0:T(8,128)}, f32[4,384,512]{2,1,0:T(8,128)}) async-done(((f32[4,128,512]{2,1,0:T(8,128)}, f32[4,384,512]{2,1,0:T(8,128)}), (f32[4,128,512]{2,1,0:T(8,128)}, f32[4,384,512]{2,1,0:T(8,128)})) %all-reduce.36.cloned.1.call-update) | async-done | bytes 4194320 | tf_op jit(solution)/shard_map/psum | solution.py:29
  1422.4 2.8 multiply_reduce_fusion.3
  1430.1 25.1 %scatter_custom_fusion = f32[8032,512]{1,0:T(8,128)} fusion(f32[8032,512]{1,0:T(8,128)} %fusion.110, s32[2048]{0:T(1024)} %bitcast.466, f32[512,512]{1,0:T(8,128)} %bitcast.380, f32[]{:T(128)} %constant.66.clone.1, f32[1536,512]{1,0:T(8,128)} %bitcast.374), kind=kCustom, calls=%fused_computation.29 | custom fusion | flops 2097152 | bytes 20644352 | tf_op jit(solution)/shard_map/add | solution.py:346
  1455.2 17.1 copy.501
  1473.0 25.4 %psum.346 = f32[7,512]{1,0:T(8,128)S(1)} all-reduce(f32[7,512]{1,0:T(8,128)S(1)} %stack.132), channel_id=1, replica_groups=mesh['dp'=8,'head'=4] {'dp'}, use_global_device_ids=true, to_apply=%region_82.83 | all-reduce | flops 3584 | bytes 28672 | tf_op jit(solution)/shard_map/psum | solution.py:357
  1498.7 268.9 %all-reduce.34.cloned.1.call-done = (f32[8032,512]{0,1:T(8,128)}, f32[3,3,512,128]{3,2,1,0:T(8,128)}, f32[3,128,512]{1,2,0:T(8,128)}, f32[2,512,512]{2,1,0:T(8,128)}, f32[2,512,512]{1,2,0:T(8,128)}) async-done(((f32[8032,512]{0,1:T(8,128)}, f32[3,3,512,128]{3,2,1,0:T(8,128)}, f32[3,128,512]{1,2,0:T(8,128)}, f32[2,512,512]{2,1,0:T(8,128)}, f32[2,512,512]{1,2,0:T(8,128)}), (f32[8032,512]{0,1:T(8,128)}, ...) | async-done | bytes 23789584 | tf_op jit(solution)/shard_map/psum | solution.py:357
  1771.9 2.7 multiply_reduce_fusion.12
  1775.4 39.8 %all-reduce.2 = (f32[]{:T(128)}, f32[3,3]{1,0:T(4,128)S(1)}, f32[3]{0:T(128)S(1)}, f32[2]{0:T(128)S(1)}, f32[2]{0:T(128)S(1)}, /*index=5*/f32[7]{0:T(128)S(1)}) all-reduce(f32[]{:T(128)} %multiply_reduce_fusion.12, f32[3,3]{1,0:T(4,128)S(1)} %multiply_reduce_fusion.29, ...), channel_id=1, replica_groups=mesh['dp'=8,'head'=4] {'dp','head'}, use_global_device_ids=true, to_apply=%region_58.59 | all-reduce | flops 24 | bytes 192 | tf_op jit(solution)/shard_map/psum | solution.py:380
  1823.6 2.5 multiply_reduce_fusion.31
  1826.1 2.7 multiply_reduce_fusion.33
  1831.1 2.7 multiply_reduce_fusion.28
  1833.8 6.7 multiply_reduce_fusion.10
  1840.4 42.0 %all-reduce.1 = (f32[1]{0:T(128)}, f32[]{:T(128)}, f32[]{:T(128)}, f32[3,3]{1,0:T(4,128)}, f32[3,3]{1,0:T(4,128)}, /*index=5*/f32[3]{0:T(128)}, f32[3]{0:T(128)}...) all-reduce(f32[1]{0:T(128)} %bitcast.64, ...), channel_id=1, replica_groups=mesh['dp'=8,'head'=4] {'dp','head'}, use_global_device_ids=true, to_apply=%region_37.38 | all-reduce | flops 49 | bytes 392 | tf_op jit(solution)/shard_map/psum | solution.py:380
  1898.2 4.0 multiply_subtract_fusion
  (464 shorter events, 165.1 us)
Async XLA Ops:
  7.2 59.9 %all-gather.6.cloned.1.call-start = ((), (), s32[]{:S(2)}) async-start(), calls=%async_computation | async-start | bytes 9289728 | tf_op jit(solution)/shard_map/all_gather | solution.py:203
  9.9 201.5 %all-reduce.22.cloned.1.call-start = ((), (), s32[]{:S(2)}) async-start(), calls=%async_computation.2 | async-start | bytes 6291456 | tf_op jit(solution)/shard_map/psum | solution.py:25
  90.1 12.1 copy-start.137
  90.2 12.8 copy-start.87
  90.2 146.8 %all-gather.8.cloned.1.call-start = ((), (), s32[]{:S(2)}) async-start(), calls=%async_computation.1 | async-start | bytes 1327104 | tf_op jit(solution)/shard_map/all_gather | solution.py:204
  90.9 171.9 %all-gather.12.cloned.1.call-start = ((), (), s32[]{:S(2)}) async-start(), calls=%async_computation.4 | async-start | bytes 1179648 | tf_op jit(solution)/shard_map/all_gather | solution.py:207
  91.9 329.1 %all-reduce.42.cloned.1.call-start = ((), (), s32[]{:S(2)}) async-start(), calls=%async_computation.14 | async-start | bytes 8388608 | tf_op jit(solution)/shard_map/psum | solution.py:25
  102.3 111.5 %copy-start.115 = (f32[1,512]{1,0:T(1,128)}, f32[1,512]{1,0:T(1,128)S(1)}, u32[]{:S(2)}) copy-start(f32[1,512]{1,0:T(1,128)S(1)} %get-tuple-element.206) | copy-start | bytes 6148
  102.3 322.9 %copy-start.107 = (f32[1,512]{1,0:T(1,128)}, f32[1,512]{1,0:T(1,128)S(1)}, u32[]{:S(2)}) copy-start(f32[1,512]{1,0:T(1,128)S(1)} %get-tuple-element.207) | copy-start | bytes 6148
  237.0 5.8 copy-start.1
  256.3 189.8 %all-gather.10.cloned.1.call-start = ((), (), s32[]{:S(2)}) async-start(), calls=%async_computation.3 | async-start | bytes 1179648 | tf_op jit(solution)/shard_map/all_gather | solution.py:206
  258.0 351.5 %all-reduce.40.cloned.1.call-start = ((), (), s32[]{:S(2)}) async-start(), calls=%async_computation.13 | async-start | bytes 8388608 | tf_op jit(solution)/shard_map/psum | solution.py:25
  425.2 10.9 copy-start.110
  427.4 18.7 copy-start.122
  446.1 5.2 copy-start.59
  454.0 226.1 %all-reduce.24.cloned.1.call-start = ((), (), s32[]{:S(2)}) async-start(), calls=%async_computation.5 | async-start | bytes 2097152 | tf_op jit(solution)/shard_map/psum | solution.py:25
  629.2 109.4 %all-reduce.26.cloned.1.call-start = ((), (), s32[]{:S(2)}) async-start(), calls=%async_computation.6 | async-start | bytes 2097152 | tf_op jit(solution)/shard_map/psum | solution.py:25
  680.2 5.5 copy-start.41
  687.2 189.2 %all-reduce.28.cloned.1.call-start = ((), (), s32[]{:S(2)}) async-start(), calls=%async_computation.7 | async-start | bytes 2097152 | tf_op jit(solution)/shard_map/psum | solution.py:29
  742.2 14.1 copy-start.39
  815.0 11.0 copy-start.10
  826.0 110.1 %all-reduce.30.cloned.1.call-start = ((), (), s32[]{:S(2)}) async-start(), calls=%async_computation.8 | async-start | bytes 2097152 | tf_op jit(solution)/shard_map/psum | solution.py:29
  876.4 5.5 copy-start.42
  876.4 5.5 copy-start.81
  884.7 185.9 %all-reduce.32.cloned.1.call-start = ((), (), s32[]{:S(2)}) async-start(), calls=%async_computation.9 | async-start | bytes 6291456 | tf_op jit(solution)/shard_map/psum | solution.py:29
  942.1 4.6 copy-start.73
  950.0 286.1 %all-reduce.38.cloned.1.call-start = ((), (), s32[]{:S(2)}) async-start(), calls=%async_computation.12 | async-start | bytes 8388608 | tf_op jit(solution)/shard_map/psum | solution.py:29
  1070.6 4.4 copy-start.4
  1070.6 4.7 copy-start.35
  1070.6 4.7 copy-start.118
  1081.6 338.9 %all-reduce.36.cloned.1.call-start = ((), (), s32[]{:S(2)}) async-start(), calls=%async_computation.11 | async-start | bytes 8388608 | tf_op jit(solution)/shard_map/psum | solution.py:29
  1083.6 14.4 copy-start.32
  1083.6 14.4 copy-start.62
  1083.6 15.9 copy-start.44
  1083.6 15.9 copy-start.109
  1083.6 15.9 copy-start.113
  1098.0 4.3 copy-start.53
  1236.1 4.4 copy-start.5
  1236.1 4.7 copy-start.16
  1236.1 8.1 slice-start
  1256.3 4.2 copy-start.40
  1256.3 4.2 copy-start.50
  1266.0 501.6 %all-reduce.34.cloned.1.call-start = ((), (), s32[]{:S(2)}) async-start(), calls=%async_computation.10 | async-start | bytes 47710208 | tf_op jit(solution)/shard_map/psum | solution.py:357
  1266.3 4.6 copy-start.17
  1270.9 4.3 copy-start.72
  1285.2 135.3 %copy-start.108 = (f32[1,512]{1,0:T(1,128)S(1)}, f32[1,512]{1,0:T(1,128)}, u32[]{:S(2)}) copy-start(f32[1,512]{1,0:T(1,128)} %copy-done.107) | copy-start | bytes 6148
  1285.2 135.3 %copy-start.111 = (f32[4,128]{1,0:T(4,128)S(1)}, f32[4,128]{1,0:T(4,128)}, u32[]{:S(2)}) copy-start(f32[4,128]{1,0:T(4,128)} %copy-done.110) | copy-start | bytes 6148
  1285.2 137.2 %copy-start.100 = (f32[4,384]{1,0:T(4,128)S(1)}, f32[4,384]{1,0:T(4,128)}, u32[]{:S(2)}) copy-start(f32[4,384]{1,0:T(4,128)} %copy-done.99) | copy-start | bytes 18436
  1285.2 137.2 %copy-start.116 = (f32[1,512]{1,0:T(1,128)S(1)}, f32[1,512]{1,0:T(1,128)}, u32[]{:S(2)}) copy-start(f32[1,512]{1,0:T(1,128)} %copy-done.115) | copy-start | bytes 6148
  1472.3 349.9 %copy-start.106 = (f32[7,64]{1,0:T(8,128)S(1)}, f32[7,64]{1,0:T(8,128)}, u32[]{:S(2)}) copy-start(f32[7,64]{1,0:T(8,128)} %param.35) | copy-start | bytes 5380
  1472.3 349.9 %copy-start.133 = (f32[7,64]{1,0:T(8,128)S(1)}, f32[7,64]{1,0:T(8,128)}, u32[]{:S(2)}) copy-start(f32[7,64]{1,0:T(8,128)} %param.41) | copy-start | bytes 5380
  1472.4 349.9 %copy-start.134 = (f32[7,64]{1,0:T(8,128)S(1)}, f32[7,64]{1,0:T(8,128)}, u32[]{:S(2)}) copy-start(f32[7,64]{1,0:T(8,128)} %param.47) | copy-start | bytes 5380
  1472.4 351.2 %copy-start.57 = (f32[2,512,64]{1,2,0:T(8,128)S(1)}, f32[2,512,64]{1,2,0:T(8,128)}, u32[]{:S(2)}) copy-start(f32[2,512,64]{1,2,0:T(8,128)} %param.34) | copy-start | bytes 786436
  1472.4 351.2 %copy-start.98 = (f32[2,512,64]{1,2,0:T(8,128)S(1)}, f32[2,512,64]{1,2,0:T(8,128)}, u32[]{:S(2)}) copy-start(f32[2,512,64]{1,2,0:T(8,128)} %param.40) | copy-start | bytes 786436
  1472.4 353.7 %copy-start.58 = (f32[2,64,512]{2,1,0:T(8,128)S(1)}, f32[2,64,512]{2,1,0:T(8,128)}, u32[]{:S(2)}) copy-start(f32[2,64,512]{2,1,0:T(8,128)} %param.33) | copy-start | bytes 786436
  1473.0 355.8 %copy-start.88 = (f32[3,128,64]{1,2,0:T(8,128)S(1)}, f32[3,128,64]{1,2,0:T(8,128)}, u32[]{:S(2)}) copy-start(f32[3,128,64]{1,2,0:T(8,128)} %param.32) | copy-start | bytes 294916
  1769.8 61.3 %copy-start.55 = (f32[3,3,64,128]{3,2,1,0:T(8,128)S(1)}, f32[3,3,64,128]{3,2,1,0:T(8,128)}, u32[]{:S(2)}) copy-start(f32[3,3,64,128]{3,2,1,0:T(8,128)} %param.31) | copy-start | bytes 884740
  1774.6 59.1 %copy-start.25 = (f32[8032,64]{0,1:T(8,128)S(1)}, f32[8032,64]{0,1:T(8,128)}, u32[]{:S(2)}) copy-start(f32[8032,64]{0,1:T(8,128)} %param.30) | copy-start | bytes 6168580
  1822.2 11.5 copy-start.63
  1822.4 67.0 %copy-start.124 = (f32[7,64]{1,0:T(8,128)}, f32[7,64]{1,0:T(8,128)S(1)}, u32[]{:S(2)}) copy-start(f32[7,64]{1,0:T(8,128)S(1)} %get-tuple-element.172) | copy-start | bytes 5380
  1822.4 67.0 %copy-start.125 = (f32[7,64]{1,0:T(8,128)}, f32[7,64]{1,0:T(8,128)S(1)}, u32[]{:S(2)}) copy-start(f32[7,64]{1,0:T(8,128)S(1)} %get-tuple-element.173) | copy-start | bytes 5380
  1826.1 64.9 %copy-start.86 = (f32[2,512,64]{1,2,0:T(8,128)}, f32[2,512,64]{1,2,0:T(8,128)S(1)}, u32[]{:S(2)}) copy-start(f32[2,512,64]{1,2,0:T(8,128)S(1)} %get-tuple-element.174) | copy-start | bytes 786436
  1833.8 62.6 %copy-start.80 = (f32[3,3,64,128]{3,2,1,0:T(8,128)}, f32[3,3,64,128]{3,2,1,0:T(8,128)S(1)}, u32[]{:S(2)}) copy-start(f32[3,3,64,128]{3,2,1,0:T(8,128)S(1)} %get-tuple-element.180) | copy-start | bytes 884740
  1889.4 8.8 copy-start.36
  (92 other events, 192.9 us)
Sparse Core Ops, SparseCore 0:
  10.5 56.5 all-gather.5
  90.3 121.0 all-reduce.21
  213.9 23.0 all-gather.7
  239.3 23.4 all-gather.11
  265.7 155.2 all-reduce.41
  423.5 22.4 all-gather.9
  454.2 155.2 all-reduce.39
  629.3 50.8 all-reduce.23
  687.3 51.1 all-reduce.25
  826.1 50.2 all-reduce.27
  884.8 51.1 all-reduce.29
  950.1 120.4 all-reduce.31
  1081.7 154.3 all-reduce.37
  1266.1 154.3 all-reduce.35
  1472.5 295.1 all-reduce.33
where the time goes:
time: 1920 us; the launch traced here: 1910 us
  waiting for transfers between devices  1310 us (68%)
  other arithmetic  182 us (9%)
  blocking collectives  168 us (9%)
  matrix products  145 us (8%)
  local copies, waits for them, and re-layouts  78.5 us (4%)
  between operations  23.8 us (1%)
    psum x5, waiting for transfers between devices, head_back(): return lax.psum(parts, 'head')  482 us
    psum x5, waiting for transfers between devices, head_sum(): return lax.psum(parts, 'head')  471 us
    psum x1, waiting for transfers between devices, body(): lax.psum((grad_table, grad_attn_in, grad_attn_out, grad_up, grad_down, gr...  269 us
    psum x2, blocking collectives, body(): lax.psum((weight_sq[0], weight_sq[1], weight_sq[2], weight_sq[3], weight_...  81.8 us
    all_gather x1, waiting for transfers between devices, body(): lax.all_gather(embed.astype(jnp.bfloat16), 'dp', axis=1, tiled=True)  57 us
  transfers between devices with their start and end apart: 15, of which 15 were waited for; matrix products, arithmetic and copies ran while one was open for 6% of the time, Pallas kernels for 0%

commit v1 on v0

v1 whole, which is shorter than its diff:
```python
import functools

import jax
import jax.numpy as jnp
from jax import lax
from jax.experimental import pallas as pl
from jax.experimental.pallas import tpu as pltpu
from jax.sharding import PartitionSpec as P

D = 512
DH = 64
STEP_NUM = 10

NORM_EPS = 1e-06
SOFTEN_FACTOR = 2.0
DIVERGENCE_SCALE = 1.0
CLIP_NORM = 0.02
BETA_ONE = 0.9
BETA_TWO = 0.999
ADAM_EPS = 1e-08
WEIGHT_DECAY = 0.01
LEARN_RATE = 0.3

BF = jnp.bfloat16
F32 = jnp.float32


def dp_swap(x, bit, dp):
    return lax.ppermute(x, "dp", [(i, i ^ bit) for i in range(dp)])


def head_shift(x, step, heads):
    return lax.ppermute(x, "head", [(i, (i + step) % heads) for i in range(heads)])


def gather_dp(x, dp):
    if dp == 8:
        half = x.shape[-2] // 2
        part_x = dp_swap(x, 2, dp)
        part_y = dp_swap(x, 4, dp)
        diag_a = dp_swap(part_y[..., :half, :], 2, dp)
        diag_b = dp_swap(part_x[..., half:, :], 4, dp)
        near = {0: x, 2: part_x, 4: part_y}
        parts = {}
        for r, value in near.items():
            parts[r] = value
            parts[r + 1] = dp_swap(value, 1, dp)
        parts[6] = jnp.concatenate([diag_a, diag_b], -2)
        parts[7] = jnp.concatenate([dp_swap(diag_a, 1, dp), dp_swap(diag_b, 1, dp)], -2)
        return [parts[r] for r in range(dp)]
    parts = [x]
    bit = 1
    while bit < dp:
        parts = parts + [dp_swap(p, bit, dp) for p in parts]
        bit *= 2
    return parts


def scatter_dp(parts, dp):
    if dp == 8:
        half = parts[0].shape[-2] // 2
        own, to_x, to_y, diag = (
            parts[r] + dp_swap(parts[r + 1].astype(BF), 1, dp).astype(F32) for r in (0, 2, 4, 6)
        )
        diag = diag.astype(BF)
        got_a = dp_swap(diag[..., :half, :], 2, dp).astype(F32)
        got_b = dp_swap(diag[..., half:, :], 4, dp).astype(F32)
        x_low = dp_swap(to_x[..., :half, :].astype(BF), 2, dp).astype(F32)
        y_high = dp_swap(to_y[..., half:, :].astype(BF), 4, dp).astype(F32)
        x_high = dp_swap((to_x[..., half:, :] + got_b).astype(BF), 2, dp).astype(F32)
        y_low = dp_swap((to_y[..., :half, :] + got_a).astype(BF), 4, dp).astype(F32)
        return own + jnp.concatenate([x_low + y_low, x_high + y_high], -2)
    bit = dp // 2
    while bit:
        low, high = parts[:bit], parts[bit:]
        parts = [
            keep + dp_swap(send.astype(BF), bit, dp).astype(F32)
            for keep, send in zip(low, high, strict=True)
        ]
        bit //= 2
    return parts[0]


def gather_head(x, heads):
    return [x] + [head_shift(x, heads - j, heads) for j in range(1, heads)]


def scatter_head(parts, heads):
    total = parts[0].astype(F32)
    for j in range(1, heads):
        total = total + head_shift(parts[j].astype(BF), j, heads).astype(F32)
    return total


def sum_all(x, dp, heads):
    bit = 1
    while bit < dp:
        x = x + dp_swap(x, bit, dp)
        bit *= 2
    total = x
    for j in range(1, heads):
        total = total + head_shift(x, j, heads)
    return total


def lookup_kernel(vocab, tile, ids_ref, table_ref, out_ref, acc_ref):
    step = pl.program_id(0)

    @pl.when(step == 0)
    def _():
        acc_ref[...] = jnp.zeros_like(acc_ref)

    rows = ids_ref.shape[0]
    place = step * tile + lax.broadcasted_iota(jnp.int32, (1, tile), 1)
    block = table_ref[...]
    block = jnp.where(place < vocab, block, jnp.zeros_like(block))
    hit = (ids_ref[...] == place).astype(BF)
    acc_ref[...] += lax.dot_general(
        hit, block, (((1,), (1,)), ((), ())), preferred_element_type=F32
    )

    @pl.when(step == pl.num_programs(0) - 1)
    def _():
        out_ref[...] = acc_ref[...].astype(BF)


def lookup(ids, table_t):
    rows, vocab = ids.shape[0], table_t.shape[1]
    tile = 1024
    return pl.pallas_call(
        functools.partial(lookup_kernel, vocab, tile),
        out_shape=jax.ShapeDtypeStruct((rows, D), BF),
        grid=(pl.cdiv(vocab, tile),),
        in_specs=[
            pl.BlockSpec((rows, 1), lambda i: (0, 0)),
            pl.BlockSpec((D, tile), lambda i: (0, i)),
        ],
        out_specs=pl.BlockSpec((rows, D), lambda i: (0, 0)),
        scratch_shapes=[pltpu.VMEM((rows, D), F32)],
        compiler_params=pltpu.CompilerParams(vmem_limit_bytes=48 * 2**20),
    )(ids.reshape(rows, 1), table_t)


def spread_kernel(tile, ids_ref, rows_ref, base_ref, out_ref):
    place = pl.program_id(0) * tile + lax.broadcasted_iota(jnp.int32, (1, tile), 1)
    hit = (ids_ref[...] == place).astype(BF)
    out_ref[...] = base_ref[...] + lax.dot_general(
        rows_ref[...], hit, (((0,), (0,)), ((), ())), preferred_element_type=F32
    )


def spread(ids, rows_low, base_t):
    rows, vocab = ids.shape[0], base_t.shape[1]
    tile = 512
    return pl.pallas_call(
        functools.partial(spread_kernel, tile),
        out_shape=jax.ShapeDtypeStruct(base_t.shape, F32),
        grid=(pl.cdiv(vocab, tile),),
        in_specs=[
            pl.BlockSpec((rows, 1), lambda i: (0, 0)),
            pl.BlockSpec((rows, D), lambda i: (0, 0)),
            pl.BlockSpec((D, tile), lambda i: (0, i)),
        ],
        out_specs=pl.BlockSpec((D, tile), lambda i: (0, i)),
        compiler_params=pltpu.CompilerParams(vmem_limit_bytes=48 * 2**20),
    )(ids.reshape(rows, 1), rows_low, base_t)


def normed(inputs, gain_row):
    return (
        inputs * lax.rsqrt(jnp.mean(inputs * inputs, -1, keepdims=True) + NORM_EPS) * gain_row
    ).astype(BF)


def norm_back(inputs, gain_row, upstream):
    factor = lax.rsqrt(jnp.mean(inputs * inputs, -1, keepdims=True) + NORM_EPS)
    scaled = upstream * gain_row
    inner = jnp.mean(scaled * inputs, -1, keepdims=True)
    return (
        factor * (scaled - inputs * factor * factor * inner),
        jnp.sum(upstream * inputs * factor, axis=(0, 1)),
    )


def dot(spec, a, b):
    return jnp.einsum(spec, a, b, preferred_element_type=F32)


def split_heads(array):
    return array.reshape(array.shape[0], array.shape[1], -1, DH)


def merge_heads(array):
    return array.reshape(array.shape[0], array.shape[1], -1)


def attn_probs(query, keys_all, allowed):
    scores = dot("bqhe,bkhe->bhqk", query, keys_all) * DH ** (-0.5)
    return jax.nn.softmax(jnp.where(allowed[:, None], scores, -1000000000.0), -1)


def attend_fwd(query_in, source, weights, allowed):
    query = split_heads(dot("bld,dh->blh", query_in, weights[0]).astype(BF))
    keys_all = split_heads(dot("bld,dh->blh", source, weights[1]).astype(BF))
    values = split_heads(dot("bld,dh->blh", source, weights[2]).astype(BF))
    probs = attn_probs(query, keys_all, allowed)
    mixed = merge_heads(dot("bhqk,bkhe->bqhe", probs.astype(BF), values).astype(BF))
    return dot("blh,dh->bld", mixed, weights[3]), (query, keys_all, values, mixed)


def attend_back(upstream, query_in, source, weights, allowed, kept):
    query, keys_all, values, mixed = kept
    up_low = upstream.astype(BF)
    grad_out = dot("bld,blh->dh", up_low, mixed)
    grad_mixed = split_heads(dot("bld,dh->blh", up_low, weights[3]).astype(BF))
    probs = attn_probs(query, keys_all, allowed)
    grad_probs = dot("bqhe,bkhe->bhqk", grad_mixed, values)
    grad_scores = (probs * (grad_probs - jnp.sum(grad_probs * probs, -1, keepdims=True))).astype(BF)
    grad_query = merge_heads(
        (dot("bhqk,bkhe->bqhe", grad_scores, keys_all) * DH ** (-0.5)).astype(BF)
    )
    grad_keys = merge_heads(
        (dot("bhqk,bqhe->bkhe", grad_scores, query) * DH ** (-0.5)).astype(BF)
    )
    grad_values = merge_heads(dot("bhqk,bqhe->bkhe", probs.astype(BF), grad_mixed).astype(BF))
    grads = [
        dot("bld,blh->dh", query_in, grad_query),
        dot("bld,blh->dh", source, grad_keys),
        dot("bld,blh->dh", source, grad_values),
        grad_out,
    ]
    back_query = dot("blh,dh->bld", grad_query, weights[0])
    back_source = dot("blh,dh->bld", grad_keys, weights[1])
    back_source = back_source + dot("blh,dh->bld", grad_values, weights[2])
    return back_query, back_source, grads


def feed_fwd(inputs, weights):
    hidden = jax.nn.relu(dot("bld,df->blf", inputs, weights[0])).astype(BF)
    return dot("blf,df->bld", hidden, weights[1]), hidden


def feed_back(upstream, inputs, weights, hidden):
    up_low = upstream.astype(BF)
    grad_down = dot("bld,blf->df", up_low, hidden)
    grad_hidden = dot("bld,df->blf", up_low, weights[1])
    grad_pre = jnp.where(hidden > 0, grad_hidden, 0.0).astype(BF)
    grad_up = dot("bld,blf->df", inputs, grad_pre)
    back_in = dot("blf,df->bld", grad_pre, weights[0])
    return back_in, [grad_up, grad_down]


def body(
    dp,
    heads,
    source_ids,
    target_ids,
    source_lens,
    target_lens,
    kl_mask,
    teacher,
    *state,
):
    def transposed(group):
        embed, attn_in, attn_out, ff_in, ff_out, gains = group
        swap = functools.partial(jnp.swapaxes, axis1=-1, axis2=-2)
        return (swap(embed), attn_in, swap(attn_out), ff_in, swap(ff_out), gains)

    masters = transposed(state[:6])
    moments = transposed(state[6:12])
    seconds = transposed(state[12:])
    embed_t, attn_in, attn_out_t, ff_in, ff_out_t, gains = masters
    low = embed_t.astype(BF)
    vocab_local = embed_t.shape[1]
    head_pos = lax.axis_index("head")
    lead = (head_pos == 0).astype(F32)
    vocab_start = head_pos * vocab_local
    batch_size, source_len = source_ids.shape
    target_len = target_ids.shape[1]
    token_count = batch_size * target_len
    each = -(-batch_size // heads)
    padded = each * heads

    gain_rows = gains.shape[0]
    width = attn_in.shape[-1]
    gain_block = jnp.pad(gains.T, ((0, 0), (0, width - gain_rows)))
    stacks = [
        jnp.concatenate([attn_in[0], attn_out_t[:1], gain_block[None]], 0),
        jnp.stack([ff_in[0], ff_out_t[0]]),
        jnp.concatenate([attn_in[1], attn_out_t[1:2], attn_in[2], attn_out_t[2:3]], 0),
        jnp.stack([ff_in[1], ff_out_t[1]]),
    ]
    table_t = jnp.stack(gather_dp(low, dp)).reshape(D, vocab_local)
    full = []
    for stack in stacks:
        wide = jnp.concatenate(gather_head(stack.astype(BF), heads), -1)
        full.append(jnp.concatenate(gather_dp(wide, dp), -2))
    w_enc, f_enc, w_dec, f_dec = full
    gain = w_enc[4, :, :gain_rows].T.astype(F32)
    w_self, w_cross = w_dec[:4], w_dec[4:]

    def fill(array):
        return jnp.pad(array, ((0, padded - batch_size),) + ((0, 0),) * (array.ndim - 1))

    dec_ids = jnp.concatenate([jnp.zeros((batch_size, 1), jnp.int32), target_ids[:, :-1]], 1)
    rows_each = each * (source_len + target_len)
    ids_all = jnp.concatenate(
        [
            fill(source_ids).reshape(heads, each * source_len),
            fill(dec_ids).reshape(heads, each * target_len),
        ],
        1,
    )
    ids_rel = jnp.roll(ids_all, -head_pos, 0).reshape(-1) - vocab_start
    looked = lookup(ids_rel, table_t).reshape(heads, rows_each, D)
    mine = scatter_head([looked[j] for j in range(heads)], heads)
    enc_embed = mine[: each * source_len].reshape(each, source_len, D)
    dec_embed = mine[each * source_len :].reshape(each, target_len, D)
    my_lens = lax.dynamic_slice_in_dim(fill(source_lens), head_pos * each, each)

    src_keys = jnp.arange(source_len)[None, :] < my_lens[:, None]
    enc_allowed = jnp.broadcast_to(src_keys[:, None, :], (each, source_len, source_len))
    cross_allowed = jnp.broadcast_to(src_keys[:, None, :], (each, target_len, source_len))
    causal = jnp.broadcast_to(
        (jnp.arange(target_len)[:, None] >= jnp.arange(target_len)[None, :])[None],
        (each, target_len, target_len),
    )
    norm_a = normed(enc_embed, gain[0])
    branch, kept_enc = attend_fwd(norm_a, norm_a, w_enc, enc_allowed)
    enc_mid = enc_embed + branch
    norm_b = normed(enc_mid, gain[1])
    branch, hidden_enc = feed_fwd(norm_b, f_enc)
    enc_last = enc_mid + branch
    encoded = normed(enc_last, gain[2])
    norm_c = normed(dec_embed, gain[3])
    branch, kept_self = attend_fwd(norm_c, norm_c, w_self, causal)
    dec_one = dec_embed + branch
    norm_d = normed(dec_one, gain[4])
    branch, kept_cross = attend_fwd(norm_d, encoded, w_cross, cross_allowed)
    dec_two = dec_one + branch
    norm_e = normed(dec_two, gain[5])
    branch, hidden_dec = feed_fwd(norm_e, f_dec)
    dec_three = dec_two + branch
    head_gain = gain[6] * D ** (-0.5)
    my_final = normed(dec_three, head_gain).reshape(each * target_len, D)

    final = jnp.concatenate(gather_head(my_final, heads), 0)
    final = jnp.roll(final, head_pos * each * target_len, 0)[:token_count]
    student_logits = dot("td,dv->tv", final, table_t)
    counted = jnp.sum((target_lens > 0).astype(F32)).reshape(1, 1)
    real_count = jnp.maximum(lax.psum(counted, "dp")[0, 0], 1.0)
    valid = (jnp.arange(target_len)[None, :] < target_lens[:, None]).astype(F32)
    token_weight = (
        valid / (jnp.maximum(target_lens, 1).astype(F32)[:, None] * real_count)
    ).reshape(token_count)
    divergence_mask = kl_mask.astype(F32).reshape(token_count)
    labels = target_ids.reshape(token_count) - vocab_start
    teacher_full = teacher.astype(F32)
    peak_s = jnp.max(student_logits, -1)
    peak_t = jnp.max(teacher_full, -1)
    shifted = student_logits - peak_s[:, None]
    teacher_exp = jnp.exp((teacher_full - peak_t[:, None]) / SOFTEN_FACTOR)
    local_hit = (labels[:, None] == jnp.arange(vocab_local)[None, :]).astype(F32)
    stats = jnp.stack(
        [
            peak_s,
            peak_t,
            jnp.sum(jnp.exp(shifted), -1),
            jnp.sum(jnp.exp(shifted / SOFTEN_FACTOR), -1),
            jnp.sum(teacher_exp, -1),
            jnp.sum(teacher_exp * (teacher_full - student_logits), -1) / SOFTEN_FACTOR,
            jnp.sum(local_hit * student_logits, -1),
            jnp.zeros_like(peak_s),
        ]
    )
    every = jnp.stack(gather_head(stats, heads))
    peak_student = jnp.max(every[:, 0], 0)
    peak_teacher = jnp.max(every[:, 1], 0)
    off_s = every[:, 0] - peak_student
    off_t = jnp.exp((every[:, 1] - peak_teacher) / SOFTEN_FACTOR)
    sum_one = jnp.sum(every[:, 2] * jnp.exp(off_s), 0)
    sum_half = jnp.sum(every[:, 3] * jnp.exp(off_s / SOFTEN_FACTOR), 0)
    sum_teacher = jnp.sum(every[:, 4] * off_t, 0)
    sum_cross = jnp.sum(every[:, 5] * off_t, 0)
    label_logprob = jnp.sum(every[:, 6], 0)
    lse_one = peak_student + jnp.log(sum_one)
    lse_half = peak_student / SOFTEN_FACTOR + jnp.log(sum_half)
    lse_teacher = peak_teacher / SOFTEN_FACTOR + jnp.log(sum_teacher)
    cross_entropy = lse_one - label_logprob
    divergence_value = sum_cross / sum_teacher - lse_teacher + lse_half
    loss_part = lead * jnp.sum(
        token_weight
        * (
            cross_entropy
            + DIVERGENCE_SCALE * SOFTEN_FACTOR * SOFTEN_FACTOR * divergence_value * divergence_mask
        )
    )
    grad_logits = (
        token_weight[:, None]
        * (
            jnp.exp(student_logits - lse_one[:, None])
            - local_hit
            + DIVERGENCE_SCALE
            * SOFTEN_FACTOR
            * (
                jnp.exp(student_logits / SOFTEN_FACTOR - lse_half[:, None])
                - jnp.exp(teacher_full / SOFTEN_FACTOR - lse_teacher[:, None])
            )
            * divergence_mask[:, None]
        )
    ).astype(BF)
    grad_table_t = dot("td,tv->dv", final, grad_logits)
    part = dot("tv,dv->td", grad_logits, table_t).reshape(batch_size, target_len, D)
    part = jnp.roll(
        fill(part).astype(BF).reshape(heads, each * target_len, D), -head_pos, 0
    )
    grad_final = scatter_head([part[j] for j in range(heads)], heads).reshape(each, target_len, D)

    grad_three, gain_six = norm_back(dec_three, head_gain, grad_final)
    back_in, grads_f_dec = feed_back(grad_three, norm_e, f_dec, hidden_dec)
    grad_norm_in, gain_five = norm_back(dec_two, gain[5], back_in)
    grad_two = grad_three + grad_norm_in
    back_query, grad_encoded, grads_cross = attend_back(
        grad_two, norm_d, encoded, w_cross, cross_allowed, kept_cross
    )
    grad_norm_in, gain_four = norm_back(dec_one, gain[4], back_query)
    grad_one = grad_two + grad_norm_in
    back_query, back_source, grads_self = attend_back(
        grad_one, norm_c, norm_c, w_self, causal, kept_self
    )
    grad_norm_in, gain_three = norm_back(dec_embed, gain[3], back_query + back_source)
    grad_dec_embed = grad_one + grad_norm_in
    grad_last, gain_two = norm_back(enc_last, gain[2], grad_encoded)
    back_in, grads_f_enc = feed_back(grad_last, norm_b, f_enc, hidden_enc)
    grad_norm_in, gain_one = norm_back(enc_mid, gain[1], back_in)
    grad_mid = grad_last + grad_norm_in
    back_query, back_source, grads_enc = attend_back(
        grad_mid, norm_a, norm_a, w_enc, enc_allowed, kept_enc
    )
    grad_norm_in, gain_zero = norm_back(enc_embed, gain[0], back_query + back_source)
    grad_enc_embed = grad_mid + grad_norm_in

    my_rows = jnp.concatenate(
        [grad_enc_embed.reshape(-1, D), grad_dec_embed.reshape(-1, D)], 0
    ).astype(BF)
    all_rows = jnp.concatenate(gather_head(my_rows, heads), 0)
    grad_table_t = spread(ids_rel, all_rows, grad_table_t)
    deep = D // dp
    grad_table_t = scatter_dp(
        [grad_table_t[r * deep : (r + 1) * deep] for r in range(dp)], dp
    )
    gain_grads = jnp.stack(
        [gain_zero, gain_one, gain_two, gain_three, gain_four, gain_five, gain_six * D ** (-0.5)]
    )
    gain_cols = jnp.tile(jnp.pad(gain_grads.T, ((0, 0), (0, width - gain_rows))), (1, heads))
    grad_stacks = [
        grads_f_dec,
        grads_cross,
        grads_self,
        grads_f_enc,
        grads_enc + [gain_cols],
    ]
    reduced = []
    for group in grad_stacks:
        whole = jnp.stack(group)
        shard = scatter_dp([whole[:, r * deep : (r + 1) * deep] for r in range(dp)], dp)
        wide = shard.shape[-1] // heads
        reduced.append(
            scatter_head([shard[..., j * wide : (j + 1) * wide] for j in range(heads)], heads)
        )
    r_fdec, r_cross, r_self, r_fenc, r_enc = reduced
    shards = [
        grad_table_t,
        jnp.stack([r_enc[:3], r_self[:3], r_cross[:3]]),
        jnp.stack([r_enc[3], r_self[3], r_cross[3]]),
        jnp.stack([r_fenc[0], r_fdec[0]]),
        jnp.stack([r_fenc[1], r_fdec[1]]),
        r_enc[4, :, :gain_rows].T,
    ]

    axes = ((0, 1), (2, 3), (1, 2), (1, 2), (1, 2), (1,))
    sizes = (1, 9, 3, 2, 2, gain_rows)

    def squares(arrays):
        out = []
        for position in range(6):
            value = jnp.sum(arrays[position] * arrays[position], axis=axes[position])
            out.append(value.reshape(-1) * (lead if position == 5 else 1.0))
        return out

    lanes = 128
    packed = jnp.concatenate(squares(masters) + squares(shards) + [loss_part.reshape(1)])
    count = packed.shape[0]
    totals = sum_all(jnp.pad(packed, (0, lanes - count)).reshape(1, lanes), dp, heads)[0]
    per = sum(sizes)
    grad_norm = jnp.sqrt(jnp.sum(totals[per : 2 * per]))
    total_loss = totals[2 * per]
    clip_scale = jnp.minimum(1.0, CLIP_NORM / grad_norm)
    bias_one = 1.0 - BETA_ONE**STEP_NUM
    bias_two = 1.0 - BETA_TWO**STEP_NUM
    updates, fresh_m, fresh_v = [], [], []
    for position in range(6):
        grad_now = shards[position] * clip_scale
        moment_new = BETA_ONE * moments[position] + (1 - BETA_ONE) * grad_now
        second_new = BETA_TWO * seconds[position] + (1 - BETA_TWO) * grad_now * grad_now
        update = (
            moment_new / bias_one / (jnp.sqrt(second_new / bias_two) + ADAM_EPS)
            + WEIGHT_DECAY * masters[position]
        )
        updates.append(update)
        fresh_m.append(moment_new)
        fresh_v.append(second_new)
    packed = jnp.concatenate(squares(updates))
    update_tot = sum_all(jnp.pad(packed, (0, lanes - per)).reshape(1, lanes), dp, heads)[0]
    rates = LEARN_RATE * jnp.sqrt(totals[:per]) / (jnp.sqrt(update_tot[:per]) + 1e-06)
    fresh_w = []
    start = 0
    for position in range(6):
        rate = rates[start : start + sizes[position]]
        start += sizes[position]
        shape = [1] * masters[position].ndim
        kept = [d for d in range(masters[position].ndim) if d not in axes[position]]
        for d in kept:
            shape[d] = masters[position].shape[d]
        fresh_w.append(masters[position] - rate.reshape(shape) * updates[position])
    return (
        total_loss.reshape(1),
        grad_norm.reshape(1),
        *transposed(fresh_w),
        *transposed(fresh_m),
        *transposed(fresh_v),
    )


def solution(mesh):
    params = (
        P("head", "dp"),
        P(None, None, "dp", "head"),
        P(None, "head", "dp"),
        P(None, "dp", "head"),
        P(None, "head", "dp"),
        P(None, "dp"),
    )
    return jax.shard_map(
        functools.partial(body, mesh.shape["dp"], mesh.shape["head"]),
        mesh=mesh,
        in_specs=(
            P("dp", None),
            P("dp", None),
            P("dp"),
            P("dp"),
            P("dp", None),
            P("dp", "head"),
            *params,
            *params,
            *params,
        ),
        out_specs=(P(), P(), *params, *params, *params),
        check_vma=False,
    )
```

time: 1920 us -> 982 us (0.51)
  waiting for transfers between devices: 1310 us -> 306 us
  starting transfers between devices: 1.71 us -> 161 us
  blocking collectives: 168 us -> 13.2 us
  local copies, waits for them, and re-layouts: 78.5 us -> 156 us
  Pallas kernels: 0 us -> 47.8 us
  other arithmetic: 182 us -> 160 us
  matrix products: 145 us -> 125 us
    psum x11 -> x0, waiting for transfers between devices: 1220 us -> none  [the longest x5 482 us: head_back(): return lax.psum(parts, 'head')]
    ppermute x0 -> x159, waiting for transfers between devices: none -> 306 us  [the longest x111 226 us: dp_swap(): return lax.ppermute(x, 'dp', [(i, i ^ bit) for i in range(dp)])]
    ppermute x0 -> x159, starting transfers between devices: none -> 161 us  [the longest x111 81.5 us: dp_swap(): return lax.ppermute(x, 'dp', [(i, i ^ bit) for i in range(dp)])]
    psum x5 -> x1, blocking collectives: 139 us -> 13.2 us  [body(): real_count = jnp.maximum(lax.psum(counted, 'dp')[0, 0], 1.0)]
    all_gather x4 -> x0, waiting for transfers between devices: 89.7 us -> none  [the longest x1 57 us: body(): lax.all_gather(embed.astype(jnp.bfloat16), 'dp', axis=1, tiled=True)]
    pallas_call x0 -> x2, Pallas kernels: none -> 47.8 us  [the longest x1 25.7 us: spread(): pl.pallas_call(functools.partial(spread_kernel, tile), out_shape=jax.Shap...]
    slice x1 -> x64, local copies, waits for them, and re-layouts: 4.26 us -> 47.8 us  [the longest x9 15.7 us: body(): whole[:, r * deep:(r + 1) * deep]]
    unnamed x286 -> x473, local copies, waits for them, and re-layouts: 29.6 us -> 67.9 us
  transfers between devices with their start and end apart: 15 -> 159, of which waited for: 15 -> 59; matrix products, arithmetic and copies ran while one was open for 6% -> 23% of each run, Pallas kernels for 0% -> 5%
where the time goes in v1:
time: 982 us; the launch traced here: 976 us
  waiting for transfers between devices  306 us (31%)
  starting transfers between devices  161 us (16%)
  other arithmetic  160 us (16%)
  local copies, waits for them, and re-layouts  156 us (16%)
  matrix products  125 us (13%)
  Pallas kernels  47.8 us (5%)
  blocking collectives  13.2 us (1%)
    ppermute x111, waiting for transfers between devices, dp_swap(): return lax.ppermute(x, 'dp', [(i, i ^ bit) for i in range(dp)])  226 us
    dot_general x66, matrix products, dot(): return jnp.einsum(spec, a, b, preferred_element_type=F32)  117 us
    ppermute x111, starting transfers between devices, dp_swap(): return lax.ppermute(x, 'dp', [(i, i ^ bit) for i in range(dp)])  81.5 us
    ppermute x48, waiting for transfers between devices, head_shift(): lax.ppermute(x, 'head', [(i, (i + step) % heads) for i in range(heads)])  80.3 us
    ppermute x48, starting transfers between devices, head_shift(): lax.ppermute(x, 'head', [(i, (i + step) % heads) for i in range(heads)])  79.5 us
    unnamed x473, local copies, waits for them, and re-layouts  67.9 us
    another operation x15, other arithmetic  31 us
    pallas_call x1, Pallas kernels, spread(): pl.pallas_call(functools.partial(spread_kernel, tile), out_shape=jax.Shap...  25.7 us
  transfers between devices with their start and end apart: 159, of which 59 were waited for; matrix products, arithmetic and copies ran while one was open for 23% of the time, Pallas kernels for 5%

profile of v1, /device:TPU:0, one launch (start us, length us, event | category | flops | bytes accessed | tf_op | source)
XLA Modules:
  0.0 975.5 jit_solution(4037696700916675109)
XLA Ops:
  5.3 3.1 collective-permute-start.14
  22.0 13.2 %psum.7 = f32[1,1]{1,0:T(1,128)} all-reduce(f32[1,1]{1,0:T(1,128)} %bitcast.56), channel_id=1, replica_groups=mesh['dp'=8,'head'=4] {'dp'}, use_global_device_ids=true, to_apply=%region_20.21 | all-reduce | flops 1 | bytes 8 | tf_op jit(solution)/shard_map/psum | solution.py:351
  48.9 4.2 collective-permute-done.37
  56.1 4.3 collective-permute-done.49
  66.6 15.9 %collective-permute-done.18 = bf16[5,64,512]{2,1,0:T(8,128)(2,1)S(1)} collective-permute-done((bf16[5,64,512]{2,1,0:T(8,128)(2,1)S(1)}, bf16[5,64,512]{2,1,0:T(8,128)(2,1)S(1)}, u32[]{:S(2)}, u32[]{:S(2)}) %collective-permute-start.18) | collective-permute-done | bytes 327712 | tf_op jit(solution)/shard_map/ppermute | solution.py:29
  98.4 4.3 collective-permute-done.54
  103.7 6.0 collective-permute-done.52
  119.3 14.7 %collective-permute-done.20 = bf16[5,32,512]{2,1,0:T(8,128)(2,1)S(1)} collective-permute-done((bf16[5,32,512]{2,1,0:T(8,128)(2,1)S(1)}, bf16[5,32,512]{2,1,0:T(8,128)(2,1)S(1)}, u32[]{:S(2)}, u32[]{:S(2)}) %collective-permute-start.20) | collective-permute-done | bytes 163872 | tf_op jit(solution)/shard_map/ppermute | solution.py:29
  140.2 19.5 %collective-permute-done.3 = bf16[64,8032]{1,0:T(8,128)(2,1)S(1)} collective-permute-done((bf16[64,8032]{1,0:T(8,128)(2,1)S(1)}, bf16[64,8032]{1,0:T(8,128)(2,1)S(1)}, u32[]{:S(2)}, u32[]{:S(2)}) %collective-permute-start.3) | collective-permute-done | bytes 1028128 | tf_op jit(solution)/shard_map/ppermute | solution.py:29
  172.0 3.4 collective-permute-done.56
  190.9 8.8 collective-permute-done.6
  204.4 3.3 copy-done.9
  207.7 22.1 %shard_map.383 = bf16[2048,512]{1,0:T(8,128)(2,1)S(1)} custom-call(s32[2048,1]{1,0:T(8,128)S(1)} %bitcast.575, bf16[512,8032]{1,0:T(8,128)(2,1)} %bitcast.581), custom_call_target="tpu_custom_call" | custom-call | tf_op jit(solution)/shard_map/pallas_call | solution.py:130
  230.0 3.8 collective-permute-start.11
  237.4 8.8 collective-permute-done.11
  246.2 32.7 %collective-permute-done.10 = bf16[512,512]{1,0:T(8,128)(2,1)S(1)} collective-permute-done((bf16[512,512]{1,0:T(8,128)(2,1)S(1)}, bf16[512,512]{1,0:T(8,128)(2,1)S(1)}, u32[]{:S(2)}, u32[]{:S(2)}) %collective-permute-start.10) | collective-permute-done | bytes 524320 | tf_op jit(solution)/shard_map/ppermute | solution.py:33
  289.3 3.9 fusion.241
  326.3 5.1 reduce_max.88
  345.6 13.7 %fusion.243 = (f32[512]{0:T(512)S(1)}, f32[512,8032]{0,1:T(8,128)}) fusion(bf16[512,8032]{1,0:T(8,128)(2,1)} %bitcast.582, bf16[1024,512]{1,0:T(8,128)(2,1)} %constant_dynamic-update-slice_fusion.36, s32[]{:T(128)S(6)} %select_n.67), kind=kOutput, calls=%fused_computation.648 | convolution fusion | flops 4215193088 | bytes 25233412 | tf_op jit(solution)/shard_map/td,dv->tv/dot_general | solution.py:186
  359.4 14.1 %exponential_reduce_fusion = (f32[512]{0:T(512)S(1)}, f32[512]{0:T(512)S(1)}, f32[512]{0:T(512)S(1)}, f32[512]{0:T(512)S(1)}, f32[512]{0:T(512)S(1)}) fusion(f32[512,8032]{0,1:T(8,128)} %get-tuple-element.321, f32[512]{0:T(512)S(1)} %get-tuple-element.320, s32[512]{0:T(512)S(1)} %copy-done.167, f32[512]{0:T(512)S(1)} %copy-done.168, bf16[512,8032]{0,1:T(8,128)(2,1)} %param.29), kind=kLoop, calls=%fused_computation.20 | loop fusion | flops 57570816 | bytes 24690688 | tf_op jit(solution)/shard_map/reduce_sum | solution.py:369
  374.2 3.4 collective-permute-start.63
  380.8 14.0 %fusion.14 = bf16[512,8032]{0,1:T(8,128)(2,1)S(1)} fusion(bf16[512,8032]{0,1:T(8,128)(2,1)} %param.29, f32[512,8032]{0,1:T(8,128)} %get-tuple-element.321, f32[512]{0:T(512)S(1)} %get-tuple-element.300, f32[512]{0:T(512)S(1)} %log_add_fusion, f32[512]{0:T(512)S(1)} %get-tuple-element.169, f32[512]{0:T(512)S(1)} %get-tuple-element.168, ...), kind=kLoop, calls=%fused_computation.17 | loop fusion | flops 57573376 | bytes 32911360 | tf_op jit(solution)/shard_map/convert_element_type | solution.py:411
  394.9 7.1 fusion.46
  403.0 3.3 collective-permute-start.68
  406.8 8.5 fusion.110.base_ref
  464.7 3.6 multiply_reduce_fusion
  468.4 3.2 multiply_convert_fusion
  473.2 3.5 convolution_convert_fusion.7
  487.4 3.5 collective-permute-start.69
  497.2 3.4 convolution_bitcast_fusion.1
  500.7 3.3 convolution_bitcast_fusion
  524.4 4.3 fusion.15
  553.9 4.1 fusion.43
  578.3 6.5 collective-permute-done.113
  591.3 6.7 collective-permute-done.100
  627.6 25.7 %shard_map.384 = f32[512,8032]{1,0:T(8,128)} custom-call(s32[2048,1]{1,0:T(8,128)S(1)} %bitcast.576, bf16[2048,512]{1,0:T(8,128)(2,1)S(1)} %constant_dynamic-update-slice_fusion.44.rows_ref, f32[512,8032]{1,0:T(8,128)} %fusion.110.base_ref), custom_call_target="tpu_custom_call" | custom-call | tf_op jit(solution)/shard_map/pallas_call | solution.py:155
  653.3 6.4 convert.166
  670.4 9.5 collective-permute-done.117
  683.0 10.0 %collective-permute-done.110 = bf16[4,32,512]{1,2,0:T(8,128)(2,1)S(1)} collective-permute-done((bf16[4,32,512]{1,2,0:T(8,128)(2,1)S(1)}, bf16[4,32,512]{1,2,0:T(8,128)(2,1)S(1)}, u32[]{:S(2)}, u32[]{:S(2)}) %collective-permute-start.110) | collective-permute-done | bytes 131104 | tf_op jit(solution)/shard_map/ppermute | solution.py:29
  696.1 9.3 collective-permute-done.104
  710.3 9.4 collective-permute-done.97
  719.7 4.1 collective-permute-start.120
  732.7 3.8 collective-permute-done.119
  742.1 4.0 collective-permute-done.106
  762.7 9.6 collective-permute-done.93
  775.1 9.7 collective-permute-done.141
  787.3 4.1 collective-permute-done.139
  794.2 3.7 collective-permute-done.128
  799.5 7.8 collective-permute-done.126
  816.7 3.5 collective-permute-done.140
  833.7 3.6 collective-permute-done.127
  838.5 3.6 collective-permute-start.145
  844.8 4.0 collective-permute-start.144
  852.2 3.1 collective-permute-start.132
  857.2 3.2 collective-permute-start.79
  860.5 3.9 collective-permute-done.132
  869.6 3.4 collective-permute-done.79
  873.3 8.9 collective-permute-done.77
  884.1 14.5 %collective-permute-done.80 = bf16[32,8032]{1,0:T(8,128)(2,1)S(1)} collective-permute-done((bf16[32,8032]{1,0:T(8,128)(2,1)S(1)}, bf16[32,8032]{1,0:T(8,128)(2,1)S(1)}, u32[]{:S(2)}, u32[]{:S(2)}) %collective-permute-start.80) | collective-permute-done | bytes 514080 | tf_op jit(solution)/shard_map/ppermute | solution.py:29
  904.3 3.3 collective-permute-done.148
  911.1 3.8 collective-permute-start.152
  935.9 5.8 multiply_reduce_fusion.1
  943.9 3.3 collective-permute-done.154
  968.7 3.1 fusion.31
  (1070 shorter events, 496.2 us)
Async XLA Ops:
  8.4 28.7 %collective-permute-start.13 = (bf16[5,64,128]{2,1,0:T(8,128)(2,1)S(1)}, bf16[5,64,128]{2,1,0:T(8,128)(2,1)}, u32[]{:S(2)}, u32[]{:S(2)}) collective-permute-start(bf16[5,64,128]{2,1,0:T(8,128)(2,1)S(1)} %pad_maximum_fusion.36), channel_id=1, source_target_pairs={{0,2},{1,3},{2,0},{3,1},{4,6},{5,7},{6,4},{7,5},{8,10},{9,11},{10,... | collective-permute-start | bytes 245768 | tf_op jit(solution)/shard_map/ppermute | solution.py:33
  11.0 26.5 %collective-permute-start.12 = (bf16[5,64,128]{2,1,0:T(8,128)(2,1)S(1)}, bf16[5,64,128]{2,1,0:T(8,128)(2,1)}, u32[]{:S(2)}, u32[]{:S(2)}) collective-permute-start(bf16[5,64,128]{2,1,0:T(8,128)(2,1)S(1)} %pad_maximum_fusion.36), channel_id=1, source_target_pairs={{0,3},{1,0},{2,1},{3,2},{4,7},{5,4},{6,5},{7,6},{8,11},{9,8},{10,9... | collective-permute-start | bytes 245768 | tf_op jit(solution)/shard_map/ppermute | solution.py:33
  15.1 25.2 %collective-permute-start.26 = (bf16[2,64,512]{2,1,0:T(8,128)(2,1)S(1)}, bf16[2,64,512]{2,1,0:T(8,128)(2,1)S(1)}, u32[]{:S(2)}, u32[]{:S(2)}) collective-permute-start(bf16[2,64,512]{2,1,0:T(8,128)(2,1)S(1)} %pad_maximum_fusion.33), channel_id=1, source_target_pairs={{0,1},{1,2},{2,3},{3,0},{4,5},{5,6},{6,7},{7,4},{8,9},{9,10},{10,1... | collective-permute-start | bytes 393224 | tf_op jit(solution)/shard_map/ppermute | solution.py:33
  15.9 27.4 %collective-permute-start.25 = (bf16[2,64,512]{2,1,0:T(8,128)(2,1)S(1)}, bf16[2,64,512]{2,1,0:T(8,128)(2,1)S(1)}, u32[]{:S(2)}, u32[]{:S(2)}) collective-permute-start(bf16[2,64,512]{2,1,0:T(8,128)(2,1)S(1)} %pad_maximum_fusion.33), channel_id=1, source_target_pairs={{0,2},{1,3},{2,0},{3,1},{4,6},{5,7},{6,4},{7,5},{8,10},{9,11},{10,... | collective-permute-start | bytes 393224 | tf_op jit(solution)/shard_map/ppermute | solution.py:33
  18.5 24.8 %collective-permute-start.24 = (bf16[2,64,512]{2,1,0:T(8,128)(2,1)S(1)}, bf16[2,64,512]{2,1,0:T(8,128)(2,1)S(1)}, u32[]{:S(2)}, u32[]{:S(2)}) collective-permute-start(bf16[2,64,512]{2,1,0:T(8,128)(2,1)S(1)} %pad_maximum_fusion.33), channel_id=1, source_target_pairs={{0,3},{1,0},{2,1},{3,2},{4,7},{5,4},{6,5},{7,6},{8,11},{9,8},{10,9... | collective-permute-start | bytes 393224 | tf_op jit(solution)/shard_map/ppermute | solution.py:33
  37.4 15.6 %collective-permute-start.37 = (bf16[8,64,128]{2,1,0:T(8,128)(2,1)S(1)}, bf16[8,64,128]{2,1,0:T(8,128)(2,1)S(1)}, u32[]{:S(2)}, u32[]{:S(2)}) collective-permute-start(bf16[8,64,128]{2,1,0:T(8,128)(2,1)S(1)} %pad_maximum_fusion.34), channel_id=1, source_target_pairs={{0,2},{1,3},{2,0},{3,1},{4,6},{5,7},{6,4},{7,5},{8,10},{9,11},{10,... | collective-permute-start | bytes 393224 | tf_op jit(solution)/shard_map/ppermute | solution.py:33
  43.3 17.1 %collective-permute-start.49 = (bf16[2,64,512]{2,1,0:T(8,128)(2,1)S(1)}, bf16[2,64,512]{2,1,0:T(8,128)(2,1)S(1)}, u32[]{:S(2)}, u32[]{:S(2)}) collective-permute-start(bf16[2,64,512]{2,1,0:T(8,128)(2,1)S(1)} %pad_maximum_fusion.35), channel_id=1, source_target_pairs={{0,2},{1,3},{2,0},{3,1},{4,6},{5,7},{6,4},{7,5},{8,10},{9,11},{10,... | collective-permute-start | bytes 393224 | tf_op jit(solution)/shard_map/ppermute | solution.py:33
  45.9 16.1 %collective-permute-start.48 = (bf16[2,64,512]{2,1,0:T(8,128)(2,1)S(1)}, bf16[2,64,512]{2,1,0:T(8,128)(2,1)S(1)}, u32[]{:S(2)}, u32[]{:S(2)}) collective-permute-start(bf16[2,64,512]{2,1,0:T(8,128)(2,1)S(1)} %pad_maximum_fusion.35), channel_id=1, source_target_pairs={{0,3},{1,0},{2,1},{3,2},{4,7},{5,4},{6,5},{7,6},{8,11},{9,8},{10,9... | collective-permute-start | bytes 393224 | tf_op jit(solution)/shard_map/ppermute | solution.py:33
  54.1 29.2 %collective-permute-start.28 = (bf16[2,64,2048]{2,1,0:T(8,128)(2,1)}, bf16[2,64,2048]{2,1,0:T(8,128)(2,1)S(1)}, u32[]{:S(2)}, u32[]{:S(2)}) collective-permute-start(bf16[2,64,2048]{2,1,0:T(8,128)(2,1)} %get-tuple-element.274), channel_id=1, source_target_pairs={{0,8},{4,12},{8,0},{12,4},{16,24},{20,28},{24,16},{28,20},{1,9},{5... | collective-permute-start | bytes 1572872 | tf_op jit(solution)/shard_map/ppermute | solution.py:29
  60.4 23.1 %collective-permute-start.30 = (bf16[2,64,2048]{2,1,0:T(8,128)(2,1)}, bf16[2,64,2048]{2,1,0:T(8,128)(2,1)S(1)}, u32[]{:S(2)}, u32[]{:S(2)}) collective-permute-start(bf16[2,64,2048]{2,1,0:T(8,128)(2,1)} %get-tuple-element.274), channel_id=1, source_target_pairs={{0,16},{4,20},{8,24},{12,28},{16,0},{20,4},{24,8},{28,12},{1,17},{... | collective-permute-start | bytes 1572872 | tf_op jit(solution)/shard_map/ppermute | solution.py:29
  62.0 23.4 %collective-permute-start.39 = (bf16[8,64,512]{2,1,0:T(8,128)(2,1)}, bf16[8,64,512]{2,1,0:T(8,128)(2,1)S(1)}, u32[]{:S(2)}, u32[]{:S(2)}) collective-permute-start(bf16[8,64,512]{2,1,0:T(8,128)(2,1)} %get-tuple-element.276), channel_id=1, source_target_pairs={{0,4},{4,0},{8,12},{12,8},{16,20},{20,16},{24,28},{28,24},{1,5},{5... | collective-permute-start | bytes 1572872 | tf_op jit(solution)/shard_map/ppermute | solution.py:29
  62.5 20.1 %collective-permute-start.18 = (bf16[5,64,512]{2,1,0:T(8,128)(2,1)S(1)}, bf16[5,64,512]{2,1,0:T(8,128)(2,1)S(1)}, u32[]{:S(2)}, u32[]{:S(2)}) collective-permute-start(bf16[5,64,512]{2,1,0:T(8,128)(2,1)S(1)} %get-tuple-element.286), channel_id=1, source_target_pairs={{0,16},{4,20},{8,24},{12,28},{16,0},{20,4},{24,8},{28,12},{1,17},{... | collective-permute-start | bytes 983048 | tf_op jit(solution)/shard_map/ppermute | solution.py:29
  63.6 30.2 %collective-permute-start.42 = (bf16[8,64,512]{2,1,0:T(8,128)(2,1)}, bf16[8,64,512]{2,1,0:T(8,128)(2,1)S(1)}, u32[]{:S(2)}, u32[]{:S(2)}) collective-permute-start(bf16[8,64,512]{2,1,0:T(8,128)(2,1)} %get-tuple-element.276), channel_id=1, source_target_pairs={{0,16},{4,20},{8,24},{12,28},{16,0},{20,4},{24,8},{28,12},{1,17},{... | collective-permute-start | bytes 1572872 | tf_op jit(solution)/shard_map/ppermute | solution.py:29
  82.5 28.4 %collective-permute-start.27 = (bf16[2,64,2048]{2,1,0:T(8,128)(2,1)}, bf16[2,64,2048]{2,1,0:T(8,128)(2,1)}, u32[]{:S(2)}, u32[]{:S(2)}) collective-permute-start(bf16[2,64,2048]{2,1,0:T(8,128)(2,1)} %get-tuple-element.274), channel_id=1, source_target_pairs={{0,4},{4,0},{8,12},{12,8},{16,20},{20,16},{24,28},{28,24},{1,5},{5... | collective-permute-start | bytes 1572872 | tf_op jit(solution)/shard_map/ppermute | solution.py:29
  83.3 15.0 %collective-permute-start.40 = (bf16[8,64,512]{2,1,0:T(8,128)(2,1)}, bf16[8,64,512]{2,1,0:T(8,128)(2,1)S(1)}, u32[]{:S(2)}, u32[]{:S(2)}) collective-permute-start(bf16[8,64,512]{2,1,0:T(8,128)(2,1)} %get-tuple-element.276), channel_id=1, source_target_pairs={{0,8},{4,12},{8,0},{12,4},{16,24},{20,28},{24,16},{28,20},{1,9},{5... | collective-permute-start | bytes 1572872 | tf_op jit(solution)/shard_map/ppermute | solution.py:29
  83.6 26.1 %collective-permute-start.52 = (bf16[2,64,2048]{2,1,0:T(8,128)(2,1)}, bf16[2,64,2048]{2,1,0:T(8,128)(2,1)}, u32[]{:S(2)}, u32[]{:S(2)}) collective-permute-start(bf16[2,64,2048]{2,1,0:T(8,128)(2,1)} %get-tuple-element.272), channel_id=1, source_target_pairs={{0,8},{4,12},{8,0},{12,4},{16,24},{20,28},{24,16},{28,20},{1,9},{5... | collective-permute-start | bytes 1572872 | tf_op jit(solution)/shard_map/ppermute | solution.py:29
  85.3 17.4 %collective-permute-start.54 = (bf16[2,64,2048]{2,1,0:T(8,128)(2,1)}, bf16[2,64,2048]{2,1,0:T(8,128)(2,1)}, u32[]{:S(2)}, u32[]{:S(2)}) collective-permute-start(bf16[2,64,2048]{2,1,0:T(8,128)(2,1)} %get-tuple-element.272), channel_id=1, source_target_pairs={{0,16},{4,20},{8,24},{12,28},{16,0},{20,4},{24,8},{28,12},{1,17},{... | collective-permute-start | bytes 1572872 | tf_op jit(solution)/shard_map/ppermute | solution.py:29
  93.8 19.9 %collective-permute-start.51 = (bf16[2,64,2048]{2,1,0:T(8,128)(2,1)}, bf16[2,64,2048]{2,1,0:T(8,128)(2,1)S(1)}, u32[]{:S(2)}, u32[]{:S(2)}) collective-permute-start(bf16[2,64,2048]{2,1,0:T(8,128)(2,1)} %get-tuple-element.272), channel_id=1, source_target_pairs={{0,4},{4,0},{8,12},{12,8},{16,20},{20,16},{24,28},{28,24},{1,5},{5... | collective-permute-start | bytes 1572872 | tf_op jit(solution)/shard_map/ppermute | solution.py:29
  98.3 41.0 %collective-permute-start = (bf16[64,8032]{1,0:T(8,128)(2,1)S(1)}, bf16[64,8032]{1,0:T(8,128)(2,1)S(1)}, u32[]{:S(2)}, u32[]{:S(2)}) collective-permute-start(bf16[64,8032]{1,0:T(8,128)(2,1)S(1)} %copy-done.94), channel_id=1, source_target_pairs={{0,4},{4,0},{8,12},{12,8},{16,20},{20,16},{24,28},{28,24},{1,5},{5... | collective-permute-start | bytes 3084296 | tf_op jit(solution)/shard_map/ppermute | solution.py:29
  102.7 36.8 %collective-permute-start.1 = (bf16[64,8032]{1,0:T(8,128)(2,1)S(1)}, bf16[64,8032]{1,0:T(8,128)(2,1)S(1)}, u32[]{:S(2)}, u32[]{:S(2)}) collective-permute-start(bf16[64,8032]{1,0:T(8,128)(2,1)S(1)} %copy-done.94), channel_id=1, source_target_pairs={{0,8},{4,12},{8,0},{12,4},{16,24},{20,28},{24,16},{28,20},{1,9},{5... | collective-permute-start | bytes 3084296 | tf_op jit(solution)/shard_map/ppermute | solution.py:29
  109.7 24.3 %collective-permute-start.20 = (bf16[5,32,512]{2,1,0:T(8,128)(2,1)S(1)}, bf16[5,32,512]{2,1,0:T(8,128)(2,1)S(1)}, u32[]{:S(2)}, u32[]{:S(2)}) collective-permute-start(bf16[5,32,512]{2,1,0:T(8,128)(2,1)S(1)} %slice.881), channel_id=1, source_target_pairs={{0,8},{4,12},{8,0},{12,4},{16,24},{20,28},{24,16},{28,20},{1,9},{5... | collective-permute-start | bytes 491528 | tf_op jit(solution)/shard_map/ppermute | solution.py:29
  113.7 21.8 %collective-permute-start.19 = (bf16[5,64,512]{2,1,0:T(8,128)(2,1)S(1)}, bf16[5,64,512]{2,1,0:T(8,128)(2,1)S(1)}, u32[]{:S(2)}, u32[]{:S(2)}) collective-permute-start(bf16[5,64,512]{2,1,0:T(8,128)(2,1)S(1)} %copy-done.98), channel_id=1, source_target_pairs={{0,4},{4,0},{8,12},{12,8},{16,20},{20,16},{24,28},{28,24},{1,5},{5... | collective-permute-start | bytes 983048 | tf_op jit(solution)/shard_map/ppermute | solution.py:29
  118.0 17.5 %collective-permute-start.21 = (bf16[5,32,512]{2,1,0:T(8,128)(2,1)S(1)}, bf16[5,32,512]{2,1,0:T(8,128)(2,1)S(1)}, u32[]{:S(2)}, u32[]{:S(2)}) collective-permute-start(bf16[5,32,512]{2,1,0:T(8,128)(2,1)S(1)} %slice.882), channel_id=1, source_target_pairs={{0,16},{4,20},{8,24},{12,28},{16,0},{20,4},{24,8},{28,12},{1,17},{... | collective-permute-start | bytes 491528 | tf_op jit(solution)/shard_map/ppermute | solution.py:29
  134.0 25.7 %collective-permute-start.3 = (bf16[64,8032]{1,0:T(8,128)(2,1)S(1)}, bf16[64,8032]{1,0:T(8,128)(2,1)S(1)}, u32[]{:S(2)}, u32[]{:S(2)}) collective-permute-start(bf16[64,8032]{1,0:T(8,128)(2,1)S(1)} %copy-done.94), channel_id=1, source_target_pairs={{0,16},{4,20},{8,24},{12,28},{16,0},{20,4},{24,8},{28,12},{1,17},{... | collective-permute-start | bytes 3084296 | tf_op jit(solution)/shard_map/ppermute | solution.py:29
  136.9 33.1 %collective-permute-start.32 = (bf16[2,32,2048]{2,1,0:T(8,128)(2,1)S(1)}, bf16[2,32,2048]{2,1,0:T(8,128)(2,1)S(1)}, u32[]{:S(2)}, u32[]{:S(2)}) collective-permute-start(bf16[2,32,2048]{2,1,0:T(8,128)(2,1)S(1)} %slice.892), channel_id=1, source_target_pairs={{0,8},{4,12},{8,0},{12,4},{16,24},{20,28},{24,16},{28,20},{1,9},{5... | collective-permute-start | bytes 786440 | tf_op jit(solution)/shard_map/ppermute | solution.py:29
  137.2 34.1 %collective-permute-start.33 = (bf16[2,32,2048]{2,1,0:T(8,128)(2,1)S(1)}, bf16[2,32,2048]{2,1,0:T(8,128)(2,1)S(1)}, u32[]{:S(2)}, u32[]{:S(2)}) collective-permute-start(bf16[2,32,2048]{2,1,0:T(8,128)(2,1)S(1)} %slice.893), channel_id=1, source_target_pairs={{0,16},{4,20},{8,24},{12,28},{16,0},{20,4},{24,8},{28,12},{1,17},{... | collective-permute-start | bytes 786440 | tf_op jit(solution)/shard_map/ppermute | solution.py:29
  139.3 20.7 %collective-permute-start.29 = (bf16[2,64,2048]{2,1,0:T(8,128)(2,1)S(1)}, bf16[2,64,2048]{2,1,0:T(8,128)(2,1)S(1)}, u32[]{:S(2)}, u32[]{:S(2)}) collective-permute-start(bf16[2,64,2048]{2,1,0:T(8,128)(2,1)S(1)} %collective-permute-done.28), channel_id=1, source_target_pairs={{0,4},{4,0},{8,12},{12,8},{16,20},{20,16},{24,28},{28,24},{1,5},{5... | collective-permute-start | bytes 1572872 | tf_op jit(solution)/shard_map/ppermute | solution.py:29
  139.5 22.3 %collective-permute-start.53 = (bf16[2,64,2048]{2,1,0:T(8,128)(2,1)}, bf16[2,64,2048]{2,1,0:T(8,128)(2,1)S(1)}, u32[]{:S(2)}, u32[]{:S(2)}) collective-permute-start(bf16[2,64,2048]{2,1,0:T(8,128)(2,1)} %collective-permute-done.52), channel_id=1, source_target_pairs={{0,4},{4,0},{8,12},{12,8},{16,20},{20,16},{24,28},{28,24},{1,5},{5... | collective-permute-start | bytes 1572872 | tf_op jit(solution)/shard_map/ppermute | solution.py:29
  159.7 22.1 %collective-permute-start.44 = (bf16[8,32,512]{2,1,0:T(8,128)(2,1)S(1)}, bf16[8,32,512]{2,1,0:T(8,128)(2,1)S(1)}, u32[]{:S(2)}, u32[]{:S(2)}) collective-permute-start(bf16[8,32,512]{2,1,0:T(8,128)(2,1)S(1)} %slice.902), channel_id=1, source_target_pairs={{0,8},{4,12},{8,0},{12,4},{16,24},{20,28},{24,16},{28,20},{1,9},{5... | collective-permute-start | bytes 786440 | tf_op jit(solution)/shard_map/ppermute | solution.py:29
  165.1 16.8 %collective-permute-start.45 = (bf16[8,32,512]{2,1,0:T(8,128)(2,1)S(1)}, bf16[8,32,512]{2,1,0:T(8,128)(2,1)S(1)}, u32[]{:S(2)}, u32[]{:S(2)}) collective-permute-start(bf16[8,32,512]{2,1,0:T(8,128)(2,1)S(1)} %slice.903), channel_id=1, source_target_pairs={{0,16},{4,20},{8,24},{12,28},{16,0},{20,4},{24,8},{28,12},{1,17},{... | collective-permute-start | bytes 786440 | tf_op jit(solution)/shard_map/ppermute | solution.py:29
  182.4 51.4 %collective-permute-start.47 = (bf16[8,32,512]{2,1,0:T(8,128)(2,1)S(1)}, bf16[8,32,512]{2,1,0:T(8,128)(2,1)S(1)}, u32[]{:S(2)}, u32[]{:S(2)}) collective-permute-start(bf16[8,32,512]{2,1,0:T(8,128)(2,1)S(1)} %collective-permute-done.45), channel_id=1, source_target_pairs={{0,4},{4,0},{8,12},{12,8},{16,20},{20,16},{24,28},{28,24},{1,5},{5... | collective-permute-start | bytes 786440 | tf_op jit(solution)/shard_map/ppermute | solution.py:29
  184.8 51.2 %collective-permute-start.58 = (bf16[2,32,2048]{2,1,0:T(8,128)(2,1)S(1)}, bf16[2,32,2048]{2,1,0:T(8,128)(2,1)S(1)}, u32[]{:S(2)}, u32[]{:S(2)}) collective-permute-start(bf16[2,32,2048]{2,1,0:T(8,128)(2,1)S(1)} %collective-permute-done.56), channel_id=1, source_target_pairs={{0,4},{4,0},{8,12},{12,8},{16,20},{20,16},{24,28},{28,24},{1,5},{5... | collective-permute-start | bytes 786440 | tf_op jit(solution)/shard_map/ppermute | solution.py:29
  199.6 37.0 %collective-permute-start.59 = (bf16[2,32,2048]{2,1,0:T(8,128)(2,1)S(1)}, bf16[2,32,2048]{2,1,0:T(8,128)(2,1)S(1)}, u32[]{:S(2)}, u32[]{:S(2)}) collective-permute-start(bf16[2,32,2048]{2,1,0:T(8,128)(2,1)S(1)} %collective-permute-done.57), channel_id=1, source_target_pairs={{0,4},{4,0},{8,12},{12,8},{16,20},{20,16},{24,28},{28,24},{1,5},{5... | collective-permute-start | bytes 786440 | tf_op jit(solution)/shard_map/ppermute | solution.py:29
  230.0 16.2 %collective-permute-start.11 = (bf16[512,512]{1,0:T(8,128)(2,1)S(1)}, bf16[512,512]{1,0:T(8,128)(2,1)S(1)}, u32[]{:S(2)}, u32[]{:S(2)}) collective-permute-start(bf16[512,512]{1,0:T(8,128)(2,1)S(1)} %get-tuple-element.236), channel_id=1, source_target_pairs={{0,3},{1,0},{2,1},{3,2},{4,7},{5,4},{6,5},{7,6},{8,11},{9,8},{10,9... | collective-permute-start | bytes 1572872 | tf_op jit(solution)/shard_map/ppermute | solution.py:33
  233.8 45.1 %collective-permute-start.10 = (bf16[512,512]{1,0:T(8,128)(2,1)S(1)}, bf16[512,512]{1,0:T(8,128)(2,1)S(1)}, u32[]{:S(2)}, u32[]{:S(2)}) collective-permute-start(bf16[512,512]{1,0:T(8,128)(2,1)S(1)} %get-tuple-element.237), channel_id=1, source_target_pairs={{0,2},{1,3},{2,0},{3,1},{4,6},{5,7},{6,4},{7,5},{8,10},{9,11},{10,... | collective-permute-start | bytes 1572872 | tf_op jit(solution)/shard_map/ppermute | solution.py:33
  233.8 45.1 %collective-permute-start.9 = (bf16[512,512]{1,0:T(8,128)(2,1)S(1)}, bf16[512,512]{1,0:T(8,128)(2,1)S(1)}, u32[]{:S(2)}, u32[]{:S(2)}) collective-permute-start(bf16[512,512]{1,0:T(8,128)(2,1)S(1)} %get-tuple-element.235), channel_id=1, source_target_pairs={{0,1},{1,2},{2,3},{3,0},{4,5},{5,6},{6,7},{7,4},{8,9},{9,10},{10,1... | collective-permute-start | bytes 1572872 | tf_op jit(solution)/shard_map/ppermute | solution.py:33
  487.4 136.3 %collective-permute-start.69 = (bf16[512,512]{1,0:T(8,128)(2,1)}, bf16[512,512]{1,0:T(8,128)(2,1)}, u32[]{:S(2)}, u32[]{:S(2)}) collective-permute-start(bf16[512,512]{1,0:T(8,128)(2,1)} %pad_maximum_fusion.23), channel_id=1, source_target_pairs={{0,3},{1,0},{2,1},{3,2},{4,7},{5,4},{6,5},{7,6},{8,11},{9,8},{10,9... | collective-permute-start | bytes 1572872 | tf_op jit(solution)/shard_map/ppermute | solution.py:33
  490.9 133.9 %collective-permute-start.70 = (bf16[512,512]{1,0:T(8,128)(2,1)}, bf16[512,512]{1,0:T(8,128)(2,1)}, u32[]{:S(2)}, u32[]{:S(2)}) collective-permute-start(bf16[512,512]{1,0:T(8,128)(2,1)} %pad_maximum_fusion.23), channel_id=1, source_target_pairs={{0,2},{1,3},{2,0},{3,1},{4,6},{5,7},{6,4},{7,5},{8,10},{9,11},{10,... | collective-permute-start | bytes 1572872 | tf_op jit(solution)/shard_map/ppermute | solution.py:33
  505.9 29.3 %collective-permute-start.112 = (bf16[4,64,512]{1,2,0:T(8,128)(2,1)}, bf16[4,64,512]{1,2,0:T(8,128)(2,1)}, u32[]{:S(2)}, u32[]{:S(2)}) collective-permute-start(bf16[4,64,512]{1,2,0:T(8,128)(2,1)} %get-tuple-element.232), channel_id=1, source_target_pairs={{0,4},{4,0},{8,12},{12,8},{16,20},{20,16},{24,28},{28,24},{1,5},{5... | collective-permute-start | bytes 786440 | tf_op jit(solution)/shard_map/ppermute | solution.py:29
  505.9 29.9 %collective-permute-start.111 = (bf16[4,64,512]{1,2,0:T(8,128)(2,1)}, bf16[4,64,512]{1,2,0:T(8,128)(2,1)}, u32[]{:S(2)}, u32[]{:S(2)}) collective-permute-start(bf16[4,64,512]{1,2,0:T(8,128)(2,1)} %get-tuple-element.233), channel_id=1, source_target_pairs={{0,4},{4,0},{8,12},{12,8},{16,20},{20,16},{24,28},{28,24},{1,5},{5... | collective-permute-start | bytes 786440 | tf_op jit(solution)/shard_map/ppermute | solution.py:29
  506.4 29.4 %collective-permute-start.109 = (bf16[4,64,512]{1,2,0:T(8,128)(2,1)}, bf16[4,64,512]{1,2,0:T(8,128)(2,1)}, u32[]{:S(2)}, u32[]{:S(2)}) collective-permute-start(bf16[4,64,512]{1,2,0:T(8,128)(2,1)} %get-tuple-element.234), channel_id=1, source_target_pairs={{0,4},{4,0},{8,12},{12,8},{16,20},{20,16},{24,28},{28,24},{1,5},{5... | collective-permute-start | bytes 786440 | tf_op jit(solution)/shard_map/ppermute | solution.py:29
  546.5 79.9 %collective-permute-start.71 = (bf16[512,512]{1,0:T(8,128)(2,1)}, bf16[512,512]{1,0:T(8,128)(2,1)}, u32[]{:S(2)}, u32[]{:S(2)}) collective-permute-start(bf16[512,512]{1,0:T(8,128)(2,1)} %pad_maximum_fusion.23), channel_id=1, source_target_pairs={{0,1},{1,2},{2,3},{3,0},{4,5},{5,6},{6,7},{7,4},{8,9},{9,10},{10,1... | collective-permute-start | bytes 1572872 | tf_op jit(solution)/shard_map/ppermute | solution.py:33
  549.0 21.8 %collective-permute-start.82 = (bf16[5,64,512]{2,1,0:T(8,128)(2,1)S(1)}, bf16[5,64,512]{2,1,0:T(8,128)(2,1)}, u32[]{:S(2)}, u32[]{:S(2)}) collective-permute-start(bf16[5,64,512]{2,1,0:T(8,128)(2,1)S(1)} %copy.266), channel_id=1, source_target_pairs={{0,4},{4,0},{8,12},{12,8},{16,20},{20,16},{24,28},{28,24},{1,5},{5... | collective-permute-start | bytes 983048 | tf_op jit(solution)/shard_map/ppermute | solution.py:29
  551.3 22.9 %collective-permute-start.115 = (bf16[4,32,512]{1,2,0:T(8,128)(2,1)}, bf16[4,32,512]{1,2,0:T(8,128)(2,1)}, u32[]{:S(2)}, u32[]{:S(2)}) collective-permute-start(bf16[4,32,512]{1,2,0:T(8,128)(2,1)} %get-tuple-element.266), channel_id=1, source_target_pairs={{0,16},{4,20},{8,24},{12,28},{16,0},{20,4},{24,8},{28,12},{1,17},{... | collective-permute-start | bytes 393224 | tf_op jit(solution)/shard_map/ppermute | solution.py:29
  588.6 30.6 %collective-permute-start.91 = (bf16[5,32,512]{2,1,0:T(8,128)(2,1)S(1)}, bf16[5,32,512]{2,1,0:T(8,128)(2,1)}, u32[]{:S(2)}, u32[]{:S(2)}) collective-permute-start(bf16[5,32,512]{2,1,0:T(8,128)(2,1)S(1)} %copy-done.140), channel_id=1, source_target_pairs={{0,16},{4,20},{8,24},{12,28},{16,0},{20,4},{24,8},{28,12},{1,17},{... | collective-permute-start | bytes 491528 | tf_op jit(solution)/shard_map/ppermute | solution.py:29
  619.2 88.8 %collective-permute-start.108 = (bf16[4,64,512]{1,2,0:T(8,128)(2,1)}, bf16[4,64,512]{1,2,0:T(8,128)(2,1)}, u32[]{:S(2)}, u32[]{:S(2)}) collective-permute-start(bf16[4,64,512]{1,2,0:T(8,128)(2,1)} %get-tuple-element.231), channel_id=1, source_target_pairs={{0,4},{4,0},{8,12},{12,8},{16,20},{20,16},{24,28},{28,24},{1,5},{5... | collective-permute-start | bytes 786440 | tf_op jit(solution)/shard_map/ppermute | solution.py:29
  621.2 102.9 %collective-permute-start.95 = (bf16[4,64,512]{1,2,0:T(8,128)(2,1)}, bf16[4,64,512]{1,2,0:T(8,128)(2,1)}, u32[]{:S(2)}, u32[]{:S(2)}) collective-permute-start(bf16[4,64,512]{1,2,0:T(8,128)(2,1)} %get-tuple-element.227), channel_id=1, source_target_pairs={{0,4},{4,0},{8,12},{12,8},{16,20},{20,16},{24,28},{28,24},{1,5},{5... | collective-permute-start | bytes 786440 | tf_op jit(solution)/shard_map/ppermute | solution.py:29
  623.7 38.3 %collective-permute-start.138 = (bf16[2,64,2048]{2,1,0:T(8,128)(2,1)}, bf16[2,64,2048]{2,1,0:T(8,128)(2,1)S(1)}, u32[]{:S(2)}, u32[]{:S(2)}) collective-permute-start(bf16[2,64,2048]{2,1,0:T(8,128)(2,1)} %get-tuple-element.212), channel_id=1, source_target_pairs={{0,4},{4,0},{8,12},{12,8},{16,20},{20,16},{24,28},{28,24},{1,5},{5... | collective-permute-start | bytes 1572872 | tf_op jit(solution)/shard_map/ppermute | solution.py:29
  624.8 37.7 %collective-permute-start.135 = (bf16[2,64,2048]{2,1,0:T(8,128)(2,1)}, bf16[2,64,2048]{2,1,0:T(8,128)(2,1)S(1)}, u32[]{:S(2)}, u32[]{:S(2)}) collective-permute-start(bf16[2,64,2048]{2,1,0:T(8,128)(2,1)} %get-tuple-element.214), channel_id=1, source_target_pairs={{0,4},{4,0},{8,12},{12,8},{16,20},{20,16},{24,28},{28,24},{1,5},{5... | collective-permute-start | bytes 1572872 | tf_op jit(solution)/shard_map/ppermute | solution.py:29
  626.5 36.1 %collective-permute-start.137 = (bf16[2,64,2048]{2,1,0:T(8,128)(2,1)}, bf16[2,64,2048]{2,1,0:T(8,128)(2,1)S(1)}, u32[]{:S(2)}, u32[]{:S(2)}) collective-permute-start(bf16[2,64,2048]{2,1,0:T(8,128)(2,1)} %get-tuple-element.213), channel_id=1, source_target_pairs={{0,4},{4,0},{8,12},{12,8},{16,20},{20,16},{24,28},{28,24},{1,5},{5... | collective-permute-start | bytes 1572872 | tf_op jit(solution)/shard_map/ppermute | solution.py:29
  665.4 156.7 %collective-permute-start.134 = (bf16[2,64,2048]{2,1,0:T(8,128)(2,1)}, bf16[2,64,2048]{2,1,0:T(8,128)(2,1)}, u32[]{:S(2)}, u32[]{:S(2)}) collective-permute-start(bf16[2,64,2048]{2,1,0:T(8,128)(2,1)} %get-tuple-element.211), channel_id=1, source_target_pairs={{0,4},{4,0},{8,12},{12,8},{16,20},{20,16},{24,28},{28,24},{1,5},{5... | collective-permute-start | bytes 1572872 | tf_op jit(solution)/shard_map/ppermute | solution.py:29
  705.4 133.1 %collective-permute-start.121 = (bf16[2,64,2048]{2,1,0:T(8,128)(2,1)}, bf16[2,64,2048]{2,1,0:T(8,128)(2,1)}, u32[]{:S(2)}, u32[]{:S(2)}) collective-permute-start(bf16[2,64,2048]{2,1,0:T(8,128)(2,1)} %get-tuple-element.207), channel_id=1, source_target_pairs={{0,4},{4,0},{8,12},{12,8},{16,20},{20,16},{24,28},{28,24},{1,5},{5... | collective-permute-start | bytes 1572872 | tf_op jit(solution)/shard_map/ppermute | solution.py:29
  708.0 15.8 %collective-permute-start.101 = (bf16[4,32,512]{1,2,0:T(8,128)(2,1)S(1)}, bf16[4,32,512]{1,2,0:T(8,128)(2,1)S(1)}, u32[]{:S(2)}, u32[]{:S(2)}) collective-permute-start(bf16[4,32,512]{1,2,0:T(8,128)(2,1)S(1)} %copy-done.117), channel_id=1, source_target_pairs={{0,16},{4,20},{8,24},{12,28},{16,0},{20,4},{24,8},{28,12},{1,17},{... | collective-permute-start | bytes 393224 | tf_op jit(solution)/shard_map/ppermute | solution.py:29
  759.0 15.4 %collective-permute-start.92 = (bf16[5,64,128]{1,2,0:T(8,128)(2,1)S(1)}, bf16[5,64,128]{1,2,0:T(8,128)(2,1)S(1)}, u32[]{:S(2)}, u32[]{:S(2)}) collective-permute-start(bf16[5,64,128]{1,2,0:T(8,128)(2,1)S(1)} %get-tuple-element.240), channel_id=1, source_target_pairs={{0,1},{1,2},{2,3},{3,0},{4,5},{5,6},{6,7},{7,4},{8,9},{9,10},{10,1... | collective-permute-start | bytes 245768 | tf_op jit(solution)/shard_map/ppermute | solution.py:33
  762.7 89.6 %collective-permute-start.76 = (bf16[64,8032]{1,0:T(8,128)(2,1)}, bf16[64,8032]{1,0:T(8,128)(2,1)}, u32[]{:S(2)}, u32[]{:S(2)}) collective-permute-start(bf16[64,8032]{1,0:T(8,128)(2,1)} %get-tuple-element.200), channel_id=1, source_target_pairs={{0,4},{4,0},{8,12},{12,8},{16,20},{20,16},{24,28},{28,24},{1,5},{5... | collective-permute-start | bytes 3084296 | tf_op jit(solution)/shard_map/ppermute | solution.py:29
  772.2 37.7 %collective-permute-start.143 = (bf16[2,32,2048]{2,1,0:T(8,128)(2,1)}, bf16[2,32,2048]{2,1,0:T(8,128)(2,1)}, u32[]{:S(2)}, u32[]{:S(2)}) collective-permute-start(bf16[2,32,2048]{2,1,0:T(8,128)(2,1)} %slice.1343), channel_id=1, source_target_pairs={{0,16},{4,20},{8,24},{12,28},{16,0},{20,4},{24,8},{28,12},{1,17},{... | collective-permute-start | bytes 786440 | tf_op jit(solution)/shard_map/ppermute | solution.py:29
  816.6 38.7 %collective-permute-start.75 = (bf16[64,8032]{1,0:T(8,128)(2,1)S(1)}, bf16[64,8032]{1,0:T(8,128)(2,1)S(1)}, u32[]{:S(2)}, u32[]{:S(2)}) collective-permute-start(bf16[64,8032]{1,0:T(8,128)(2,1)S(1)} %copy-done.96), channel_id=1, source_target_pairs={{0,4},{4,0},{8,12},{12,8},{16,20},{20,16},{24,28},{28,24},{1,5},{5... | collective-permute-start | bytes 3084296 | tf_op jit(solution)/shard_map/ppermute | solution.py:29
  833.7 21.6 %collective-permute-start.73 = (bf16[64,8032]{1,0:T(8,128)(2,1)S(1)}, bf16[64,8032]{1,0:T(8,128)(2,1)S(1)}, u32[]{:S(2)}, u32[]{:S(2)}) collective-permute-start(bf16[64,8032]{1,0:T(8,128)(2,1)S(1)} %copy-done.95), channel_id=1, source_target_pairs={{0,4},{4,0},{8,12},{12,8},{16,20},{20,16},{24,28},{28,24},{1,5},{5... | collective-permute-start | bytes 3084296 | tf_op jit(solution)/shard_map/ppermute | solution.py:29
  849.6 49.4 %collective-permute-start.72 = (bf16[64,8032]{1,0:T(8,128)(2,1)}, bf16[64,8032]{1,0:T(8,128)(2,1)S(1)}, u32[]{:S(2)}, u32[]{:S(2)}) collective-permute-start(bf16[64,8032]{1,0:T(8,128)(2,1)} %get-tuple-element.199), channel_id=1, source_target_pairs={{0,4},{4,0},{8,12},{12,8},{16,20},{20,16},{24,28},{28,24},{1,5},{5... | collective-permute-start | bytes 3084296 | tf_op jit(solution)/shard_map/ppermute | solution.py:29
  857.2 15.9 %collective-permute-start.79 = (bf16[32,8032]{1,0:T(8,128)(2,1)S(1)}, bf16[32,8032]{1,0:T(8,128)(2,1)S(1)}, u32[]{:S(2)}, u32[]{:S(2)}) collective-permute-start(bf16[32,8032]{1,0:T(8,128)(2,1)S(1)} %get-tuple-element.239), channel_id=1, source_target_pairs={{0,16},{4,20},{8,24},{12,28},{16,0},{20,4},{24,8},{28,12},{1,17},{... | collective-permute-start | bytes 1542152 | tf_op jit(solution)/shard_map/ppermute | solution.py:29
  864.7 19.5 %collective-permute-start.81 = (bf16[32,8032]{1,0:T(8,128)(2,1)S(1)}, bf16[32,8032]{1,0:T(8,128)(2,1)S(1)}, u32[]{:S(2)}, u32[]{:S(2)}) collective-permute-start(bf16[32,8032]{1,0:T(8,128)(2,1)S(1)} %slice.1341), channel_id=1, source_target_pairs={{0,16},{4,20},{8,24},{12,28},{16,0},{20,4},{24,8},{28,12},{1,17},{... | collective-permute-start | bytes 1542152 | tf_op jit(solution)/shard_map/ppermute | solution.py:29
  867.7 31.1 %collective-permute-start.74 = (bf16[32,8032]{1,0:T(8,128)(2,1)S(1)}, bf16[32,8032]{1,0:T(8,128)(2,1)S(1)}, u32[]{:S(2)}, u32[]{:S(2)}) collective-permute-start(bf16[32,8032]{1,0:T(8,128)(2,1)S(1)} %slice.1342), channel_id=1, source_target_pairs={{0,8},{4,12},{8,0},{12,4},{16,24},{20,28},{24,16},{28,20},{1,9},{5... | collective-permute-start | bytes 1542152 | tf_op jit(solution)/shard_map/ppermute | solution.py:29
  873.2 25.4 %collective-permute-start.80 = (bf16[32,8032]{1,0:T(8,128)(2,1)S(1)}, bf16[32,8032]{1,0:T(8,128)(2,1)S(1)}, u32[]{:S(2)}, u32[]{:S(2)}) collective-permute-start(bf16[32,8032]{1,0:T(8,128)(2,1)S(1)} %fusion.90), channel_id=1, source_target_pairs={{0,8},{4,12},{8,0},{12,4},{16,24},{20,28},{24,16},{28,20},{1,9},{5... | collective-permute-start | bytes 1542152 | tf_op jit(solution)/shard_map/ppermute | solution.py:29
  882.3 16.5 %collective-permute-start.78 = (bf16[32,8032]{1,0:T(8,128)(2,1)S(1)}, bf16[32,8032]{1,0:T(8,128)(2,1)S(1)}, u32[]{:S(2)}, u32[]{:S(2)}) collective-permute-start(bf16[32,8032]{1,0:T(8,128)(2,1)S(1)} %fusion.91), channel_id=1, source_target_pairs={{0,16},{4,20},{8,24},{12,28},{16,0},{20,4},{24,8},{28,12},{1,17},{... | collective-permute-start | bytes 1542152 | tf_op jit(solution)/shard_map/ppermute | solution.py:29
  (302 other events, 4081.9 us)

commit v2 on v1

v2 whole, which is shorter than its diff:
```python
import functools

import jax
import jax.numpy as jnp
from jax import lax
from jax.experimental import pallas as pl
from jax.experimental.pallas import tpu as pltpu
from jax.sharding import PartitionSpec as P

D = 512
DH = 64
STEP_NUM = 10

NORM_EPS = 1e-06
SOFTEN_FACTOR = 2.0
DIVERGENCE_SCALE = 1.0
CLIP_NORM = 0.02
BETA_ONE = 0.9
BETA_TWO = 0.999
ADAM_EPS = 1e-08
WEIGHT_DECAY = 0.01
LEARN_RATE = 0.3

BF = jnp.bfloat16
F32 = jnp.float32


def dp_swap(x, bit, dp):
    return lax.ppermute(x, "dp", [(i, i ^ bit) for i in range(dp)])


def head_shift(x, step, heads):
    return lax.ppermute(x, "head", [(i, (i + step) % heads) for i in range(heads)])


def after(x, *earlier):
    return lax.optimization_barrier((x, *earlier))[0]


def tie(chain, *arrived):
    return lax.optimization_barrier((chain, *arrived))


class GatherDp:
    def __init__(self, x, dp):
        self.x, self.dp = x, dp
        self.rows = x.shape[0]
        self.near = (dp_swap(x, 4, dp), dp_swap(x, 2, dp)) if dp == 8 else ()
        self.far = ()

    def go_far(self):
        if self.dp == 8:
            half = self.rows // 2
            part_y, part_x = self.near
            self.far = (dp_swap(part_y[:half], 2, self.dp), dp_swap(part_x[half:], 4, self.dp))

    def parts(self):
        dp = self.dp
        if dp == 8:
            here = [self.x, *self.near, *self.far]
            return here + [dp_swap(part, 1, dp) for part in here]
        whole = self.x
        bit = dp // 2
        while bit:
            whole = jnp.concatenate([whole, dp_swap(whole, bit, dp)], 0)
            bit //= 2
        return [whole]


def gather_head(x, heads):
    return [x] + [head_shift(x, heads - j, heads) for j in range(1, heads)]


def scatter_head(parts, heads):
    total = parts[0].astype(F32)
    for j in range(1, heads):
        total = total + head_shift(parts[j].astype(BF), j, heads).astype(F32)
    return total


def sum_head(x, heads):
    total = x
    for j in range(1, heads):
        total = total + head_shift(x, j, heads)
    return total


def sum_all(x, dp, heads):
    return sum_head(sum_dp(x, dp), heads)


def sum_dp(x, dp):
    bit = 1
    while bit < dp:
        x = x + dp_swap(x, bit, dp)
        bit *= 2
    return x


def stacked(refs):
    return refs[0][...] if len(refs) == 1 else jnp.concatenate([ref[...] for ref in refs], 0)


def lookup_kernel(vocab, tile, ids_ref, *refs):
    *table_refs, out_ref, rows_ref, acc_ref = refs
    step = pl.program_id(0)

    @pl.when(step == 0)
    def _():
        acc_ref[...] = jnp.zeros_like(acc_ref)

    place = lax.broadcasted_iota(jnp.int32, (1, tile), 1)
    block = stacked(table_refs)
    block = jnp.where(place < vocab - step * tile, block, jnp.zeros_like(block)).T
    rows_ref[...] = block
    hit = (ids_ref[...] - step * tile == place).astype(BF)
    acc_ref[...] += jnp.dot(hit, block, preferred_element_type=F32)

    @pl.when(step == pl.num_programs(0) - 1)
    def _():
        out_ref[...] = acc_ref[...].astype(BF)


def column_specs(parts, tile):
    return [pl.BlockSpec((part.shape[0], tile), lambda i: (0, i)) for part in parts]


def fixed(shape):
    return pl.BlockSpec(shape, lambda i: (0,) * len(shape))


VMEM_LIMIT = 56 * 2**20


def padded_to(columns, step=128):
    return -(-columns // step) * step


def lookup(ids, table_parts):
    rows, vocab = ids.shape[0], table_parts[0].shape[1]
    tile = 1024
    return pl.pallas_call(
        functools.partial(lookup_kernel, vocab, tile),
        out_shape=[
            jax.ShapeDtypeStruct((rows, D), BF),
            jax.ShapeDtypeStruct((padded_to(vocab), D), BF),
        ],
        grid=(pl.cdiv(vocab, tile),),
        in_specs=[fixed((rows, 1))] + column_specs(table_parts, tile),
        out_specs=[fixed((rows, D)), pl.BlockSpec((tile, D), lambda i: (i, 0))],
        scratch_shapes=[pltpu.VMEM((rows, D), F32)],
        compiler_params=pltpu.CompilerParams(vmem_limit_bytes=VMEM_LIMIT),
    )(ids.reshape(rows, 1), *table_parts)


def spread_kernel(tile, ids_ref, rows_ref, *refs):
    step = pl.program_id(0)
    turned_ref = refs[-1]

    @pl.when(step == 0)
    def _():
        turned_ref[...] = rows_ref[...].T

    place = step * tile + lax.broadcasted_iota(jnp.int32, (1, tile), 1)
    hit = (ids_ref[...] == place).astype(BF)
    total = jnp.dot(turned_ref[...], hit, preferred_element_type=F32)
    if len(refs) == 4:
        final_ref, slope_ref, out_ref, _ = refs
        out_ref[...] = total + lax.dot_general(
            final_ref[...], slope_ref[...], (((1,), (1,)), ((), ())), preferred_element_type=F32
        )
    else:
        base_ref, *keep_refs, send_ref, _ = refs
        total = base_ref[...] + total
        deep = D // 8
        for number, keep_ref in enumerate(keep_refs):
            keep_ref[...] = total[number * deep : (number + 1) * deep]
        send_ref[...] = total[D // 2 :].astype(BF)


def spread(ids, rows_low, columns, final_t=None, slope=None, base=None):
    rows = ids.shape[0]
    tile = 1024
    if base is None:
        shapes = [((D, columns), F32)]
        more = [final_t, slope]
        specs = [fixed(final_t.shape), pl.BlockSpec((tile, slope.shape[1]), lambda i: (i, 0))]
    else:
        shapes = [((D // 8, columns), F32)] * 4 + [((D // 2, columns), BF)]
        more = [base]
        specs = [pl.BlockSpec((D, tile), lambda i: (0, i))]
    return pl.pallas_call(
        functools.partial(spread_kernel, tile),
        out_shape=[jax.ShapeDtypeStruct(*shape) for shape in shapes],
        grid=(pl.cdiv(columns, tile),),
        in_specs=[fixed((rows, 1)), fixed((rows, D))] + specs,
        out_specs=[pl.BlockSpec((shape[0][0], tile), lambda i: (0, i)) for shape in shapes],
        scratch_shapes=[pltpu.VMEM((D, rows), BF)],
        compiler_params=pltpu.CompilerParams(vmem_limit_bytes=VMEM_LIMIT),
    )(ids.reshape(rows, 1), rows_low, *more)


def column_call(kernel, inputs, outputs, tile, sums=(), columns=None):
    columns = columns or inputs[0].shape[1]
    out_shape = [jax.ShapeDtypeStruct((rows, columns), dtype) for rows, dtype in outputs]
    out_specs = [pl.BlockSpec((rows, tile), lambda i: (0, i)) for rows, _ in outputs]
    for shape in sums:
        out_shape.append(jax.ShapeDtypeStruct(shape, F32))
        out_specs.append(fixed(shape))
    return pl.pallas_call(
        kernel,
        out_shape=out_shape,
        grid=(pl.cdiv(columns, tile),),
        in_specs=[
            pl.BlockSpec((array.shape[0], tile), lambda i: (0, i))
            if array.shape[1] >= columns
            else fixed(array.shape)
            for array in inputs
        ],
        out_specs=out_specs,
        compiler_params=pltpu.CompilerParams(vmem_limit_bytes=VMEM_LIMIT),
    )(*inputs)


def first_sums_kernel(y_ref, x_ref, d_ref, got_ref, d_low, d_high, x_low, y_high, y_low, x_high):
    deep = y_ref.shape[0]
    half = deep // 2
    got = got_ref[...].astype(F32)
    y = y_ref[...] + got[deep : 2 * deep]
    x = x_ref[...] + got[2 * deep : 3 * deep]
    d = (d_ref[...] + got[3 * deep :]).astype(BF)
    d_low[...] = d[:half]
    d_high[...] = d[half:]
    x_low[...] = x[:half].astype(BF)
    y_high[...] = y[half:].astype(BF)
    y_low[...] = y[:half]
    x_high[...] = x[half:]


def second_sums_kernel(y_low, got_a, x_high, got_b, y_out, x_out):
    y_out[...] = (y_low[...] + got_a[...].astype(F32)).astype(BF)
    x_out[...] = (x_high[...] + got_b[...].astype(F32)).astype(BF)


def lane_sums(value):
    rows, columns = value.shape
    total = value[:, :128]
    for start in range(128, columns, 128):
        total = total + value[:, start : start + 128]
    out = total[:8]
    for start in range(8, rows, 8):
        out = out + total[start : start + 8]
    return out


def inside(columns, tile, value):
    place = pl.program_id(0) * tile + lax.broadcasted_iota(jnp.int32, (1, tile), 1)
    return jnp.where(place < columns, value, 0.0)


def last_sums_kernel(columns, tile, own, got, x_low, y_high, y_low, x_high, out, squares):
    half = x_low.shape[0]
    low = own[:half] + got[:half].astype(F32) + (x_low[...].astype(F32) + y_low[...].astype(F32))
    high = (
        own[half:]
        + got[half : 2 * half].astype(F32)
        + (x_high[...].astype(F32) + y_high[...].astype(F32))
    )
    whole = jnp.concatenate([low, high], 0)
    out[...] = whole

    @pl.when(pl.program_id(0) == 0)
    def _():
        squares[...] = jnp.zeros_like(squares)

    squares[...] += lane_sums(inside(columns, tile, whole * whole))


class ScatterDp:
    def __init__(self, keeps, send, dp):
        self.keeps, self.dp = keeps, dp
        self.got = dp_swap(send, 1, dp)

    def run(self, columns):
        dp = self.dp
        tile = 4096
        if dp != 8:
            total = jnp.concatenate(self.keeps, 0) + self.got.astype(F32)
            bit = 2
            while bit < dp:
                rows = total.shape[0] // 2
                total = total[:rows] + dp_swap(total[rows:].astype(BF), bit, dp).astype(F32)
                bit *= 2
            total = total[:, :columns]
            squares = jnp.sum(total * total)
            return total, jnp.zeros((8, 128), F32).at[0, 0].set(squares)
        own, y, x, d = self.keeps
        half = own.shape[0] // 2
        d_low, d_high, x_low, y_high, y_low, x_high = column_call(
            first_sums_kernel, [y, x, d, self.got], [(half, BF)] * 4 + [(half, F32)] * 2, tile
        )
        got_a, got_b = dp_swap(d_low, 2, dp), dp_swap(d_high, 4, dp)
        x_low, y_high = dp_swap(x_low, 2, dp), dp_swap(y_high, 4, dp)
        y_low, x_high = column_call(
            second_sums_kernel, [y_low, got_a, x_high, got_b], [(half, BF)] * 2, tile
        )
        y_low, x_high = dp_swap(y_low, 4, dp), dp_swap(x_high, 2, dp)
        return column_call(
            functools.partial(last_sums_kernel, columns, tile),
            [own, self.got, x_low, y_high, y_low, x_high],
            [(2 * half, F32)],
            tile,
            sums=[(8, 128)],
            columns=columns,
        )


def logits_kernel(vocab, tile, final_ref, label_ref, teacher_ref, table_ref, out_ref, *stats):
    top_s, top_t, one, half, teach, cross, label = stats
    step = pl.program_id(0)
    last = pl.num_programs(0) - 1

    @pl.when(step == 0)
    def _():
        top_s[...] = jnp.full_like(top_s, -1e30)
        top_t[...] = jnp.full_like(top_t, -1e30)
        for ref in (one, half, teach, cross, label):
            ref[...] = jnp.zeros_like(ref)

    def work(valid):
        logits = jnp.dot(table_ref[...], final_ref[...], preferred_element_type=F32)
        tokens = logits.shape[1]

        def folded(value):
            return value.reshape(tile // 8, 8, tokens)

        student = folded(logits)
        teacher = folded(teacher_ref[...].astype(F32))
        place = 8 * lax.broadcasted_iota(jnp.int32, (tile // 8, 8, 1), 0)
        place = place + lax.broadcasted_iota(jnp.int32, (tile // 8, 8, 1), 1)
        if valid < tile:
            student = jnp.where(place < valid, student, -1e30)
            teacher = jnp.where(place < valid, teacher, -1e30)
        old_s, old_t = top_s[...], top_t[...]
        new_s = jnp.maximum(old_s, jnp.max(student, 0))
        new_t = jnp.maximum(old_t, jnp.max(teacher, 0))
        top_s[...] = new_s
        top_t[...] = new_t
        scale_s = jnp.exp((old_s - new_s) * 0.5)
        scale_t = jnp.exp((old_t - new_t) * 0.5)
        e = jnp.exp((student - new_s[None]) * 0.5)
        half[...] = half[...] * scale_s + jnp.sum(e, 0)
        one[...] = one[...] * (scale_s * scale_s) + jnp.sum(e * e, 0)
        e = jnp.exp((teacher - new_t[None]) * 0.5)
        teach[...] = teach[...] * scale_t + jnp.sum(e, 0)
        cross[...] = cross[...] * scale_t + jnp.sum(e * (teacher - student), 0)
        labels = (label_ref[...] - step * tile)[None]
        label[...] += jnp.sum(jnp.where(labels == place, student, 0.0), 0)

    rest = vocab - (pl.cdiv(vocab, tile) - 1) * tile
    if rest == tile:
        work(tile)
    else:

        @pl.when(step < last)
        def _():
            work(tile)

        @pl.when(step == last)
        def _():
            work(rest)

    @pl.when(step == last)
    def _():
        peak_s = jnp.max(top_s[...], 0, keepdims=True)
        peak_t = jnp.max(top_t[...], 0, keepdims=True)
        by_s = jnp.exp((top_s[...] - peak_s) * 0.5)
        by_t = jnp.exp((top_t[...] - peak_t) * 0.5)

        def total(value):
            return jnp.sum(value, 0, keepdims=True)

        out_ref[0:1] = peak_s
        out_ref[1:2] = peak_t
        out_ref[2:3] = total(one[...] * (by_s * by_s))
        out_ref[3:4] = total(half[...] * by_s)
        out_ref[4:5] = total(teach[...] * by_t)
        out_ref[5:6] = total(cross[...] * by_t) * 0.5
        out_ref[6:7] = total(label[...])
        out_ref[7:8] = jnp.zeros_like(peak_s)


def logits_stats(final_t, labels, teacher_t, table_rows):
    vocab, tokens = teacher_t.shape
    tile = 1024
    return pl.pallas_call(
        functools.partial(logits_kernel, vocab, tile),
        out_shape=jax.ShapeDtypeStruct((8, tokens), F32),
        grid=(pl.cdiv(vocab, tile),),
        in_specs=[
            fixed(final_t.shape),
            fixed((1, tokens)),
            pl.BlockSpec((tile, tokens), lambda i: (i, 0)),
            pl.BlockSpec((tile, D), lambda i: (i, 0)),
        ],
        out_specs=fixed((8, tokens)),
        scratch_shapes=[pltpu.VMEM((8, tokens), F32)] * 7,
        compiler_params=pltpu.CompilerParams(vmem_limit_bytes=VMEM_LIMIT),
    )(final_t, labels.reshape(1, tokens), teacher_t, table_rows)


def logits_back_kernel(vocab, tile, final_ref, label_ref, scalar_ref, teacher_ref, *refs):
    rows_ref, *table_refs, slope_ref, back_ref, acc_ref = refs
    step = pl.program_id(0)
    last = pl.num_programs(0) - 1

    @pl.when(step == 0)
    def _():
        acc_ref[...] = jnp.zeros_like(acc_ref)

    good = lax.broadcasted_iota(jnp.int32, (1, tile), 1) < vocab - step * tile
    block = stacked(table_refs)
    block = jnp.where(good, block, jnp.zeros_like(block))
    place = lax.broadcasted_iota(jnp.int32, (tile, 1), 0)
    logits = jnp.dot(rows_ref[...], final_ref[...], preferred_element_type=F32)
    lse_half = scalar_ref[0:1]
    lse_teacher = scalar_ref[1:2]
    soft_one = scalar_ref[2:3]
    soft_half = scalar_ref[3:4]
    weight = scalar_ref[4:5]
    student = jnp.exp(logits * 0.5 - lse_half)
    teacher = jnp.exp(teacher_ref[...].astype(F32) * 0.5 - lse_teacher)
    labels = label_ref[...] - step * tile
    slope = student * (soft_one * student + soft_half) - soft_half * teacher
    slope = slope - jnp.where(labels == place, weight, 0.0)
    slope = jnp.where(place < vocab - step * tile, slope, 0.0).astype(BF)
    slope_ref[...] = slope
    acc_ref[...] += jnp.dot(block, slope, preferred_element_type=F32)

    @pl.when(step == last)
    def _():
        back_ref[...] = acc_ref[...].astype(BF)


def logits_back(final_t, labels, scalars, teacher_t, table_rows, table_parts):
    vocab, tokens = teacher_t.shape
    tile = 1024
    return pl.pallas_call(
        functools.partial(logits_back_kernel, vocab, tile),
        out_shape=[
            jax.ShapeDtypeStruct((padded_to(vocab), tokens), BF),
            jax.ShapeDtypeStruct((D, tokens), BF),
        ],
        grid=(pl.cdiv(vocab, tile),),
        in_specs=[
            fixed(final_t.shape),
            fixed((1, tokens)),
            fixed(scalars.shape),
            pl.BlockSpec((tile, tokens), lambda i: (i, 0)),
            pl.BlockSpec((tile, D), lambda i: (i, 0)),
        ]
        + column_specs(table_parts, tile),
        out_specs=[pl.BlockSpec((tile, tokens), lambda i: (i, 0)), fixed((D, tokens))],
        scratch_shapes=[pltpu.VMEM((D, tokens), F32)],
        compiler_params=pltpu.CompilerParams(vmem_limit_bytes=VMEM_LIMIT),
    )(final_t, labels.reshape(1, tokens), scalars, teacher_t, table_rows, *table_parts)


BIAS_ONE = 1.0 - BETA_ONE**STEP_NUM
BIAS_TWO = 1.0 - BETA_TWO**STEP_NUM


def lamb(weight, moment, second, grad, clip):
    grad = grad * clip
    moment = BETA_ONE * moment + (1 - BETA_ONE) * grad
    second = BETA_TWO * second + (1 - BETA_TWO) * grad * grad
    update = (
        moment * (1.0 / BIAS_ONE) / (jnp.sqrt(second * (1.0 / BIAS_TWO)) + ADAM_EPS)
        + WEIGHT_DECAY * weight
    )
    return moment, second, update


def lamb_columns_kernel(columns, tile, w, m, v, g, clip, m_out, v_out, u_out, squares):
    moment, second, update = lamb(w[...], m[...], v[...], g[...], clip[0:1, 0:1])
    m_out[...] = moment
    v_out[...] = second
    u_out[...] = update

    @pl.when(pl.program_id(0) == 0)
    def _():
        squares[...] = jnp.zeros_like(squares)

    squares[...] += lane_sums(inside(columns, tile, update * update))


def lamb_matrices_kernel(places, clip_ref, *refs):
    grads = refs[:2]
    count = len(places)
    states = refs[2 : 2 + 3 * count]
    outs = refs[2 + 3 * count : -1]
    squares = refs[-1]
    squares[...] = jnp.zeros_like(squares)
    clip = clip_ref[0:1, 0:1]
    row = 0
    for group, matrices in enumerate(places):
        w, m, v = states[3 * group : 3 * group + 3]
        m_out, v_out, u_out = outs[3 * group : 3 * group + 3]
        width = w.shape[-1]
        for number, (array, start) in enumerate(matrices):
            grad = grads[array][:, start : start + width]
            moment, second, update = lamb(w[number], m[number], v[number], grad, clip)
            m_out[number] = moment
            v_out[number] = second
            u_out[number] = update
            total = jnp.sum(update * update, 0, keepdims=True)
            lanes = min(128, width)
            line = total[:, :lanes]
            for first in range(lanes, width, lanes):
                line = line + total[:, first : first + lanes]
            squares[row : row + 1, :lanes] = line
            row += 1


def lamb_matrices(clip, grads, groups, places):
    flat = [array for group in groups for array in group]
    shapes = [jax.ShapeDtypeStruct(group[0].shape, F32) for group in groups for _ in range(3)]
    rows = 8 * pl.cdiv(sum(len(matrices) for matrices in places), 8)
    return pl.pallas_call(
        functools.partial(lamb_matrices_kernel, places),
        out_shape=shapes + [jax.ShapeDtypeStruct((rows, 128), F32)],
        compiler_params=pltpu.CompilerParams(vmem_limit_bytes=VMEM_LIMIT),
    )(clip, *grads, *flat)


def pack_kernel(heads_of, *refs):
    *in_refs, out_ref = refs
    start = 0
    for number, index in heads_of:
        value = in_refs[number][...] if index is None else in_refs[number][index]
        out_ref[:, start : start + value.shape[1]] = value.astype(BF)
        start += value.shape[1]


def pack(arrays, plan):
    columns = sum(arrays[number].shape[-1] for number, _ in plan)
    return pl.pallas_call(
        functools.partial(pack_kernel, plan),
        out_shape=jax.ShapeDtypeStruct((arrays[0].shape[-2], columns), BF),
        compiler_params=pltpu.CompilerParams(vmem_limit_bytes=VMEM_LIMIT),
    )(*arrays)


def restack_kernel(split, *refs):
    *in_refs, left_ref, right_ref = refs
    rows = in_refs[0].shape[0]
    for number, ref in enumerate(in_refs):
        left_ref[number * rows : (number + 1) * rows] = ref[:, :split]
        right_ref[number * rows : (number + 1) * rows] = ref[:, split:]


def restack(parts, split):
    rows, columns = parts[0].shape
    total = rows * len(parts)
    return pl.pallas_call(
        functools.partial(restack_kernel, split),
        out_shape=[
            jax.ShapeDtypeStruct((total, split), BF),
            jax.ShapeDtypeStruct((total, columns - split), BF),
        ],
        compiler_params=pltpu.CompilerParams(vmem_limit_bytes=VMEM_LIMIT),
    )(*parts)


def assemble_kernel(widths, heads, order_ref, in_ref, *out_refs):
    deep = in_ref.shape[-2] // heads
    start = 0
    for width, out_ref in zip(widths, out_refs, strict=True):
        shards = out_ref.shape[-1] // width
        for j in range(shards):
            out_ref[:, j * width : (j + 1) * width] = in_ref[
                0, j * deep : (j + 1) * deep, start : start + width
            ]
        start += width


def assemble(order, gathered, widths, heads, single):
    dp, rows, columns = gathered.shape
    deep = rows // heads
    wides = [w * heads for w in widths[: len(widths) - single]] + widths[len(widths) - single :]
    return pl.pallas_call(
        functools.partial(assemble_kernel, widths, heads),
        out_shape=[jax.ShapeDtypeStruct((dp * deep, w), BF) for w in wides],
        grid_spec=pltpu.PrefetchScalarGridSpec(
            num_scalar_prefetch=1,
            grid=(dp,),
            in_specs=[pl.BlockSpec((1, rows, columns), lambda p, order: (order[p], 0, 0))],
            out_specs=[pl.BlockSpec((deep, w), lambda p, order: (p, 0)) for w in wides],
        ),
    )(order, gathered)


def assemble_parts_kernel(widths, heads, deep, *refs):
    outs = refs[len(refs) - len(widths) :]
    row = 0
    for ref in refs[: len(refs) - len(widths)]:
        for first in range(0, ref.shape[0], deep):
            place, j = divmod(row // deep, heads)
            start = 0
            for width, out_ref in zip(widths, outs, strict=True):
                if out_ref.shape[-1] > width:
                    out_ref[place * deep : (place + 1) * deep, j * width : (j + 1) * width] = ref[
                        first : first + deep, start : start + width
                    ]
                elif j == 0:
                    out_ref[place * deep : (place + 1) * deep] = ref[
                        first : first + deep, start : start + width
                    ]
                start += width
            row += deep


def assemble_parts(parts, widths, heads, single, dp):
    deep = D // dp
    wides = [w * heads for w in widths[: len(widths) - single]] + widths[len(widths) - single :]
    return pl.pallas_call(
        functools.partial(assemble_parts_kernel, widths, heads, deep),
        out_shape=[jax.ShapeDtypeStruct((D, w), BF) for w in wides],
        compiler_params=pltpu.CompilerParams(vmem_limit_bytes=VMEM_LIMIT),
    )(*parts)


def weight_grad_kernel(widths, single, order_ref, *refs):
    out_ref = refs[-1]
    dp, heads, deep, _ = out_ref.shape

    def put(j, start, stop, value):
        for place in range(dp):
            out_ref[order_ref[place], j, :, start:stop] = value[place * deep : (place + 1) * deep]

    start = 0
    for number, width in enumerate(widths):
        left = refs[2 * number][...]
        together = max(1, 512 // width)
        for first in range(0, heads, together):
            whole = lax.dot_general(
                left,
                refs[2 * number + 1][:, first * width : (first + together) * width],
                (((0,), (0,)), ((), ())),
                preferred_element_type=F32,
            ).astype(BF)
            for j in range(together):
                put(first + j, start, start + width, whole[:, j * width : (j + 1) * width])
        start += width
    if single:
        value = refs[-2][...].astype(BF)
        for j in range(heads):
            put(j, start, start + value.shape[1], value)


def weight_grads(order, pairs, heads, extra=None):
    dp = order.shape[0]
    flat = []
    for left, right in pairs:
        flat += [left.reshape(-1, left.shape[-1]), right.reshape(-1, right.shape[-1])]
    widths = [right.shape[-1] // heads for _, right in pairs]
    columns = sum(widths)
    if extra is not None:
        flat.append(extra)
        columns += extra.shape[1]
    return pl.pallas_call(
        functools.partial(weight_grad_kernel, widths, extra is not None),
        out_shape=jax.ShapeDtypeStruct((dp, heads, D // dp, columns), BF),
        in_specs=[pl.BlockSpec(memory_space=pltpu.SMEM)]
        + [pl.BlockSpec(memory_space=pltpu.VMEM)] * len(flat),
        out_specs=pl.BlockSpec(memory_space=pltpu.VMEM),
        compiler_params=pltpu.CompilerParams(vmem_limit_bytes=48 * 2**20),
    )(order, *flat)


def normed(inputs, gain_row):
    return (
        inputs * lax.rsqrt(jnp.mean(inputs * inputs, -1, keepdims=True) + NORM_EPS) * gain_row
    ).astype(BF)


def norm_back(inputs, gain_row, upstream):
    factor = lax.rsqrt(jnp.mean(inputs * inputs, -1, keepdims=True) + NORM_EPS)
    scaled = upstream * gain_row
    inner = jnp.mean(scaled * inputs, -1, keepdims=True)
    return (
        factor * (scaled - inputs * factor * factor * inner),
        jnp.sum(upstream * inputs * factor, axis=(0, 1)),
    )


def dot(spec, a, b):
    return jnp.einsum(spec, a, b, preferred_element_type=F32)


def split_heads(array):
    return array.reshape(array.shape[0], array.shape[1], -1, DH)


def merge_heads(array):
    return array.reshape(array.shape[0], array.shape[1], -1)


def attn_probs(query, keys_all, allowed):
    scores = dot("bqhe,bkhe->bhqk", query, keys_all) * DH ** (-0.5)
    return jax.nn.softmax(jnp.where(allowed[:, None], scores, -1000000000.0), -1)


def attend_fwd(query_in, source, weights, allowed):
    query = split_heads(dot("bld,dh->blh", query_in, weights[0]).astype(BF))
    keys_all = split_heads(dot("bld,dh->blh", source, weights[1]).astype(BF))
    values = split_heads(dot("bld,dh->blh", source, weights[2]).astype(BF))
    probs = attn_probs(query, keys_all, allowed)
    mixed = merge_heads(dot("bhqk,bkhe->bqhe", probs.astype(BF), values).astype(BF))
    return dot("blh,dh->bld", mixed, weights[3]), (query, keys_all, values, mixed)


def attend_back(upstream, query_in, source, weights, allowed, kept):
    query, keys_all, values, mixed = kept
    up_low = upstream.astype(BF)
    grad_mixed = split_heads(dot("bld,dh->blh", up_low, weights[3]).astype(BF))
    probs = attn_probs(query, keys_all, allowed)
    grad_probs = dot("bqhe,bkhe->bhqk", grad_mixed, values)
    grad_scores = (probs * (grad_probs - jnp.sum(grad_probs * probs, -1, keepdims=True))).astype(BF)
    grad_query = merge_heads(
        (dot("bhqk,bkhe->bqhe", grad_scores, keys_all) * DH ** (-0.5)).astype(BF)
    )
    grad_keys = merge_heads(
        (dot("bhqk,bqhe->bkhe", grad_scores, query) * DH ** (-0.5)).astype(BF)
    )
    grad_values = merge_heads(dot("bhqk,bqhe->bkhe", probs.astype(BF), grad_mixed).astype(BF))
    pairs = [(query_in, grad_query), (source, grad_keys), (source, grad_values), (up_low, mixed)]
    back_query = dot("blh,dh->bld", grad_query, weights[0])
    back_source = dot("blh,dh->bld", grad_keys, weights[1])
    back_source = back_source + dot("blh,dh->bld", grad_values, weights[2])
    return back_query, back_source, pairs


def feed_fwd(inputs, weights):
    hidden = jax.nn.relu(dot("bld,df->blf", inputs, weights[0])).astype(BF)
    return dot("blf,df->bld", hidden, weights[1]), hidden


def feed_back(upstream, inputs, weights, hidden):
    up_low = upstream.astype(BF)
    grad_hidden = dot("bld,df->blf", up_low, weights[1])
    grad_pre = jnp.where(hidden > 0, grad_hidden, 0.0).astype(BF)
    back_in = dot("blf,df->bld", grad_pre, weights[0])
    return back_in, [(inputs, grad_pre), (up_low, hidden)]


def body(
    dp,
    heads,
    source_ids,
    target_ids,
    source_lens,
    target_lens,
    kl_mask,
    teacher,
    *state,
):
    def transposed(group):
        embed, attn_in, attn_out, ff_in, ff_out, gains = group
        swap = functools.partial(jnp.swapaxes, axis1=-1, axis2=-2)
        return (swap(embed), attn_in, swap(attn_out), ff_in, swap(ff_out), gains)

    masters = transposed(state[:6])
    moments = transposed(state[6:12])
    seconds = transposed(state[12:])
    embed_t, attn_in, attn_out_t, ff_in, ff_out_t, gains = masters
    low = embed_t.astype(BF)
    vocab_local = embed_t.shape[1]
    head_pos = lax.axis_index("head")
    lead = (head_pos == 0).astype(F32)
    vocab_start = head_pos * vocab_local
    batch_size, source_len = source_ids.shape
    target_len = target_ids.shape[1]
    token_count = batch_size * target_len
    each = -(-batch_size // heads)
    padded = each * heads

    sides = [
        [attn_in[0, 0], attn_in[0, 1], attn_in[0, 2], attn_out_t[0], ff_in[0], ff_out_t[0]],
        [attn_in[1, 0], attn_in[1, 1], attn_in[1, 2], attn_out_t[1]]
        + [attn_in[2, 0], attn_in[2, 1], attn_in[2, 2], attn_out_t[2], ff_in[1], ff_out_t[1]],
    ]
    widths = [[matrix.shape[-1] for matrix in side] for side in sides]
    lanes = 128
    gain_rows = gains.shape[0]
    counted = jnp.full((1, gains.shape[1]), jnp.sum((target_lens > 0).astype(F32)))
    gain_block = jnp.pad(
        jnp.concatenate([gains, counted], 0).T, ((0, 0), (0, lanes - gain_rows - 1))
    )
    places = [0]
    bit = dp // 2
    while bit:
        places = places + [place ^ bit for place in places]
        bit //= 2
    order = lax.axis_index("dp") ^ jnp.array(places, jnp.int32)
    flat_in = attn_in.reshape((9,) + attn_in.shape[2:])
    arrays = [flat_in, attn_out_t, ff_in, ff_out_t, gain_block]
    plan = [(0, 0), (0, 1), (0, 2), (1, 0), (2, 0), (3, 0), (4, None)]
    plan += [(0, 3), (0, 4), (0, 5), (1, 1), (0, 6), (0, 7), (0, 8), (1, 2), (2, 1), (3, 1)]
    split = sum(widths[0]) + lanes
    packed = pack(arrays, plan)
    low, packed = tie(low, packed)
    came = gather_head(packed, heads)
    table = GatherDp(low, dp)
    table.go_far()
    came = tie(came[0], *came[1:], *table.far)[:heads]
    enc_wide, dec_wide = restack(came, split)
    enc_gather = GatherDp(enc_wide, dp)
    dec_gathered = lax.all_gather(dec_wide, "dp", axis=0)
    table_parts = table.parts()

    def fill(array):
        return jnp.pad(array, ((0, padded - batch_size),) + ((0, 0),) * (array.ndim - 1))

    dec_ids = jnp.concatenate([jnp.zeros((batch_size, 1), jnp.int32), target_ids[:, :-1]], 1)
    enc_ids = jnp.roll(fill(source_ids).reshape(heads, -1), -head_pos, 0) - vocab_start
    dec_ids = jnp.roll(fill(dec_ids).reshape(heads, -1), -head_pos, 0) - vocab_start
    enc_rows_count = heads * each * source_len
    looked, table_rows = lookup(
        jnp.concatenate([enc_ids.reshape(-1), dec_ids.reshape(-1)]), table_parts
    )
    enc_looked = looked[:enc_rows_count].reshape(heads, -1, D)
    dec_looked = looked[enc_rows_count:]
    came = [enc_looked[0]] + [head_shift(enc_looked[j], j, heads) for j in range(1, heads)]
    dec_looked, *enc_gather.near = tie(dec_looked, *enc_gather.near)
    enc_gather.go_far()
    *enc_list, gain = assemble_parts(enc_gather.parts(), widths[0] + [lanes], heads, 1, dp)
    w_enc, f_enc = enc_list[:4], enc_list[4:]
    gain = gain[:, : gain_rows + 1].astype(F32).T
    real_count = jnp.maximum(jnp.sum(gain[gain_rows].reshape(dp, -1)[:, 0]), 1.0)
    enc_embed = functools.reduce(jnp.add, came).astype(F32).reshape(each, source_len, D)
    my_lens = lax.dynamic_slice_in_dim(fill(source_lens), head_pos * each, each)

    src_keys = jnp.arange(source_len)[None, :] < my_lens[:, None]
    enc_allowed = jnp.broadcast_to(src_keys[:, None, :], (each, source_len, source_len))
    cross_allowed = jnp.broadcast_to(src_keys[:, None, :], (each, target_len, source_len))
    causal = jnp.broadcast_to(
        (jnp.arange(target_len)[:, None] >= jnp.arange(target_len)[None, :])[None],
        (each, target_len, target_len),
    )
    norm_a = normed(enc_embed, gain[0])
    branch, kept_enc = attend_fwd(norm_a, norm_a, w_enc, enc_allowed)
    enc_mid = enc_embed + branch
    enc_mid, dec_looked = tie(enc_mid, dec_looked)
    looked = dec_looked.reshape(heads, -1, D)
    dec_came = [looked[0]] + [head_shift(looked[j], j, heads) for j in range(1, heads)]
    norm_b = normed(enc_mid, gain[1])
    branch, hidden_enc = feed_fwd(norm_b, f_enc)
    enc_last = enc_mid + branch
    encoded = normed(enc_last, gain[2])
    dec_list = assemble(order, dec_gathered, widths[1], heads, 0)
    w_self, w_cross, f_dec = dec_list[:4], dec_list[4:8], dec_list[8:]
    dec_embed = functools.reduce(jnp.add, dec_came).astype(F32).reshape(each, target_len, D)
    norm_c = normed(dec_embed, gain[3])
    branch, kept_self = attend_fwd(norm_c, norm_c, w_self, causal)
    dec_one = dec_embed + branch
    norm_d = normed(dec_one, gain[4])
    branch, kept_cross = attend_fwd(norm_d, encoded, w_cross, cross_allowed)
    dec_two = dec_one + branch
    norm_e = normed(dec_two, gain[5])
    branch, hidden_dec = feed_fwd(norm_e, f_dec)
    dec_three = dec_two + branch
    head_gain = gain[6] * D ** (-0.5)
    my_final = normed(dec_three, head_gain).reshape(each * target_len, D)

    final = jnp.concatenate(gather_head(my_final, heads), 0)
    final = jnp.roll(final, head_pos * each * target_len, 0)[:token_count]
    valid = (jnp.arange(target_len)[None, :] < target_lens[:, None]).astype(F32)
    token_weight = (
        valid / (jnp.maximum(target_lens, 1).astype(F32)[:, None] * real_count)
    ).reshape(token_count)
    divergence_mask = kl_mask.astype(F32).reshape(token_count)
    labels = target_ids.reshape(token_count) - vocab_start
    labels = jnp.where((labels >= 0) & (labels < vocab_local), labels, -1)
    final_t = final.T
    teacher_t = teacher.T
    stats = logits_stats(final_t, labels, teacher_t, table_rows)
    every = jnp.stack(gather_head(stats, heads))
    peak_student = jnp.max(every[:, 0], 0)
    peak_teacher = jnp.max(every[:, 1], 0)
    off_s = every[:, 0] - peak_student
    off_t = jnp.exp((every[:, 1] - peak_teacher) / SOFTEN_FACTOR)
    sum_one = jnp.sum(every[:, 2] * jnp.exp(off_s), 0)
    sum_half = jnp.sum(every[:, 3] * jnp.exp(off_s / SOFTEN_FACTOR), 0)
    sum_teacher = jnp.sum(every[:, 4] * off_t, 0)
    sum_cross = jnp.sum(every[:, 5] * off_t, 0)
    label_logprob = jnp.sum(every[:, 6], 0)
    lse_one = peak_student + jnp.log(sum_one)
    lse_half = peak_student / SOFTEN_FACTOR + jnp.log(sum_half)
    lse_teacher = peak_teacher / SOFTEN_FACTOR + jnp.log(sum_teacher)
    cross_entropy = lse_one - label_logprob
    divergence_value = sum_cross / sum_teacher - lse_teacher + lse_half
    loss_part = lead * jnp.sum(
        token_weight
        * (
            cross_entropy
            + DIVERGENCE_SCALE * SOFTEN_FACTOR * SOFTEN_FACTOR * divergence_value * divergence_mask
        )
    )
    soft_half = DIVERGENCE_SCALE * SOFTEN_FACTOR * divergence_mask * token_weight
    soft_one = token_weight * jnp.exp(SOFTEN_FACTOR * lse_half - lse_one)
    nothing = jnp.zeros_like(lse_half)
    scalars = jnp.stack(
        [lse_half, lse_teacher, soft_one, soft_half, token_weight, nothing, nothing, nothing]
    )
    slope, part = logits_back(final_t, labels, scalars, teacher_t, table_rows, table_parts)
    part = part.T.reshape(batch_size, target_len, D)
    part = jnp.roll(fill(part).reshape(heads, each * target_len, D), -head_pos, 0)
    grad_final = scatter_head([part[j] for j in range(heads)], heads).reshape(each, target_len, D)

    grad_three, gain_six = norm_back(dec_three, head_gain, grad_final)
    back_in, pairs_f_dec = feed_back(grad_three, norm_e, f_dec, hidden_dec)
    grad_norm_in, gain_five = norm_back(dec_two, gain[5], back_in)
    grad_two = grad_three + grad_norm_in
    back_query, grad_encoded, pairs_cross = attend_back(
        grad_two, norm_d, encoded, w_cross, cross_allowed, kept_cross
    )
    grad_norm_in, gain_four = norm_back(dec_one, gain[4], back_query)
    grad_one = grad_two + grad_norm_in
    back_query, back_source, pairs_self = attend_back(
        grad_one, norm_c, norm_c, w_self, causal, kept_self
    )
    grad_norm_in, gain_three = norm_back(dec_embed, gain[3], back_query + back_source)
    grad_dec_embed = grad_one + grad_norm_in
    dec_rows = gather_head(grad_dec_embed.reshape(-1, D).astype(BF), heads)
    dec_grads = weight_grads(order, pairs_self + pairs_cross + pairs_f_dec, heads)
    grad_encoded, dec_grads = tie(grad_encoded, dec_grads)
    dec_shard = lax.psum_scatter(dec_grads, "dp", scatter_dimension=0)
    grad_last, gain_two = norm_back(enc_last, gain[2], grad_encoded)
    back_in, pairs_f_enc = feed_back(grad_last, norm_b, f_enc, hidden_enc)
    back_in, *dec_rows = tie(back_in, *dec_rows)
    grad_norm_in, gain_one = norm_back(enc_mid, gain[1], back_in)
    grad_mid = grad_last + grad_norm_in
    back_query, back_source, pairs_enc = attend_back(
        grad_mid, norm_a, norm_a, w_enc, enc_allowed, kept_enc
    )
    grad_norm_in, gain_zero = norm_back(enc_embed, gain[0], back_query + back_source)
    grad_enc_embed = grad_mid + grad_norm_in

    gain_grads = jnp.stack(
        [gain_zero, gain_one, gain_two, gain_three, gain_four, gain_five, gain_six * D ** (-0.5)]
    )
    gain_cols = jnp.pad(gain_grads.T, ((0, 0), (0, lanes - gain_rows)))
    enc_low = grad_enc_embed.reshape(-1, D).astype(BF)
    enc_rows = gather_head(enc_low, heads)
    enc_grads = weight_grads(order, pairs_enc + pairs_f_enc, heads, gain_cols)
    enc_low, enc_grads = tie(enc_low, enc_grads)
    enc_shard = lax.psum_scatter(enc_grads, "dp", scatter_dimension=0)
    near_ids = jnp.concatenate([dec_ids.reshape(-1), enc_ids[0]])
    near_rows = jnp.concatenate(dec_rows + [enc_low], 0)
    columns = padded_to(vocab_local)
    (grad_table_t,) = spread(near_ids, near_rows, columns, final_t=final_t, slope=slope)

    def send_heads(shard):
        return [shard[0]] + [head_shift(shard[j], j, heads) for j in range(1, heads)]

    far_ids = enc_ids[1:].reshape(-1)
    far_rows = jnp.concatenate(enc_rows[1:], 0)
    dec_sums = send_heads(dec_shard)
    *keeps, send = spread(far_ids, far_rows, columns, base=grad_table_t)
    g_table, table_squares = ScatterDp(keeps, send, dp).run(vocab_local)
    enc_sums = send_heads(enc_shard)
    g_dec = functools.reduce(jnp.add, [value.astype(F32) for value in dec_sums])
    g_enc = functools.reduce(jnp.add, [value.astype(F32) for value in enc_sums])

    def squares(array, axes):
        return jnp.sum(array * array, axis=axes).reshape(-1)

    weight_squares = jnp.concatenate(
        [
            squares(embed_t, (0, 1)),
            squares(attn_in, (2, 3)),
            squares(attn_out_t, (1, 2)),
            squares(ff_in, (1, 2)),
            squares(ff_out_t, (1, 2)),
            squares(gains, (1,)) * lead,
        ]
    )
    matrix_count = weight_squares.shape[0]
    gain_at = sum(widths[0])
    g_gain = g_enc[:, gain_at : gain_at + gain_rows]
    grad_squares = (
        jnp.sum(g_dec * g_dec)
        + jnp.sum(g_enc[:, :gain_at] * g_enc[:, :gain_at])
        + lead * jnp.sum(g_gain * g_gain)
    )
    first_line = jnp.pad(
        jnp.concatenate([weight_squares, loss_part.reshape(1), grad_squares.reshape(1)]),
        (0, lanes - matrix_count - 2),
    ).reshape(1, lanes)
    totals = sum_all(jnp.concatenate([first_line, table_squares], 0), dp, heads)
    grad_norm = jnp.sqrt(totals[0, matrix_count + 1] + jnp.sum(totals[1:]))
    total_loss = totals[0, matrix_count]
    clip = jnp.full((8, 128), jnp.minimum(1.0, CLIP_NORM / grad_norm))
    m_table, v_table, u_table, squares_table = column_call(
        functools.partial(lamb_columns_kernel, vocab_local, 1024),
        [masters[0], moments[0], seconds[0], g_table, clip],
        [(embed_t.shape[0], F32)] * 3,
        1024,
        sums=[(8, 128)],
    )

    def flat9(array):
        return array.reshape((9,) + array.shape[2:])

    def starts(width):
        out = [0]
        for columns in width:
            out.append(out[-1] + columns)
        return out

    at_enc, at_dec = starts(widths[0]), starts(widths[1])
    places = [
        [(0, at_enc[k]) for k in range(3)]
        + [(1, at_dec[k]) for k in range(3)]
        + [(1, at_dec[k]) for k in range(4, 7)],
        [(0, at_enc[3]), (1, at_dec[3]), (1, at_dec[7])],
        [(0, at_enc[4]), (1, at_dec[8])],
        [(0, at_enc[5]), (1, at_dec[9])],
    ]
    groups = [
        tuple(flat9(stack[1]) if k == 1 else stack[k] for stack in (masters, moments, seconds))
        for k in range(1, 5)
    ]
    *fresh, squares_small = lamb_matrices(clip, [g_enc, g_dec], groups, places)
    m_gain, v_gain, u_gain = lamb(gains, moments[5], seconds[5], g_gain.T, clip[0, 0])
    gain_squares = jnp.pad(squares(u_gain, (1,)) * lead, (0, lanes - gain_rows)).reshape(1, lanes)
    small_count = sum(len(matrices) for matrices in places)
    update_totals = sum_all(
        jnp.concatenate([squares_table, squares_small, gain_squares], 0), dp, heads
    )
    update_squares = jnp.concatenate(
        [
            jnp.sum(update_totals[:8]).reshape(1),
            jnp.sum(update_totals[8 : 8 + small_count], 1),
            update_totals[-1, :gain_rows],
        ]
    )
    rates = LEARN_RATE * jnp.sqrt(totals[0, :matrix_count]) / (jnp.sqrt(update_squares) + 1e-06)
    fresh_m = [m_table] + list(fresh[0::3]) + [m_gain]
    fresh_v = [v_table] + list(fresh[1::3]) + [v_gain]
    updates = [u_table] + list(fresh[2::3]) + [u_gain]
    for stack in (fresh_m, fresh_v, updates):
        stack[1] = stack[1].reshape(attn_in.shape)
    shapes = [(1, 1), (3, 3, 1, 1), (3, 1, 1), (2, 1, 1), (2, 1, 1), (gain_rows, 1)]
    fresh_w, start = [], 0
    for master, update, shape in zip(masters, updates, shapes, strict=True):
        count = 1
        for extent in shape:
            count *= extent
        fresh_w.append(master - rates[start : start + count].reshape(shape) * update)
        start += count
    return (
        total_loss.reshape(1),
        grad_norm.reshape(1),
        *transposed(fresh_w),
        *transposed(fresh_m),
        *transposed(fresh_v),
    )


def solution(mesh):
    params = (
        P("head", "dp"),
        P(None, None, "dp", "head"),
        P(None, "head", "dp"),
        P(None, "dp", "head"),
        P(None, "head", "dp"),
        P(None, "dp"),
    )
    return jax.shard_map(
        functools.partial(body, mesh.shape["dp"], mesh.shape["head"]),
        mesh=mesh,
        in_specs=(
            P("dp", None),
            P("dp", None),
            P("dp"),
            P("dp"),
            P("dp", None),
            P("dp", "head"),
            *params,
            *params,
            *params,
        ),
        out_specs=(P(), P(), *params, *params, *params),
        check_vma=False,
    )
```

time: 982 us -> 678 us (0.69)
  Pallas kernels: 47.8 us -> 166 us
  other arithmetic: 160 us -> 52.9 us
  local copies, waits for them, and re-layouts: 156 us -> 61.6 us
  waiting for transfers between devices: 306 us -> 215 us
  starting transfers between devices: 161 us -> 88.9 us
  matrix products: 125 us -> 63.9 us
  between operations: 7.62 us -> 22.4 us
  blocking collectives: 13.2 us -> 0 us
    ppermute x111 -> x31, waiting for transfers between devices: 226 us -> 95.3 us  [dp_swap(): return lax.ppermute(x, 'dp', [(i, i ^ bit) for i in range(dp)])]
    pallas_call x2 -> x16, Pallas kernels: 47.8 us -> 166 us  [the longest x2 37.5 us: spread(): pl.pallas_call(functools.partial(spread_kernel, tile), out_shape=[jax.Sha...]
    dot_general x66 -> x47, matrix products: 117 us -> 55.6 us  [dot(): return jnp.einsum(spec, a, b, preferred_element_type=F32)]
    ppermute x111 -> x31, starting transfers between devices: 81.5 us -> 24.2 us  [dp_swap(): return lax.ppermute(x, 'dp', [(i, i ^ bit) for i in range(dp)])]
    unnamed x473 -> x373, local copies, waits for them, and re-layouts: 67.9 us -> 23.9 us
    slice x64 -> x13, local copies, waits for them, and re-layouts: 47.8 us -> 5.59 us  [the longest x1 1.39 us: body(): enc_looked[j]]
    another operation x20 -> x5, other arithmetic: 36 us -> 3.37 us
    convert_element_type x20 -> x6, other arithmetic: 38.7 us -> 7.66 us  [the longest x1 2.53 us: body(): enc_low = grad_enc_embed.reshape(-1, D).astype(BF)]
  transfers between devices with their start and end apart: 159 -> 70, of which waited for: 59 -> 37; matrix products, arithmetic and copies ran while one was open for 23% -> 11% of each run, Pallas kernels for 5% -> 14%
where the time goes in v2:
time: 678 us; the launch traced here: 670 us
  waiting for transfers between devices  215 us (32%)
  Pallas kernels  166 us (24%)
  starting transfers between devices  88.9 us (13%)
  matrix products  63.9 us (9%)
  local copies, waits for them, and re-layouts  61.6 us (9%)
  other arithmetic  52.9 us (8%)
  between operations  22.4 us (3%)
    ppermute x36, waiting for transfers between devices, head_shift(): lax.ppermute(x, 'head', [(i, (i + step) % heads) for i in range(heads)])  105 us
    ppermute x31, waiting for transfers between devices, dp_swap(): return lax.ppermute(x, 'dp', [(i, i ^ bit) for i in range(dp)])  95.3 us
    ppermute x36, starting transfers between devices, head_shift(): lax.ppermute(x, 'head', [(i, (i + step) % heads) for i in range(heads)])  64.6 us
    dot_general x47, matrix products, dot(): return jnp.einsum(spec, a, b, preferred_element_type=F32)  55.6 us
    pallas_call x2, Pallas kernels, spread(): pl.pallas_call(functools.partial(spread_kernel, tile), out_shape=[jax.Sha...  37.5 us
    pallas_call x1, Pallas kernels, lookup(): pl.pallas_call(functools.partial(lookup_kernel, vocab, tile), out_shape=[...  25.8 us
    ppermute x31, starting transfers between devices, dp_swap(): return lax.ppermute(x, 'dp', [(i, i ^ bit) for i in range(dp)])  24.2 us
    unnamed x373, local copies, waits for them, and re-layouts  23.9 us
  transfers between devices with their start and end apart: 70, of which 37 were waited for; matrix products, arithmetic and copies ran while one was open for 11% of the time, Pallas kernels for 14%

profile of v2, /device:TPU:0, one launch (start us, length us, event | category | flops | bytes accessed | tf_op | source)
XLA Modules:
  0.0 670.4 jit_solution(11814416059267754170)
XLA Ops:
  14.3 3.0 collective-permute-start.3
  18.8 21.3 %collective-permute-done.3.refs_1_.refs_2_ = bf16[64,8032]{1,0:T(8,128)(2,1)S(1)} collective-permute-done((bf16[64,8032]{1,0:T(8,128)(2,1)S(1)}, bf16[64,8032]{1,0:T(8,128)(2,1)S(1)}, u32[]{:S(2)}, u32[]{:S(2)}) %collective-permute-start.3) | collective-permute-done | bytes 1028128 | tf_op jit(solution)/shard_map/ppermute | solution.py:29
  44.6 3.6 collective-permute-start
  49.2 10.7 %collective-permute-done.refs_1_ = bf16[64,3712]{1,0:T(8,128)(2,1)S(1)} collective-permute-done((bf16[64,3712]{1,0:T(8,128)(2,1)}, bf16[64,3712]{1,0:T(8,128)(2,1)S(1)}, u32[]{:S(2)}, u32[]{:S(2)}) %collective-permute-start) | collective-permute-done | bytes 475168 | tf_op jit(solution)/shard_map/ppermute | solution.py:33
  59.9 27.7 %collective-permute-done.1.refs_2_ = bf16[64,3712]{1,0:T(8,128)(2,1)S(1)} collective-permute-done((bf16[64,3712]{1,0:T(8,128)(2,1)}, bf16[64,3712]{1,0:T(8,128)(2,1)S(1)}, u32[]{:S(2)}, u32[]{:S(2)}) %collective-permute-start.1) | collective-permute-done | bytes 475168 | tf_op jit(solution)/shard_map/ppermute | solution.py:33
  88.5 3.0 shard_map.393
  94.9 3.2 collective-permute-done.10.refs_8_.refs_9_
  100.0 25.8 %shard_map.394 = (bf16[2048,512]{1,0:T(8,128)(2,1)}, bf16[8064,512]{1,0:T(8,128)(2,1)}) custom-call(s32[2048,1]{1,0:T(8,128)} %copy.228.ids_ref, bf16[64,8032]{1,0:T(8,128)(2,1)} %copy-done.31, bf16[64,8032]{1,0:T(8,128)(2,1)} %copy-done.39, bf16[64,8032]{1,0:T(8,128)(2,1)} %copy-done.40, bf16[32,8032]{1,0:T(8,128)(2,1)} %copy-done.69, ...), custom_call_target="tpu_custom_call" | custom-call | tf_op jit(solution)/shard_map/pallas_call | solution.py:142
  130.1 3.0 collective-permute-start.23
  138.1 3.3 collective-permute-done.21
  141.4 15.8 %collective-permute-done.22 = bf16[384,512]{1,0:T(8,128)(2,1)} collective-permute-done((bf16[384,512]{1,0:T(8,128)(2,1)S(1)}, bf16[384,512]{1,0:T(8,128)(2,1)}, u32[]{:S(2)}, u32[]{:S(2)}) %collective-permute-start.22) | collective-permute-done | bytes 393248 | tf_op jit(solution)/shard_map/ppermute | solution.py:33
  161.7 6.9 %collective-permute-done.14.refs_3_ = bf16[128,1664]{1,0:T(8,128)(2,1)S(1)} collective-permute-done((bf16[128,1664]{1,0:T(8,128)(2,1)S(1)}, bf16[128,1664]{1,0:T(8,128)(2,1)S(1)}, u32[]{:S(2)}, u32[]{:S(2)}) %collective-permute-start.14) | collective-permute-done | bytes 426016 | tf_op jit(solution)/shard_map/ppermute | solution.py:29
  174.1 6.0 shard_map.395
  185.2 4.6 fusion.115
  189.8 2.9 convolution_convert_fusion.8
  193.2 8.0 %collective-permute-start.24 = (bf16[128,512]{1,0:T(8,128)(2,1)S(1)}, bf16[128,512]{1,0:T(8,128)(2,1)S(1)}, u32[]{:S(2)}, u32[]{:S(2)}) collective-permute-start(bf16[128,512]{1,0:T(8,128)(2,1)S(1)} %get-tuple-element.314), channel_id=1, source_target_pairs={{0,1},{1,2},{2,3},{3,0},{4,5},{5,6},{6,7},{7,4},{8,9},{9,10},{10,1... | collective-permute-start | bytes 393224 | tf_op jit(solution)/shard_map/ppermute | solution.py:33
  207.2 5.3 collective-permute-done.25
  212.8 9.8 %shard_map.396 = (bf16[512,512]{1,0:T(8,128)(2,1)}, bf16[512,512]{1,0:T(8,128)(2,1)}, bf16[512,512]{1,0:T(8,128)(2,1)}, bf16[512,512]{1,0:T(8,128)(2,1)}, bf16[5...) custom-call(s32[8]{0:T(128)} %broadcast_xor_fusion.order_ref, ...), custom_call_target="tpu_custom_call" | custom-call | tf_op jit(solution)/shard_map/pallas_call | solution.py:591
  231.6 2.5 fusion.117
  239.7 3.5 collective-permute-start.27
  247.6 8.7 %collective-permute-done.28 = bf16[128,512]{1,0:T(8,128)(2,1)S(1)} collective-permute-done((bf16[128,512]{1,0:T(8,128)(2,1)S(1)}, bf16[128,512]{1,0:T(8,128)(2,1)S(1)}, u32[]{:S(2)}, u32[]{:S(2)}) %collective-permute-start.28) | collective-permute-done | bytes 131104 | tf_op jit(solution)/shard_map/ppermute | solution.py:33
  262.4 17.2 %shard_map.397 = f32[8,512]{1,0:T(8,128)} custom-call(bf16[512,512]{1,0:T(8,128)(2,1)} %copy.240.final_ref.refs_0_, s32[1,512]{1,0:T(1,128)} %and_select_fusion.label_ref, bf16[8032,512]{1,0:T(8,128)(2,1)} %bitcast.386, bf16[8064,512]{1,0:T(8,128)(2,1)} %get-tuple-element.126.table_ref.refs_0_), custom_call_target="tpu_custom_call" | custom-call | tf_op jit(solution)/shard_map/pallas_call | solution.py:396
  280.4 2.4 collective-permute-start.32
  289.8 22.0 %shard_map.398 = (bf16[8064,512]{1,0:T(8,128)(2,1)}, bf16[512,512]{1,0:T(8,128)(2,1)}) custom-call(bf16[512,512]{1,0:T(8,128)(2,1)} %copy.240.final_ref.refs_0_, s32[1,512]{1,0:T(1,128)} %and_select_fusion.label_ref, f32[8,512]{1,0:T(8,128)} %stack.53.scalar_ref, bf16[8032,512]{1,0:T(8,128)(2,1)} %bitcast.387, ...), custom_call_target="tpu_custom_call" | custom-call | tf_op jit(solution)/shard_map/pallas_call | solution.py:448
  322.5 3.4 collective-permute-done.34
  340.0 2.3 convolution_convert_fusion.9
  346.8 2.9 collective-permute-start.39
  354.8 2.6 convolution_convert_fusion.1
  359.6 2.5 fusion.118
  363.4 2.9 fusion.11
  366.3 7.4 %shard_map.399 = bf16[8,4,64,2048]{3,2,1,0:T(8,128)(2,1)} custom-call(s32[8]{0:T(128)S(1)} %copy-done.18, bf16[128,512]{1,0:T(8,128)(2,1)S(1)} %fusion.53.refs_0_.refs_2_.refs_4_, bf16[128,512]{1,0:T(8,128)(2,1)S(1)} %copy-done.16, bf16[128,512]{1,0:T(8,128)(2,1)S(1)} %fusion.53.refs_0_.refs_2_.refs_4_, bf16[128,512]{1,0:T(8,128)(2,1)S(1)} %copy-done.15, ...), custom_call_target="tpu_custom_call" | custom-call | tf_op jit(solution)/shard_map/pallas_call | solution.py:671
  373.8 2.3 multiply_reduce_fusion.3
  377.0 2.8 select_convert_fusion.refs_9_
  384.8 3.5 multiply_reduce_fusion
  394.3 2.8 convolution_add_fusion
  398.4 3.4 fusion.37
  405.2 2.5 fusion.47
  407.7 8.0 %shard_map.400 = bf16[8,4,64,1664]{3,2,1,0:T(8,128)(2,1)} custom-call(s32[8]{0:T(128)S(1)} %copy-done.18, bf16[384,512]{1,0:T(8,128)(2,1)S(1)} %fusion.27.refs_0_.refs_2_.refs_4_, bf16[384,512]{1,0:T(8,128)(2,1)S(1)} %copy.266.refs_1_, bf16[384,512]{1,0:T(8,128)(2,1)S(1)} %fusion.27.refs_0_.refs_2_.refs_4_, bf16[384,512]{1,0:T(8,128)(2,1)S(1)} %copy.267.refs_3_, ...), custom_call_target="tpu_custom_call" | custom-call | tf_op jit(solution)/shard_map/pallas_call | solution.py:671
  418.6 3.8 collective-permute-start.45
  427.7 19.0 %shard_map.401.refs_0_ = f32[512,8064]{1,0:T(8,128)} custom-call(s32[896,1]{1,0:T(8,128)} %reshape.1149.ids_ref, bf16[896,512]{1,0:T(8,128)(2,1)} %copy-done.84, bf16[512,512]{1,0:T(8,128)(2,1)} %copy.240.final_ref.refs_0_, bf16[8064,512]{1,0:T(8,128)(2,1)} %get-tuple-element.137.refs_1_), custom_call_target="tpu_custom_call" | custom-call | tf_op jit(solution)/shard_map/pallas_call | solution.py:192
  446.8 8.1 %collective-permute-done.46 = bf16[384,512]{1,0:T(8,128)(2,1)S(1)} collective-permute-done((bf16[384,512]{1,0:T(8,128)(2,1)S(1)}, bf16[384,512]{1,0:T(8,128)(2,1)S(1)}, u32[]{:S(2)}, u32[]{:S(2)}) %collective-permute-start.46) | collective-permute-done | bytes 393248 | tf_op jit(solution)/shard_map/ppermute | solution.py:33
  456.0 18.4 %shard_map.402 = (f32[64,8064]{1,0:T(8,128)}, f32[64,8064]{1,0:T(8,128)}, f32[64,8064]{1,0:T(8,128)}, f32[64,8064]{1,0:T(8,128)}, bf16[256,8064]{1,0:T(8,128)(2,1)}) custom-call(s32[1152,1]{1,0:T(8,128)} %bitcast.401, bf16[1152,512]{1,0:T(8,128)(2,1)} %pad_maximum_fusion.rows_ref, f32[512,8064]{1,0:T(8,128)} %shard_map.401.refs_0_), custom_call_target="tpu_custom_call" | custom-call | tf_op jit(solution)/shard_map/pallas_call | solution.py:192
  474.4 7.3 %collective-permute-done.48.got_ref.got = bf16[256,8064]{1,0:T(8,128)(2,1)S(1)} collective-permute-done((bf16[256,8064]{1,0:T(8,128)(2,1)}, bf16[256,8064]{1,0:T(8,128)(2,1)S(1)}, u32[]{:S(2)}, u32[]{:S(2)}) %collective-permute-start.48) | collective-permute-done | bytes 4128800 | tf_op jit(solution)/shard_map/ppermute | solution.py:29
  483.7 6.3 shard_map.403
  495.5 9.3 %collective-permute-done.51.got_a = bf16[32,8064]{1,0:T(8,128)(2,1)S(1)} collective-permute-done((bf16[32,8064]{1,0:T(8,128)(2,1)}, bf16[32,8064]{1,0:T(8,128)(2,1)S(1)}, u32[]{:S(2)}, u32[]{:S(2)}) %collective-permute-start.51) | collective-permute-done | bytes 516128 | tf_op jit(solution)/shard_map/ppermute | solution.py:29
  505.9 2.7 shard_map.404
  511.3 9.0 %collective-permute-done.49.x_low = bf16[32,8064]{1,0:T(8,128)(2,1)S(1)} collective-permute-done((bf16[32,8064]{1,0:T(8,128)(2,1)}, bf16[32,8064]{1,0:T(8,128)(2,1)S(1)}, u32[]{:S(2)}, u32[]{:S(2)}) %collective-permute-start.49) | collective-permute-done | bytes 516128 | tf_op jit(solution)/shard_map/ppermute | solution.py:29
  522.2 21.0 %collective-permute-done.53.y_low = bf16[32,8064]{1,0:T(8,128)(2,1)S(1)} collective-permute-done((bf16[32,8064]{1,0:T(8,128)(2,1)}, bf16[32,8064]{1,0:T(8,128)(2,1)S(1)}, u32[]{:S(2)}, u32[]{:S(2)}) %collective-permute-start.53) | collective-permute-done | bytes 516128 | tf_op jit(solution)/shard_map/ppermute | solution.py:29
  544.2 4.8 shard_map.405
  552.4 2.8 collective-permute-start.44
  555.2 13.9 %reduce-scatter.3.cloned.1.call-done = bf16[1,4,64,2048]{3,2,1,0:T(8,128)(2,1)} async-done(((bf16[8,4,64,2048]{3,2,1,0:T(8,128)(2,1)}), bf16[1,4,64,2048]{3,2,1,0:T(8,128)(2,1)}) %reduce-scatter.3.cloned.1.call-update) | async-done | bytes 1048592 | tf_op jit(solution)/shard_map/reduce_scatter | solution.py:938
  571.8 2.4 collective-permute-start.37
  578.7 2.7 collective-permute-done.36
  581.5 10.1 %collective-permute-done.37 = bf16[64,2048]{1,0:T(8,128)(2,1)S(1)} collective-permute-done((bf16[64,2048]{1,0:T(8,128)(2,1)S(1)}, bf16[64,2048]{1,0:T(8,128)(2,1)S(1)}, u32[]{:S(2)}, u32[]{:S(2)}) %collective-permute-start.37) | collective-permute-done | bytes 262176 | tf_op jit(solution)/shard_map/ppermute | solution.py:33
  591.5 2.5 multiply_reduce_fusion.9
  598.7 2.3 collective-permute-done.56
  602.4 2.3 collective-permute-done.57
  604.6 6.1 collective-permute-start.58
  619.3 9.4 %shard_map.406 = (f32[64,8032]{1,0:T(8,128)}, f32[64,8032]{1,0:T(8,128)}, f32[64,8032]{1,0:T(8,128)}, f32[8,128]{1,0:T(8,128)}) custom-call(f32[64,8032]{1,0:T(8,128)} %bitcast.385, f32[64,8032]{1,0:T(8,128)} %bitcast.403, f32[64,8032]{1,0:T(8,128)} %bitcast.404, f32[64,8032]{1,0:T(8,128)} %get-tuple-element.152.g, f32[8,128]{1,0:T(8,128)} %broadcast_in_dim.64.clip.clip_ref), custom_call_target="tpu_custom_call" | custom-call | tf_op jit(solution)/shard_map/pallas_call | solution.py:210
  628.8 3.8 shard_map.407
  636.8 2.4 collective-permute-done.62
  640.6 2.4 collective-permute-done.63
  642.9 3.2 collective-permute-start.65
  659.3 3.1 subtract_bitcast_fusion
  (684 shorter events, 199.5 us)
Async XLA Ops:
  7.2 205.6 %all-gather.3.cloned.1.call-start = ((), (), s32[]{:S(2)}) async-start(), calls=%async_computation.4 | async-start | bytes 9437184 | tf_op jit(solution)/shard_map/all_gather | solution.py:819
  14.3 25.8 %collective-permute-start.3 = (bf16[64,8032]{1,0:T(8,128)(2,1)S(1)}, bf16[64,8032]{1,0:T(8,128)(2,1)S(1)}, u32[]{:S(2)}, u32[]{:S(2)}) collective-permute-start(bf16[64,8032]{1,0:T(8,128)(2,1)S(1)} %bitcast_convert_fusion.refs_0_.refs_1_), channel_id=1, source_target_pairs={{0,16},{4,20},{8,24},{12,28},{16,0},{20,4},{24,8},{28,12},{1,17},{... | collective-permute-start | bytes 3084296 | tf_op jit(solution)/shard_map/ppermute | solution.py:29
  17.3 24.7 %collective-permute-start.5 = (bf16[64,8032]{1,0:T(8,128)(2,1)S(1)}, bf16[64,8032]{1,0:T(8,128)(2,1)S(1)}, u32[]{:S(2)}, u32[]{:S(2)}) collective-permute-start(bf16[64,8032]{1,0:T(8,128)(2,1)S(1)} %bitcast_convert_fusion.refs_0_.refs_1_), channel_id=1, source_target_pairs={{0,8},{4,12},{8,0},{12,4},{16,24},{20,28},{24,16},{28,20},{1,9},{5... | collective-permute-start | bytes 3084296 | tf_op jit(solution)/shard_map/ppermute | solution.py:29
  40.1 47.4 %collective-permute-start.4 = (bf16[32,8032]{1,0:T(8,128)(2,1)S(1)}, bf16[32,8032]{1,0:T(8,128)(2,1)S(1)}, u32[]{:S(2)}, u32[]{:S(2)}) collective-permute-start(bf16[32,8032]{1,0:T(8,128)(2,1)S(1)} %slice.271), channel_id=1, source_target_pairs={{0,8},{4,12},{8,0},{12,4},{16,24},{20,28},{24,16},{28,20},{1,9},{5... | collective-permute-start | bytes 1542152 | tf_op jit(solution)/shard_map/ppermute | solution.py:29
  43.0 44.6 %collective-permute-start.6 = (bf16[32,8032]{1,0:T(8,128)(2,1)S(1)}, bf16[32,8032]{1,0:T(8,128)(2,1)S(1)}, u32[]{:S(2)}, u32[]{:S(2)}) collective-permute-start(bf16[32,8032]{1,0:T(8,128)(2,1)S(1)} %slice.272), channel_id=1, source_target_pairs={{0,16},{4,20},{8,24},{12,28},{16,0},{20,4},{24,8},{28,12},{1,17},{... | collective-permute-start | bytes 1542152 | tf_op jit(solution)/shard_map/ppermute | solution.py:29
  44.6 15.3 %collective-permute-start = (bf16[64,3712]{1,0:T(8,128)(2,1)}, bf16[64,3712]{1,0:T(8,128)(2,1)S(1)}, u32[]{:S(2)}, u32[]{:S(2)}) collective-permute-start(bf16[64,3712]{1,0:T(8,128)(2,1)} %shard_map.392.refs_0_), channel_id=1, source_target_pairs={{0,3},{1,0},{2,1},{3,2},{4,7},{5,4},{6,5},{7,6},{8,11},{9,8},{10,9... | collective-permute-start | bytes 1425416 | tf_op jit(solution)/shard_map/ppermute | solution.py:33
  48.2 39.3 %collective-permute-start.1 = (bf16[64,3712]{1,0:T(8,128)(2,1)}, bf16[64,3712]{1,0:T(8,128)(2,1)S(1)}, u32[]{:S(2)}, u32[]{:S(2)}) collective-permute-start(bf16[64,3712]{1,0:T(8,128)(2,1)} %shard_map.392.refs_0_), channel_id=1, source_target_pairs={{0,2},{1,3},{2,0},{3,1},{4,6},{5,7},{6,4},{7,5},{8,10},{9,11},{10,... | collective-permute-start | bytes 1425416 | tf_op jit(solution)/shard_map/ppermute | solution.py:33
  48.2 39.3 %collective-permute-start.2 = (bf16[64,3712]{1,0:T(8,128)(2,1)}, bf16[64,3712]{1,0:T(8,128)(2,1)S(1)}, u32[]{:S(2)}, u32[]{:S(2)}) collective-permute-start(bf16[64,3712]{1,0:T(8,128)(2,1)} %shard_map.392.refs_0_), channel_id=1, source_target_pairs={{0,1},{1,2},{2,3},{3,0},{4,5},{5,6},{6,7},{7,4},{8,9},{9,10},{10,1... | collective-permute-start | bytes 1425416 | tf_op jit(solution)/shard_map/ppermute | solution.py:33
  91.5 457.5 %reduce-scatter.5.cloned.1.call-start = ((), (), s32[]{:S(2)}) async-start(), calls=%async_computation.3 | async-start | bytes 7667712 | tf_op jit(solution)/shard_map/reduce_scatter | solution.py:958
  91.7 8.3 %collective-permute-start.8 = (bf16[64,8032]{1,0:T(8,128)(2,1)S(1)}, bf16[64,8032]{1,0:T(8,128)(2,1)}, u32[]{:S(2)}, u32[]{:S(2)}) collective-permute-start(bf16[64,8032]{1,0:T(8,128)(2,1)S(1)} %collective-permute-done.3.refs_1_.refs_2_), channel_id=1, source_target_pairs={{0,4},{4,0},{8,12},{12,8},{16,20},{20,16},{24,28},{28,24},{1,5},{5... | collective-permute-start | bytes 3084296 | tf_op jit(solution)/shard_map/ppermute | solution.py:29
  92.2 7.9 %collective-permute-start.9 = (bf16[64,8032]{1,0:T(8,128)(2,1)}, bf16[64,8032]{1,0:T(8,128)(2,1)}, u32[]{:S(2)}, u32[]{:S(2)}) collective-permute-start(bf16[64,8032]{1,0:T(8,128)(2,1)} %copy-done.40), channel_id=1, source_target_pairs={{0,4},{4,0},{8,12},{12,8},{16,20},{20,16},{24,28},{28,24},{1,5},{5... | collective-permute-start | bytes 3084296 | tf_op jit(solution)/shard_map/ppermute | solution.py:29
  92.2 5.9 collective-permute-start.10
  92.7 7.3 %collective-permute-start.11 = (bf16[32,8032]{1,0:T(8,128)(2,1)S(1)}, bf16[32,8032]{1,0:T(8,128)(2,1)}, u32[]{:S(2)}, u32[]{:S(2)}) collective-permute-start(bf16[32,8032]{1,0:T(8,128)(2,1)S(1)} %collective-permute-done.6.refs_4_.refs_5_), channel_id=1, source_target_pairs={{0,4},{4,0},{8,12},{12,8},{16,20},{20,16},{24,28},{28,24},{1,5},{5... | collective-permute-start | bytes 1542152 | tf_op jit(solution)/shard_map/ppermute | solution.py:29
  94.4 40.9 %collective-permute-start.12 = (bf16[256,1664]{1,0:T(8,128)(2,1)}, bf16[256,1664]{1,0:T(8,128)(2,1)}, u32[]{:S(2)}, u32[]{:S(2)}) collective-permute-start(bf16[256,1664]{1,0:T(8,128)(2,1)} %get-tuple-element.101.refs_0_), channel_id=1, source_target_pairs={{0,16},{4,20},{8,24},{12,28},{16,0},{20,4},{24,8},{28,12},{1,17},{... | collective-permute-start | bytes 2555912 | tf_op jit(solution)/shard_map/ppermute | solution.py:29
  98.1 37.3 %collective-permute-start.13 = (bf16[256,1664]{1,0:T(8,128)(2,1)}, bf16[256,1664]{1,0:T(8,128)(2,1)}, u32[]{:S(2)}, u32[]{:S(2)}) collective-permute-start(bf16[256,1664]{1,0:T(8,128)(2,1)} %get-tuple-element.101.refs_0_), channel_id=1, source_target_pairs={{0,8},{4,12},{8,0},{12,4},{16,24},{20,28},{24,16},{28,20},{1,9},{5... | collective-permute-start | bytes 2555912 | tf_op jit(solution)/shard_map/ppermute | solution.py:29
  127.3 14.0 %collective-permute-start.21 = (bf16[384,512]{1,0:T(8,128)(2,1)S(1)}, bf16[384,512]{1,0:T(8,128)(2,1)}, u32[]{:S(2)}, u32[]{:S(2)}) collective-permute-start(bf16[384,512]{1,0:T(8,128)(2,1)S(1)} %get-tuple-element.302), channel_id=1, source_target_pairs={{0,1},{1,2},{2,3},{3,0},{4,5},{5,6},{6,7},{7,4},{8,9},{9,10},{10,1... | collective-permute-start | bytes 1179656 | tf_op jit(solution)/shard_map/ppermute | solution.py:33
  128.5 28.7 %collective-permute-start.22 = (bf16[384,512]{1,0:T(8,128)(2,1)S(1)}, bf16[384,512]{1,0:T(8,128)(2,1)}, u32[]{:S(2)}, u32[]{:S(2)}) collective-permute-start(bf16[384,512]{1,0:T(8,128)(2,1)S(1)} %get-tuple-element.304), channel_id=1, source_target_pairs={{0,2},{1,3},{2,0},{3,1},{4,6},{5,7},{6,4},{7,5},{8,10},{9,11},{10,... | collective-permute-start | bytes 1179656 | tf_op jit(solution)/shard_map/ppermute | solution.py:33
  130.1 28.7 %collective-permute-start.23 = (bf16[384,512]{1,0:T(8,128)(2,1)S(1)}, bf16[384,512]{1,0:T(8,128)(2,1)}, u32[]{:S(2)}, u32[]{:S(2)}) collective-permute-start(bf16[384,512]{1,0:T(8,128)(2,1)S(1)} %get-tuple-element.303), channel_id=1, source_target_pairs={{0,3},{1,0},{2,1},{3,2},{4,7},{5,4},{6,5},{7,6},{8,11},{9,8},{10,9... | collective-permute-start | bytes 1179656 | tf_op jit(solution)/shard_map/ppermute | solution.py:33
  135.3 36.3 %collective-permute-start.16 = (bf16[256,1664]{1,0:T(8,128)(2,1)S(1)}, bf16[256,1664]{1,0:T(8,128)(2,1)S(1)}, u32[]{:S(2)}, u32[]{:S(2)}) collective-permute-start(bf16[256,1664]{1,0:T(8,128)(2,1)S(1)} %copy-done.89), channel_id=1, source_target_pairs={{0,4},{4,0},{8,12},{12,8},{16,20},{20,16},{24,28},{28,24},{1,5},{5... | collective-permute-start | bytes 2555912 | tf_op jit(solution)/shard_map/ppermute | solution.py:29
  136.4 35.2 %collective-permute-start.17 = (bf16[256,1664]{1,0:T(8,128)(2,1)}, bf16[256,1664]{1,0:T(8,128)(2,1)S(1)}, u32[]{:S(2)}, u32[]{:S(2)}) collective-permute-start(bf16[256,1664]{1,0:T(8,128)(2,1)} %collective-permute-done.12.refs_1_), channel_id=1, source_target_pairs={{0,4},{4,0},{8,12},{12,8},{16,20},{20,16},{24,28},{28,24},{1,5},{5... | collective-permute-start | bytes 2555912 | tf_op jit(solution)/shard_map/ppermute | solution.py:29
  141.3 30.3 %collective-permute-start.18 = (bf16[256,1664]{1,0:T(8,128)(2,1)}, bf16[256,1664]{1,0:T(8,128)(2,1)S(1)}, u32[]{:S(2)}, u32[]{:S(2)}) collective-permute-start(bf16[256,1664]{1,0:T(8,128)(2,1)} %collective-permute-done.13.refs_2_), channel_id=1, source_target_pairs={{0,4},{4,0},{8,12},{12,8},{16,20},{20,16},{24,28},{28,24},{1,5},{5... | collective-permute-start | bytes 2555912 | tf_op jit(solution)/shard_map/ppermute | solution.py:29
  157.2 11.4 %collective-permute-start.14 = (bf16[128,1664]{1,0:T(8,128)(2,1)S(1)}, bf16[128,1664]{1,0:T(8,128)(2,1)S(1)}, u32[]{:S(2)}, u32[]{:S(2)}) collective-permute-start(bf16[128,1664]{1,0:T(8,128)(2,1)S(1)} %slice.215), channel_id=1, source_target_pairs={{0,8},{4,12},{8,0},{12,4},{16,24},{20,28},{24,16},{28,20},{1,9},{5... | collective-permute-start | bytes 1277960 | tf_op jit(solution)/shard_map/ppermute | solution.py:29
  158.8 10.9 %collective-permute-start.15 = (bf16[128,1664]{1,0:T(8,128)(2,1)S(1)}, bf16[128,1664]{1,0:T(8,128)(2,1)S(1)}, u32[]{:S(2)}, u32[]{:S(2)}) collective-permute-start(bf16[128,1664]{1,0:T(8,128)(2,1)S(1)} %slice.216), channel_id=1, source_target_pairs={{0,16},{4,20},{8,24},{12,28},{16,0},{20,4},{24,8},{28,12},{1,17},{... | collective-permute-start | bytes 1277960 | tf_op jit(solution)/shard_map/ppermute | solution.py:29
  193.2 14.0 %collective-permute-start.24 = (bf16[128,512]{1,0:T(8,128)(2,1)S(1)}, bf16[128,512]{1,0:T(8,128)(2,1)S(1)}, u32[]{:S(2)}, u32[]{:S(2)}) collective-permute-start(bf16[128,512]{1,0:T(8,128)(2,1)S(1)} %get-tuple-element.314), channel_id=1, source_target_pairs={{0,1},{1,2},{2,3},{3,0},{4,5},{5,6},{6,7},{7,4},{8,9},{9,10},{10,1... | collective-permute-start | bytes 393224 | tf_op jit(solution)/shard_map/ppermute | solution.py:33
  201.2 11.3 %collective-permute-start.25 = (bf16[128,512]{1,0:T(8,128)(2,1)S(1)}, bf16[128,512]{1,0:T(8,128)(2,1)S(1)}, u32[]{:S(2)}, u32[]{:S(2)}) collective-permute-start(bf16[128,512]{1,0:T(8,128)(2,1)S(1)} %get-tuple-element.316), channel_id=1, source_target_pairs={{0,2},{1,3},{2,0},{3,1},{4,6},{5,7},{6,4},{7,5},{8,10},{9,11},{10,... | collective-permute-start | bytes 393224 | tf_op jit(solution)/shard_map/ppermute | solution.py:33
  203.3 9.2 %collective-permute-start.26 = (bf16[128,512]{1,0:T(8,128)(2,1)S(1)}, bf16[128,512]{1,0:T(8,128)(2,1)S(1)}, u32[]{:S(2)}, u32[]{:S(2)}) collective-permute-start(bf16[128,512]{1,0:T(8,128)(2,1)S(1)} %get-tuple-element.315), channel_id=1, source_target_pairs={{0,3},{1,0},{2,1},{3,2},{4,7},{5,4},{6,5},{7,6},{8,11},{9,8},{10,9... | collective-permute-start | bytes 393224 | tf_op jit(solution)/shard_map/ppermute | solution.py:33
  239.7 7.2 %collective-permute-start.27 = (bf16[128,512]{1,0:T(8,128)(2,1)S(1)}, bf16[128,512]{1,0:T(8,128)(2,1)S(1)}, u32[]{:S(2)}, u32[]{:S(2)}) collective-permute-start(bf16[128,512]{1,0:T(8,128)(2,1)S(1)} %get-tuple-element.297), channel_id=1, source_target_pairs={{0,3},{1,0},{2,1},{3,2},{4,7},{5,4},{6,5},{7,6},{8,11},{9,8},{10,9... | collective-permute-start | bytes 393224 | tf_op jit(solution)/shard_map/ppermute | solution.py:33
  243.9 12.4 %collective-permute-start.28 = (bf16[128,512]{1,0:T(8,128)(2,1)S(1)}, bf16[128,512]{1,0:T(8,128)(2,1)S(1)}, u32[]{:S(2)}, u32[]{:S(2)}) collective-permute-start(bf16[128,512]{1,0:T(8,128)(2,1)S(1)} %get-tuple-element.297), channel_id=1, source_target_pairs={{0,2},{1,3},{2,0},{3,1},{4,6},{5,7},{6,4},{7,5},{8,10},{9,11},{10,... | collective-permute-start | bytes 393224 | tf_op jit(solution)/shard_map/ppermute | solution.py:33
  246.4 10.6 %collective-permute-start.29 = (bf16[128,512]{1,0:T(8,128)(2,1)S(1)}, bf16[128,512]{1,0:T(8,128)(2,1)S(1)}, u32[]{:S(2)}, u32[]{:S(2)}) collective-permute-start(bf16[128,512]{1,0:T(8,128)(2,1)S(1)} %get-tuple-element.297), channel_id=1, source_target_pairs={{0,1},{1,2},{2,3},{3,0},{4,5},{5,6},{6,7},{7,4},{8,9},{9,10},{10,1... | collective-permute-start | bytes 393224 | tf_op jit(solution)/shard_map/ppermute | solution.py:33
  279.6 3.9 collective-permute-start.30
  279.6 4.8 collective-permute-start.31
  280.4 6.1 collective-permute-start.32
  314.0 8.4 %collective-permute-start.33 = (bf16[128,512]{1,0:T(8,128)(2,1)}, bf16[128,512]{1,0:T(8,128)(2,1)S(1)}, u32[]{:S(2)}, u32[]{:S(2)}) collective-permute-start(bf16[128,512]{1,0:T(8,128)(2,1)} %get-tuple-element.311), channel_id=1, source_target_pairs={{0,1},{1,2},{2,3},{3,0},{4,5},{5,6},{6,7},{7,4},{8,9},{9,10},{10,1... | collective-permute-start | bytes 393224 | tf_op jit(solution)/shard_map/ppermute | solution.py:33
  314.2 11.7 %collective-permute-start.34 = (bf16[128,512]{1,0:T(8,128)(2,1)}, bf16[128,512]{1,0:T(8,128)(2,1)}, u32[]{:S(2)}, u32[]{:S(2)}) collective-permute-start(bf16[128,512]{1,0:T(8,128)(2,1)} %get-tuple-element.312), channel_id=1, source_target_pairs={{0,2},{1,3},{2,0},{3,1},{4,6},{5,7},{6,4},{7,5},{8,10},{9,11},{10,... | collective-permute-start | bytes 393224 | tf_op jit(solution)/shard_map/ppermute | solution.py:33
  316.4 9.5 %collective-permute-start.35 = (bf16[128,512]{1,0:T(8,128)(2,1)}, bf16[128,512]{1,0:T(8,128)(2,1)}, u32[]{:S(2)}, u32[]{:S(2)}) collective-permute-start(bf16[128,512]{1,0:T(8,128)(2,1)} %get-tuple-element.313), channel_id=1, source_target_pairs={{0,3},{1,0},{2,1},{3,2},{4,7},{5,4},{6,5},{7,6},{8,11},{9,8},{10,9... | collective-permute-start | bytes 393224 | tf_op jit(solution)/shard_map/ppermute | solution.py:33
  346.8 34.8 %collective-permute-start.39 = (bf16[128,512]{1,0:T(8,128)(2,1)}, bf16[128,512]{1,0:T(8,128)(2,1)}, u32[]{:S(2)}, u32[]{:S(2)}) collective-permute-start(bf16[128,512]{1,0:T(8,128)(2,1)} %fusion.58), channel_id=1, source_target_pairs={{0,3},{1,0},{2,1},{3,2},{4,7},{5,4},{6,5},{7,6},{8,11},{9,8},{10,9... | collective-permute-start | bytes 393224 | tf_op jit(solution)/shard_map/ppermute | solution.py:33
  349.7 31.9 %collective-permute-start.40 = (bf16[128,512]{1,0:T(8,128)(2,1)}, bf16[128,512]{1,0:T(8,128)(2,1)}, u32[]{:S(2)}, u32[]{:S(2)}) collective-permute-start(bf16[128,512]{1,0:T(8,128)(2,1)} %fusion.58), channel_id=1, source_target_pairs={{0,2},{1,3},{2,0},{3,1},{4,6},{5,7},{6,4},{7,5},{8,10},{9,11},{10,... | collective-permute-start | bytes 393224 | tf_op jit(solution)/shard_map/ppermute | solution.py:33
  350.6 31.0 %collective-permute-start.41 = (bf16[128,512]{1,0:T(8,128)(2,1)}, bf16[128,512]{1,0:T(8,128)(2,1)}, u32[]{:S(2)}, u32[]{:S(2)}) collective-permute-start(bf16[128,512]{1,0:T(8,128)(2,1)} %fusion.58), channel_id=1, source_target_pairs={{0,1},{1,2},{2,3},{3,0},{4,5},{5,6},{6,7},{7,4},{8,9},{9,10},{10,1... | collective-permute-start | bytes 393224 | tf_op jit(solution)/shard_map/ppermute | solution.py:33
  415.8 153.3 %reduce-scatter.3.cloned.1.call-start = ((), (), s32[]{:S(2)}) async-start(), calls=%async_computation.2 | async-start | bytes 9437184 | tf_op jit(solution)/shard_map/reduce_scatter | solution.py:938
  418.6 28.1 %collective-permute-start.45 = (bf16[384,512]{1,0:T(8,128)(2,1)S(1)}, bf16[384,512]{1,0:T(8,128)(2,1)S(1)}, u32[]{:S(2)}, u32[]{:S(2)}) collective-permute-start(bf16[384,512]{1,0:T(8,128)(2,1)S(1)} %copy-done.79), channel_id=1, source_target_pairs={{0,3},{1,0},{2,1},{3,2},{4,7},{5,4},{6,5},{7,6},{8,11},{9,8},{10,9... | collective-permute-start | bytes 1179656 | tf_op jit(solution)/shard_map/ppermute | solution.py:33
  422.4 32.4 %collective-permute-start.46 = (bf16[384,512]{1,0:T(8,128)(2,1)S(1)}, bf16[384,512]{1,0:T(8,128)(2,1)S(1)}, u32[]{:S(2)}, u32[]{:S(2)}) collective-permute-start(bf16[384,512]{1,0:T(8,128)(2,1)S(1)} %copy-done.79), channel_id=1, source_target_pairs={{0,2},{1,3},{2,0},{3,1},{4,6},{5,7},{6,4},{7,5},{8,10},{9,11},{10,... | collective-permute-start | bytes 1179656 | tf_op jit(solution)/shard_map/ppermute | solution.py:33
  422.7 32.2 %collective-permute-start.47 = (bf16[384,512]{1,0:T(8,128)(2,1)S(1)}, bf16[384,512]{1,0:T(8,128)(2,1)S(1)}, u32[]{:S(2)}, u32[]{:S(2)}) collective-permute-start(bf16[384,512]{1,0:T(8,128)(2,1)S(1)} %copy-done.79), channel_id=1, source_target_pairs={{0,1},{1,2},{2,3},{3,0},{4,5},{5,6},{6,7},{7,4},{8,9},{9,10},{10,1... | collective-permute-start | bytes 1179656 | tf_op jit(solution)/shard_map/ppermute | solution.py:33
  474.4 7.3 %collective-permute-start.48 = (bf16[256,8064]{1,0:T(8,128)(2,1)}, bf16[256,8064]{1,0:T(8,128)(2,1)S(1)}, u32[]{:S(2)}, u32[]{:S(2)}) collective-permute-start(bf16[256,8064]{1,0:T(8,128)(2,1)} %get-tuple-element.139), channel_id=1, source_target_pairs={{0,4},{4,0},{8,12},{12,8},{16,20},{20,16},{24,28},{28,24},{1,5},{5... | collective-permute-start | bytes 12386312 | tf_op jit(solution)/shard_map/ppermute | solution.py:29
  490.0 14.8 %collective-permute-start.51 = (bf16[32,8064]{1,0:T(8,128)(2,1)}, bf16[32,8064]{1,0:T(8,128)(2,1)S(1)}, u32[]{:S(2)}, u32[]{:S(2)}) collective-permute-start(bf16[32,8064]{1,0:T(8,128)(2,1)} %get-tuple-element.146), channel_id=1, source_target_pairs={{0,8},{4,12},{8,0},{12,4},{16,24},{20,28},{24,16},{28,20},{1,9},{5... | collective-permute-start | bytes 1548296 | tf_op jit(solution)/shard_map/ppermute | solution.py:29
  490.9 14.9 %collective-permute-start.52 = (bf16[32,8064]{1,0:T(8,128)(2,1)}, bf16[32,8064]{1,0:T(8,128)(2,1)}, u32[]{:S(2)}, u32[]{:S(2)}) collective-permute-start(bf16[32,8064]{1,0:T(8,128)(2,1)} %get-tuple-element.148), channel_id=1, source_target_pairs={{0,16},{4,20},{8,24},{12,28},{16,0},{20,4},{24,8},{28,12},{1,17},{... | collective-permute-start | bytes 1548296 | tf_op jit(solution)/shard_map/ppermute | solution.py:29
  493.3 26.9 %collective-permute-start.49 = (bf16[32,8064]{1,0:T(8,128)(2,1)}, bf16[32,8064]{1,0:T(8,128)(2,1)S(1)}, u32[]{:S(2)}, u32[]{:S(2)}) collective-permute-start(bf16[32,8064]{1,0:T(8,128)(2,1)} %get-tuple-element.143), channel_id=1, source_target_pairs={{0,8},{4,12},{8,0},{12,4},{16,24},{20,28},{24,16},{28,20},{1,9},{5... | collective-permute-start | bytes 1548296 | tf_op jit(solution)/shard_map/ppermute | solution.py:29
  494.1 28.1 %collective-permute-start.50 = (bf16[32,8064]{1,0:T(8,128)(2,1)}, bf16[32,8064]{1,0:T(8,128)(2,1)S(1)}, u32[]{:S(2)}, u32[]{:S(2)}) collective-permute-start(bf16[32,8064]{1,0:T(8,128)(2,1)} %get-tuple-element.144), channel_id=1, source_target_pairs={{0,16},{4,20},{8,24},{12,28},{16,0},{20,4},{24,8},{28,12},{1,17},{... | collective-permute-start | bytes 1548296 | tf_op jit(solution)/shard_map/ppermute | solution.py:29
  508.6 34.6 %collective-permute-start.53 = (bf16[32,8064]{1,0:T(8,128)(2,1)}, bf16[32,8064]{1,0:T(8,128)(2,1)S(1)}, u32[]{:S(2)}, u32[]{:S(2)}) collective-permute-start(bf16[32,8064]{1,0:T(8,128)(2,1)} %get-tuple-element.149), channel_id=1, source_target_pairs={{0,16},{4,20},{8,24},{12,28},{16,0},{20,4},{24,8},{28,12},{1,17},{... | collective-permute-start | bytes 1548296 | tf_op jit(solution)/shard_map/ppermute | solution.py:29
  509.5 33.7 %collective-permute-start.54 = (bf16[32,8064]{1,0:T(8,128)(2,1)}, bf16[32,8064]{1,0:T(8,128)(2,1)S(1)}, u32[]{:S(2)}, u32[]{:S(2)}) collective-permute-start(bf16[32,8064]{1,0:T(8,128)(2,1)} %get-tuple-element.150), channel_id=1, source_target_pairs={{0,8},{4,12},{8,0},{12,4},{16,24},{20,28},{24,16},{28,20},{1,9},{5... | collective-permute-start | bytes 1548296 | tf_op jit(solution)/shard_map/ppermute | solution.py:29
  550.2 24.0 %collective-permute-start.42 = (bf16[64,1664]{1,0:T(8,128)(2,1)S(1)}, bf16[64,1664]{1,0:T(8,128)(2,1)S(1)}, u32[]{:S(2)}, u32[]{:S(2)}) collective-permute-start(bf16[64,1664]{1,0:T(8,128)(2,1)S(1)} %get-tuple-element.308), channel_id=1, source_target_pairs={{0,1},{1,2},{2,3},{3,0},{4,5},{5,6},{6,7},{7,4},{8,9},{9,10},{10,1... | collective-permute-start | bytes 638984 | tf_op jit(solution)/shard_map/ppermute | solution.py:33
  550.3 25.4 %collective-permute-start.43 = (bf16[64,1664]{1,0:T(8,128)(2,1)S(1)}, bf16[64,1664]{1,0:T(8,128)(2,1)S(1)}, u32[]{:S(2)}, u32[]{:S(2)}) collective-permute-start(bf16[64,1664]{1,0:T(8,128)(2,1)S(1)} %get-tuple-element.310), channel_id=1, source_target_pairs={{0,2},{1,3},{2,0},{3,1},{4,6},{5,7},{6,4},{7,5},{8,10},{9,11},{10,... | collective-permute-start | bytes 638984 | tf_op jit(solution)/shard_map/ppermute | solution.py:33
  552.4 23.3 %collective-permute-start.44 = (bf16[64,1664]{1,0:T(8,128)(2,1)S(1)}, bf16[64,1664]{1,0:T(8,128)(2,1)S(1)}, u32[]{:S(2)}, u32[]{:S(2)}) collective-permute-start(bf16[64,1664]{1,0:T(8,128)(2,1)S(1)} %get-tuple-element.309), channel_id=1, source_target_pairs={{0,3},{1,0},{2,1},{3,2},{4,7},{5,4},{6,5},{7,6},{8,11},{9,8},{10,9... | collective-permute-start | bytes 638984 | tf_op jit(solution)/shard_map/ppermute | solution.py:33
  570.3 11.2 %collective-permute-start.36 = (bf16[64,2048]{1,0:T(8,128)(2,1)S(1)}, bf16[64,2048]{1,0:T(8,128)(2,1)S(1)}, u32[]{:S(2)}, u32[]{:S(2)}) collective-permute-start(bf16[64,2048]{1,0:T(8,128)(2,1)S(1)} %get-tuple-element.305), channel_id=1, source_target_pairs={{0,1},{1,2},{2,3},{3,0},{4,5},{5,6},{6,7},{7,4},{8,9},{9,10},{10,1... | collective-permute-start | bytes 786440 | tf_op jit(solution)/shard_map/ppermute | solution.py:33
  571.8 19.7 %collective-permute-start.37 = (bf16[64,2048]{1,0:T(8,128)(2,1)S(1)}, bf16[64,2048]{1,0:T(8,128)(2,1)S(1)}, u32[]{:S(2)}, u32[]{:S(2)}) collective-permute-start(bf16[64,2048]{1,0:T(8,128)(2,1)S(1)} %get-tuple-element.307), channel_id=1, source_target_pairs={{0,2},{1,3},{2,0},{3,1},{4,6},{5,7},{6,4},{7,5},{8,10},{9,11},{10,... | collective-permute-start | bytes 786440 | tf_op jit(solution)/shard_map/ppermute | solution.py:33
  574.2 17.3 %collective-permute-start.38 = (bf16[64,2048]{1,0:T(8,128)(2,1)S(1)}, bf16[64,2048]{1,0:T(8,128)(2,1)S(1)}, u32[]{:S(2)}, u32[]{:S(2)}) collective-permute-start(bf16[64,2048]{1,0:T(8,128)(2,1)S(1)} %get-tuple-element.306), channel_id=1, source_target_pairs={{0,3},{1,0},{2,1},{3,2},{4,7},{5,4},{6,5},{7,6},{8,11},{9,8},{10,9... | collective-permute-start | bytes 786440 | tf_op jit(solution)/shard_map/ppermute | solution.py:33
  597.3 3.7 collective-permute-start.56
  604.6 9.0 %collective-permute-start.58 = (f32[9,128]{1,0:T(8,128)S(1)}, f32[9,128]{1,0:T(8,128)S(1)}, u32[]{:S(2)}, u32[]{:S(2)}) collective-permute-start(f32[9,128]{1,0:T(8,128)S(1)} %add.395), channel_id=1, source_target_pairs={{0,1},{1,2},{2,3},{3,0},{4,5},{5,6},{6,7},{7,4},{8,9},{9,10},{10,1... | collective-permute-start | bytes 13832 | tf_op jit(solution)/shard_map/ppermute | solution.py:33
  610.7 4.5 collective-permute-start.59
  612.2 3.9 collective-permute-start.60
  635.4 3.7 collective-permute-start.62
  639.2 3.7 collective-permute-start.63
  642.9 5.7 collective-permute-start.64
  642.9 5.7 collective-permute-start.65
  646.2 3.7 collective-permute-start.66
  (184 other events, 1343.0 us)
Sparse Core Ops, SparseCore 0:
  91.6 63.6 all-gather.2
  415.9 64.3 reduce-scatter.4
  484.2 84.9 reduce-scatter.2

commit v3 on v2

--- a/solution.py
+++ b/solution.py
@@ -281,7 +281,7 @@
         self.keeps, self.dp = keeps, dp
         self.got = dp_swap(send, 1, dp)
 
-    def run(self, columns):
+    def run(self, columns, middle, late):
         dp = self.dp
         tile = 4096
         if dp != 8:
@@ -301,10 +301,12 @@
         )
         got_a, got_b = dp_swap(d_low, 2, dp), dp_swap(d_high, 4, dp)
         x_low, y_high = dp_swap(x_low, 2, dp), dp_swap(y_high, 4, dp)
+        got_a, *middle[:] = tie(got_a, *middle)
         y_low, x_high = column_call(
             second_sums_kernel, [y_low, got_a, x_high, got_b], [(half, BF)] * 2, tile
         )
         y_low, x_high = dp_swap(y_low, 4, dp), dp_swap(x_high, 2, dp)
+        y_low, *late[:] = tie(y_low, *late)
         return column_call(
             functools.partial(last_sums_kernel, columns, tile),
             [own, self.got, x_low, y_high, y_low, x_high],
@@ -551,207 +553,514 @@
     )(*arrays)
 
 
-def restack_kernel(split, *refs):
-    *in_refs, left_ref, right_ref = refs
-    rows = in_refs[0].shape[0]
-    for number, ref in enumerate(in_refs):
-        left_ref[number * rows : (number + 1) * rows] = ref[:, :split]
-        right_ref[number * rows : (number + 1) * rows] = ref[:, split:]
-
-
-def restack(parts, split):
-    rows, columns = parts[0].shape
-    total = rows * len(parts)
-    return pl.pallas_call(
-        functools.partial(restack_kernel, split),
-        out_shape=[
-            jax.ShapeDtypeStruct((total, split), BF),
-            jax.ShapeDtypeStruct((total, columns - split), BF),
-        ],
-        compiler_params=pltpu.CompilerParams(vmem_limit_bytes=VMEM_LIMIT),
-    )(*parts)
-
-
-def assemble_kernel(widths, heads, order_ref, in_ref, *out_refs):
-    deep = in_ref.shape[-2] // heads
-    start = 0
-    for width, out_ref in zip(widths, out_refs, strict=True):
-        shards = out_ref.shape[-1] // width
-        for j in range(shards):
-            out_ref[:, j * width : (j + 1) * width] = in_ref[
-                0, j * deep : (j + 1) * deep, start : start + width
-            ]
-        start += width
-
-
-def assemble(order, gathered, widths, heads, single):
-    dp, rows, columns = gathered.shape
-    deep = rows // heads
-    wides = [w * heads for w in widths[: len(widths) - single]] + widths[len(widths) - single :]
-    return pl.pallas_call(
-        functools.partial(assemble_kernel, widths, heads),
-        out_shape=[jax.ShapeDtypeStruct((dp * deep, w), BF) for w in wides],
-        grid_spec=pltpu.PrefetchScalarGridSpec(
-            num_scalar_prefetch=1,
-            grid=(dp,),
-            in_specs=[pl.BlockSpec((1, rows, columns), lambda p, order: (order[p], 0, 0))],
-            out_specs=[pl.BlockSpec((deep, w), lambda p, order: (p, 0)) for w in wides],
-        ),
-    )(order, gathered)
-
-
-def assemble_parts_kernel(widths, heads, deep, *refs):
-    outs = refs[len(refs) - len(widths) :]
-    row = 0
-    for ref in refs[: len(refs) - len(widths)]:
-        for first in range(0, ref.shape[0], deep):
-            place, j = divmod(row // deep, heads)
-            start = 0
-            for width, out_ref in zip(widths, outs, strict=True):
-                if out_ref.shape[-1] > width:
-                    out_ref[place * deep : (place + 1) * deep, j * width : (j + 1) * width] = ref[
-                        first : first + deep, start : start + width
-                    ]
-                elif j == 0:
-                    out_ref[place * deep : (place + 1) * deep] = ref[
-                        first : first + deep, start : start + width
-                    ]
-                start += width
-            row += deep
-
-
-def assemble_parts(parts, widths, heads, single, dp):
-    deep = D // dp
-    wides = [w * heads for w in widths[: len(widths) - single]] + widths[len(widths) - single :]
-    return pl.pallas_call(
-        functools.partial(assemble_parts_kernel, widths, heads, deep),
-        out_shape=[jax.ShapeDtypeStruct((D, w), BF) for w in wides],
-        compiler_params=pltpu.CompilerParams(vmem_limit_bytes=VMEM_LIMIT),
-    )(*parts)
-
-
-def weight_grad_kernel(widths, single, order_ref, *refs):
-    out_ref = refs[-1]
-    dp, heads, deep, _ = out_ref.shape
-
-    def put(j, start, stop, value):
-        for place in range(dp):
-            out_ref[order_ref[place], j, :, start:stop] = value[place * deep : (place + 1) * deep]
-
-    start = 0
-    for number, width in enumerate(widths):
-        left = refs[2 * number][...]
-        together = max(1, 512 // width)
-        for first in range(0, heads, together):
-            whole = lax.dot_general(
-                left,
-                refs[2 * number + 1][:, first * width : (first + together) * width],
-                (((0,), (0,)), ((), ())),
-                preferred_element_type=F32,
-            ).astype(BF)
-            for j in range(together):
-                put(first + j, start, start + width, whole[:, j * width : (j + 1) * width])
-        start += width
-    if single:
-        value = refs[-2][...].astype(BF)
-        for j in range(heads):
-            put(j, start, start + value.shape[1], value)
-
-
-def weight_grads(order, pairs, heads, extra=None):
-    dp = order.shape[0]
-    flat = []
-    for left, right in pairs:
-        flat += [left.reshape(-1, left.shape[-1]), right.reshape(-1, right.shape[-1])]
-    widths = [right.shape[-1] // heads for _, right in pairs]
-    columns = sum(widths)
-    if extra is not None:
-        flat.append(extra)
-        columns += extra.shape[1]
-    return pl.pallas_call(
-        functools.partial(weight_grad_kernel, widths, extra is not None),
-        out_shape=jax.ShapeDtypeStruct((dp, heads, D // dp, columns), BF),
-        in_specs=[pl.BlockSpec(memory_space=pltpu.SMEM)]
-        + [pl.BlockSpec(memory_space=pltpu.VMEM)] * len(flat),
-        out_specs=pl.BlockSpec(memory_space=pltpu.VMEM),
-        compiler_params=pltpu.CompilerParams(vmem_limit_bytes=48 * 2**20),
-    )(order, *flat)
+def dot(a, b):
+    return jnp.dot(a, b, preferred_element_type=F32)
+
+
+def dot_nt(a, b):
+    return lax.dot_general(a, b, (((1,), (1,)), ((), ())), preferred_element_type=F32)
+
+
+def dot_tn(a, b):
+    return lax.dot_general(a, b, (((0,), (0,)), ((), ())), preferred_element_type=F32)
+
+
+def root(inputs):
+    return lax.rsqrt(jnp.mean(inputs * inputs, -1, keepdims=True) + NORM_EPS)
 
 
 def normed(inputs, gain_row):
-    return (
-        inputs * lax.rsqrt(jnp.mean(inputs * inputs, -1, keepdims=True) + NORM_EPS) * gain_row
-    ).astype(BF)
+    return (inputs * root(inputs) * gain_row).astype(BF)
 
 
 def norm_back(inputs, gain_row, upstream):
-    factor = lax.rsqrt(jnp.mean(inputs * inputs, -1, keepdims=True) + NORM_EPS)
+    factor = root(inputs)
     scaled = upstream * gain_row
     inner = jnp.mean(scaled * inputs, -1, keepdims=True)
     return (
         factor * (scaled - inputs * factor * factor * inner),
-        jnp.sum(upstream * inputs * factor, axis=(0, 1)),
-    )
-
-
-def dot(spec, a, b):
-    return jnp.einsum(spec, a, b, preferred_element_type=F32)
-
-
-def split_heads(array):
-    return array.reshape(array.shape[0], array.shape[1], -1, DH)
-
-
-def merge_heads(array):
-    return array.reshape(array.shape[0], array.shape[1], -1)
+        jnp.sum(upstream * inputs * factor, axis=0, keepdims=True),
+    )
 
 
 def attn_probs(query, keys_all, allowed):
-    scores = dot("bqhe,bkhe->bhqk", query, keys_all) * DH ** (-0.5)
-    return jax.nn.softmax(jnp.where(allowed[:, None], scores, -1000000000.0), -1)
-
-
-def attend_fwd(query_in, source, weights, allowed):
-    query = split_heads(dot("bld,dh->blh", query_in, weights[0]).astype(BF))
-    keys_all = split_heads(dot("bld,dh->blh", source, weights[1]).astype(BF))
-    values = split_heads(dot("bld,dh->blh", source, weights[2]).astype(BF))
-    probs = attn_probs(query, keys_all, allowed)
-    mixed = merge_heads(dot("bhqk,bkhe->bqhe", probs.astype(BF), values).astype(BF))
-    return dot("blh,dh->bld", mixed, weights[3]), (query, keys_all, values, mixed)
-
-
-def attend_back(upstream, query_in, source, weights, allowed, kept):
-    query, keys_all, values, mixed = kept
-    up_low = upstream.astype(BF)
-    grad_mixed = split_heads(dot("bld,dh->blh", up_low, weights[3]).astype(BF))
-    probs = attn_probs(query, keys_all, allowed)
-    grad_probs = dot("bqhe,bkhe->bhqk", grad_mixed, values)
-    grad_scores = (probs * (grad_probs - jnp.sum(grad_probs * probs, -1, keepdims=True))).astype(BF)
-    grad_query = merge_heads(
-        (dot("bhqk,bkhe->bqhe", grad_scores, keys_all) * DH ** (-0.5)).astype(BF)
-    )
-    grad_keys = merge_heads(
-        (dot("bhqk,bqhe->bkhe", grad_scores, query) * DH ** (-0.5)).astype(BF)
-    )
-    grad_values = merge_heads(dot("bhqk,bqhe->bkhe", probs.astype(BF), grad_mixed).astype(BF))
-    pairs = [(query_in, grad_query), (source, grad_keys), (source, grad_values), (up_low, mixed)]
-    back_query = dot("blh,dh->bld", grad_query, weights[0])
-    back_source = dot("blh,dh->bld", grad_keys, weights[1])
-    back_source = back_source + dot("blh,dh->bld", grad_values, weights[2])
-    return back_query, back_source, pairs
-
-
-def feed_fwd(inputs, weights):
-    hidden = jax.nn.relu(dot("bld,df->blf", inputs, weights[0])).astype(BF)
-    return dot("blf,df->bld", hidden, weights[1]), hidden
-
-
-def feed_back(upstream, inputs, weights, hidden):
-    up_low = upstream.astype(BF)
-    grad_hidden = dot("bld,df->blf", up_low, weights[1])
-    grad_pre = jnp.where(hidden > 0, grad_hidden, 0.0).astype(BF)
-    back_in = dot("blf,df->bld", grad_pre, weights[0])
-    return back_in, [(inputs, grad_pre), (up_low, hidden)]
+    scores = jnp.where(allowed, dot_nt(query, keys_all) * DH ** (-0.5), -1000000000.0)
+    grown = jnp.exp(scores - jnp.max(scores, -1, keepdims=True))
+    return grown * (1.0 / jnp.sum(grown, -1, keepdims=True))
+
+
+def key_mask(count, keys):
+    return lax.broadcasted_iota(jnp.int32, (1, keys), 1) < count
+
+
+def causal_mask(rows):
+    return lax.broadcasted_iota(jnp.int32, (rows, rows), 0) >= lax.broadcasted_iota(
+        jnp.int32, (rows, rows), 1
+    )
+
+
+def weights_of(ref, order_ref, start, stop):
+    return jnp.concatenate(
+        [ref[order_ref[place], 0, :, start:stop] for place in range(ref.shape[0])], 0
+    )
+
+
+def attend_heads(query, keys_all, values, each, mask_of):
+    rows, source = query.shape[0] // each, keys_all.shape[0] // each
+    out = []
+    for number in range(each):
+        a, b = number * rows, number * source
+        line = []
+        for first in range(0, query.shape[1], DH):
+            probs = attn_probs(
+                query[a : a + rows, first : first + DH],
+                keys_all[b : b + source, first : first + DH],
+                mask_of(number),
+            ).astype(BF)
+            line.append(dot(probs, values[b : b + source, first : first + DH]).astype(BF))
+        out.append(jnp.concatenate(line, 1) if len(line) > 1 else line[0])
+    return jnp.concatenate(out, 0) if each > 1 else out[0]
+
+
+def attend_heads_back(query, keys_all, values, grad_mixed, each, mask_of):
+    rows, source = query.shape[0] // each, keys_all.shape[0] // each
+    outs = ([], [], [])
+    for number in range(each):
+        a, b = number * rows, number * source
+        lines = ([], [], [])
+        for first in range(0, query.shape[1], DH):
+            q = query[a : a + rows, first : first + DH]
+            k = keys_all[b : b + source, first : first + DH]
+            v = values[b : b + source, first : first + DH]
+            g = grad_mixed[a : a + rows, first : first + DH]
+            probs = attn_probs(q, k, mask_of(number))
+            grad_probs = dot_nt(g, v)
+            slope = probs * (grad_probs - jnp.sum(grad_probs * probs, -1, keepdims=True))
+            slope = slope.astype(BF)
+            lines[0].append((dot(slope, k) * DH ** (-0.5)).astype(BF))
+            lines[1].append((dot_tn(slope, q) * DH ** (-0.5)).astype(BF))
+            lines[2].append(dot_tn(probs.astype(BF), g).astype(BF))
+        for out, line in zip(outs, lines, strict=True):
+            out.append(jnp.concatenate(line, 1) if len(line) > 1 else line[0])
+    return [jnp.concatenate(out, 0) if each > 1 else out[0] for out in outs]
+
+
+def at_phase(step, phase, heads):
+    return jnp.clip(step - phase * heads, 0, heads - 1)
+
+
+class Layers:
+    def __init__(self, order, head_pos, lens, weights, gain, each):
+        self.prefetch = (order, head_pos.reshape(1), lens)
+        self.weights, self.gain, self.each = weights, gain, each
+        self.dp, self.heads, self.deep, _ = weights.shape
+        self.width = 4 * D // self.heads
+        self.unit = self.width // 4
+
+    def weight_spec(self, block, phase):
+        heads = self.heads
+
+        def index(step, order, head, lens):
+            return (0, lax.rem(head[0] + at_phase(step, phase, heads), heads), 0, block)
+
+        return pl.BlockSpec((self.dp, 1, self.deep, self.width), index)
+
+    def kept_spec(self, shape, phase):
+        heads = self.heads
+        return pl.BlockSpec(
+            (1,) + shape[1:], lambda step, *_: (at_phase(step, phase, heads), 0, 0)
+        )
+
+    @staticmethod
+    def whole(shape):
+        return pl.BlockSpec(shape, lambda *_: (0,) * len(shape))
+
+    def call(self, kernel, phases, arrays, outs, scratch):
+        return pl.pallas_call(
+            kernel,
+            out_shape=[jax.ShapeDtypeStruct(shape, dtype) for shape, dtype, _ in outs],
+            grid_spec=pltpu.PrefetchScalarGridSpec(
+                num_scalar_prefetch=3,
+                grid=(phases * self.heads,),
+                in_specs=[spec or self.whole(array.shape) for array, spec in arrays],
+                out_specs=[spec or self.whole(shape) for shape, _, spec in outs],
+                scratch_shapes=[pltpu.VMEM(shape, dtype) for shape, dtype in scratch],
+            ),
+            compiler_params=pltpu.CompilerParams(vmem_limit_bytes=VMEM_LIMIT),
+        )(*self.prefetch, *[array for array, _ in arrays])
+
+    def encoder(self, x):
+        heads, each, unit, width = self.heads, self.each, self.unit, self.width
+        rows = x.shape[0]
+
+        def kernel(order, head, lens, x_ref, gain, a_ref, u_ref, d_ref, *refs):
+            kept, mid, hidden, last, encoded, low, acc = refs
+            step = pl.program_id(0)
+
+            @pl.when(step == 0)
+            def _():
+                acc[...] = x_ref[...]
+                low[...] = normed(x_ref[...], gain[0:1])
+
+            @pl.when(step < heads)
+            def _():
+                w = weights_of(a_ref, order, 0, width)
+                qkv = dot(low[...], w[:, : 3 * unit]).astype(BF)
+                mixed = attend_heads(
+                    qkv[:, :unit],
+                    qkv[:, unit : 2 * unit],
+                    qkv[:, 2 * unit :],
+                    each,
+                    lambda n: key_mask(lens[n], rows // each),
+                )
+                kept[0, :, : 3 * unit] = qkv
+                kept[0, :, 3 * unit :] = mixed
+                acc[...] += dot_nt(mixed, w[:, 3 * unit :])
+
+            @pl.when(step == heads)
+            def _():
+                mid[...] = acc[...]
+                low[...] = normed(acc[...], gain[1:2])
+
+            @pl.when(step >= heads)
+            def _():
+                grown = jax.nn.relu(dot(low[...], weights_of(u_ref, order, 0, width))).astype(BF)
+                hidden[0] = grown
+                acc[...] += dot_nt(grown, weights_of(d_ref, order, 0, width))
+
+            @pl.when(step == 2 * heads - 1)
+            def _():
+                last[...] = acc[...]
+                encoded[...] = normed(acc[...], gain[2:3])
+
+        shape = (heads, rows, width)
+        return self.call(
+            kernel,
+            2,
+            [(x, None), (self.gain, None)]
+            + [(self.weights, self.weight_spec(*at)) for at in ((0, 0), (1, 1), (2, 1))],
+            [
+                (shape, BF, self.kept_spec(shape, 0)),
+                ((rows, D), F32, None),
+                (shape, BF, self.kept_spec(shape, 1)),
+                ((rows, D), F32, None),
+                ((rows, D), BF, None),
+            ],
+            [((rows, D), BF), ((rows, D), F32)],
+        )
+
+    def decoder(self, x, encoded):
+        heads, each, unit, width = self.heads, self.each, self.unit, self.width
+        rows, source = x.shape[0], encoded.shape[0]
+
+        def kernel(order, head, lens, x_ref, enc_ref, gain, s_ref, c_ref, u_ref, d_ref, *refs):
+            kept, one, kept_q, kept_k, two, hidden, three, final, low, acc = refs
+            step = pl.program_id(0)
+
+            @pl.when(step == 0)
+            def _():
+                acc[...] = x_ref[...]
+                low[...] = normed(x_ref[...], gain[3:4])
+
+            @pl.when(step < heads)
+            def _():
+                w = weights_of(s_ref, order, 0, width)
+                qkv = dot(low[...], w[:, : 3 * unit]).astype(BF)
+                mixed = attend_heads(
+                    qkv[:, :unit],
+                    qkv[:, unit : 2 * unit],
+                    qkv[:, 2 * unit :],
+                    each,
+                    lambda n: causal_mask(rows // each),
+                )
+                kept[0, :, : 3 * unit] = qkv
+                kept[0, :, 3 * unit :] = mixed
+                acc[...] += dot_nt(mixed, w[:, 3 * unit :])
+
+            @pl.when(step == heads)
+            def _():
+                one[...] = acc[...]
+                low[...] = normed(acc[...], gain[4:5])
+
+            @pl.when((step >= heads) & (step < 2 * heads))
+            def _():
+                w = weights_of(c_ref, order, 0, width)
+                query = dot(low[...], w[:, :unit]).astype(BF)
+                both = dot(enc_ref[...], w[:, unit : 3 * unit]).astype(BF)
+                mixed = attend_heads(
+                    query,
+                    both[:, :unit],
+                    both[:, unit:],
+                    each,
+                    lambda n: key_mask(lens[n], source // each),
+                )
+                kept_q[0, :, :unit] = query
+                kept_q[0, :, unit:] = mixed
+                kept_k[0] = both
+                acc[...] += dot_nt(mixed, w[:, 3 * unit :])
+
+            @pl.when(step == 2 * heads)
+            def _():
+                two[...] = acc[...]
+                low[...] = normed(acc[...], gain[5:6])
+
+            @pl.when(step >= 2 * heads)
+            def _():
+                grown = jax.nn.relu(dot(low[...], weights_of(u_ref, order, 0, width))).astype(BF)
+                hidden[0] = grown
+                acc[...] += dot_nt(grown, weights_of(d_ref, order, 0, width))
+
+            @pl.when(step == 3 * heads - 1)
+            def _():
+                three[...] = acc[...]
+                final[...] = normed(acc[...], gain[6:7] * D ** (-0.5))
+
+        shape = (heads, rows, width)
+        shape_q, shape_k = (heads, rows, 2 * unit), (heads, source, 2 * unit)
+        return self.call(
+            kernel,
+            3,
+            [(x, None), (encoded, None), (self.gain, None)]
+            + [(self.weights, self.weight_spec(*at)) for at in ((3, 0), (4, 1), (5, 2), (6, 2))],
+            [
+                (shape, BF, self.kept_spec(shape, 0)),
+                ((rows, D), F32, None),
+                (shape_q, BF, self.kept_spec(shape_q, 1)),
+                (shape_k, BF, self.kept_spec(shape_k, 1)),
+                ((rows, D), F32, None),
+                (shape, BF, self.kept_spec(shape, 2)),
+                ((rows, D), F32, None),
+                ((rows, D), BF, None),
+            ],
+            [((rows, D), BF), ((rows, D), F32)],
+        )
+
+    def put(self, out_ref, order, j, start, value):
+        low = value.astype(BF)
+        for place in range(self.dp):
+            out_ref[order[place], j, :, start : start + value.shape[1]] = low[
+                place * self.deep : (place + 1) * self.deep
+            ]
+
+    def feed_step(self, order, j, u_ref, d_ref, hidden, out, at, low, up_t, in_t, back):
+        width = self.width
+        up, down = weights_of(u_ref, order, 0, width), weights_of(d_ref, order, 0, width)
+        grad_pre = jnp.where(hidden > 0, dot(low[...], down), 0.0).astype(BF)
+        self.put(out, order, j, at, dot(in_t[...], grad_pre))
+        self.put(out, order, j, at + width, dot(up_t[...], hidden))
+        back[...] += dot_nt(grad_pre, up)
+
+    def decoder_back(self, grad_final, x, encoded, kept_all):
+        heads, each, unit, width = self.heads, self.each, self.unit, self.width
+        kept, one, kept_q, kept_k, two, hidden, three = kept_all
+        rows, source = x.shape[0], encoded.shape[0]
+
+        def kernel(order, head, lens, *refs):
+            g_ref, x_ref, enc_ref, gain, one, two, three, kept, kept_q, kept_k, hid = refs[:11]
+            s_ref, c_ref, u_ref, d_ref = refs[11:15]
+            out, gains_out, grad_enc, grad_x = refs[15:19]
+            grad, low, up_t, in_t, enc_t, back = refs[19:]
+            step = pl.program_id(0)
+
+            def enter(value, inputs, gain_row):
+                grad[...] = value
+                low[...] = value.astype(BF)
+                up_t[...] = low[...].T
+                in_t[...] = normed(inputs, gain_row).T
+                back[...] = jnp.zeros_like(back)
+
+            @pl.when(step == 0)
+            def _():
+                gains_out[...] = jnp.zeros_like(gains_out)
+                value, slope = norm_back(three[...], gain[6:7] * D ** (-0.5), g_ref[...])
+                gains_out[6:7] = slope * D ** (-0.5)
+                enter(value, two[...], gain[5:6])
+
+            @pl.when(step < heads)
+            def _():
+                self.feed_step(
+                    order, step, u_ref, d_ref, hid[0], out, 2 * width, low, up_t, in_t, back
+                )
+
+            @pl.when(step == heads)
+            def _():
+                value, slope = norm_back(two[...], gain[5:6], back[...])
+                gains_out[5:6] = slope
+                enter(grad[...] + value, one[...], gain[4:5])
+                enc_t[...] = enc_ref[...].T
+                grad_enc[...] = jnp.zeros_like(grad_enc)
+
+            @pl.when((step >= heads) & (step < 2 * heads))
+            def _():
+                j = step - heads
+                w = weights_of(c_ref, order, 0, width)
+                grad_mixed = dot(low[...], w[:, 3 * unit :]).astype(BF)
+                query, mixed = kept_q[0, :, :unit], kept_q[0, :, unit:]
+                dq, dk, dv = attend_heads_back(
+                    query,
+                    kept_k[0, :, :unit],
+                    kept_k[0, :, unit:],
+                    grad_mixed,
+                    each,
+                    lambda n: key_mask(lens[n], source // each),
+                )
+                both = jnp.concatenate([dk, dv], 1)
+                self.put(out, order, j, width, dot(in_t[...], dq))
+                self.put(out, order, j, width + unit, dot(enc_t[...], both))
+                self.put(out, order, j, width + 3 * unit, dot(up_t[...], mixed))
+                back[...] += dot_nt(dq, w[:, :unit])
+                grad_enc[...] += dot_nt(both, w[:, unit : 3 * unit])
+
+            @pl.when(step == 2 * heads)
+            def _():
+                value, slope = norm_back(one[...], gain[4:5], back[...])
+                gains_out[4:5] = slope
+                enter(grad[...] + value, x_ref[...], gain[3:4])
+
+            @pl.when(step >= 2 * heads)
+            def _():
+                self.self_step(
+                    order, step - 2 * heads, s_ref, kept, out, 0, low, up_t, in_t, back,
+                    lambda n: causal_mask(rows // each),
+                )
+
+            @pl.when(step == 3 * heads - 1)
+            def _():
+                value, slope = norm_back(x_ref[...], gain[3:4], back[...])
+                gains_out[3:4] = slope
+                grad_x[...] = (grad[...] + value).astype(BF)
+
+        return self.call(
+            kernel,
+            3,
+            [
+                (grad_final, None),
+                (x, None),
+                (encoded, None),
+                (self.gain, None),
+                (one, None),
+                (two, None),
+                (three, None),
+                (kept, self.kept_spec(kept.shape, 2)),
+                (kept_q, self.kept_spec(kept_q.shape, 1)),
+                (kept_k, self.kept_spec(kept_k.shape, 1)),
+                (hidden, self.kept_spec(hidden.shape, 0)),
+            ]
+            + [(self.weights, self.weight_spec(*at)) for at in ((3, 2), (4, 1), (5, 0), (6, 0))],
+            [
+                ((self.dp, heads, self.deep, 4 * width), BF, None),
+                ((8, D), F32, None),
+                ((source, D), F32, None),
+                ((rows, D), BF, None),
+            ],
+            [
+                ((rows, D), F32),
+                ((rows, D), BF),
+                ((D, rows), BF),
+                ((D, rows), BF),
+                ((D, source), BF),
+                ((rows, D), F32),
+            ],
+        )
+
+    def self_step(self, order, j, a_ref, kept, out, at, low, up_t, in_t, back, mask_of):
+        unit, width = self.unit, self.width
+        w = weights_of(a_ref, order, 0, width)
+        grad_mixed = dot(low[...], w[:, 3 * unit :]).astype(BF)
+        slopes = attend_heads_back(
+            kept[0, :, :unit],
+            kept[0, :, unit : 2 * unit],
+            kept[0, :, 2 * unit : 3 * unit],
+            grad_mixed,
+            self.each,
+            mask_of,
+        )
+        three = jnp.concatenate(slopes, 1)
+        self.put(out, order, j, at, dot(in_t[...], three))
+        self.put(out, order, j, at + 3 * unit, dot(up_t[...], kept[0, :, 3 * unit :]))
+        back[...] += dot_nt(three, w[:, : 3 * unit])
+
+    def encoder_back(self, grad_encoded, gain_grads, x, kept_all, lanes):
+        heads, each, width = self.heads, self.each, self.width
+        kept, mid, hidden, last = kept_all
+        rows = x.shape[0]
+
+        def kernel(order, head, lens, *refs):
+            g_ref, more_ref, x_ref, gain, mid, last, kept, hid, a_ref, u_ref, d_ref = refs[:11]
+            out, grad_x = refs[11:13]
+            grad, low, up_t, in_t, back, gains = refs[13:]
+            step = pl.program_id(0)
+
+            def enter(value, inputs, gain_row):
+                grad[...] = value
+                low[...] = value.astype(BF)
+                up_t[...] = low[...].T
+                in_t[...] = normed(inputs, gain_row).T
+                back[...] = jnp.zeros_like(back)
+
+            @pl.when(step == 0)
+            def _():
+                gains[...] = jnp.zeros_like(gains)
+                gains[0:8] = more_ref[...]
+                value, slope = norm_back(last[...], gain[2:3], g_ref[...])
+                gains[2:3] = slope
+                enter(value, mid[...], gain[1:2])
+
+            @pl.when(step < heads)
+            def _():
+                self.feed_step(
+                    order, step, u_ref, d_ref, hid[0], out, width, low, up_t, in_t, back
+                )
+
+            @pl.when(step == heads)
+            def _():
+                value, slope = norm_back(mid[...], gain[1:2], back[...])
+                gains[1:2] = slope
+                enter(grad[...] + value, x_ref[...], gain[0:1])
+
+            @pl.when(step >= heads)
+            def _():
+                self.self_step(
+                    order, step - heads, a_ref, kept, out, 0, low, up_t, in_t, back,
+                    lambda n: key_mask(lens[n], rows // each),
+                )
+
+            @pl.when(step == 2 * heads - 1)
+            def _():
+                value, slope = norm_back(x_ref[...], gain[0:1], back[...])
+                gains[0:1] = slope
+                grad_x[...] = (grad[...] + value).astype(BF)
+                turned = gains[...].T
+                for j in range(heads):
+                    self.put(out, order, j, 3 * width, turned)
+
+        return self.call(
+            kernel,
+            2,
+            [
+                (grad_encoded, None),
+                (gain_grads, None),
+                (x, None),
+                (self.gain, None),
+                (mid, None),
+                (last, None),
+                (kept, self.kept_spec(kept.shape, 1)),
+                (hidden, self.kept_spec(hidden.shape, 0)),
+            ]
+            + [(self.weights, self.weight_spec(*at)) for at in ((0, 1), (1, 0), (2, 0))],
+            [
+                ((self.dp, heads, self.deep, 3 * width + lanes), BF, None),
+                ((rows, D), BF, None),
+            ],
+            [
+                ((rows, D), F32),
+                ((rows, D), BF),
+                ((D, rows), BF),
+                ((D, rows), BF),
+                ((rows, D), F32),
+                ((lanes, D), F32),
+            ],
+        )
 
 
 def body(
@@ -805,18 +1114,14 @@
     order = lax.axis_index("dp") ^ jnp.array(places, jnp.int32)
     flat_in = attn_in.reshape((9,) + attn_in.shape[2:])
     arrays = [flat_in, attn_out_t, ff_in, ff_out_t, gain_block]
-    plan = [(0, 0), (0, 1), (0, 2), (1, 0), (2, 0), (3, 0), (4, None)]
+    plan = [(0, 0), (0, 1), (0, 2), (1, 0), (2, 0), (3, 0)]
     plan += [(0, 3), (0, 4), (0, 5), (1, 1), (0, 6), (0, 7), (0, 8), (1, 2), (2, 1), (3, 1)]
-    split = sum(widths[0]) + lanes
-    packed = pack(arrays, plan)
+    packed = pack(arrays, plan + [(4, None)])
     low, packed = tie(low, packed)
-    came = gather_head(packed, heads)
+    weights = lax.all_gather(packed, ("dp", "head"), axis=0)
+    weights = weights.reshape((dp, heads) + packed.shape)
     table = GatherDp(low, dp)
     table.go_far()
-    came = tie(came[0], *came[1:], *table.far)[:heads]
-    enc_wide, dec_wide = restack(came, split)
-    enc_gather = GatherDp(enc_wide, dp)
-    dec_gathered = lax.all_gather(dec_wide, "dp", axis=0)
     table_parts = table.parts()
 
     def fill(array):
@@ -832,46 +1137,18 @@
     enc_looked = looked[:enc_rows_count].reshape(heads, -1, D)
     dec_looked = looked[enc_rows_count:]
     came = [enc_looked[0]] + [head_shift(enc_looked[j], j, heads) for j in range(1, heads)]
-    dec_looked, *enc_gather.near = tie(dec_looked, *enc_gather.near)
-    enc_gather.go_far()
-    *enc_list, gain = assemble_parts(enc_gather.parts(), widths[0] + [lanes], heads, 1, dp)
-    w_enc, f_enc = enc_list[:4], enc_list[4:]
-    gain = gain[:, : gain_rows + 1].astype(F32).T
+    gain = jnp.take(weights[:, 0, :, sum(widths[0]) + sum(widths[1]) :], order, axis=0)
+    gain = gain[..., :8].astype(F32).reshape(D, 8).T
     real_count = jnp.maximum(jnp.sum(gain[gain_rows].reshape(dp, -1)[:, 0]), 1.0)
-    enc_embed = functools.reduce(jnp.add, came).astype(F32).reshape(each, source_len, D)
     my_lens = lax.dynamic_slice_in_dim(fill(source_lens), head_pos * each, each)
-
-    src_keys = jnp.arange(source_len)[None, :] < my_lens[:, None]
-    enc_allowed = jnp.broadcast_to(src_keys[:, None, :], (each, source_len, source_len))
-    cross_allowed = jnp.broadcast_to(src_keys[:, None, :], (each, target_len, source_len))
-    causal = jnp.broadcast_to(
-        (jnp.arange(target_len)[:, None] >= jnp.arange(target_len)[None, :])[None],
-        (each, target_len, target_len),
-    )
-    norm_a = normed(enc_embed, gain[0])
-    branch, kept_enc = attend_fwd(norm_a, norm_a, w_enc, enc_allowed)
-    enc_mid = enc_embed + branch
-    enc_mid, dec_looked = tie(enc_mid, dec_looked)
-    looked = dec_looked.reshape(heads, -1, D)
+    layers = Layers(order, head_pos, my_lens, weights, gain, each)
+    enc_embed = functools.reduce(jnp.add, came).astype(F32)
+    *kept_enc, encoded = layers.encoder(enc_embed)
+    looked, encoded = tie(dec_looked, encoded)
+    looked = looked.reshape(heads, -1, D)
     dec_came = [looked[0]] + [head_shift(looked[j], j, heads) for j in range(1, heads)]
-    norm_b = normed(enc_mid, gain[1])
-    branch, hidden_enc = feed_fwd(norm_b, f_enc)
-    enc_last = enc_mid + branch
-    encoded = normed(enc_last, gain[2])
-    dec_list = assemble(order, dec_gathered, widths[1], heads, 0)
-    w_self, w_cross, f_dec = dec_list[:4], dec_list[4:8], dec_list[8:]
-    dec_embed = functools.reduce(jnp.add, dec_came).astype(F32).reshape(each, target_len, D)
-    norm_c = normed(dec_embed, gain[3])
-    branch, kept_self = attend_fwd(norm_c, norm_c, w_self, causal)
-    dec_one = dec_embed + branch
-    norm_d = normed(dec_one, gain[4])
-    branch, kept_cross = attend_fwd(norm_d, encoded, w_cross, cross_allowed)
-    dec_two = dec_one + branch
-    norm_e = normed(dec_two, gain[5])
-    branch, hidden_dec = feed_fwd(norm_e, f_dec)
-    dec_three = dec_two + branch
-    head_gain = gain[6] * D ** (-0.5)
-    my_final = normed(dec_three, head_gain).reshape(each * target_len, D)
+    dec_embed = functools.reduce(jnp.add, dec_came).astype(F32)
+    *kept_dec, my_final = layers.decoder(dec_embed, encoded)
 
     final = jnp.concatenate(gather_head(my_final, heads), 0)
     final = jnp.roll(final, head_pos * each * target_len, 0)[:token_count]
@@ -916,46 +1193,18 @@
     slope, part = logits_back(final_t, labels, scalars, teacher_t, table_rows, table_parts)
     part = part.T.reshape(batch_size, target_len, D)
     part = jnp.roll(fill(part).reshape(heads, each * target_len, D), -head_pos, 0)
-    grad_final = scatter_head([part[j] for j in range(heads)], heads).reshape(each, target_len, D)
-
-    grad_three, gain_six = norm_back(dec_three, head_gain, grad_final)
-    back_in, pairs_f_dec = feed_back(grad_three, norm_e, f_dec, hidden_dec)
-    grad_norm_in, gain_five = norm_back(dec_two, gain[5], back_in)
-    grad_two = grad_three + grad_norm_in
-    back_query, grad_encoded, pairs_cross = attend_back(
-        grad_two, norm_d, encoded, w_cross, cross_allowed, kept_cross
-    )
-    grad_norm_in, gain_four = norm_back(dec_one, gain[4], back_query)
-    grad_one = grad_two + grad_norm_in
-    back_query, back_source, pairs_self = attend_back(
-        grad_one, norm_c, norm_c, w_self, causal, kept_self
-    )
-    grad_norm_in, gain_three = norm_back(dec_embed, gain[3], back_query + back_source)
-    grad_dec_embed = grad_one + grad_norm_in
-    dec_rows = gather_head(grad_dec_embed.reshape(-1, D).astype(BF), heads)
-    dec_grads = weight_grads(order, pairs_self + pairs_cross + pairs_f_dec, heads)
-    grad_encoded, dec_grads = tie(grad_encoded, dec_grads)
+    grad_final = scatter_head([part[j] for j in range(heads)], heads)
+
+    dec_grads, gain_grads, grad_encoded, dec_low = layers.decoder_back(
+        grad_final, dec_embed, encoded, kept_dec
+    )
     dec_shard = lax.psum_scatter(dec_grads, "dp", scatter_dimension=0)
-    grad_last, gain_two = norm_back(enc_last, gain[2], grad_encoded)
-    back_in, pairs_f_enc = feed_back(grad_last, norm_b, f_enc, hidden_enc)
-    back_in, *dec_rows = tie(back_in, *dec_rows)
-    grad_norm_in, gain_one = norm_back(enc_mid, gain[1], back_in)
-    grad_mid = grad_last + grad_norm_in
-    back_query, back_source, pairs_enc = attend_back(
-        grad_mid, norm_a, norm_a, w_enc, enc_allowed, kept_enc
-    )
-    grad_norm_in, gain_zero = norm_back(enc_embed, gain[0], back_query + back_source)
-    grad_enc_embed = grad_mid + grad_norm_in
-
-    gain_grads = jnp.stack(
-        [gain_zero, gain_one, gain_two, gain_three, gain_four, gain_five, gain_six * D ** (-0.5)]
-    )
-    gain_cols = jnp.pad(gain_grads.T, ((0, 0), (0, lanes - gain_rows)))
-    enc_low = grad_enc_embed.reshape(-1, D).astype(BF)
+    dec_rows = gather_head(dec_low, heads)
+    enc_grads, enc_low = layers.encoder_back(grad_encoded, gain_grads, enc_embed, kept_enc, lanes)
+    enc_low, *dec_rows = tie(enc_low, *dec_rows)
+
     enc_rows = gather_head(enc_low, heads)
-    enc_grads = weight_grads(order, pairs_enc + pairs_f_enc, heads, gain_cols)
-    enc_low, enc_grads = tie(enc_low, enc_grads)
-    enc_shard = lax.psum_scatter(enc_grads, "dp", scatter_dimension=0)
+    enc_shard = lax.psum_scatter(after(enc_grads, dec_shard), "dp", scatter_dimension=0)
     near_ids = jnp.concatenate([dec_ids.reshape(-1), enc_ids[0]])
     near_rows = jnp.concatenate(dec_rows + [enc_low], 0)
     columns = padded_to(vocab_local)
@@ -968,8 +1217,8 @@
     far_rows = jnp.concatenate(enc_rows[1:], 0)
     dec_sums = send_heads(dec_shard)
     *keeps, send = spread(far_ids, far_rows, columns, base=grad_table_t)
-    g_table, table_squares = ScatterDp(keeps, send, dp).run(vocab_local)
     enc_sums = send_heads(enc_shard)
+    g_table, table_squares = ScatterDp(keeps, send, dp).run(vocab_local, dec_sums, enc_sums)
     g_dec = functools.reduce(jnp.add, [value.astype(F32) for value in dec_sums])
     g_enc = functools.reduce(jnp.add, [value.astype(F32) for value in enc_sums])
 

time: 678 us -> 614 us (0.906)
  matrix products: 63.9 us -> 0 us
  Pallas kernels: 166 us -> 220 us
  local copies, waits for them, and re-layouts: 61.6 us -> 30.1 us
  starting transfers between devices: 88.9 us -> 66 us
  other arithmetic: 52.9 us -> 31.9 us
  waiting for transfers between devices: 215 us -> 235 us
    dot_general x47 -> x0, matrix products: 55.6 us -> none  [dot(): return jnp.einsum(spec, a, b, preferred_element_type=F32)]
    pallas_call x5 -> x4, Pallas kernels: 34.2 us -> 88.4 us  [call(): pl.pallas_call(kernel, out_shape=[jax.ShapeDtypeStruct(shape, dtype) for...]
    reduce_scatter x1, waiting for transfers between devices: 0.01 us -> 21.4 us  [body(): lax.psum_scatter(after(enc_grads, dec_shard), 'dp', scatter_dimension=0)]
    ppermute x36 -> x33, starting transfers between devices: 64.6 us -> 48.6 us  [head_shift(): lax.ppermute(x, 'head', [(i, (i + step) % heads) for i in range(heads)])]
    unnamed x373 -> x88, local copies, waits for them, and re-layouts: 23.9 us -> 8.74 us
    ppermute x36 -> x33, waiting for transfers between devices: 105 us -> 119 us  [head_shift(): lax.ppermute(x, 'head', [(i, (i + step) % heads) for i in range(heads)])]
    reduce_scatter x1, waiting for transfers between devices: 13.9 us -> 0.01 us  [body(): dec_shard = lax.psum_scatter(dec_grads, 'dp', scatter_dimension=0)]
    another operation x14 -> x0, local copies, waits for them, and re-layouts: 13.1 us -> none
  transfers between devices with their start and end apart: 70 -> 58, of which waited for: 37 -> 37; matrix products, arithmetic and copies ran while one was open for 11% -> 4% of each run, Pallas kernels for 14% -> 16%
where the time goes in v3:
time: 614 us; the launch traced here: 604 us
  waiting for transfers between devices  235 us (38%)
  Pallas kernels  220 us (36%)
  starting transfers between devices  66 us (11%)
  other arithmetic  31.9 us (5%)
  local copies, waits for them, and re-layouts  30.1 us (5%)
  between operations  20.6 us (3%)
    ppermute x33, waiting for transfers between devices, head_shift(): lax.ppermute(x, 'head', [(i, (i + step) % heads) for i in range(heads)])  119 us
    pallas_call x4, Pallas kernels, call(): pl.pallas_call(kernel, out_shape=[jax.ShapeDtypeStruct(shape, dtype) for...  88.4 us
    ppermute x22, waiting for transfers between devices, dp_swap(): return lax.ppermute(x, 'dp', [(i, i ^ bit) for i in range(dp)])  83.8 us
    ppermute x33, starting transfers between devices, head_shift(): lax.ppermute(x, 'head', [(i, (i + step) % heads) for i in range(heads)])  48.6 us
    pallas_call x2, Pallas kernels, spread(): pl.pallas_call(functools.partial(spread_kernel, tile), out_shape=[jax.Sha...  37.9 us
    pallas_call x1, Pallas kernels, lookup(): pl.pallas_call(functools.partial(lookup_kernel, vocab, tile), out_shape=[...  25.9 us
    pallas_call x4, Pallas kernels, column_call(): pl.pallas_call(kernel, out_shape=out_shape, grid=(pl.cdiv(columns, tile),...  23.1 us
    pallas_call x1, Pallas kernels, logits_back(): pl.pallas_call(functools.partial(logits_back_kernel, vocab, tile), out_sh...  22 us
  transfers between devices with their start and end apart: 58, of which 37 were waited for; matrix products, arithmetic and copies ran while one was open for 4% of the time, Pallas kernels for 16%

profile of v3, /device:TPU:0, one launch (start us, length us, event | category | flops | bytes accessed | tf_op | source)
XLA Modules:
  0.0 603.9 jit_solution(4649854426131302443)
XLA Ops:
  9.3 1.7 bitcast_convert_fusion.1.refs_0_.refs_1_
  12.4 2.0 shard_map.392
  14.4 3.0 collective-permute-start
  19.0 24.7 %collective-permute-done.refs_1_.refs_2_ = bf16[64,8032]{1,0:T(8,128)(2,1)S(1)} collective-permute-done((bf16[64,8032]{1,0:T(8,128)(2,1)S(1)}, bf16[64,8032]{1,0:T(8,128)(2,1)S(1)}, u32[]{:S(2)}, u32[]{:S(2)}) %collective-permute-start) | collective-permute-done | bytes 1028128 | tf_op jit(solution)/shard_map/ppermute | solution.py:29
  44.6 1.7 collective-permute-start.2
  49.4 17.4 %collective-permute-done.2.refs_3_.refs_4_ = bf16[32,8032]{1,0:T(8,128)(2,1)} collective-permute-done((bf16[32,8032]{1,0:T(8,128)(2,1)}, bf16[32,8032]{1,0:T(8,128)(2,1)}, u32[]{:S(2)}, u32[]{:S(2)}) %collective-permute-start.2) | collective-permute-done | bytes 514080 | tf_op jit(solution)/shard_map/ppermute | solution.py:29
  69.8 25.9 %shard_map.393 = (bf16[2048,512]{1,0:T(8,128)(2,1)}, bf16[8064,512]{1,0:T(8,128)(2,1)}) custom-call(s32[2048,1]{1,0:T(8,128)} %copy.96.ids_ref, bf16[64,8032]{1,0:T(8,128)(2,1)} %copy-done.3, bf16[64,8032]{1,0:T(8,128)(2,1)} %copy-done.4, bf16[64,8032]{1,0:T(8,128)(2,1)} %copy-done.5, bf16[32,8032]{1,0:T(8,128)(2,1)} %collective-permute-done.2.refs_3_.refs_4_, ...), custom_call_target="tpu_custom_call" | custom-call | tf_op jit(solution)/shard_map/pallas_call | solution.py:142
  97.0 2.6 collective-permute-start.10
  103.2 32.1 %collective-permute-done.10 = bf16[384,512]{1,0:T(8,128)(2,1)S(1)} collective-permute-done((bf16[384,512]{1,0:T(8,128)(2,1)S(1)}, bf16[384,512]{1,0:T(8,128)(2,1)S(1)}, u32[]{:S(2)}, u32[]{:S(2)}) %collective-permute-start.10) | collective-permute-done | bytes 393248 | tf_op jit(solution)/shard_map/ppermute | solution.py:33
  136.5 16.2 %collective-permute-done.9 = bf16[384,512]{1,0:T(8,128)(2,1)S(1)} collective-permute-done((bf16[384,512]{1,0:T(8,128)(2,1)S(1)}, bf16[384,512]{1,0:T(8,128)(2,1)S(1)}, u32[]{:S(2)}, u32[]{:S(2)}) %collective-permute-start.9) | collective-permute-done | bytes 393248 | tf_op jit(solution)/shard_map/ppermute | solution.py:33
  152.8 2.0 add_convert_fusion.x_ref.refs_2_
  154.8 10.7 %all-gather.3.cloned.1.call-done = bf16[2048,3712]{1,0:T(8,128)(2,1)} async-done(((bf16[64,3712]{1,0:T(8,128)(2,1)}), bf16[2048,3712]{1,0:T(8,128)(2,1)}) %all-gather.3.cloned.1.call-update) | async-done | bytes 15204368 | tf_op jit(solution)/shard_map/all_gather | solution.py:1121
  167.8 15.8 %shard_map.394 = (bf16[4,384,512]{2,1,0:T(8,128)(2,1)}, f32[384,512]{1,0:T(8,128)}, bf16[4,384,512]{2,1,0:T(8,128)(2,1)}, f32[384,512]{1,0:T(8,128)}, bf16[384,512]{1,0:T(8,128)(2,1)}) custom-call(s32[8]{0:T(128)} %broadcast_xor_fusion.order, s32[1]{0:T(128)} %bitcast.10.head, s32[1]{0:T(128)} %dynamic_slice.19.lens, ...), custom_call_target="tpu_custom_call" | custom-call | tf_op jit(solution)/shard_map/pallas_call | solution.py:679
  183.6 1.9 collective-permute-start.12
  185.5 2.6 collective-permute-start.14
  189.5 2.4 collective-permute-done.12
  191.9 4.9 collective-permute-done.13
  197.6 19.5 %shard_map.395 = (bf16[4,128,512]{2,1,0:T(8,128)(2,1)}, f32[128,512]{1,0:T(8,128)}, bf16[4,128,256]{2,1,0:T(8,128)(2,1)}, bf16[4,384,256]{2,1,0:T(8,128)(2,1)}, ...) custom-call(s32[8]{0:T(128)} %broadcast_xor_fusion.order, ...), custom_call_target="tpu_custom_call" | custom-call | tf_op jit(solution)/shard_map/pallas_call | solution.py:679
  218.1 3.0 collective-permute-start.15
  222.3 1.8 collective-permute-start.16
  225.1 9.6 %collective-permute-done.16 = bf16[128,512]{0,1:T(8,128)(2,1)S(1)} collective-permute-done((bf16[128,512]{0,1:T(8,128)(2,1)S(1)}, bf16[128,512]{0,1:T(8,128)(2,1)S(1)}, u32[]{:S(2)}, u32[]{:S(2)}) %collective-permute-start.16) | collective-permute-done | bytes 131104 | tf_op jit(solution)/shard_map/ppermute | solution.py:33
  235.8 17.2 %shard_map.396 = f32[8,512]{1,0:T(8,128)} custom-call(bf16[512,512]{1,0:T(8,128)(2,1)} %dynamic-slice_bitcast_fusion.final_ref.refs_0_, s32[1,512]{1,0:T(1,128)} %and_select_fusion.label_ref, bf16[8032,512]{1,0:T(8,128)(2,1)} %bitcast.189, bf16[8064,512]{1,0:T(8,128)(2,1)} %get-tuple-element.101.table_ref.refs_0_), custom_call_target="tpu_custom_call" | custom-call | tf_op jit(solution)/shard_map/pallas_call | solution.py:398
  253.7 2.0 collective-permute-start.20
  262.7 22.0 %shard_map.397 = (bf16[8064,512]{1,0:T(8,128)(2,1)}, bf16[512,512]{1,0:T(8,128)(2,1)}) custom-call(bf16[512,512]{1,0:T(8,128)(2,1)} %dynamic-slice_bitcast_fusion.final_ref.refs_0_, s32[1,512]{1,0:T(1,128)} %and_select_fusion.label_ref, f32[8,512]{1,0:T(8,128)} %stack.31.scalar_ref, bf16[8032,512]{1,0:T(8,128)(2,1)} %bitcast.190, ...), custom_call_target="tpu_custom_call" | custom-call | tf_op jit(solution)/shard_map/pallas_call | solution.py:450
  286.6 2.0 collective-permute-start.22
  290.1 4.5 collective-permute-done.21
  294.5 3.3 collective-permute-done.22
  298.6 27.5 %shard_map.398 = (bf16[8,4,64,2048]{3,2,1,0:T(8,128)(2,1)}, f32[8,512]{1,0:T(8,128)}, f32[384,512]{1,0:T(8,128)}, bf16[128,512]{1,0:T(8,128)(2,1)}) custom-call(s32[8]{0:T(128)} %broadcast_xor_fusion.order, s32[1]{0:T(128)} %bitcast.10.head, s32[1]{0:T(128)} %dynamic_slice.19.lens, f32[128,512]{1,0:T(8,128)} %fusion.3.refs_0_, ...), custom_call_target="tpu_custom_call" | custom-call | tf_op jit(solution)/shard_map/pallas_call | solution.py:679
  326.5 25.6 %shard_map.399 = (bf16[8,4,64,1664]{3,2,1,0:T(8,128)(2,1)}, bf16[384,512]{1,0:T(8,128)(2,1)}) custom-call(s32[8]{0:T(128)} %broadcast_xor_fusion.order, s32[1]{0:T(128)} %bitcast.10.head, s32[1]{0:T(128)} %dynamic_slice.19.lens, f32[384,512]{1,0:T(8,128)} %get-tuple-element.110.refs_0_, f32[8,512]{1,0:T(8,128)} %get-tuple-element.111.refs_1_, ...), custom_call_target="tpu_custom_call" | custom-call | tf_op jit(solution)/shard_map/pallas_call | solution.py:679
  353.1 2.6 collective-permute-start.24
  359.7 8.1 %collective-permute-done.25 = bf16[128,512]{1,0:T(8,128)(2,1)S(1)} collective-permute-done((bf16[128,512]{1,0:T(8,128)(2,1)S(1)}, bf16[128,512]{1,0:T(8,128)(2,1)S(1)}, u32[]{:S(2)}, u32[]{:S(2)}) %collective-permute-start.25) | collective-permute-done | bytes 131104 | tf_op jit(solution)/shard_map/ppermute | solution.py:33
  368.5 2.0 collective-permute-start.29
  371.5 18.6 %shard_map.400.refs_0_ = f32[512,8064]{1,0:T(8,128)} custom-call(s32[896,1]{1,0:T(8,128)} %reshape.414.ids_ref, bf16[896,512]{1,0:T(8,128)(2,1)} %copy-done.15, bf16[512,512]{1,0:T(8,128)(2,1)} %dynamic-slice_bitcast_fusion.final_ref.refs_0_, bf16[8064,512]{1,0:T(8,128)(2,1)} %get-tuple-element.123.refs_1_), custom_call_target="tpu_custom_call" | custom-call | tf_op jit(solution)/shard_map/pallas_call | solution.py:192
  390.1 12.1 %collective-permute-done.28 = bf16[384,512]{1,0:T(8,128)(2,1)S(1)} collective-permute-done((bf16[384,512]{1,0:T(8,128)(2,1)S(1)}, bf16[384,512]{1,0:T(8,128)(2,1)S(1)}, u32[]{:S(2)}, u32[]{:S(2)}) %collective-permute-start.28) | collective-permute-done | bytes 393248 | tf_op jit(solution)/shard_map/ppermute | solution.py:33
  403.4 19.3 %shard_map.401 = (f32[64,8064]{1,0:T(8,128)}, f32[64,8064]{1,0:T(8,128)}, f32[64,8064]{1,0:T(8,128)}, f32[64,8064]{1,0:T(8,128)}, bf16[256,8064]{1,0:T(8,128)(2,1)}) custom-call(s32[1152,1]{1,0:T(8,128)} %bitcast.195, bf16[1152,512]{1,0:T(8,128)(2,1)} %pad_maximum_fusion.rows_ref, f32[512,8064]{1,0:T(8,128)} %shard_map.400.refs_0_), custom_call_target="tpu_custom_call" | custom-call | tf_op jit(solution)/shard_map/pallas_call | solution.py:192
  424.2 5.7 collective-permute-done.30.got_ref.got
  430.0 2.0 copy-done.2
  431.9 6.1 %shard_map.402 = (bf16[32,8064]{1,0:T(8,128)(2,1)}, bf16[32,8064]{1,0:T(8,128)(2,1)}, bf16[32,8064]{1,0:T(8,128)(2,1)}, bf16[32,8064]{1,0:T(8,128)(2,1)}, f32[32,8064]{1,0:T(8,128)}, /*index=5*/f32[32,8064]{1,0:T(8,128)}) custom-call(f32[64,8064]{1,0:T(8,128)} %get-tuple-element.124.y_ref, f32[64,8064]{1,0:T(8,128)} %get-tuple-element.125.x_ref, ...), custom_call_target="tpu_custom_call" | custom-call | tf_op jit(solution)/shard_map/pallas_call | solution.py:210
  441.2 2.0 slice_bitcast_fusion
  444.7 2.9 collective-permute-start.34
  448.5 12.5 %collective-permute-done.31.got_a = bf16[32,8064]{1,0:T(8,128)(2,1)S(1)} collective-permute-done((bf16[32,8064]{1,0:T(8,128)(2,1)}, bf16[32,8064]{1,0:T(8,128)(2,1)S(1)}, u32[]{:S(2)}, u32[]{:S(2)}) %collective-permute-start.31) | collective-permute-done | bytes 516128 | tf_op jit(solution)/shard_map/ppermute | solution.py:29
  461.3 3.1 collective-permute-done.33
  465.2 2.7 shard_map.403
  468.5 21.4 %reduce-scatter.5.cloned.1.call-done = bf16[1,4,64,1664]{3,2,1,0:T(8,128)(2,1)} async-done(((bf16[8,4,64,1664]{3,2,1,0:T(8,128)(2,1)}), bf16[1,4,64,1664]{3,2,1,0:T(8,128)(2,1)}) %reduce-scatter.5.cloned.1.call-update) | async-done | bytes 851984 | tf_op jit(solution)/shard_map/reduce_scatter | solution.py:1207
  491.2 4.8 collective-permute-start.37
  496.0 2.0 collective-permute-start.38
  500.5 3.1 collective-permute-done.37
  504.2 8.0 %collective-permute-done.38 = bf16[64,1664]{1,0:T(8,128)(2,1)S(1)} collective-permute-done((bf16[64,1664]{1,0:T(8,128)(2,1)S(1)}, bf16[64,1664]{1,0:T(8,128)(2,1)S(1)}, u32[]{:S(2)}, u32[]{:S(2)}) %collective-permute-start.38) | collective-permute-done | bytes 213024 | tf_op jit(solution)/shard_map/ppermute | solution.py:33
  517.2 8.8 %collective-permute-done.42.x_high = bf16[32,8064]{1,0:T(8,128)(2,1)S(1)} collective-permute-done((bf16[32,8064]{1,0:T(8,128)(2,1)}, bf16[32,8064]{1,0:T(8,128)(2,1)S(1)}, u32[]{:S(2)}, u32[]{:S(2)}) %collective-permute-start.42) | collective-permute-done | bytes 516128 | tf_op jit(solution)/shard_map/ppermute | solution.py:29
  526.7 4.8 shard_map.404
  534.8 2.9 collective-permute-done.44
  538.3 3.1 collective-permute-done.45
  541.4 1.8 collective-permute-start.46
  543.2 3.4 collective-permute-start.47
  548.2 2.0 collective-permute-done.48
  553.5 9.4 %shard_map.405 = (f32[64,8032]{1,0:T(8,128)}, f32[64,8032]{1,0:T(8,128)}, f32[64,8032]{1,0:T(8,128)}, f32[8,128]{1,0:T(8,128)}) custom-call(f32[64,8032]{1,0:T(8,128)} %bitcast.188, f32[64,8032]{1,0:T(8,128)} %bitcast.197, f32[64,8032]{1,0:T(8,128)} %bitcast.198, f32[64,8032]{1,0:T(8,128)} %get-tuple-element.150.g, f32[8,128]{1,0:T(8,128)} %broadcast_in_dim.29.clip.clip_ref), custom_call_target="tpu_custom_call" | custom-call | tf_op jit(solution)/shard_map/pallas_call | solution.py:210
  563.0 3.8 shard_map.406
  570.7 2.6 collective-permute-done.50
  573.9 3.2 collective-permute-done.51
  577.1 2.4 collective-permute-start.53
  585.8 1.8 subtract_bitcast_fusion.1
  587.5 1.8 multiply_subtract_fusion.1
  590.9 1.8 multiply_subtract_fusion
  592.7 3.1 subtract_bitcast_fusion
  (263 shorter events, 81.8 us)
Async XLA Ops:
  7.2 158.3 %all-gather.3.cloned.1.call-start = ((), (), s32[]{:S(2)}) async-start(), calls=%async_computation.4 | async-start | bytes 15679488 | tf_op jit(solution)/shard_map/all_gather | solution.py:1121
  11.0 38.3 %copy-start.3 = (bf16[64,8032]{1,0:T(8,128)(2,1)}, bf16[64,8032]{1,0:T(8,128)(2,1)S(1)}, u32[]{:S(2)}) copy-start(bf16[64,8032]{1,0:T(8,128)(2,1)S(1)} %bitcast_convert_fusion.1.refs_0_.refs_1_) | copy-start | bytes 3084292
  11.0 38.2 %copy-start.27 = (s32[4,384]{1,0:T(4,128)S(1)}, s32[4,384]{1,0:T(4,128)}, u32[]{:S(2)}) copy-start(s32[4,384]{1,0:T(4,128)} %param.25) | copy-start | bytes 18436
  11.7 37.5 %copy-start.26 = (s32[4,128]{1,0:T(4,128)S(1)}, s32[4,128]{1,0:T(4,128)}, u32[]{:S(2)}) copy-start(s32[4,128]{1,0:T(4,128)} %param.26) | copy-start | bytes 6148
  14.4 54.3 %copy-start.34 = (s32[4]{0:T(128)S(1)}, s32[4]{0:T(128)}, u32[]{:S(2)}) copy-start(s32[4]{0:T(128)} %param.27) | copy-start | bytes 52
  14.4 54.9 %copy-start.32 = (s32[8]{0:T(128)S(1)}, s32[8]{0:T(128)}, u32[]{:S(2)}) copy-start(s32[8]{0:T(128)} %constant.144.clone) | copy-start | bytes 100
  14.4 426.8 %reduce-scatter.3.cloned.1.call-start = ((), (), s32[]{:S(2)}) async-start(), calls=%async_computation.2 | async-start | bytes 9437184 | tf_op jit(solution)/shard_map/reduce_scatter | solution.py:1201
  14.4 29.2 %collective-permute-start = (bf16[64,8032]{1,0:T(8,128)(2,1)S(1)}, bf16[64,8032]{1,0:T(8,128)(2,1)S(1)}, u32[]{:S(2)}, u32[]{:S(2)}) collective-permute-start(bf16[64,8032]{1,0:T(8,128)(2,1)S(1)} %bitcast_convert_fusion.1.refs_0_.refs_1_), channel_id=1, source_target_pairs={{0,16},{4,20},{8,24},{12,28},{16,0},{20,4},{24,8},{28,12},{1,17},{... | collective-permute-start | bytes 3084296 | tf_op jit(solution)/shard_map/ppermute | solution.py:29
  17.5 28.8 %collective-permute-start.1 = (bf16[64,8032]{1,0:T(8,128)(2,1)S(1)}, bf16[64,8032]{1,0:T(8,128)(2,1)S(1)}, u32[]{:S(2)}, u32[]{:S(2)}) collective-permute-start(bf16[64,8032]{1,0:T(8,128)(2,1)S(1)} %bitcast_convert_fusion.1.refs_0_.refs_1_), channel_id=1, source_target_pairs={{0,8},{4,12},{8,0},{12,4},{16,24},{20,28},{24,16},{28,20},{1,9},{5... | collective-permute-start | bytes 3084296 | tf_op jit(solution)/shard_map/ppermute | solution.py:29
  44.6 22.2 %collective-permute-start.2 = (bf16[32,8032]{1,0:T(8,128)(2,1)}, bf16[32,8032]{1,0:T(8,128)(2,1)}, u32[]{:S(2)}, u32[]{:S(2)}) collective-permute-start(bf16[32,8032]{1,0:T(8,128)(2,1)} %slice.238), channel_id=1, source_target_pairs={{0,8},{4,12},{8,0},{12,4},{16,24},{20,28},{24,16},{28,20},{1,9},{5... | collective-permute-start | bytes 1542152 | tf_op jit(solution)/shard_map/ppermute | solution.py:29
  47.2 19.6 %collective-permute-start.3 = (bf16[32,8032]{1,0:T(8,128)(2,1)}, bf16[32,8032]{1,0:T(8,128)(2,1)}, u32[]{:S(2)}, u32[]{:S(2)}) collective-permute-start(bf16[32,8032]{1,0:T(8,128)(2,1)} %slice.239), channel_id=1, source_target_pairs={{0,16},{4,20},{8,24},{12,28},{16,0},{20,4},{24,8},{28,12},{1,17},{... | collective-permute-start | bytes 1542152 | tf_op jit(solution)/shard_map/ppermute | solution.py:29
  48.7 20.6 %collective-permute-start.4 = (bf16[64,8032]{1,0:T(8,128)(2,1)S(1)}, bf16[64,8032]{1,0:T(8,128)(2,1)}, u32[]{:S(2)}, u32[]{:S(2)}) collective-permute-start(bf16[64,8032]{1,0:T(8,128)(2,1)S(1)} %bitcast_convert_fusion.1.refs_0_.refs_1_), channel_id=1, source_target_pairs={{0,4},{4,0},{8,12},{12,8},{16,20},{20,16},{24,28},{28,24},{1,5},{5... | collective-permute-start | bytes 3084296 | tf_op jit(solution)/shard_map/ppermute | solution.py:29
  48.7 21.1 %collective-permute-start.5 = (bf16[64,8032]{1,0:T(8,128)(2,1)S(1)}, bf16[64,8032]{1,0:T(8,128)(2,1)}, u32[]{:S(2)}, u32[]{:S(2)}) collective-permute-start(bf16[64,8032]{1,0:T(8,128)(2,1)S(1)} %collective-permute-done.refs_1_.refs_2_), channel_id=1, source_target_pairs={{0,4},{4,0},{8,12},{12,8},{16,20},{20,16},{24,28},{28,24},{1,5},{5... | collective-permute-start | bytes 3084296 | tf_op jit(solution)/shard_map/ppermute | solution.py:29
  49.2 20.6 %collective-permute-start.6 = (bf16[64,8032]{1,0:T(8,128)(2,1)S(1)}, bf16[64,8032]{1,0:T(8,128)(2,1)}, u32[]{:S(2)}, u32[]{:S(2)}) collective-permute-start(bf16[64,8032]{1,0:T(8,128)(2,1)S(1)} %collective-permute-done.1.refs_2_.refs_3_), channel_id=1, source_target_pairs={{0,4},{4,0},{8,12},{12,8},{16,20},{20,16},{24,28},{28,24},{1,5},{5... | collective-permute-start | bytes 3084296 | tf_op jit(solution)/shard_map/ppermute | solution.py:29
  66.8 2.5 collective-permute-start.7
  66.8 3.0 collective-permute-start.8
  97.0 38.3 %collective-permute-start.10 = (bf16[384,512]{1,0:T(8,128)(2,1)S(1)}, bf16[384,512]{1,0:T(8,128)(2,1)S(1)}, u32[]{:S(2)}, u32[]{:S(2)}) collective-permute-start(bf16[384,512]{1,0:T(8,128)(2,1)S(1)} %get-tuple-element.249), channel_id=1, source_target_pairs={{0,2},{1,3},{2,0},{3,1},{4,6},{5,7},{6,4},{7,5},{8,10},{9,11},{10,... | collective-permute-start | bytes 1179656 | tf_op jit(solution)/shard_map/ppermute | solution.py:33
  99.6 37.0 %collective-permute-start.11 = (bf16[384,512]{1,0:T(8,128)(2,1)S(1)}, bf16[384,512]{1,0:T(8,128)(2,1)S(1)}, u32[]{:S(2)}, u32[]{:S(2)}) collective-permute-start(bf16[384,512]{1,0:T(8,128)(2,1)S(1)} %get-tuple-element.248), channel_id=1, source_target_pairs={{0,3},{1,0},{2,1},{3,2},{4,7},{5,4},{6,5},{7,6},{8,11},{9,8},{10,9... | collective-permute-start | bytes 1179656 | tf_op jit(solution)/shard_map/ppermute | solution.py:33
  100.9 51.9 %collective-permute-start.9 = (bf16[384,512]{1,0:T(8,128)(2,1)S(1)}, bf16[384,512]{1,0:T(8,128)(2,1)S(1)}, u32[]{:S(2)}, u32[]{:S(2)}) collective-permute-start(bf16[384,512]{1,0:T(8,128)(2,1)S(1)} %get-tuple-element.247), channel_id=1, source_target_pairs={{0,1},{1,2},{2,3},{3,0},{4,5},{5,6},{6,7},{7,4},{8,9},{9,10},{10,1... | collective-permute-start | bytes 1179656 | tf_op jit(solution)/shard_map/ppermute | solution.py:33
  183.6 8.3 %collective-permute-start.12 = (bf16[128,512]{1,0:T(8,128)(2,1)S(1)}, bf16[128,512]{1,0:T(8,128)(2,1)S(1)}, u32[]{:S(2)}, u32[]{:S(2)}) collective-permute-start(bf16[128,512]{1,0:T(8,128)(2,1)S(1)} %get-tuple-element.261), channel_id=1, source_target_pairs={{0,1},{1,2},{2,3},{3,0},{4,5},{5,6},{6,7},{7,4},{8,9},{9,10},{10,1... | collective-permute-start | bytes 393224 | tf_op jit(solution)/shard_map/ppermute | solution.py:33
  185.5 11.3 %collective-permute-start.13 = (bf16[128,512]{1,0:T(8,128)(2,1)S(1)}, bf16[128,512]{1,0:T(8,128)(2,1)S(1)}, u32[]{:S(2)}, u32[]{:S(2)}) collective-permute-start(bf16[128,512]{1,0:T(8,128)(2,1)S(1)} %get-tuple-element.263), channel_id=1, source_target_pairs={{0,2},{1,3},{2,0},{3,1},{4,6},{5,7},{6,4},{7,5},{8,10},{9,11},{10,... | collective-permute-start | bytes 393224 | tf_op jit(solution)/shard_map/ppermute | solution.py:33
  185.5 11.3 %collective-permute-start.14 = (bf16[128,512]{1,0:T(8,128)(2,1)S(1)}, bf16[128,512]{1,0:T(8,128)(2,1)S(1)}, u32[]{:S(2)}, u32[]{:S(2)}) collective-permute-start(bf16[128,512]{1,0:T(8,128)(2,1)S(1)} %get-tuple-element.262), channel_id=1, source_target_pairs={{0,3},{1,0},{2,1},{3,2},{4,7},{5,4},{6,5},{7,6},{8,11},{9,8},{10,9... | collective-permute-start | bytes 393224 | tf_op jit(solution)/shard_map/ppermute | solution.py:33
  218.1 6.9 %collective-permute-start.15 = (bf16[128,512]{0,1:T(8,128)(2,1)S(1)}, bf16[128,512]{0,1:T(8,128)(2,1)S(1)}, u32[]{:S(2)}, u32[]{:S(2)}) collective-permute-start(bf16[128,512]{0,1:T(8,128)(2,1)S(1)} %copy.100), channel_id=1, source_target_pairs={{0,3},{1,0},{2,1},{3,2},{4,7},{5,4},{6,5},{7,6},{8,11},{9,8},{10,9... | collective-permute-start | bytes 393224 | tf_op jit(solution)/shard_map/ppermute | solution.py:33
  222.3 12.3 %collective-permute-start.16 = (bf16[128,512]{0,1:T(8,128)(2,1)S(1)}, bf16[128,512]{0,1:T(8,128)(2,1)S(1)}, u32[]{:S(2)}, u32[]{:S(2)}) collective-permute-start(bf16[128,512]{0,1:T(8,128)(2,1)S(1)} %copy.100), channel_id=1, source_target_pairs={{0,2},{1,3},{2,0},{3,1},{4,6},{5,7},{6,4},{7,5},{8,10},{9,11},{10,... | collective-permute-start | bytes 393224 | tf_op jit(solution)/shard_map/ppermute | solution.py:33
  224.2 10.5 %collective-permute-start.17 = (bf16[128,512]{0,1:T(8,128)(2,1)S(1)}, bf16[128,512]{0,1:T(8,128)(2,1)S(1)}, u32[]{:S(2)}, u32[]{:S(2)}) collective-permute-start(bf16[128,512]{0,1:T(8,128)(2,1)S(1)} %copy.100), channel_id=1, source_target_pairs={{0,1},{1,2},{2,3},{3,0},{4,5},{5,6},{6,7},{7,4},{8,9},{9,10},{10,1... | collective-permute-start | bytes 393224 | tf_op jit(solution)/shard_map/ppermute | solution.py:33
  252.9 3.9 collective-permute-start.18
  252.9 4.8 collective-permute-start.19
  253.7 5.7 collective-permute-start.20
  286.2 8.3 %collective-permute-start.21 = (bf16[128,512]{1,0:T(8,128)(2,1)S(1)}, bf16[128,512]{1,0:T(8,128)(2,1)S(1)}, u32[]{:S(2)}, u32[]{:S(2)}) collective-permute-start(bf16[128,512]{1,0:T(8,128)(2,1)S(1)} %get-tuple-element.258), channel_id=1, source_target_pairs={{0,1},{1,2},{2,3},{3,0},{4,5},{5,6},{6,7},{7,4},{8,9},{9,10},{10,1... | collective-permute-start | bytes 393224 | tf_op jit(solution)/shard_map/ppermute | solution.py:33
  286.6 11.3 %collective-permute-start.22 = (bf16[128,512]{1,0:T(8,128)(2,1)S(1)}, bf16[128,512]{1,0:T(8,128)(2,1)S(1)}, u32[]{:S(2)}, u32[]{:S(2)}) collective-permute-start(bf16[128,512]{1,0:T(8,128)(2,1)S(1)} %get-tuple-element.259), channel_id=1, source_target_pairs={{0,2},{1,3},{2,0},{3,1},{4,6},{5,7},{6,4},{7,5},{8,10},{9,11},{10,... | collective-permute-start | bytes 393224 | tf_op jit(solution)/shard_map/ppermute | solution.py:33
  288.6 9.2 %collective-permute-start.23 = (bf16[128,512]{1,0:T(8,128)(2,1)S(1)}, bf16[128,512]{1,0:T(8,128)(2,1)S(1)}, u32[]{:S(2)}, u32[]{:S(2)}) collective-permute-start(bf16[128,512]{1,0:T(8,128)(2,1)S(1)} %get-tuple-element.260), channel_id=1, source_target_pairs={{0,3},{1,0},{2,1},{3,2},{4,7},{5,4},{6,5},{7,6},{8,11},{9,8},{10,9... | collective-permute-start | bytes 393224 | tf_op jit(solution)/shard_map/ppermute | solution.py:33
  326.2 163.7 %reduce-scatter.5.cloned.1.call-start = ((), (), s32[]{:S(2)}) async-start(), calls=%async_computation.3 | async-start | bytes 7667712 | tf_op jit(solution)/shard_map/reduce_scatter | solution.py:1207
  353.1 6.6 %collective-permute-start.24 = (bf16[128,512]{1,0:T(8,128)(2,1)S(1)}, bf16[128,512]{1,0:T(8,128)(2,1)S(1)}, u32[]{:S(2)}, u32[]{:S(2)}) collective-permute-start(bf16[128,512]{1,0:T(8,128)(2,1)S(1)} %copy-done.23), channel_id=1, source_target_pairs={{0,3},{1,0},{2,1},{3,2},{4,7},{5,4},{6,5},{7,6},{8,11},{9,8},{10,9... | collective-permute-start | bytes 393224 | tf_op jit(solution)/shard_map/ppermute | solution.py:33
  355.8 12.0 %collective-permute-start.25 = (bf16[128,512]{1,0:T(8,128)(2,1)S(1)}, bf16[128,512]{1,0:T(8,128)(2,1)S(1)}, u32[]{:S(2)}, u32[]{:S(2)}) collective-permute-start(bf16[128,512]{1,0:T(8,128)(2,1)S(1)} %copy-done.23), channel_id=1, source_target_pairs={{0,2},{1,3},{2,0},{3,1},{4,6},{5,7},{6,4},{7,5},{8,10},{9,11},{10,... | collective-permute-start | bytes 393224 | tf_op jit(solution)/shard_map/ppermute | solution.py:33
  357.0 10.8 %collective-permute-start.26 = (bf16[128,512]{1,0:T(8,128)(2,1)S(1)}, bf16[128,512]{1,0:T(8,128)(2,1)S(1)}, u32[]{:S(2)}, u32[]{:S(2)}) collective-permute-start(bf16[128,512]{1,0:T(8,128)(2,1)S(1)} %copy-done.23), channel_id=1, source_target_pairs={{0,1},{1,2},{2,3},{3,0},{4,5},{5,6},{6,7},{7,4},{8,9},{9,10},{10,1... | collective-permute-start | bytes 393224 | tf_op jit(solution)/shard_map/ppermute | solution.py:33
  367.8 22.3 %collective-permute-start.27 = (bf16[384,512]{1,0:T(8,128)(2,1)S(1)}, bf16[384,512]{1,0:T(8,128)(2,1)S(1)}, u32[]{:S(2)}, u32[]{:S(2)}) collective-permute-start(bf16[384,512]{1,0:T(8,128)(2,1)S(1)} %copy-done.22), channel_id=1, source_target_pairs={{0,3},{1,0},{2,1},{3,2},{4,7},{5,4},{6,5},{7,6},{8,11},{9,8},{10,9... | collective-permute-start | bytes 1179656 | tf_op jit(solution)/shard_map/ppermute | solution.py:33
  367.8 34.4 %collective-permute-start.28 = (bf16[384,512]{1,0:T(8,128)(2,1)S(1)}, bf16[384,512]{1,0:T(8,128)(2,1)S(1)}, u32[]{:S(2)}, u32[]{:S(2)}) collective-permute-start(bf16[384,512]{1,0:T(8,128)(2,1)S(1)} %copy-done.22), channel_id=1, source_target_pairs={{0,2},{1,3},{2,0},{3,1},{4,6},{5,7},{6,4},{7,5},{8,10},{9,11},{10,... | collective-permute-start | bytes 1179656 | tf_op jit(solution)/shard_map/ppermute | solution.py:33
  368.5 33.8 %collective-permute-start.29 = (bf16[384,512]{1,0:T(8,128)(2,1)S(1)}, bf16[384,512]{1,0:T(8,128)(2,1)S(1)}, u32[]{:S(2)}, u32[]{:S(2)}) collective-permute-start(bf16[384,512]{1,0:T(8,128)(2,1)S(1)} %copy-done.22), channel_id=1, source_target_pairs={{0,1},{1,2},{2,3},{3,0},{4,5},{5,6},{6,7},{7,4},{8,9},{9,10},{10,1... | collective-permute-start | bytes 1179656 | tf_op jit(solution)/shard_map/ppermute | solution.py:33
  422.7 7.3 %collective-permute-start.30 = (bf16[256,8064]{1,0:T(8,128)(2,1)}, bf16[256,8064]{1,0:T(8,128)(2,1)S(1)}, u32[]{:S(2)}, u32[]{:S(2)}) collective-permute-start(bf16[256,8064]{1,0:T(8,128)(2,1)} %get-tuple-element.127), channel_id=1, source_target_pairs={{0,4},{4,0},{8,12},{12,8},{16,20},{20,16},{24,28},{28,24},{1,5},{5... | collective-permute-start | bytes 12386312 | tf_op jit(solution)/shard_map/ppermute | solution.py:29
  438.1 22.9 %collective-permute-start.31 = (bf16[32,8064]{1,0:T(8,128)(2,1)}, bf16[32,8064]{1,0:T(8,128)(2,1)S(1)}, u32[]{:S(2)}, u32[]{:S(2)}) collective-permute-start(bf16[32,8064]{1,0:T(8,128)(2,1)} %get-tuple-element.128), channel_id=1, source_target_pairs={{0,8},{4,12},{8,0},{12,4},{16,24},{20,28},{24,16},{28,20},{1,9},{5... | collective-permute-start | bytes 1548296 | tf_op jit(solution)/shard_map/ppermute | solution.py:29
  439.7 24.7 %collective-permute-start.35 = (bf16[32,8064]{1,0:T(8,128)(2,1)}, bf16[32,8064]{1,0:T(8,128)(2,1)S(1)}, u32[]{:S(2)}, u32[]{:S(2)}) collective-permute-start(bf16[32,8064]{1,0:T(8,128)(2,1)} %get-tuple-element.137), channel_id=1, source_target_pairs={{0,16},{4,20},{8,24},{12,28},{16,0},{20,4},{24,8},{28,12},{1,17},{... | collective-permute-start | bytes 1548296 | tf_op jit(solution)/shard_map/ppermute | solution.py:29
  443.2 18.1 %collective-permute-start.32 = (bf16[64,2048]{1,0:T(8,128)(2,1)}, bf16[64,2048]{1,0:T(8,128)(2,1)S(1)}, u32[]{:S(2)}, u32[]{:S(2)}) collective-permute-start(bf16[64,2048]{1,0:T(8,128)(2,1)} %get-tuple-element.252), channel_id=1, source_target_pairs={{0,1},{1,2},{2,3},{3,0},{4,5},{5,6},{6,7},{7,4},{8,9},{9,10},{10,1... | collective-permute-start | bytes 786440 | tf_op jit(solution)/shard_map/ppermute | solution.py:33
  443.2 21.2 %collective-permute-start.33 = (bf16[64,2048]{1,0:T(8,128)(2,1)S(1)}, bf16[64,2048]{1,0:T(8,128)(2,1)S(1)}, u32[]{:S(2)}, u32[]{:S(2)}) collective-permute-start(bf16[64,2048]{1,0:T(8,128)(2,1)S(1)} %get-tuple-element.251), channel_id=1, source_target_pairs={{0,2},{1,3},{2,0},{3,1},{4,6},{5,7},{6,4},{7,5},{8,10},{9,11},{10,... | collective-permute-start | bytes 786440 | tf_op jit(solution)/shard_map/ppermute | solution.py:33
  444.7 19.7 %collective-permute-start.34 = (bf16[64,2048]{1,0:T(8,128)(2,1)S(1)}, bf16[64,2048]{1,0:T(8,128)(2,1)S(1)}, u32[]{:S(2)}, u32[]{:S(2)}) collective-permute-start(bf16[64,2048]{1,0:T(8,128)(2,1)S(1)} %get-tuple-element.250), channel_id=1, source_target_pairs={{0,3},{1,0},{2,1},{3,2},{4,7},{5,4},{6,5},{7,6},{8,11},{9,8},{10,9... | collective-permute-start | bytes 786440 | tf_op jit(solution)/shard_map/ppermute | solution.py:33
  461.0 56.1 %collective-permute-start.40 = (bf16[32,8064]{1,0:T(8,128)(2,1)}, bf16[32,8064]{1,0:T(8,128)(2,1)S(1)}, u32[]{:S(2)}, u32[]{:S(2)}) collective-permute-start(bf16[32,8064]{1,0:T(8,128)(2,1)} %get-tuple-element.145), channel_id=1, source_target_pairs={{0,8},{4,12},{8,0},{12,4},{16,24},{20,28},{24,16},{28,20},{1,9},{5... | collective-permute-start | bytes 1548296 | tf_op jit(solution)/shard_map/ppermute | solution.py:29
  467.9 45.0 %collective-permute-start.36 = (bf16[32,8064]{1,0:T(8,128)(2,1)}, bf16[32,8064]{1,0:T(8,128)(2,1)S(1)}, u32[]{:S(2)}, u32[]{:S(2)}) collective-permute-start(bf16[32,8064]{1,0:T(8,128)(2,1)} %get-tuple-element.138), channel_id=1, source_target_pairs={{0,16},{4,20},{8,24},{12,28},{16,0},{20,4},{24,8},{28,12},{1,17},{... | collective-permute-start | bytes 1548296 | tf_op jit(solution)/shard_map/ppermute | solution.py:29
  491.2 12.4 %collective-permute-start.37 = (bf16[64,1664]{1,0:T(8,128)(2,1)S(1)}, bf16[64,1664]{1,0:T(8,128)(2,1)S(1)}, u32[]{:S(2)}, u32[]{:S(2)}) collective-permute-start(bf16[64,1664]{1,0:T(8,128)(2,1)S(1)} %get-tuple-element.256), channel_id=1, source_target_pairs={{0,1},{1,2},{2,3},{3,0},{4,5},{5,6},{6,7},{7,4},{8,9},{9,10},{10,1... | collective-permute-start | bytes 638984 | tf_op jit(solution)/shard_map/ppermute | solution.py:33
  496.0 16.2 %collective-permute-start.38 = (bf16[64,1664]{1,0:T(8,128)(2,1)S(1)}, bf16[64,1664]{1,0:T(8,128)(2,1)S(1)}, u32[]{:S(2)}, u32[]{:S(2)}) collective-permute-start(bf16[64,1664]{1,0:T(8,128)(2,1)S(1)} %get-tuple-element.255), channel_id=1, source_target_pairs={{0,2},{1,3},{2,0},{3,1},{4,6},{5,7},{6,4},{7,5},{8,10},{9,11},{10,... | collective-permute-start | bytes 638984 | tf_op jit(solution)/shard_map/ppermute | solution.py:33
  498.0 14.9 %collective-permute-start.39 = (bf16[64,1664]{1,0:T(8,128)(2,1)S(1)}, bf16[64,1664]{1,0:T(8,128)(2,1)S(1)}, u32[]{:S(2)}, u32[]{:S(2)}) collective-permute-start(bf16[64,1664]{1,0:T(8,128)(2,1)S(1)} %get-tuple-element.254), channel_id=1, source_target_pairs={{0,3},{1,0},{2,1},{3,2},{4,7},{5,4},{6,5},{7,6},{8,11},{9,8},{10,9... | collective-permute-start | bytes 638984 | tf_op jit(solution)/shard_map/ppermute | solution.py:33
  503.6 13.5 %collective-permute-start.41 = (bf16[32,8064]{1,0:T(8,128)(2,1)S(1)}, bf16[32,8064]{1,0:T(8,128)(2,1)S(1)}, u32[]{:S(2)}, u32[]{:S(2)}) collective-permute-start(bf16[32,8064]{1,0:T(8,128)(2,1)S(1)} %copy-done.33), channel_id=1, source_target_pairs={{0,16},{4,20},{8,24},{12,28},{16,0},{20,4},{24,8},{28,12},{1,17},{... | collective-permute-start | bytes 1548296 | tf_op jit(solution)/shard_map/ppermute | solution.py:29
  512.2 13.8 %collective-permute-start.42 = (bf16[32,8064]{1,0:T(8,128)(2,1)}, bf16[32,8064]{1,0:T(8,128)(2,1)S(1)}, u32[]{:S(2)}, u32[]{:S(2)}) collective-permute-start(bf16[32,8064]{1,0:T(8,128)(2,1)} %get-tuple-element.148), channel_id=1, source_target_pairs={{0,8},{4,12},{8,0},{12,4},{16,24},{20,28},{24,16},{28,20},{1,9},{5... | collective-permute-start | bytes 1548296 | tf_op jit(solution)/shard_map/ppermute | solution.py:29
  513.0 39.8 %copy-start.12 = (f32[64,1664]{1,0:T(8,128)}, f32[64,1664]{1,0:T(8,128)S(1)}, u32[]{:S(2)}) copy-start(f32[64,1664]{1,0:T(8,128)S(1)} %convert_add_fusion.1.refs_0_) | copy-start | bytes 1277956
  532.2 1.2 collective-permute-start.43
  534.1 3.7 collective-permute-start.44
  537.7 3.7 collective-permute-start.45
  541.4 6.3 %collective-permute-start.46 = (f32[9,128]{1,0:T(8,128)S(1)}, f32[9,128]{1,0:T(8,128)S(1)}, u32[]{:S(2)}, u32[]{:S(2)}) collective-permute-start(f32[9,128]{1,0:T(8,128)S(1)} %add.250), channel_id=1, source_target_pairs={{0,1},{1,2},{2,3},{3,0},{4,5},{5,6},{6,7},{7,4},{8,9},{9,10},{10,1... | collective-permute-start | bytes 13832 | tf_op jit(solution)/shard_map/ppermute | solution.py:33
  543.2 5.0 collective-permute-start.47
  546.6 3.7 collective-permute-start.48
  567.7 1.2 collective-permute-start.49
  569.6 3.7 collective-permute-start.50
  573.3 3.7 collective-permute-start.51
  577.1 5.5 collective-permute-start.52
  577.1 5.5 collective-permute-start.53
  579.5 3.7 collective-permute-start.54
  (29 other events, 434.0 us)
Sparse Core Ops, SparseCore 0:
  14.5 150.8 all-gather.2
  326.3 71.4 reduce-scatter.2
  401.6 88.2 reduce-scatter.4

commit v4 on v3

--- a/solution.py
+++ b/solution.py
@@ -97,6 +97,19 @@
     return x
 
 
+def ordered(kernel, count, waits):
+    if not waits:
+        return kernel
+
+    def body(*refs):
+        kernel(*refs[:count], *refs[count + len(waits) :])
+
+    return body
+
+
+ANYWHERE = pl.BlockSpec(memory_space=pl.ANY)
+
+
 def stacked(refs):
     return refs[0][...] if len(refs) == 1 else jnp.concatenate([ref[...] for ref in refs], 0)
 
@@ -130,6 +143,14 @@
 
 
 VMEM_LIMIT = 56 * 2**20
+
+
+def cost(microseconds):
+    return pl.CostEstimate(
+        flops=int(1.15e9 * microseconds),
+        bytes_accessed=int(3.7e6 * microseconds),
+        transcendentals=0,
+    )
 
 
 def padded_to(columns, step=128):
@@ -149,8 +170,44 @@
         in_specs=[fixed((rows, 1))] + column_specs(table_parts, tile),
         out_specs=[fixed((rows, D)), pl.BlockSpec((tile, D), lambda i: (i, 0))],
         scratch_shapes=[pltpu.VMEM((rows, D), F32)],
+        cost_estimate=cost(26),
         compiler_params=pltpu.CompilerParams(vmem_limit_bytes=VMEM_LIMIT),
     )(ids.reshape(rows, 1), *table_parts)
+
+
+def pick(ids, table_rows, waits):
+    rows, vocab = ids.shape[0], table_rows.shape[0]
+    tile = 1024
+    return pl.pallas_call(
+        ordered(functools.partial(pick_kernel, vocab, tile), 2, waits),
+        out_shape=jax.ShapeDtypeStruct((rows, D), BF),
+        grid=(pl.cdiv(vocab, tile),),
+        in_specs=[fixed((rows, 1)), pl.BlockSpec((tile, D), lambda i: (i, 0))]
+        + [ANYWHERE] * len(waits),
+        out_specs=fixed((rows, D)),
+        scratch_shapes=[pltpu.VMEM((rows, D), F32)],
+        cost_estimate=cost(12),
+        compiler_params=pltpu.CompilerParams(vmem_limit_bytes=VMEM_LIMIT),
+    )(ids.reshape(rows, 1), table_rows, *waits)
+
+
+def pick_kernel(vocab, tile, ids_ref, rows_ref, out_ref, acc_ref):
+    step = pl.program_id(0)
+
+    @pl.when(step == 0)
+    def _():
+        acc_ref[...] = jnp.zeros_like(acc_ref)
+
+    place = lax.broadcasted_iota(jnp.int32, (1, tile), 1)
+    below = lax.broadcasted_iota(jnp.int32, (tile, 1), 0)
+    block = rows_ref[...]
+    block = jnp.where(below < vocab - step * tile, block, jnp.zeros_like(block))
+    hit = (ids_ref[...] - step * tile == place).astype(BF)
+    acc_ref[...] += jnp.dot(hit, block, preferred_element_type=F32)
+
+    @pl.when(step == pl.num_programs(0) - 1)
+    def _():
+        out_ref[...] = acc_ref[...].astype(BF)
 
 
 def spread_kernel(tile, ids_ref, rows_ref, *refs):
@@ -178,7 +235,7 @@
         send_ref[...] = total[D // 2 :].astype(BF)
 
 
-def spread(ids, rows_low, columns, final_t=None, slope=None, base=None):
+def spread(ids, rows_low, columns, final_t=None, slope=None, base=None, waits=()):
     rows = ids.shape[0]
     tile = 1024
     if base is None:
@@ -190,17 +247,18 @@
         more = [base]
         specs = [pl.BlockSpec((D, tile), lambda i: (0, i))]
     return pl.pallas_call(
-        functools.partial(spread_kernel, tile),
+        ordered(functools.partial(spread_kernel, tile), 2 + len(more), waits),
         out_shape=[jax.ShapeDtypeStruct(*shape) for shape in shapes],
         grid=(pl.cdiv(columns, tile),),
-        in_specs=[fixed((rows, 1)), fixed((rows, D))] + specs,
+        in_specs=[fixed((rows, 1)), fixed((rows, D))] + specs + [ANYWHERE] * len(waits),
         out_specs=[pl.BlockSpec((shape[0][0], tile), lambda i: (0, i)) for shape in shapes],
         scratch_shapes=[pltpu.VMEM((D, rows), BF)],
+        cost_estimate=cost(18),
         compiler_params=pltpu.CompilerParams(vmem_limit_bytes=VMEM_LIMIT),
-    )(ids.reshape(rows, 1), rows_low, *more)
-
-
-def column_call(kernel, inputs, outputs, tile, sums=(), columns=None):
+    )(ids.reshape(rows, 1), rows_low, *more, *waits)
+
+
+def column_call(kernel, inputs, outputs, tile, sums=(), columns=None, waits=()):
     columns = columns or inputs[0].shape[1]
     out_shape = [jax.ShapeDtypeStruct((rows, columns), dtype) for rows, dtype in outputs]
     out_specs = [pl.BlockSpec((rows, tile), lambda i: (0, i)) for rows, _ in outputs]
@@ -208,7 +266,7 @@
         out_shape.append(jax.ShapeDtypeStruct(shape, F32))
         out_specs.append(fixed(shape))
     return pl.pallas_call(
-        kernel,
+        ordered(kernel, len(inputs), waits),
         out_shape=out_shape,
         grid=(pl.cdiv(columns, tile),),
         in_specs=[
@@ -216,30 +274,35 @@
             if array.shape[1] >= columns
             else fixed(array.shape)
             for array in inputs
-        ],
+        ]
+        + [ANYWHERE] * len(waits),
         out_specs=out_specs,
+        cost_estimate=cost(5),
         compiler_params=pltpu.CompilerParams(vmem_limit_bytes=VMEM_LIMIT),
-    )(*inputs)
-
-
-def first_sums_kernel(y_ref, x_ref, d_ref, got_ref, d_low, d_high, x_low, y_high, y_low, x_high):
-    deep = y_ref.shape[0]
-    half = deep // 2
-    got = got_ref[...].astype(F32)
-    y = y_ref[...] + got[deep : 2 * deep]
-    x = x_ref[...] + got[2 * deep : 3 * deep]
-    d = (d_ref[...] + got[3 * deep :]).astype(BF)
-    d_low[...] = d[:half]
-    d_high[...] = d[half:]
-    x_low[...] = x[:half].astype(BF)
-    y_high[...] = y[half:].astype(BF)
-    y_low[...] = y[:half]
-    x_high[...] = x[half:]
-
-
-def second_sums_kernel(y_low, got_a, x_high, got_b, y_out, x_out):
-    y_out[...] = (y_low[...] + got_a[...].astype(F32)).astype(BF)
-    x_out[...] = (x_high[...] + got_b[...].astype(F32)).astype(BF)
+    )(*inputs, *waits)
+
+
+def first_sums_kernel(groups, *refs):
+    d_low, d_high, x_sum, y_sum = refs[4 * groups :]
+    start = 0
+    for group in range(groups):
+        y_ref, x_ref, d_ref, got_ref = refs[4 * group : 4 * group + 4]
+        deep, columns = y_ref.shape
+        half, stop = deep // 2, start + columns
+        y_sum[:, start:stop] = y_ref[...] + got_ref[deep : 2 * deep].astype(F32)
+        x_sum[:, start:stop] = x_ref[...] + got_ref[2 * deep : 3 * deep].astype(F32)
+        d = (d_ref[...] + got_ref[3 * deep :].astype(F32)).astype(BF)
+        d_low[:, start:stop] = d[:half]
+        d_high[:, start:stop] = d[half:]
+        start = stop
+
+
+def second_sums_kernel(y_sum, got_a, x_sum, got_b, y_out, x_out):
+    half = got_a.shape[0]
+    y_out[:half] = (y_sum[:half] + got_a[...].astype(F32)).astype(BF)
+    y_out[half:] = y_sum[half:].astype(BF)
+    x_out[:half] = x_sum[:half].astype(BF)
+    x_out[half:] = (x_sum[half:] + got_b[...].astype(F32)).astype(BF)
 
 
 def lane_sums(value):
@@ -258,63 +321,103 @@
     return jnp.where(place < columns, value, 0.0)
 
 
-def last_sums_kernel(columns, tile, own, got, x_low, y_high, y_low, x_high, out, squares):
-    half = x_low.shape[0]
-    low = own[:half] + got[:half].astype(F32) + (x_low[...].astype(F32) + y_low[...].astype(F32))
-    high = (
-        own[half:]
-        + got[half : 2 * half].astype(F32)
-        + (x_high[...].astype(F32) + y_high[...].astype(F32))
-    )
-    whole = jnp.concatenate([low, high], 0)
-    out[...] = whole
-
-    @pl.when(pl.program_id(0) == 0)
-    def _():
-        squares[...] = jnp.zeros_like(squares)
-
-    squares[...] += lane_sums(inside(columns, tile, whole * whole))
+def last_sums_kernel(groups, columns, tile, *refs):
+    y_ref, x_ref, out = refs[2 * groups : 2 * groups + 3]
+    more = x_ref[...].astype(F32) + y_ref[...].astype(F32)
+    start = 0
+    for group in range(groups):
+        own, got = refs[2 * group : 2 * group + 2]
+        deep, stop = own.shape[0], start + own.shape[1]
+        out[:, start:stop] = own[...] + got[:deep].astype(F32) + more[:, start:stop]
+        start = stop
+    if columns is not None:
+        squares = refs[-1]
+
+        @pl.when(pl.program_id(0) == 0)
+        def _():
+            squares[...] = jnp.zeros_like(squares)
+
+        squares[...] += lane_sums(inside(columns, tile, out[...] * out[...]))
 
 
 class ScatterDp:
-    def __init__(self, keeps, send, dp):
-        self.keeps, self.dp = keeps, dp
-        self.got = dp_swap(send, 1, dp)
-
-    def run(self, columns, middle, late):
+    def __init__(self, dp):
+        self.dp, self.groups = dp, []
+
+    def add(self, keeps, send):
+        self.groups.append((*keeps, dp_swap(send, 1, self.dp)))
+
+    def far(self, tile, waits=()):
         dp = self.dp
-        tile = 4096
+        self.pieces = ()
+        if dp == 8:
+            rows = self.groups[0][0].shape[0]
+            inputs, columns = [], 0
+            for own, y, x, d, got in self.groups:
+                inputs += [y, x, d, got]
+                columns += own.shape[1]
+            outputs = [(rows // 2, BF)] * 2 + [(rows, F32)] * 2
+            kernel = functools.partial(first_sums_kernel, len(self.groups))
+            d_low, d_high, *self.later = sums_call(
+                kernel, inputs, outputs, columns, tile, waits=waits
+            )
+            self.pieces = [dp_swap(d_low, 2, dp), dp_swap(d_high, 4, dp)]
+
+    def near(self, tile):
+        dp = self.dp
+        self.last = self.ready = ()
+        if dp == 8:
+            x_sum, y_sum = self.later
+            rows, columns = y_sum.shape
+            y_sum, x_sum = sums_call(
+                second_sums_kernel,
+                [y_sum, self.pieces[0], x_sum, self.pieces[1]],
+                [(rows, BF)] * 2,
+                columns,
+                tile,
+            )
+            self.ready = [y_sum, x_sum]
+            self.last = [dp_swap(y_sum, 4, dp), dp_swap(x_sum, 2, dp)]
+
+    def result(self, tile, columns=None):
+        dp = self.dp
         if dp != 8:
-            total = jnp.concatenate(self.keeps, 0) + self.got.astype(F32)
+            total = jnp.concatenate(
+                [
+                    jnp.concatenate(group[:4], 0) + group[4].astype(F32)
+                    for group in self.groups
+                ],
+                1,
+            )
             bit = 2
             while bit < dp:
                 rows = total.shape[0] // 2
                 total = total[:rows] + dp_swap(total[rows:].astype(BF), bit, dp).astype(F32)
                 bit *= 2
             total = total[:, :columns]
-            squares = jnp.sum(total * total)
-            return total, jnp.zeros((8, 128), F32).at[0, 0].set(squares)
-        own, y, x, d = self.keeps
-        half = own.shape[0] // 2
-        d_low, d_high, x_low, y_high, y_low, x_high = column_call(
-            first_sums_kernel, [y, x, d, self.got], [(half, BF)] * 4 + [(half, F32)] * 2, tile
-        )
-        got_a, got_b = dp_swap(d_low, 2, dp), dp_swap(d_high, 4, dp)
-        x_low, y_high = dp_swap(x_low, 2, dp), dp_swap(y_high, 4, dp)
-        got_a, *middle[:] = tie(got_a, *middle)
-        y_low, x_high = column_call(
-            second_sums_kernel, [y_low, got_a, x_high, got_b], [(half, BF)] * 2, tile
-        )
-        y_low, x_high = dp_swap(y_low, 4, dp), dp_swap(x_high, 2, dp)
-        y_low, *late[:] = tie(y_low, *late)
-        return column_call(
-            functools.partial(last_sums_kernel, columns, tile),
-            [own, self.got, x_low, y_high, y_low, x_high],
-            [(2 * half, F32)],
-            tile,
-            sums=[(8, 128)],
-            columns=columns,
-        )
+            if columns is None:
+                return [total]
+            return [total, jnp.zeros((8, 128), F32).at[0, 0].set(jnp.sum(total * total))]
+        inputs, wide = [], 0
+        for own, _, _, _, got in self.groups:
+            inputs += [own, got]
+            wide += own.shape[1]
+        inputs += self.last
+        kernel = functools.partial(last_sums_kernel, len(self.groups), columns, tile)
+        sums = [] if columns is None else [(8, 128)]
+        rows = self.groups[0][0].shape[0]
+        return sums_call(kernel, inputs, [(rows, F32)], columns or wide, tile, sums)
+
+
+def sums_call(kernel, inputs, outputs, columns, tile, sums=(), waits=()):
+    if tile is not None:
+        return column_call(kernel, inputs, outputs, tile, sums, columns, waits)
+    return pl.pallas_call(
+        kernel,
+        out_shape=[jax.ShapeDtypeStruct((rows, columns), dtype) for rows, dtype in outputs],
+        cost_estimate=cost(5),
+        compiler_params=pltpu.CompilerParams(vmem_limit_bytes=VMEM_LIMIT),
+    )(*inputs)
 
 
 def logits_kernel(vocab, tile, final_ref, label_ref, teacher_ref, table_ref, out_ref, *stats):
@@ -407,6 +510,7 @@
         ],
         out_specs=fixed((8, tokens)),
         scratch_shapes=[pltpu.VMEM((8, tokens), F32)] * 7,
+        cost_estimate=cost(17),
         compiler_params=pltpu.CompilerParams(vmem_limit_bytes=VMEM_LIMIT),
     )(final_t, labels.reshape(1, tokens), teacher_t, table_rows)
 
@@ -464,6 +568,7 @@
         + column_specs(table_parts, tile),
         out_specs=[pl.BlockSpec((tile, tokens), lambda i: (i, 0)), fixed((D, tokens))],
         scratch_shapes=[pltpu.VMEM((D, tokens), F32)],
+        cost_estimate=cost(22),
         compiler_params=pltpu.CompilerParams(vmem_limit_bytes=VMEM_LIMIT),
     )(final_t, labels.reshape(1, tokens), scalars, teacher_t, table_rows, *table_parts)
 
@@ -531,6 +636,7 @@
     return pl.pallas_call(
         functools.partial(lamb_matrices_kernel, places),
         out_shape=shapes + [jax.ShapeDtypeStruct((rows, 128), F32)],
+        cost_estimate=cost(4),
         compiler_params=pltpu.CompilerParams(vmem_limit_bytes=VMEM_LIMIT),
     )(clip, *grads, *flat)
 
@@ -549,6 +655,7 @@
     return pl.pallas_call(
         functools.partial(pack_kernel, plan),
         out_shape=jax.ShapeDtypeStruct((arrays[0].shape[-2], columns), BF),
+        cost_estimate=cost(2),
         compiler_params=pltpu.CompilerParams(vmem_limit_bytes=VMEM_LIMIT),
     )(*arrays)
 
@@ -599,10 +706,8 @@
     )
 
 
-def weights_of(ref, order_ref, start, stop):
-    return jnp.concatenate(
-        [ref[order_ref[place], 0, :, start:stop] for place in range(ref.shape[0])], 0
-    )
+def weights_of(ref, order_ref, j):
+    return jnp.concatenate([ref[order_ref[place], j] for place in range(ref.shape[0])], 0)
 
 
 def attend_heads(query, keys_all, values, each, mask_of):
@@ -645,210 +750,245 @@
     return [jnp.concatenate(out, 0) if each > 1 else out[0] for out in outs]
 
 
-def at_phase(step, phase, heads):
-    return jnp.clip(step - phase * heads, 0, heads - 1)
-
-
 class Layers:
-    def __init__(self, order, head_pos, lens, weights, gain, each):
+    def __init__(self, order, head_pos, lens, enc_weights, dec_weights, gain, each):
         self.prefetch = (order, head_pos.reshape(1), lens)
-        self.weights, self.gain, self.each = weights, gain, each
-        self.dp, self.heads, self.deep, _ = weights.shape
+        self.sides, self.gain, self.each = (enc_weights, dec_weights), gain, each
+        self.dp, self.heads, self.deep, _ = enc_weights.shape
         self.width = 4 * D // self.heads
         self.unit = self.width // 4
 
-    def weight_spec(self, block, phase):
-        heads = self.heads
-
-        def index(step, order, head, lens):
-            return (0, lax.rem(head[0] + at_phase(step, phase, heads), heads), 0, block)
-
-        return pl.BlockSpec((self.dp, 1, self.deep, self.width), index)
-
-    def kept_spec(self, shape, phase):
-        heads = self.heads
-        return pl.BlockSpec(
-            (1,) + shape[1:], lambda step, *_: (at_phase(step, phase, heads), 0, 0)
-        )
+    def weight_specs(self, side, first, stride, fixed_block=None):
+        shape = (self.dp, self.heads, self.deep, self.width)
+        weights = self.sides[side]
+        out = [
+            (
+                weights,
+                pl.BlockSpec(shape, lambda step, *_: (0, 0, 0, first + stride * step)),
+            )
+        ]
+        if fixed_block is not None:
+            out.append(
+                (weights, pl.BlockSpec(shape, lambda step, *_: (0, 0, 0, fixed_block)))
+            )
+        return out
 
     @staticmethod
     def whole(shape):
         return pl.BlockSpec(shape, lambda *_: (0,) * len(shape))
 
-    def call(self, kernel, phases, arrays, outs, scratch):
+    def call(self, kernel, phases, arrays, outs, scratch, time):
+        arrays = [a if isinstance(a, tuple) else (a, self.whole(a.shape)) for a in arrays]
         return pl.pallas_call(
             kernel,
-            out_shape=[jax.ShapeDtypeStruct(shape, dtype) for shape, dtype, _ in outs],
+            out_shape=[jax.ShapeDtypeStruct(shape, dtype) for shape, dtype in outs],
             grid_spec=pltpu.PrefetchScalarGridSpec(
                 num_scalar_prefetch=3,
-                grid=(phases * self.heads,),
-                in_specs=[spec or self.whole(array.shape) for array, spec in arrays],
-                out_specs=[spec or self.whole(shape) for shape, _, spec in outs],
+                grid=(phases,),
+                in_specs=[spec for _, spec in arrays],
+                out_specs=[self.whole(shape) for shape, _ in outs],
                 scratch_shapes=[pltpu.VMEM(shape, dtype) for shape, dtype in scratch],
             ),
+            cost_estimate=cost(time),
             compiler_params=pltpu.CompilerParams(vmem_limit_bytes=VMEM_LIMIT),
         )(*self.prefetch, *[array for array, _ in arrays])
 
+    def self_attention(self, low, w_of, kept, mask_of):
+        unit = self.unit
+        total = None
+        for j in range(self.heads):
+            w = w_of(j)
+            qkv = dot(low, w[:, : 3 * unit]).astype(BF)
+            mixed = attend_heads(
+                qkv[:, :unit], qkv[:, unit : 2 * unit], qkv[:, 2 * unit :], self.each, mask_of
+            )
+            kept[j, :, : 3 * unit] = qkv
+            kept[j, :, 3 * unit :] = mixed
+            part = dot_nt(mixed, w[:, 3 * unit :])
+            total = part if total is None else total + part
+        return total
+
+    def feed(self, low, up_of, down_of, hidden):
+        total = None
+        for j in range(self.heads):
+            grown = jax.nn.relu(dot(low, up_of(j))).astype(BF)
+            hidden[j] = grown
+            part = dot_nt(grown, down_of(j))
+            total = part if total is None else total + part
+        return total
+
     def encoder(self, x):
-        heads, each, unit, width = self.heads, self.each, self.unit, self.width
+        heads, each, width = self.heads, self.each, self.width
         rows = x.shape[0]
 
-        def kernel(order, head, lens, x_ref, gain, a_ref, u_ref, d_ref, *refs):
-            kept, mid, hidden, last, encoded, low, acc = refs
+        def kernel(order, head, lens, x_ref, gain, w_ref, d_ref, kept, mid, hidden, last, encoded):
             step = pl.program_id(0)
+            w_of = functools.partial(weights_of, w_ref, order)
 
             @pl.when(step == 0)
             def _():
-                acc[...] = x_ref[...]
-                low[...] = normed(x_ref[...], gain[0:1])
-
-            @pl.when(step < heads)
+                low = normed(x_ref[...], gain[0:1])
+                mid[...] = x_ref[...] + self.self_attention(
+                    low, w_of, kept, lambda n: key_mask(lens[n], rows // each)
+                )
+
+            @pl.when(step == 1)
             def _():
-                w = weights_of(a_ref, order, 0, width)
-                qkv = dot(low[...], w[:, : 3 * unit]).astype(BF)
-                mixed = attend_heads(
-                    qkv[:, :unit],
-                    qkv[:, unit : 2 * unit],
-                    qkv[:, 2 * unit :],
-                    each,
-                    lambda n: key_mask(lens[n], rows // each),
-                )
-                kept[0, :, : 3 * unit] = qkv
-                kept[0, :, 3 * unit :] = mixed
-                acc[...] += dot_nt(mixed, w[:, 3 * unit :])
-
-            @pl.when(step == heads)
-            def _():
-                mid[...] = acc[...]
-                low[...] = normed(acc[...], gain[1:2])
-
-            @pl.when(step >= heads)
-            def _():
-                grown = jax.nn.relu(dot(low[...], weights_of(u_ref, order, 0, width))).astype(BF)
-                hidden[0] = grown
-                acc[...] += dot_nt(grown, weights_of(d_ref, order, 0, width))
-
-            @pl.when(step == 2 * heads - 1)
-            def _():
-                last[...] = acc[...]
-                encoded[...] = normed(acc[...], gain[2:3])
-
-        shape = (heads, rows, width)
+                low = normed(mid[...], gain[1:2])
+                d_of = functools.partial(weights_of, d_ref, order)
+                value = mid[...] + self.feed(low, w_of, d_of, hidden)
+                last[...] = value
+                encoded[...] = normed(value, gain[2:3])
+
         return self.call(
             kernel,
             2,
-            [(x, None), (self.gain, None)]
-            + [(self.weights, self.weight_spec(*at)) for at in ((0, 0), (1, 1), (2, 1))],
+            [x, self.gain] + self.weight_specs(0, 0, 1, 2),
             [
-                (shape, BF, self.kept_spec(shape, 0)),
-                ((rows, D), F32, None),
-                (shape, BF, self.kept_spec(shape, 1)),
-                ((rows, D), F32, None),
-                ((rows, D), BF, None),
+                ((heads, rows, width), BF),
+                ((rows, D), F32),
+                ((heads, rows, width), BF),
+                ((rows, D), F32),
+                ((rows, D), BF),
             ],
-            [((rows, D), BF), ((rows, D), F32)],
+            [],
+            14,
         )
 
     def decoder(self, x, encoded):
         heads, each, unit, width = self.heads, self.each, self.unit, self.width
         rows, source = x.shape[0], encoded.shape[0]
 
-        def kernel(order, head, lens, x_ref, enc_ref, gain, s_ref, c_ref, u_ref, d_ref, *refs):
-            kept, one, kept_q, kept_k, two, hidden, three, final, low, acc = refs
+        def kernel(order, head, lens, x_ref, enc_ref, gain, w_ref, d_ref, *refs):
+            kept, one, kept_q, kept_k, two, hidden, three, final = refs
             step = pl.program_id(0)
+            w_of = functools.partial(weights_of, w_ref, order)
 
             @pl.when(step == 0)
             def _():
-                acc[...] = x_ref[...]
-                low[...] = normed(x_ref[...], gain[3:4])
-
-            @pl.when(step < heads)
+                low = normed(x_ref[...], gain[3:4])
+                one[...] = x_ref[...] + self.self_attention(
+                    low, w_of, kept, lambda n: causal_mask(rows // each)
+                )
+
+            @pl.when(step == 1)
             def _():
-                w = weights_of(s_ref, order, 0, width)
-                qkv = dot(low[...], w[:, : 3 * unit]).astype(BF)
-                mixed = attend_heads(
-                    qkv[:, :unit],
-                    qkv[:, unit : 2 * unit],
-                    qkv[:, 2 * unit :],
-                    each,
-                    lambda n: causal_mask(rows // each),
-                )
-                kept[0, :, : 3 * unit] = qkv
-                kept[0, :, 3 * unit :] = mixed
-                acc[...] += dot_nt(mixed, w[:, 3 * unit :])
-
-            @pl.when(step == heads)
+                low = normed(one[...], gain[4:5])
+                total = one[...]
+                for j in range(heads):
+                    w = w_of(j)
+                    query = dot(low, w[:, :unit]).astype(BF)
+                    both = dot(enc_ref[...], w[:, unit : 3 * unit]).astype(BF)
+                    mixed = attend_heads(
+                        query,
+                        both[:, :unit],
+                        both[:, unit:],
+                        each,
+                        lambda n: key_mask(lens[n], source // each),
+                    )
+                    kept_q[j, :, :unit] = query
+                    kept_q[j, :, unit:] = mixed
+                    kept_k[j] = both
+                    total = total + dot_nt(mixed, w[:, 3 * unit :])
+                two[...] = total
+
+            @pl.when(step == 2)
             def _():
-                one[...] = acc[...]
-                low[...] = normed(acc[...], gain[4:5])
-
-            @pl.when((step >= heads) & (step < 2 * heads))
-            def _():
-                w = weights_of(c_ref, order, 0, width)
-                query = dot(low[...], w[:, :unit]).astype(BF)
-                both = dot(enc_ref[...], w[:, unit : 3 * unit]).astype(BF)
-                mixed = attend_heads(
-                    query,
-                    both[:, :unit],
-                    both[:, unit:],
-                    each,
-                    lambda n: key_mask(lens[n], source // each),
-                )
-                kept_q[0, :, :unit] = query
-                kept_q[0, :, unit:] = mixed
-                kept_k[0] = both
-                acc[...] += dot_nt(mixed, w[:, 3 * unit :])
-
-            @pl.when(step == 2 * heads)
-            def _():
-                two[...] = acc[...]
-                low[...] = normed(acc[...], gain[5:6])
-
-            @pl.when(step >= 2 * heads)
-            def _():
-                grown = jax.nn.relu(dot(low[...], weights_of(u_ref, order, 0, width))).astype(BF)
-                hidden[0] = grown
-                acc[...] += dot_nt(grown, weights_of(d_ref, order, 0, width))
-
-            @pl.when(step == 3 * heads - 1)
-            def _():
-                three[...] = acc[...]
-                final[...] = normed(acc[...], gain[6:7] * D ** (-0.5))
-
-        shape = (heads, rows, width)
-        shape_q, shape_k = (heads, rows, 2 * unit), (heads, source, 2 * unit)
+                low = normed(two[...], gain[5:6])
+                d_of = functools.partial(weights_of, d_ref, order)
+                value = two[...] + self.feed(low, w_of, d_of, hidden)
+                three[...] = value
+                final[...] = normed(value, gain[6:7] * D ** (-0.5))
+
         return self.call(
             kernel,
             3,
-            [(x, None), (encoded, None), (self.gain, None)]
-            + [(self.weights, self.weight_spec(*at)) for at in ((3, 0), (4, 1), (5, 2), (6, 2))],
+            [x, encoded, self.gain] + self.weight_specs(1, 0, 1, 3),
             [
-                (shape, BF, self.kept_spec(shape, 0)),
-                ((rows, D), F32, None),
-                (shape_q, BF, self.kept_spec(shape_q, 1)),
-                (shape_k, BF, self.kept_spec(shape_k, 1)),
-                ((rows, D), F32, None),
-                (shape, BF, self.kept_spec(shape, 2)),
-                ((rows, D), F32, None),
-                ((rows, D), BF, None),
+                ((heads, rows, width), BF),
+                ((rows, D), F32),
+                ((heads, rows, 2 * unit), BF),
+                ((heads, source, 2 * unit), BF),
+                ((rows, D), F32),
+                ((heads, rows, width), BF),
+                ((rows, D), F32),
+                ((rows, D), BF),
             ],
-            [((rows, D), BF), ((rows, D), F32)],
+            [],
+            16,
         )
 
-    def put(self, out_ref, order, j, start, value):
-        low = value.astype(BF)
-        for place in range(self.dp):
-            out_ref[order[place], j, :, start : start + value.shape[1]] = low[
-                place * self.deep : (place + 1) * self.deep
-            ]
-
-    def feed_step(self, order, j, u_ref, d_ref, hidden, out, at, low, up_t, in_t, back):
+    def feed_back(self, grad, inputs, gain_row, w_of, d_of, hidden, put):
         width = self.width
-        up, down = weights_of(u_ref, order, 0, width), weights_of(d_ref, order, 0, width)
-        grad_pre = jnp.where(hidden > 0, dot(low[...], down), 0.0).astype(BF)
-        self.put(out, order, j, at, dot(in_t[...], grad_pre))
-        self.put(out, order, j, at + width, dot(up_t[...], hidden))
-        back[...] += dot_nt(grad_pre, up)
+        low = grad.astype(BF)
+        up_t, in_t = low.T, normed(inputs, gain_row).T
+        back = None
+        for j in range(self.heads):
+            up, down, grown = w_of(j), d_of(j), hidden[j]
+            grad_pre = jnp.where(grown > 0, dot(low, down), 0.0).astype(BF)
+            put(j, 0, dot(in_t, grad_pre))
+            put(j, width, dot(up_t, grown))
+            part = dot_nt(grad_pre, up)
+            back = part if back is None else back + part
+        value, slope = norm_back(inputs, gain_row, back)
+        return grad + value, slope
+
+    def self_back(self, grad, inputs, gain_row, w_of, kept, mask_of, put):
+        unit = self.unit
+        low = grad.astype(BF)
+        up_t, in_t = low.T, normed(inputs, gain_row).T
+        back = None
+        for j in range(self.heads):
+            w = w_of(j)
+            grad_mixed = dot(low, w[:, 3 * unit :]).astype(BF)
+            slopes = attend_heads_back(
+                kept[j, :, :unit],
+                kept[j, :, unit : 2 * unit],
+                kept[j, :, 2 * unit : 3 * unit],
+                grad_mixed,
+                self.each,
+                mask_of,
+            )
+            three = jnp.concatenate(slopes, 1)
+            put(j, 0, dot(in_t, three))
+            put(j, 3 * unit, dot(up_t, kept[j, :, 3 * unit :]))
+            part = dot_nt(three, w[:, : 3 * unit])
+            back = part if back is None else back + part
+        value, slope = norm_back(inputs, gain_row, back)
+        return grad + value, slope
+
+    def absolute_put(self, out_ref, order, head, base):
+        def put(j, start, value):
+            low = value.astype(BF)
+            target = lax.rem(head[0] + j, self.heads)
+            for place in range(self.dp):
+                out_ref[order[place], target, :, base + start : base + start + value.shape[1]] = low[
+                    place * self.deep : (place + 1) * self.deep
+                ]
+
+        return put
+
+    def relative_put(self, keep_refs, send_ref):
+        quarter = self.dp // 8
+
+        def put(j, start, value):
+            stop = start + value.shape[1]
+            for place in range(self.dp):
+                piece = value[place * self.deep : (place + 1) * self.deep]
+                if place < 4 * quarter:
+                    keep_refs[place // quarter][place % quarter, j, :, start:stop] = piece
+                else:
+                    send_ref[place - 4 * quarter, j, :, start:stop] = piece.astype(BF)
+
+        return put
+
+    def relative_outs(self, columns):
+        quarter = self.dp // 8
+        shape = (self.heads, self.deep, columns)
+        return [((quarter,) + shape, F32)] * 4 + [((4 * quarter,) + shape, BF)]
+
+    def flat(self, keeps_send):
+        return [array.reshape(-1, array.shape[-1]) for array in keeps_send]
 
     def decoder_back(self, grad_final, x, encoded, kept_all):
         heads, each, unit, width = self.heads, self.each, self.unit, self.width
@@ -857,210 +997,142 @@
 
         def kernel(order, head, lens, *refs):
             g_ref, x_ref, enc_ref, gain, one, two, three, kept, kept_q, kept_k, hid = refs[:11]
-            s_ref, c_ref, u_ref, d_ref = refs[11:15]
-            out, gains_out, grad_enc, grad_x = refs[15:19]
-            grad, low, up_t, in_t, enc_t, back = refs[19:]
+            w_ref, d_ref, out, gains_out, grad_enc, grad_x, grad_ref = refs[11:]
             step = pl.program_id(0)
-
-            def enter(value, inputs, gain_row):
-                grad[...] = value
-                low[...] = value.astype(BF)
-                up_t[...] = low[...].T
-                in_t[...] = normed(inputs, gain_row).T
-                back[...] = jnp.zeros_like(back)
+            w_of = functools.partial(weights_of, w_ref, order)
 
             @pl.when(step == 0)
             def _():
                 gains_out[...] = jnp.zeros_like(gains_out)
                 value, slope = norm_back(three[...], gain[6:7] * D ** (-0.5), g_ref[...])
                 gains_out[6:7] = slope * D ** (-0.5)
-                enter(value, two[...], gain[5:6])
-
-            @pl.when(step < heads)
+                d_of = functools.partial(weights_of, d_ref, order)
+                grad_ref[...], gains_out[5:6] = self.feed_back(
+                    value,
+                    two[...],
+                    gain[5:6],
+                    w_of,
+                    d_of,
+                    hid,
+                    self.absolute_put(out, order, head, 2 * width),
+                )
+
+            @pl.when(step == 1)
             def _():
-                self.feed_step(
-                    order, step, u_ref, d_ref, hid[0], out, 2 * width, low, up_t, in_t, back
+                put = self.absolute_put(out, order, head, width)
+                low = grad_ref[...].astype(BF)
+                up_t, in_t = low.T, normed(one[...], gain[4:5]).T
+                enc_t = enc_ref[...].T
+                back, back_enc = None, None
+                for j in range(heads):
+                    w = w_of(j)
+                    grad_mixed = dot(low, w[:, 3 * unit :]).astype(BF)
+                    dq, dk, dv = attend_heads_back(
+                        kept_q[j, :, :unit],
+                        kept_k[j, :, :unit],
+                        kept_k[j, :, unit:],
+                        grad_mixed,
+                        each,
+                        lambda n: key_mask(lens[n], source // each),
+                    )
+                    both = jnp.concatenate([dk, dv], 1)
+                    put(j, 0, dot(in_t, dq))
+                    put(j, unit, dot(enc_t, both))
+                    put(j, 3 * unit, dot(up_t, kept_q[j, :, unit:]))
+                    part, part_enc = dot_nt(dq, w[:, :unit]), dot_nt(both, w[:, unit : 3 * unit])
+                    back = part if back is None else back + part
+                    back_enc = part_enc if back_enc is None else back_enc + part_enc
+                grad_enc[...] = back_enc
+                value, gains_out[4:5] = norm_back(one[...], gain[4:5], back)
+                grad_ref[...] += value
+
+            @pl.when(step == 2)
+            def _():
+                value, gains_out[3:4] = self.self_back(
+                    grad_ref[...],
+                    x_ref[...],
+                    gain[3:4],
+                    w_of,
+                    kept,
+                    lambda n: causal_mask(rows // each),
+                    self.absolute_put(out, order, head, 0),
                 )
-
-            @pl.when(step == heads)
-            def _():
-                value, slope = norm_back(two[...], gain[5:6], back[...])
-                gains_out[5:6] = slope
-                enter(grad[...] + value, one[...], gain[4:5])
-                enc_t[...] = enc_ref[...].T
-                grad_enc[...] = jnp.zeros_like(grad_enc)
-
-            @pl.when((step >= heads) & (step < 2 * heads))
-            def _():
-                j = step - heads
-                w = weights_of(c_ref, order, 0, width)
-                grad_mixed = dot(low[...], w[:, 3 * unit :]).astype(BF)
-                query, mixed = kept_q[0, :, :unit], kept_q[0, :, unit:]
-                dq, dk, dv = attend_heads_back(
-                    query,
-                    kept_k[0, :, :unit],
-                    kept_k[0, :, unit:],
-                    grad_mixed,
-                    each,
-                    lambda n: key_mask(lens[n], source // each),
-                )
-                both = jnp.concatenate([dk, dv], 1)
-                self.put(out, order, j, width, dot(in_t[...], dq))
-                self.put(out, order, j, width + unit, dot(enc_t[...], both))
-                self.put(out, order, j, width + 3 * unit, dot(up_t[...], mixed))
-                back[...] += dot_nt(dq, w[:, :unit])
-                grad_enc[...] += dot_nt(both, w[:, unit : 3 * unit])
-
-            @pl.when(step == 2 * heads)
-            def _():
-                value, slope = norm_back(one[...], gain[4:5], back[...])
-                gains_out[4:5] = slope
-                enter(grad[...] + value, x_ref[...], gain[3:4])
-
-            @pl.when(step >= 2 * heads)
-            def _():
-                self.self_step(
-                    order, step - 2 * heads, s_ref, kept, out, 0, low, up_t, in_t, back,
-                    lambda n: causal_mask(rows // each),
-                )
-
-            @pl.when(step == 3 * heads - 1)
-            def _():
-                value, slope = norm_back(x_ref[...], gain[3:4], back[...])
-                gains_out[3:4] = slope
-                grad_x[...] = (grad[...] + value).astype(BF)
+                grad_x[...] = value.astype(BF)
 
         return self.call(
             kernel,
             3,
+            [grad_final, x, encoded, self.gain, one, two, three, kept, kept_q, kept_k, hidden]
+            + self.weight_specs(1, 2, -1, 3),
             [
-                (grad_final, None),
-                (x, None),
-                (encoded, None),
-                (self.gain, None),
-                (one, None),
-                (two, None),
-                (three, None),
-                (kept, self.kept_spec(kept.shape, 2)),
-                (kept_q, self.kept_spec(kept_q.shape, 1)),
-                (kept_k, self.kept_spec(kept_k.shape, 1)),
-                (hidden, self.kept_spec(hidden.shape, 0)),
-            ]
-            + [(self.weights, self.weight_spec(*at)) for at in ((3, 2), (4, 1), (5, 0), (6, 0))],
-            [
-                ((self.dp, heads, self.deep, 4 * width), BF, None),
-                ((8, D), F32, None),
-                ((source, D), F32, None),
-                ((rows, D), BF, None),
+                ((self.dp, heads, self.deep, 4 * width), BF),
+                ((8, D), F32),
+                ((source, D), F32),
+                ((rows, D), BF),
             ],
-            [
-                ((rows, D), F32),
-                ((rows, D), BF),
-                ((D, rows), BF),
-                ((D, rows), BF),
-                ((D, source), BF),
-                ((rows, D), F32),
-            ],
+            [((rows, D), F32)],
+            24,
         )
 
-    def self_step(self, order, j, a_ref, kept, out, at, low, up_t, in_t, back, mask_of):
-        unit, width = self.unit, self.width
-        w = weights_of(a_ref, order, 0, width)
-        grad_mixed = dot(low[...], w[:, 3 * unit :]).astype(BF)
-        slopes = attend_heads_back(
-            kept[0, :, :unit],
-            kept[0, :, unit : 2 * unit],
-            kept[0, :, 2 * unit : 3 * unit],
-            grad_mixed,
-            self.each,
-            mask_of,
+    def encoder_feed_back(self, grad_encoded, gain_grads, kept_all):
+        _, mid, hidden, last = kept_all
+
+        def kernel(order, head, lens, g_ref, more_ref, gain, mid, last, hid, w_ref, d_ref, *refs):
+            *outs, grad, gains = refs
+            gains[...] = more_ref[...]
+            value, gains[2:3] = norm_back(last[...], gain[2:3], g_ref[...])
+            grad[...], gains[1:2] = self.feed_back(
+                value,
+                mid[...],
+                gain[1:2],
+                functools.partial(weights_of, w_ref, order),
+                functools.partial(weights_of, d_ref, order),
+                hid,
+                self.relative_put(outs[:4], outs[4]),
+            )
+
+        *outs, grad, gains = self.call(
+            kernel,
+            1,
+            [grad_encoded, gain_grads, self.gain, mid, last, hidden] + self.weight_specs(0, 1, 0, 2),
+            self.relative_outs(2 * self.width) + [(mid.shape, F32), ((8, D), F32)],
+            [],
+            13,
         )
-        three = jnp.concatenate(slopes, 1)
-        self.put(out, order, j, at, dot(in_t[...], three))
-        self.put(out, order, j, at + 3 * unit, dot(up_t[...], kept[0, :, 3 * unit :]))
-        back[...] += dot_nt(three, w[:, : 3 * unit])
-
-    def encoder_back(self, grad_encoded, gain_grads, x, kept_all, lanes):
-        heads, each, width = self.heads, self.each, self.width
-        kept, mid, hidden, last = kept_all
+        return self.flat(outs), grad, gains
+
+    def encoder_self_back(self, grad_mid, gain_grads, x, kept, lanes):
+        width = self.width
         rows = x.shape[0]
 
-        def kernel(order, head, lens, *refs):
-            g_ref, more_ref, x_ref, gain, mid, last, kept, hid, a_ref, u_ref, d_ref = refs[:11]
-            out, grad_x = refs[11:13]
-            grad, low, up_t, in_t, back, gains = refs[13:]
-            step = pl.program_id(0)
-
-            def enter(value, inputs, gain_row):
-                grad[...] = value
-                low[...] = value.astype(BF)
-                up_t[...] = low[...].T
-                in_t[...] = normed(inputs, gain_row).T
-                back[...] = jnp.zeros_like(back)
-
-            @pl.when(step == 0)
-            def _():
-                gains[...] = jnp.zeros_like(gains)
-                gains[0:8] = more_ref[...]
-                value, slope = norm_back(last[...], gain[2:3], g_ref[...])
-                gains[2:3] = slope
-                enter(value, mid[...], gain[1:2])
-
-            @pl.when(step < heads)
-            def _():
-                self.feed_step(
-                    order, step, u_ref, d_ref, hid[0], out, width, low, up_t, in_t, back
-                )
-
-            @pl.when(step == heads)
-            def _():
-                value, slope = norm_back(mid[...], gain[1:2], back[...])
-                gains[1:2] = slope
-                enter(grad[...] + value, x_ref[...], gain[0:1])
-
-            @pl.when(step >= heads)
-            def _():
-                self.self_step(
-                    order, step - heads, a_ref, kept, out, 0, low, up_t, in_t, back,
-                    lambda n: key_mask(lens[n], rows // each),
-                )
-
-            @pl.when(step == 2 * heads - 1)
-            def _():
-                value, slope = norm_back(x_ref[...], gain[0:1], back[...])
-                gains[0:1] = slope
-                grad_x[...] = (grad[...] + value).astype(BF)
-                turned = gains[...].T
-                for j in range(heads):
-                    self.put(out, order, j, 3 * width, turned)
-
-        return self.call(
+        def kernel(order, head, lens, g_ref, more_ref, x_ref, gain, kept, w_ref, *refs):
+            *outs, grad_x = refs
+            put = self.relative_put(outs[:4], outs[4])
+            value, slope = self.self_back(
+                g_ref[...],
+                x_ref[...],
+                gain[0:1],
+                functools.partial(weights_of, w_ref, order),
+                kept,
+                lambda n: key_mask(lens[n], rows // self.each),
+                put,
+            )
+            grad_x[...] = value.astype(BF)
+            gains = jnp.concatenate(
+                [slope, more_ref[1:8], jnp.zeros((lanes - 8, D), F32)], 0
+            ).T
+            for j in range(self.heads):
+                put(j, width, gains)
+
+        *outs, grad_x = self.call(
             kernel,
-            2,
-            [
-                (grad_encoded, None),
-                (gain_grads, None),
-                (x, None),
-                (self.gain, None),
-                (mid, None),
-                (last, None),
-                (kept, self.kept_spec(kept.shape, 1)),
-                (hidden, self.kept_spec(hidden.shape, 0)),
-            ]
-            + [(self.weights, self.weight_spec(*at)) for at in ((0, 1), (1, 0), (2, 0))],
-            [
-                ((self.dp, heads, self.deep, 3 * width + lanes), BF, None),
-                ((rows, D), BF, None),
-            ],
-            [
-                ((rows, D), F32),
-                ((rows, D), BF),
-                ((D, rows), BF),
-                ((D, rows), BF),
-                ((rows, D), F32),
-                ((lanes, D), F32),
-            ],
+            1,
+            [grad_mid, gain_grads, x, self.gain, kept] + self.weight_specs(0, 0, 0),
+            self.relative_outs(width + lanes) + [((rows, D), BF)],
+            [],
+            16,
         )
+        return self.flat(outs), grad_x
 
 
 def body(
@@ -1114,15 +1186,19 @@
     order = lax.axis_index("dp") ^ jnp.array(places, jnp.int32)
     flat_in = attn_in.reshape((9,) + attn_in.shape[2:])
     arrays = [flat_in, attn_out_t, ff_in, ff_out_t, gain_block]
-    plan = [(0, 0), (0, 1), (0, 2), (1, 0), (2, 0), (3, 0)]
-    plan += [(0, 3), (0, 4), (0, 5), (1, 1), (0, 6), (0, 7), (0, 8), (1, 2), (2, 1), (3, 1)]
-    packed = pack(arrays, plan + [(4, None)])
-    low, packed = tie(low, packed)
-    weights = lax.all_gather(packed, ("dp", "head"), axis=0)
-    weights = weights.reshape((dp, heads) + packed.shape)
+    enc_plan = [(0, 0), (0, 1), (0, 2), (1, 0), (2, 0), (3, 0), (4, None)]
+    dec_plan = [(0, 3), (0, 4), (0, 5), (1, 1), (0, 6), (0, 7), (0, 8), (1, 2), (2, 1), (3, 1)]
+    enc_packed = pack(arrays, enc_plan)
+    dec_packed = pack(arrays, dec_plan)
+    low, enc_packed, dec_packed = tie(low, enc_packed, dec_packed)
     table = GatherDp(low, dp)
+    enc_came = gather_head(enc_packed, heads)
+    if table.near:
+        *table.near, enc_came[0] = tie(*table.near, *enc_came)[:3]
+    enc_weights = lax.all_gather(jnp.stack(enc_came), "dp", axis=0)
     table.go_far()
     table_parts = table.parts()
+    dec_came = gather_head(after(dec_packed, *enc_came[1:], *table.far), heads)
 
     def fill(array):
         return jnp.pad(array, ((0, padded - batch_size),) + ((0, 0),) * (array.ndim - 1))
@@ -1130,23 +1206,26 @@
     dec_ids = jnp.concatenate([jnp.zeros((batch_size, 1), jnp.int32), target_ids[:, :-1]], 1)
     enc_ids = jnp.roll(fill(source_ids).reshape(heads, -1), -head_pos, 0) - vocab_start
     dec_ids = jnp.roll(fill(dec_ids).reshape(heads, -1), -head_pos, 0) - vocab_start
-    enc_rows_count = heads * each * source_len
-    looked, table_rows = lookup(
-        jnp.concatenate([enc_ids.reshape(-1), dec_ids.reshape(-1)]), table_parts
-    )
-    enc_looked = looked[:enc_rows_count].reshape(heads, -1, D)
-    dec_looked = looked[enc_rows_count:]
-    came = [enc_looked[0]] + [head_shift(enc_looked[j], j, heads) for j in range(1, heads)]
-    gain = jnp.take(weights[:, 0, :, sum(widths[0]) + sum(widths[1]) :], order, axis=0)
+    far_looked, table_rows = lookup(enc_ids[1:].reshape(-1), table_parts)
+    own_ids = jnp.concatenate([enc_ids[0], dec_ids.reshape(-1)])
+    own_looked = pick(own_ids, table_rows, [far_looked])
+    dec_came[0] = after(dec_came[0], far_looked)
+    dec_weights = lax.all_gather(jnp.stack(dec_came), "dp", axis=0)
+    mine = each * source_len
+    came = [own_looked[:mine]]
+    for j in range(1, heads):
+        came.append(head_shift(far_looked[(j - 1) * mine : j * mine], j, heads))
+    dec_looked = own_looked[mine:]
+    gain = jnp.take(enc_weights[:, 0, :, sum(widths[0]) :], order, axis=0)
     gain = gain[..., :8].astype(F32).reshape(D, 8).T
     real_count = jnp.maximum(jnp.sum(gain[gain_rows].reshape(dp, -1)[:, 0]), 1.0)
     my_lens = lax.dynamic_slice_in_dim(fill(source_lens), head_pos * each, each)
-    layers = Layers(order, head_pos, my_lens, weights, gain, each)
+    layers = Layers(order, head_pos, my_lens, enc_weights, dec_weights, gain, each)
     enc_embed = functools.reduce(jnp.add, came).astype(F32)
+    looked = after(dec_looked, enc_embed).reshape(heads, -1, D)
     *kept_enc, encoded = layers.encoder(enc_embed)
-    looked, encoded = tie(dec_looked, encoded)
-    looked = looked.reshape(heads, -1, D)
     dec_came = [looked[0]] + [head_shift(looked[j], j, heads) for j in range(1, heads)]
+    dec_came[0] = after(dec_came[0], encoded)
     dec_embed = functools.reduce(jnp.add, dec_came).astype(F32)
     *kept_dec, my_final = layers.decoder(dec_embed, encoded)
 
@@ -1199,12 +1278,22 @@
         grad_final, dec_embed, encoded, kept_dec
     )
     dec_shard = lax.psum_scatter(dec_grads, "dp", scatter_dimension=0)
+    dec_done = dec_shard
+    dec_shard = lax.psum_scatter(dec_shard, "head", scatter_dimension=0)
     dec_rows = gather_head(dec_low, heads)
-    enc_grads, enc_low = layers.encoder_back(grad_encoded, gain_grads, enc_embed, kept_enc, lanes)
-    enc_low, *dec_rows = tie(enc_low, *dec_rows)
-
+    feed_group, grad_mid, gain_grads = layers.encoder_feed_back(grad_encoded, gain_grads, kept_enc)
+    grad_mid, *dec_rows = tie(grad_mid, *dec_rows)
+    enc_scatter = ScatterDp(dp)
+    enc_scatter.add(feed_group[:4], feed_group[4])
+    self_group, enc_low = layers.encoder_self_back(
+        grad_mid, gain_grads, enc_embed, kept_enc[0], lanes
+    )
+
+    enc_scatter.add(self_group[:4], self_group[4])
+    enc_scatter.far(None)
+    if enc_scatter.pieces:
+        enc_low, *enc_scatter.later = tie(enc_low, *enc_scatter.later)
     enc_rows = gather_head(enc_low, heads)
-    enc_shard = lax.psum_scatter(after(enc_grads, dec_shard), "dp", scatter_dimension=0)
     near_ids = jnp.concatenate([dec_ids.reshape(-1), enc_ids[0]])
     near_rows = jnp.concatenate(dec_rows + [enc_low], 0)
     columns = padded_to(vocab_local)
@@ -1215,11 +1304,20 @@
 
     far_ids = enc_ids[1:].reshape(-1)
     far_rows = jnp.concatenate(enc_rows[1:], 0)
-    dec_sums = send_heads(dec_shard)
-    *keeps, send = spread(far_ids, far_rows, columns, base=grad_table_t)
-    enc_sums = send_heads(enc_shard)
-    g_table, table_squares = ScatterDp(keeps, send, dp).run(vocab_local, dec_sums, enc_sums)
-    g_dec = functools.reduce(jnp.add, [value.astype(F32) for value in dec_sums])
+    enc_scatter.near(None)
+    waits = [dec_done, *enc_scatter.last]
+    *keeps, send = spread(far_ids, far_rows, columns, base=grad_table_t, waits=waits)
+    scatter = ScatterDp(dp)
+    scatter.add(keeps, send)
+    (enc_shard,) = enc_scatter.result(None)
+    scatter.far(4096, [enc_shard])
+    enc_sums = send_heads(enc_shard.astype(BF).reshape(heads, -1, enc_shard.shape[1]))
+    enc_sums[0] = enc_shard.reshape(heads, -1, enc_shard.shape[1])[0]
+    scatter.near(4096)
+    if scatter.last:
+        scatter.last[0], dec_shard, *enc_sums = tie(scatter.last[0], dec_shard, *enc_sums)
+    g_table, table_squares = scatter.result(4096, vocab_local)
+    g_dec = dec_shard.astype(F32)
     g_enc = functools.reduce(jnp.add, [value.astype(F32) for value in enc_sums])
 
     def squares(array, axes):
@@ -1237,6 +1335,7 @@
     )
     matrix_count = weight_squares.shape[0]
     gain_at = sum(widths[0])
+    unit, wide = widths[0][0], widths[0][4]
     g_gain = g_enc[:, gain_at : gain_at + gain_rows]
     grad_squares = (
         jnp.sum(g_dec * g_dec)
@@ -1252,10 +1351,10 @@
     total_loss = totals[0, matrix_count]
     clip = jnp.full((8, 128), jnp.minimum(1.0, CLIP_NORM / grad_norm))
     m_table, v_table, u_table, squares_table = column_call(
-        functools.partial(lamb_columns_kernel, vocab_local, 1024),
+        functools.partial(lamb_columns_kernel, vocab_local, 2048),
         [masters[0], moments[0], seconds[0], g_table, clip],
         [(embed_t.shape[0], F32)] * 3,
-        1024,
+        2048,
         sums=[(8, 128)],
     )
 
@@ -1268,7 +1367,8 @@
             out.append(out[-1] + columns)
         return out
 
-    at_enc, at_dec = starts(widths[0]), starts(widths[1])
+    at_enc = [2 * wide + k * unit for k in range(4)] + [0, wide]
+    at_dec = starts(widths[1])
     places = [
         [(0, at_enc[k]) for k in range(3)]
         + [(1, at_dec[k]) for k in range(3)]

time: 614 us -> 533 us (0.87)
  waiting for transfers between devices: 235 us -> 132 us
  starting transfers between devices: 66 us -> 79.7 us
  Pallas kernels: 220 us -> 232 us
    ppermute x33 -> x36, waiting for transfers between devices: 119 us -> 72.7 us  [head_shift(): lax.ppermute(x, 'head', [(i, (i + step) % heads) for i in range(heads)])]
    pallas_call x6 -> x10, Pallas kernels: 61 us -> 85.8 us  [the longest x2 37 us: spread(): pl.pallas_call(ordered(functools.partial(spread_kernel, tile), 2 + len(mo...]
    ppermute x22 -> x26, waiting for transfers between devices: 83.8 us -> 59.5 us  [dp_swap(): return lax.ppermute(x, 'dp', [(i, i ^ bit) for i in range(dp)])]
    reduce_scatter x1, waiting for transfers between devices: 21.4 us -> 0.01 us  [body(): dec_shard = lax.psum_scatter(dec_shard, 'head', scatter_dimension=0)]
    ppermute x33 -> x36, starting transfers between devices: 48.6 us -> 61.2 us  [head_shift(): lax.ppermute(x, 'head', [(i, (i + step) % heads) for i in range(heads)])]
    all_gather x1 -> x2, waiting for transfers between devices: 10.7 us -> 0.01 us  [the longest x1 0.01 us: body(): enc_weights = lax.all_gather(jnp.stack(enc_came), 'dp', axis=0)]
    pallas_call x1, Pallas kernels: 25.9 us -> 16.2 us  [lookup(): pl.pallas_call(functools.partial(lookup_kernel, vocab, tile), out_shape=[...]
    pallas_call x4 -> x5, Pallas kernels: 88.4 us -> 83.1 us  [call(): pl.pallas_call(kernel, out_shape=[jax.ShapeDtypeStruct(shape, dtype) for...]
  transfers between devices with their start and end apart: 58 -> 66, of which waited for: 37 -> 35; matrix products, arithmetic and copies ran while one was open for 4% -> 5% of each run, Pallas kernels for 16% -> 21%
where the time goes in v4:
time: 533 us; the launch traced here: 526 us
  Pallas kernels  232 us (44%)
  waiting for transfers between devices  132 us (25%)
  starting transfers between devices  79.7 us (15%)
  other arithmetic  35.2 us (7%)
  local copies, waits for them, and re-layouts  26.1 us (5%)
  between operations  20.5 us (4%)
    pallas_call x5, Pallas kernels, call(): pl.pallas_call(kernel, out_shape=[jax.ShapeDtypeStruct(shape, dtype) for...  83.1 us
    ppermute x36, waiting for transfers between devices, head_shift(): lax.ppermute(x, 'head', [(i, (i + step) % heads) for i in range(heads)])  72.7 us
    ppermute x36, starting transfers between devices, head_shift(): lax.ppermute(x, 'head', [(i, (i + step) % heads) for i in range(heads)])  61.2 us
    ppermute x26, waiting for transfers between devices, dp_swap(): return lax.ppermute(x, 'dp', [(i, i ^ bit) for i in range(dp)])  59.5 us
    pallas_call x2, Pallas kernels, spread(): pl.pallas_call(ordered(functools.partial(spread_kernel, tile), 2 + len(mo...  37 us
    pallas_call x4, Pallas kernels, column_call(): pl.pallas_call(ordered(kernel, len(inputs), waits), out_shape=out_shape,...  22.9 us
    pallas_call x1, Pallas kernels, logits_back(): pl.pallas_call(functools.partial(logits_back_kernel, vocab, tile), out_sh...  22.1 us
    ppermute x26, starting transfers between devices, dp_swap(): return lax.ppermute(x, 'dp', [(i, i ^ bit) for i in range(dp)])  18.4 us
  transfers between devices with their start and end apart: 66, of which 35 were waited for; matrix products, arithmetic and copies ran while one was open for 5% of the time, Pallas kernels for 21%

profile of v4, /device:TPU:0, one launch (start us, length us, event | category | flops | bytes accessed | tf_op | source)
XLA Modules:
  0.0 525.9 jit_solution(6325451053181610141)
XLA Ops:
  10.6 1.9 shard_map.393
  12.5 2.0 shard_map.392
  14.6 3.0 collective-permute-start
  19.2 3.6 collective-permute-start.2
  23.8 4.7 collective-permute-done.2
  28.5 11.8 %collective-permute-done.3 = bf16[64,1664]{1,0:T(8,128)(2,1)S(1)} collective-permute-done((bf16[64,1664]{1,0:T(8,128)(2,1)S(1)}, bf16[64,1664]{1,0:T(8,128)(2,1)S(1)}, u32[]{:S(2)}, u32[]{:S(2)}) %collective-permute-start.3) | collective-permute-done | bytes 213024 | tf_op jit(solution)/shard_map/ppermute | solution.py:33
  46.1 15.5 %collective-permute-done.5.refs_3_.refs_4_ = bf16[32,8032]{1,0:T(8,128)(2,1)} collective-permute-done((bf16[32,8032]{1,0:T(8,128)(2,1)S(1)}, bf16[32,8032]{1,0:T(8,128)(2,1)}, u32[]{:S(2)}, u32[]{:S(2)}) %collective-permute-start.5) | collective-permute-done | bytes 514080 | tf_op jit(solution)/shard_map/ppermute | solution.py:29
  61.6 2.4 collective-permute-done.6.refs_4_.refs_5_
  65.2 3.9 collective-permute-start.18
  70.0 16.2 %shard_map.394 = (bf16[1152,512]{1,0:T(8,128)(2,1)}, bf16[8064,512]{1,0:T(8,128)(2,1)}) custom-call(s32[1152,1]{1,0:T(8,128)} %bitcast.189, bf16[64,8032]{1,0:T(8,128)(2,1)} %copy-done.13, bf16[64,8032]{1,0:T(8,128)(2,1)} %copy-done.20, bf16[64,8032]{1,0:T(8,128)(2,1)} %copy-done.21, bf16[32,8032]{1,0:T(8,128)(2,1)} %collective-permute-done.5.refs_3_.refs_4_, ...), custom_call_target="tpu_custom_call" | custom-call | flops 29899999232 | bytes 96200000 | tf_op jit(solution)/shard_map/pallas_call | solution.py:163
  86.2 5.6 %collective-permute-done.19 = bf16[64,2048]{1,0:T(8,128)(2,1)S(1)} collective-permute-done((bf16[64,2048]{1,0:T(8,128)(2,1)S(1)}, bf16[64,2048]{1,0:T(8,128)(2,1)S(1)}, u32[]{:S(2)}, u32[]{:S(2)}) %collective-permute-start.19) | collective-permute-done | bytes 262176 | tf_op jit(solution)/shard_map/ppermute | solution.py:33
  97.6 2.0 collective-permute-start.13
  99.6 2.8 collective-permute-start.14
  102.4 12.2 %shard_map.395 = bf16[896,512]{1,0:T(8,128)(2,1)} custom-call(s32[896,1]{1,0:T(8,128)} %reshape.431.refs_0_, bf16[8064,512]{1,0:T(8,128)(2,1)} %get-tuple-element.119.refs_1_.table_ref.refs_0_, bf16[1152,512]{1,0:T(8,128)(2,1)} %get-tuple-element.120.refs_2_), custom_call_target="tpu_custom_call" | custom-call | flops 13799999488 | bytes 44400000 | tf_op jit(solution)/shard_map/pallas_call | solution.py:181
  114.6 11.6 %collective-permute-done.13 = bf16[384,512]{1,0:T(8,128)(2,1)S(1)} collective-permute-done((bf16[384,512]{1,0:T(8,128)(2,1)S(1)}, bf16[384,512]{1,0:T(8,128)(2,1)S(1)}, u32[]{:S(2)}, u32[]{:S(2)}) %collective-permute-start.13) | collective-permute-done | bytes 393248 | tf_op jit(solution)/shard_map/ppermute | solution.py:33
  126.2 2.0 fusion.4.x_ref
  128.2 8.4 %collective-permute-start.15 = (bf16[128,512]{1,0:T(8,128)(2,1)S(1)}, bf16[128,512]{1,0:T(8,128)(2,1)S(1)}, u32[]{:S(2)}, u32[]{:S(2)}) collective-permute-start(bf16[128,512]{1,0:T(8,128)(2,1)S(1)} %get-tuple-element.314), channel_id=1, source_target_pairs={{0,1},{1,2},{2,3},{3,0},{4,5},{5,6},{6,7},{7,4},{8,9},{9,10},{10,1... | collective-permute-start | bytes 393224 | tf_op jit(solution)/shard_map/ppermute | solution.py:33
  136.6 2.3 collective-permute-start.16
  141.5 14.1 %shard_map.396 = (bf16[4,384,512]{2,1,0:T(8,128)(2,1)}, f32[384,512]{1,0:T(8,128)}, bf16[4,384,512]{2,1,0:T(8,128)(2,1)}, f32[384,512]{1,0:T(8,128)}, bf16[384,512]{1,0:T(8,128)(2,1)}) custom-call(s32[8]{0:T(128)} %broadcast_xor_fusion.order, s32[1]{0:T(128)} %bitcast.14.head, s32[1]{0:T(128)} %dynamic_slice.19.lens, f32[384,512]{1,0:T(8,128)} %fusion.4.x_ref, ...), custom_call_target="tpu_custom_call" | custom-call | flops 16099999744 | bytes 51800000 | tf_op jit(solution)/shard_map/pallas_call | solution.py:782
  157.1 15.6 %shard_map.397 = (bf16[4,128,512]{2,1,0:T(8,128)(2,1)}, f32[128,512]{1,0:T(8,128)}, bf16[4,128,256]{2,1,0:T(8,128)(2,1)}, bf16[4,384,256]{2,1,0:T(8,128)(2,1)}, ...) custom-call(s32[8]{0:T(128)} %broadcast_xor_fusion.order, ...), custom_call_target="tpu_custom_call" | custom-call | flops 18400000000 | bytes 59200000 | tf_op jit(solution)/shard_map/pallas_call | solution.py:782
  173.7 2.0 collective-permute-start.21
  179.7 8.8 %collective-permute-done.22 = bf16[128,512]{0,1:T(8,128)(2,1)S(1)} collective-permute-done((bf16[128,512]{0,1:T(8,128)(2,1)S(1)}, bf16[128,512]{0,1:T(8,128)(2,1)S(1)}, u32[]{:S(2)}, u32[]{:S(2)}) %collective-permute-start.22) | collective-permute-done | bytes 131104 | tf_op jit(solution)/shard_map/ppermute | solution.py:33
  189.7 17.2 %shard_map.398 = f32[8,512]{1,0:T(8,128)} custom-call(bf16[512,512]{1,0:T(8,128)(2,1)} %dynamic-slice_bitcast_fusion.final_ref.refs_0_, s32[1,512]{1,0:T(1,128)} %and_select_fusion.label_ref, bf16[8032,512]{1,0:T(8,128)(2,1)} %bitcast.239, bf16[8064,512]{1,0:T(8,128)(2,1)} %get-tuple-element.119.refs_1_.table_ref.refs_0_), custom_call_target="tpu_custom_call" | custom-call | flops 19549999104 | bytes 62900000 | tf_op jit(solution)/shard_map/pallas_call | solution.py:501
  207.5 2.0 collective-permute-start.26
  216.5 22.1 %shard_map.399 = (bf16[8064,512]{1,0:T(8,128)(2,1)}, bf16[512,512]{1,0:T(8,128)(2,1)}) custom-call(bf16[512,512]{1,0:T(8,128)(2,1)} %dynamic-slice_bitcast_fusion.final_ref.refs_0_, s32[1,512]{1,0:T(1,128)} %and_select_fusion.label_ref, f32[8,512]{1,0:T(8,128)} %stack.71.scalar_ref, bf16[8032,512]{1,0:T(8,128)(2,1)} %bitcast.240, ...), custom_call_target="tpu_custom_call" | custom-call | flops 25300000768 | bytes 81400000 | tf_op jit(solution)/shard_map/pallas_call | solution.py:554
  240.6 2.0 collective-permute-start.28
  242.6 1.8 collective-permute-start.29
  244.4 4.0 collective-permute-done.27
  248.5 3.1 collective-permute-done.28
  252.4 23.9 %shard_map.400 = (bf16[8,4,64,2048]{3,2,1,0:T(8,128)(2,1)}, f32[8,512]{1,0:T(8,128)}, f32[384,512]{1,0:T(8,128)}, bf16[128,512]{1,0:T(8,128)(2,1)}) custom-call(s32[8]{0:T(128)} %broadcast_xor_fusion.order, s32[1]{0:T(128)} %bitcast.14.head, s32[1]{0:T(128)} %dynamic_slice.19.lens, f32[128,512]{1,0:T(8,128)} %fusion.6.refs_0_, ...), custom_call_target="tpu_custom_call" | custom-call | flops 27599998976 | bytes 88800000 | tf_op jit(solution)/shard_map/pallas_call | solution.py:782
  277.1 2.9 collective-permute-start.30
  281.1 13.7 %shard_map.401 = (f32[1,4,64,1024]{3,2,1,0:T(8,128)}, f32[1,4,64,1024]{3,2,1,0:T(8,128)}, f32[1,4,64,1024]{3,2,1,0:T(8,128)}, f32[1,4,64,1024]{3,2,1,0:T(8,128)}...) custom-call(s32[8]{0:T(128)} %broadcast_xor_fusion.order, s32[1]{0:T(128)} %bitcast.14.head, ...), custom_call_target="tpu_custom_call" | custom-call | flops 14949999616 | bytes 48100000 | tf_op jit(solution)/shard_map/pallas_call | solution.py:782
  294.9 15.9 %shard_map.402 = (f32[1,4,64,640]{3,2,1,0:T(8,128)}, f32[1,4,64,640]{3,2,1,0:T(8,128)}, f32[1,4,64,640]{3,2,1,0:T(8,128)}, f32[1,4,64,640]{3,2,1,0:T(8,128)}, bf...) custom-call(s32[8]{0:T(128)} %broadcast_xor_fusion.order, s32[1]{0:T(128)} %bitcast.14.head, ...), custom_call_target="tpu_custom_call" | custom-call | flops 18400000000 | bytes 59200000 | tf_op jit(solution)/shard_map/pallas_call | solution.py:782
  312.2 1.9 collective-permute-done.34.refs_7_.refs_3_
  315.9 5.9 %shard_map.403 = (bf16[128,1664]{1,0:T(8,128)(2,1)}, bf16[128,1664]{1,0:T(8,128)(2,1)}, f32[256,1664]{1,0:T(8,128)}, f32[256,1664]{1,0:T(8,128)}) custom-call(f32[256,1024]{1,0:T(8,128)} %bitcast.254, f32[256,1024]{1,0:T(8,128)} %bitcast.255, f32[256,1024]{1,0:T(8,128)} %bitcast.256, bf16[1024,1024]{1,0:T(8,128)(2,1)} %copy-done.36, f32[256,640]{1,0:T(8,128)} %bitcast.258, ...), custom_call_target="tpu_custom_call" | custom-call | flops 5750000128 | bytes 18500000 | tf_op jit(solution)/shard_map/pallas_call | solution.py:415
  322.4 4.1 collective-permute-start.35
  327.1 7.0 %collective-permute-done.38.got_a = bf16[128,1664]{1,0:T(8,128)(2,1)S(1)} collective-permute-done((bf16[128,1664]{1,0:T(8,128)(2,1)}, bf16[128,1664]{1,0:T(8,128)(2,1)S(1)}, u32[]{:S(2)}, u32[]{:S(2)}) %collective-permute-start.38) | collective-permute-done | bytes 426016 | tf_op jit(solution)/shard_map/ppermute | solution.py:29
  335.6 3.5 shard_map.405
  340.9 18.6 %shard_map.404.refs_2_ = f32[512,8064]{1,0:T(8,128)} custom-call(s32[896,1]{1,0:T(8,128)} %reshape.432.ids_ref, bf16[896,512]{1,0:T(8,128)(2,1)} %copy-done.24, bf16[512,512]{1,0:T(8,128)(2,1)} %dynamic-slice_bitcast_fusion.final_ref.refs_0_, bf16[8064,512]{1,0:T(8,128)(2,1)} %get-tuple-element.162.refs_1_), custom_call_target="tpu_custom_call" | custom-call | flops 20700000256 | bytes 66600000 | tf_op jit(solution)/shard_map/pallas_call | solution.py:249
  362.1 1.9 collective-permute-done.40.refs_4_
  365.2 18.3 %shard_map.406 = (f32[64,8064]{1,0:T(8,128)}, f32[64,8064]{1,0:T(8,128)}, f32[64,8064]{1,0:T(8,128)}, f32[64,8064]{1,0:T(8,128)}, bf16[256,8064]{1,0:T(8,128)(2,1)}) custom-call(s32[1152,1]{1,0:T(8,128)} %bitcast.190, bf16[1152,512]{1,0:T(8,128)(2,1)} %pad_maximum_fusion.refs_1_, f32[512,8064]{1,0:T(8,128)} %shard_map.404.refs_2_, ...), custom_call_target="tpu_custom_call" | custom-call | flops 20700000256 | bytes 66600000 | tf_op jit(solution)/shard_map/pallas_call | solution.py:249
  383.5 4.4 shard_map.407.refs_4_
  387.9 2.8 collective-permute-done.42.refs_3_.refs_1_
  390.8 2.0 copy-done.35
  392.7 6.5 %shard_map.408 = (bf16[32,8064]{1,0:T(8,128)(2,1)}, bf16[32,8064]{1,0:T(8,128)(2,1)}, f32[64,8064]{1,0:T(8,128)}, f32[64,8064]{1,0:T(8,128)}) custom-call(f32[64,8064]{1,0:T(8,128)} %get-tuple-element.170.refs_0_, f32[64,8064]{1,0:T(8,128)} %get-tuple-element.171.refs_1_, f32[64,8064]{1,0:T(8,128)} %get-tuple-element.172.refs_2_, ...), custom_call_target="tpu_custom_call" | custom-call | flops 5750000128 | bytes 18500000 | tf_op jit(solution)/shard_map/pallas_call | solution.py:268
  402.6 10.7 %collective-permute-done.43.got_a = bf16[32,8064]{1,0:T(8,128)(2,1)S(1)} collective-permute-done((bf16[32,8064]{1,0:T(8,128)(2,1)}, bf16[32,8064]{1,0:T(8,128)(2,1)S(1)}, u32[]{:S(2)}, u32[]{:S(2)}) %collective-permute-start.43) | collective-permute-done | bytes 516128 | tf_op jit(solution)/shard_map/ppermute | solution.py:29
  415.3 3.7 shard_map.409
  419.9 2.5 collective-permute-start.46
  422.4 1.8 collective-permute-start.47
  427.5 6.2 %collective-permute-done.46 = bf16[64,1664]{1,0:T(8,128)(2,1)S(1)} collective-permute-done((bf16[64,1664]{1,0:T(8,128)(2,1)S(1)}, bf16[64,1664]{1,0:T(8,128)(2,1)S(1)}, u32[]{:S(2)}, u32[]{:S(2)}) %collective-permute-start.46) | collective-permute-done | bytes 213024 | tf_op jit(solution)/shard_map/ppermute | solution.py:33
  433.7 7.8 %collective-permute-done.47 = bf16[64,1664]{1,0:T(8,128)(2,1)} collective-permute-done((bf16[64,1664]{1,0:T(8,128)(2,1)S(1)}, bf16[64,1664]{1,0:T(8,128)(2,1)}, u32[]{:S(2)}, u32[]{:S(2)}) %collective-permute-start.47) | collective-permute-done | bytes 213024 | tf_op jit(solution)/shard_map/ppermute | solution.py:33
  450.0 4.7 shard_map.410
  458.1 2.8 collective-permute-done.51
  461.5 3.1 collective-permute-done.52
  464.6 3.4 collective-permute-start.53
  476.3 8.0 %shard_map.411 = (f32[64,8032]{1,0:T(8,128)}, f32[64,8032]{1,0:T(8,128)}, f32[64,8032]{1,0:T(8,128)}, f32[8,128]{1,0:T(8,128)}) custom-call(f32[64,8032]{1,0:T(8,128)} %bitcast.177, f32[64,8032]{1,0:T(8,128)} %bitcast.242, f32[64,8032]{1,0:T(8,128)} %bitcast.243, f32[64,8032]{1,0:T(8,128)} %get-tuple-element.190.g, f32[8,128]{1,0:T(8,128)} %broadcast_in_dim.29.clip.clip_ref), custom_call_target="tpu_custom_call" | custom-call | flops 5750000128 | bytes 18500000 | tf_op jit(solution)/shard_map/pallas_call | solution.py:268
  484.4 3.8 shard_map.412
  492.4 2.3 collective-permute-done.57
  496.2 2.3 collective-permute-done.58
  498.6 3.2 collective-permute-start.60
  508.0 1.8 subtract_bitcast_fusion.1
  509.8 1.8 multiply_subtract_fusion.1
  513.1 1.8 multiply_subtract_fusion
  514.9 3.1 subtract_bitcast_fusion
  (310 shorter events, 92.9 us)
Async XLA Ops:
  7.2 132.0 %all-gather.5.cloned.1.call-start = ((), (), s32[]{:S(2)}) async-start(), calls=%async_computation.4 | async-start | bytes 7667712 | tf_op jit(solution)/shard_map/all_gather | solution.py:1198
  14.6 25.8 %collective-permute-start = (bf16[64,8032]{1,0:T(8,128)(2,1)S(1)}, bf16[64,8032]{1,0:T(8,128)(2,1)S(1)}, u32[]{:S(2)}, u32[]{:S(2)}) collective-permute-start(bf16[64,8032]{1,0:T(8,128)(2,1)S(1)} %bitcast_convert_fusion.1.refs_0_.refs_1_), channel_id=1, source_target_pairs={{0,16},{4,20},{8,24},{12,28},{16,0},{20,4},{24,8},{28,12},{1,17},{... | collective-permute-start | bytes 3084296 | tf_op jit(solution)/shard_map/ppermute | solution.py:29
  17.7 24.3 %collective-permute-start.1 = (bf16[64,8032]{1,0:T(8,128)(2,1)S(1)}, bf16[64,8032]{1,0:T(8,128)(2,1)S(1)}, u32[]{:S(2)}, u32[]{:S(2)}) collective-permute-start(bf16[64,8032]{1,0:T(8,128)(2,1)S(1)} %bitcast_convert_fusion.1.refs_0_.refs_1_), channel_id=1, source_target_pairs={{0,8},{4,12},{8,0},{12,4},{16,24},{20,28},{24,16},{28,20},{1,9},{5... | collective-permute-start | bytes 3084296 | tf_op jit(solution)/shard_map/ppermute | solution.py:29
  19.2 9.4 %collective-permute-start.2 = (bf16[64,1664]{1,0:T(8,128)(2,1)S(1)}, bf16[64,1664]{1,0:T(8,128)(2,1)S(1)}, u32[]{:S(2)}, u32[]{:S(2)}) collective-permute-start(bf16[64,1664]{1,0:T(8,128)(2,1)S(1)} %copy-done.22), channel_id=1, source_target_pairs={{0,3},{1,0},{2,1},{3,2},{4,7},{5,4},{6,5},{7,6},{8,11},{9,8},{10,9... | collective-permute-start | bytes 638984 | tf_op jit(solution)/shard_map/ppermute | solution.py:33
  22.8 17.5 %collective-permute-start.3 = (bf16[64,1664]{1,0:T(8,128)(2,1)S(1)}, bf16[64,1664]{1,0:T(8,128)(2,1)S(1)}, u32[]{:S(2)}, u32[]{:S(2)}) collective-permute-start(bf16[64,1664]{1,0:T(8,128)(2,1)S(1)} %copy-done.22), channel_id=1, source_target_pairs={{0,2},{1,3},{2,0},{3,1},{4,6},{5,7},{6,4},{7,5},{8,10},{9,11},{10,... | collective-permute-start | bytes 638984 | tf_op jit(solution)/shard_map/ppermute | solution.py:33
  22.8 17.5 %collective-permute-start.4 = (bf16[64,1664]{1,0:T(8,128)(2,1)S(1)}, bf16[64,1664]{1,0:T(8,128)(2,1)S(1)}, u32[]{:S(2)}, u32[]{:S(2)}) collective-permute-start(bf16[64,1664]{1,0:T(8,128)(2,1)S(1)} %copy-done.22), channel_id=1, source_target_pairs={{0,1},{1,2},{2,3},{3,0},{4,5},{5,6},{6,7},{7,4},{8,9},{9,10},{10,1... | collective-permute-start | bytes 638984 | tf_op jit(solution)/shard_map/ppermute | solution.py:33
  43.1 114.0 %all-gather.7.cloned.1.call-start = ((), (), s32[]{:S(2)}) async-start(), calls=%async_computation.5 | async-start | bytes 9437184 | tf_op jit(solution)/shard_map/all_gather | solution.py:1213
  43.2 22.0 %collective-permute-start.7 = (bf16[64,8032]{1,0:T(8,128)(2,1)S(1)}, bf16[64,8032]{1,0:T(8,128)(2,1)}, u32[]{:S(2)}, u32[]{:S(2)}) collective-permute-start(bf16[64,8032]{1,0:T(8,128)(2,1)S(1)} %bitcast_convert_fusion.1.refs_0_.refs_1_), channel_id=1, source_target_pairs={{0,4},{4,0},{8,12},{12,8},{16,20},{20,16},{24,28},{28,24},{1,5},{5... | collective-permute-start | bytes 3084296 | tf_op jit(solution)/shard_map/ppermute | solution.py:29
  43.3 18.2 %collective-permute-start.5 = (bf16[32,8032]{1,0:T(8,128)(2,1)S(1)}, bf16[32,8032]{1,0:T(8,128)(2,1)}, u32[]{:S(2)}, u32[]{:S(2)}) collective-permute-start(bf16[32,8032]{1,0:T(8,128)(2,1)S(1)} %slice.165), channel_id=1, source_target_pairs={{0,8},{4,12},{8,0},{12,4},{16,24},{20,28},{24,16},{28,20},{1,9},{5... | collective-permute-start | bytes 1542152 | tf_op jit(solution)/shard_map/ppermute | solution.py:29
  44.9 19.1 %collective-permute-start.6 = (bf16[32,8032]{1,0:T(8,128)(2,1)S(1)}, bf16[32,8032]{1,0:T(8,128)(2,1)}, u32[]{:S(2)}, u32[]{:S(2)}) collective-permute-start(bf16[32,8032]{1,0:T(8,128)(2,1)S(1)} %slice.166), channel_id=1, source_target_pairs={{0,16},{4,20},{8,24},{12,28},{16,0},{20,4},{24,8},{28,12},{1,17},{... | collective-permute-start | bytes 1542152 | tf_op jit(solution)/shard_map/ppermute | solution.py:29
  45.6 24.4 %collective-permute-start.8 = (bf16[64,8032]{1,0:T(8,128)(2,1)S(1)}, bf16[64,8032]{1,0:T(8,128)(2,1)}, u32[]{:S(2)}, u32[]{:S(2)}) collective-permute-start(bf16[64,8032]{1,0:T(8,128)(2,1)S(1)} %collective-permute-done.refs_1_.refs_2_), channel_id=1, source_target_pairs={{0,4},{4,0},{8,12},{12,8},{16,20},{20,16},{24,28},{28,24},{1,5},{5... | collective-permute-start | bytes 3084296 | tf_op jit(solution)/shard_map/ppermute | solution.py:29
  45.6 24.4 %collective-permute-start.9 = (bf16[64,8032]{1,0:T(8,128)(2,1)S(1)}, bf16[64,8032]{1,0:T(8,128)(2,1)}, u32[]{:S(2)}, u32[]{:S(2)}) collective-permute-start(bf16[64,8032]{1,0:T(8,128)(2,1)S(1)} %collective-permute-done.1.refs_2_.refs_3_), channel_id=1, source_target_pairs={{0,4},{4,0},{8,12},{12,8},{16,20},{20,16},{24,28},{28,24},{1,5},{5... | collective-permute-start | bytes 3084296 | tf_op jit(solution)/shard_map/ppermute | solution.py:29
  61.6 7.5 %collective-permute-start.10 = (bf16[32,8032]{1,0:T(8,128)(2,1)}, bf16[32,8032]{1,0:T(8,128)(2,1)}, u32[]{:S(2)}, u32[]{:S(2)}) collective-permute-start(bf16[32,8032]{1,0:T(8,128)(2,1)} %collective-permute-done.5.refs_3_.refs_4_), channel_id=1, source_target_pairs={{0,4},{4,0},{8,12},{12,8},{16,20},{20,16},{24,28},{28,24},{1,5},{5... | collective-permute-start | bytes 1542152 | tf_op jit(solution)/shard_map/ppermute | solution.py:29
  64.0 5.1 collective-permute-start.11
  65.2 21.1 %collective-permute-start.18 = (bf16[64,2048]{1,0:T(8,128)(2,1)S(1)}, bf16[64,2048]{1,0:T(8,128)(2,1)S(1)}, u32[]{:S(2)}, u32[]{:S(2)}) collective-permute-start(bf16[64,2048]{1,0:T(8,128)(2,1)S(1)} %copy-done.19), channel_id=1, source_target_pairs={{0,3},{1,0},{2,1},{3,2},{4,7},{5,4},{6,5},{7,6},{8,11},{9,8},{10,9... | collective-permute-start | bytes 786440 | tf_op jit(solution)/shard_map/ppermute | solution.py:33
  69.0 22.8 %collective-permute-start.19 = (bf16[64,2048]{1,0:T(8,128)(2,1)S(1)}, bf16[64,2048]{1,0:T(8,128)(2,1)S(1)}, u32[]{:S(2)}, u32[]{:S(2)}) collective-permute-start(bf16[64,2048]{1,0:T(8,128)(2,1)S(1)} %copy-done.19), channel_id=1, source_target_pairs={{0,2},{1,3},{2,0},{3,1},{4,6},{5,7},{6,4},{7,5},{8,10},{9,11},{10,... | collective-permute-start | bytes 786440 | tf_op jit(solution)/shard_map/ppermute | solution.py:33
  69.0 22.8 %collective-permute-start.20 = (bf16[64,2048]{1,0:T(8,128)(2,1)S(1)}, bf16[64,2048]{1,0:T(8,128)(2,1)S(1)}, u32[]{:S(2)}, u32[]{:S(2)}) collective-permute-start(bf16[64,2048]{1,0:T(8,128)(2,1)S(1)} %copy-done.19), channel_id=1, source_target_pairs={{0,1},{1,2},{2,3},{3,0},{4,5},{5,6},{6,7},{7,4},{8,9},{9,10},{10,1... | collective-permute-start | bytes 786440 | tf_op jit(solution)/shard_map/ppermute | solution.py:33
  93.0 271.1 %reduce-scatter.3.cloned.1.call-start = ((), (), s32[]{:S(2)}) async-start(), calls=%async_computation.2 | async-start | bytes 9437184 | tf_op jit(solution)/shard_map/reduce_scatter | solution.py:1280
  96.5 18.0 %collective-permute-start.12 = (bf16[384,512]{1,0:T(8,128)(2,1)S(1)}, bf16[384,512]{1,0:T(8,128)(2,1)S(1)}, u32[]{:S(2)}, u32[]{:S(2)}) collective-permute-start(bf16[384,512]{1,0:T(8,128)(2,1)S(1)} %get-tuple-element.305), channel_id=1, source_target_pairs={{0,1},{1,2},{2,3},{3,0},{4,5},{5,6},{6,7},{7,4},{8,9},{9,10},{10,1... | collective-permute-start | bytes 1179656 | tf_op jit(solution)/shard_map/ppermute | solution.py:33
  97.6 28.6 %collective-permute-start.13 = (bf16[384,512]{1,0:T(8,128)(2,1)S(1)}, bf16[384,512]{1,0:T(8,128)(2,1)S(1)}, u32[]{:S(2)}, u32[]{:S(2)}) collective-permute-start(bf16[384,512]{1,0:T(8,128)(2,1)S(1)} %get-tuple-element.307), channel_id=1, source_target_pairs={{0,2},{1,3},{2,0},{3,1},{4,6},{5,7},{6,4},{7,5},{8,10},{9,11},{10,... | collective-permute-start | bytes 1179656 | tf_op jit(solution)/shard_map/ppermute | solution.py:33
  99.6 26.6 %collective-permute-start.14 = (bf16[384,512]{1,0:T(8,128)(2,1)S(1)}, bf16[384,512]{1,0:T(8,128)(2,1)S(1)}, u32[]{:S(2)}, u32[]{:S(2)}) collective-permute-start(bf16[384,512]{1,0:T(8,128)(2,1)S(1)} %get-tuple-element.306), channel_id=1, source_target_pairs={{0,3},{1,0},{2,1},{3,2},{4,7},{5,4},{6,5},{7,6},{8,11},{9,8},{10,9... | collective-permute-start | bytes 1179656 | tf_op jit(solution)/shard_map/ppermute | solution.py:33
  128.2 28.2 %collective-permute-start.15 = (bf16[128,512]{1,0:T(8,128)(2,1)S(1)}, bf16[128,512]{1,0:T(8,128)(2,1)S(1)}, u32[]{:S(2)}, u32[]{:S(2)}) collective-permute-start(bf16[128,512]{1,0:T(8,128)(2,1)S(1)} %get-tuple-element.314), channel_id=1, source_target_pairs={{0,1},{1,2},{2,3},{3,0},{4,5},{5,6},{6,7},{7,4},{8,9},{9,10},{10,1... | collective-permute-start | bytes 393224 | tf_op jit(solution)/shard_map/ppermute | solution.py:33
  136.6 19.8 %collective-permute-start.16 = (bf16[128,512]{1,0:T(8,128)(2,1)S(1)}, bf16[128,512]{1,0:T(8,128)(2,1)S(1)}, u32[]{:S(2)}, u32[]{:S(2)}) collective-permute-start(bf16[128,512]{1,0:T(8,128)(2,1)S(1)} %get-tuple-element.316), channel_id=1, source_target_pairs={{0,2},{1,3},{2,0},{3,1},{4,6},{5,7},{6,4},{7,5},{8,10},{9,11},{10,... | collective-permute-start | bytes 393224 | tf_op jit(solution)/shard_map/ppermute | solution.py:33
  138.8 17.5 %collective-permute-start.17 = (bf16[128,512]{1,0:T(8,128)(2,1)S(1)}, bf16[128,512]{1,0:T(8,128)(2,1)S(1)}, u32[]{:S(2)}, u32[]{:S(2)}) collective-permute-start(bf16[128,512]{1,0:T(8,128)(2,1)S(1)} %get-tuple-element.315), channel_id=1, source_target_pairs={{0,3},{1,0},{2,1},{3,2},{4,7},{5,4},{6,5},{7,6},{8,11},{9,8},{10,9... | collective-permute-start | bytes 393224 | tf_op jit(solution)/shard_map/ppermute | solution.py:33
  173.7 5.9 %collective-permute-start.21 = (bf16[128,512]{0,1:T(8,128)(2,1)S(1)}, bf16[128,512]{0,1:T(8,128)(2,1)S(1)}, u32[]{:S(2)}, u32[]{:S(2)}) collective-permute-start(bf16[128,512]{0,1:T(8,128)(2,1)S(1)} %copy.129), channel_id=1, source_target_pairs={{0,3},{1,0},{2,1},{3,2},{4,7},{5,4},{6,5},{7,6},{8,11},{9,8},{10,9... | collective-permute-start | bytes 393224 | tf_op jit(solution)/shard_map/ppermute | solution.py:33
  177.0 11.5 %collective-permute-start.22 = (bf16[128,512]{0,1:T(8,128)(2,1)S(1)}, bf16[128,512]{0,1:T(8,128)(2,1)S(1)}, u32[]{:S(2)}, u32[]{:S(2)}) collective-permute-start(bf16[128,512]{0,1:T(8,128)(2,1)S(1)} %copy.129), channel_id=1, source_target_pairs={{0,2},{1,3},{2,0},{3,1},{4,6},{5,7},{6,4},{7,5},{8,10},{9,11},{10,... | collective-permute-start | bytes 393224 | tf_op jit(solution)/shard_map/ppermute | solution.py:33
  178.5 10.1 %collective-permute-start.23 = (bf16[128,512]{0,1:T(8,128)(2,1)S(1)}, bf16[128,512]{0,1:T(8,128)(2,1)S(1)}, u32[]{:S(2)}, u32[]{:S(2)}) collective-permute-start(bf16[128,512]{0,1:T(8,128)(2,1)S(1)} %copy.129), channel_id=1, source_target_pairs={{0,1},{1,2},{2,3},{3,0},{4,5},{5,6},{6,7},{7,4},{8,9},{9,10},{10,1... | collective-permute-start | bytes 393224 | tf_op jit(solution)/shard_map/ppermute | solution.py:33
  206.9 3.9 collective-permute-start.24
  206.9 4.8 collective-permute-start.25
  207.5 5.9 %collective-permute-start.26 = (f32[8,512]{1,0:T(8,128)}, f32[8,512]{1,0:T(8,128)S(1)}, u32[]{:S(2)}, u32[]{:S(2)}) collective-permute-start(f32[8,512]{1,0:T(8,128)} %shard_map.398), channel_id=1, source_target_pairs={{0,1},{1,2},{2,3},{3,0},{4,5},{5,6},{6,7},{7,4},{8,9},{9,10},{10,1... | collective-permute-start | bytes 49160 | tf_op jit(solution)/shard_map/ppermute | solution.py:33
  240.1 8.3 %collective-permute-start.27 = (bf16[128,512]{1,0:T(8,128)(2,1)S(1)}, bf16[128,512]{1,0:T(8,128)(2,1)S(1)}, u32[]{:S(2)}, u32[]{:S(2)}) collective-permute-start(bf16[128,512]{1,0:T(8,128)(2,1)S(1)} %get-tuple-element.311), channel_id=1, source_target_pairs={{0,1},{1,2},{2,3},{3,0},{4,5},{5,6},{6,7},{7,4},{8,9},{9,10},{10,1... | collective-permute-start | bytes 393224 | tf_op jit(solution)/shard_map/ppermute | solution.py:33
  240.6 11.0 %collective-permute-start.28 = (bf16[128,512]{1,0:T(8,128)(2,1)S(1)}, bf16[128,512]{1,0:T(8,128)(2,1)S(1)}, u32[]{:S(2)}, u32[]{:S(2)}) collective-permute-start(bf16[128,512]{1,0:T(8,128)(2,1)S(1)} %get-tuple-element.312), channel_id=1, source_target_pairs={{0,2},{1,3},{2,0},{3,1},{4,6},{5,7},{6,4},{7,5},{8,10},{9,11},{10,... | collective-permute-start | bytes 393224 | tf_op jit(solution)/shard_map/ppermute | solution.py:33
  242.6 9.0 %collective-permute-start.29 = (bf16[128,512]{1,0:T(8,128)(2,1)S(1)}, bf16[128,512]{1,0:T(8,128)(2,1)S(1)}, u32[]{:S(2)}, u32[]{:S(2)}) collective-permute-start(bf16[128,512]{1,0:T(8,128)(2,1)S(1)} %get-tuple-element.313), channel_id=1, source_target_pairs={{0,3},{1,0},{2,1},{3,2},{4,7},{5,4},{6,5},{7,6},{8,11},{9,8},{10,9... | collective-permute-start | bytes 393224 | tf_op jit(solution)/shard_map/ppermute | solution.py:33
  276.3 165.2 %reduce-scatter.5.cloned.1.call-start = ((), (), s32[]{:S(2)}) async-start(), calls=%async_computation.3 | async-start | bytes 1310720 | tf_op jit(solution)/shard_map/reduce_scatter | solution.py:1282
  277.1 17.7 %collective-permute-start.30 = (bf16[128,512]{1,0:T(8,128)(2,1)S(1)}, bf16[128,512]{1,0:T(8,128)(2,1)S(1)}, u32[]{:S(2)}, u32[]{:S(2)}) collective-permute-start(bf16[128,512]{1,0:T(8,128)(2,1)S(1)} %copy-done.23), channel_id=1, source_target_pairs={{0,3},{1,0},{2,1},{3,2},{4,7},{5,4},{6,5},{7,6},{8,11},{9,8},{10,9... | collective-permute-start | bytes 393224 | tf_op jit(solution)/shard_map/ppermute | solution.py:33
  280.1 14.8 %collective-permute-start.31 = (bf16[128,512]{1,0:T(8,128)(2,1)S(1)}, bf16[128,512]{1,0:T(8,128)(2,1)S(1)}, u32[]{:S(2)}, u32[]{:S(2)}) collective-permute-start(bf16[128,512]{1,0:T(8,128)(2,1)S(1)} %copy-done.23), channel_id=1, source_target_pairs={{0,2},{1,3},{2,0},{3,1},{4,6},{5,7},{6,4},{7,5},{8,10},{9,11},{10,... | collective-permute-start | bytes 393224 | tf_op jit(solution)/shard_map/ppermute | solution.py:33
  281.0 13.9 %collective-permute-start.32 = (bf16[128,512]{1,0:T(8,128)(2,1)S(1)}, bf16[128,512]{1,0:T(8,128)(2,1)S(1)}, u32[]{:S(2)}, u32[]{:S(2)}) collective-permute-start(bf16[128,512]{1,0:T(8,128)(2,1)S(1)} %copy-done.23), channel_id=1, source_target_pairs={{0,1},{1,2},{2,3},{3,0},{4,5},{5,6},{6,7},{7,4},{8,9},{9,10},{10,1... | collective-permute-start | bytes 393224 | tf_op jit(solution)/shard_map/ppermute | solution.py:33
  294.8 19.3 %collective-permute-start.33 = (bf16[1024,1024]{1,0:T(8,128)(2,1)}, bf16[1024,1024]{1,0:T(8,128)(2,1)S(1)}, u32[]{:S(2)}, u32[]{:S(2)}) collective-permute-start(bf16[1024,1024]{1,0:T(8,128)(2,1)} %bitcast.241), channel_id=1, source_target_pairs={{0,4},{4,0},{8,12},{12,8},{16,20},{20,16},{24,28},{28,24},{1,5},{5... | collective-permute-start | bytes 6291464 | tf_op jit(solution)/shard_map/ppermute | solution.py:29
  310.7 3.4 collective-permute-start.34
  321.8 12.3 %collective-permute-start.38 = (bf16[128,1664]{1,0:T(8,128)(2,1)}, bf16[128,1664]{1,0:T(8,128)(2,1)S(1)}, u32[]{:S(2)}, u32[]{:S(2)}) collective-permute-start(bf16[128,1664]{1,0:T(8,128)(2,1)} %get-tuple-element.165), channel_id=1, source_target_pairs={{0,8},{4,12},{8,0},{12,4},{16,24},{20,28},{24,16},{28,20},{1,9},{5... | collective-permute-start | bytes 1277960 | tf_op jit(solution)/shard_map/ppermute | solution.py:29
  321.8 12.4 %collective-permute-start.39 = (bf16[128,1664]{1,0:T(8,128)(2,1)}, bf16[128,1664]{1,0:T(8,128)(2,1)S(1)}, u32[]{:S(2)}, u32[]{:S(2)}) collective-permute-start(bf16[128,1664]{1,0:T(8,128)(2,1)} %get-tuple-element.167), channel_id=1, source_target_pairs={{0,16},{4,20},{8,24},{12,28},{16,0},{20,4},{24,8},{28,12},{1,17},{... | collective-permute-start | bytes 1277960 | tf_op jit(solution)/shard_map/ppermute | solution.py:29
  322.4 37.2 %collective-permute-start.35 = (bf16[384,512]{1,0:T(8,128)(2,1)S(1)}, bf16[384,512]{1,0:T(8,128)(2,1)S(1)}, u32[]{:S(2)}, u32[]{:S(2)}) collective-permute-start(bf16[384,512]{1,0:T(8,128)(2,1)S(1)} %copy-done.14), channel_id=1, source_target_pairs={{0,3},{1,0},{2,1},{3,2},{4,7},{5,4},{6,5},{7,6},{8,11},{9,8},{10,9... | collective-permute-start | bytes 1179656 | tf_op jit(solution)/shard_map/ppermute | solution.py:33
  326.4 34.6 %collective-permute-start.36 = (bf16[384,512]{1,0:T(8,128)(2,1)S(1)}, bf16[384,512]{1,0:T(8,128)(2,1)S(1)}, u32[]{:S(2)}, u32[]{:S(2)}) collective-permute-start(bf16[384,512]{1,0:T(8,128)(2,1)S(1)} %copy-done.14), channel_id=1, source_target_pairs={{0,2},{1,3},{2,0},{3,1},{4,6},{5,7},{6,4},{7,5},{8,10},{9,11},{10,... | collective-permute-start | bytes 1179656 | tf_op jit(solution)/shard_map/ppermute | solution.py:33
  326.6 34.4 %collective-permute-start.37 = (bf16[384,512]{1,0:T(8,128)(2,1)S(1)}, bf16[384,512]{1,0:T(8,128)(2,1)S(1)}, u32[]{:S(2)}, u32[]{:S(2)}) collective-permute-start(bf16[384,512]{1,0:T(8,128)(2,1)S(1)} %copy-done.14), channel_id=1, source_target_pairs={{0,1},{1,2},{2,3},{3,0},{4,5},{5,6},{6,7},{7,4},{8,9},{9,10},{10,1... | collective-permute-start | bytes 1179656 | tf_op jit(solution)/shard_map/ppermute | solution.py:33
  339.1 24.9 %collective-permute-start.40 = (bf16[256,1664]{1,0:T(8,128)(2,1)}, bf16[256,1664]{1,0:T(8,128)(2,1)S(1)}, u32[]{:S(2)}, u32[]{:S(2)}) collective-permute-start(bf16[256,1664]{1,0:T(8,128)(2,1)} %get-tuple-element.168), channel_id=1, source_target_pairs={{0,16},{4,20},{8,24},{12,28},{16,0},{20,4},{24,8},{28,12},{1,17},{... | collective-permute-start | bytes 2555912 | tf_op jit(solution)/shard_map/ppermute | solution.py:29
  340.4 23.6 %collective-permute-start.41 = (bf16[256,1664]{1,0:T(8,128)(2,1)}, bf16[256,1664]{1,0:T(8,128)(2,1)S(1)}, u32[]{:S(2)}, u32[]{:S(2)}) collective-permute-start(bf16[256,1664]{1,0:T(8,128)(2,1)} %get-tuple-element.169), channel_id=1, source_target_pairs={{0,8},{4,12},{8,0},{12,4},{16,24},{20,28},{24,16},{28,20},{1,9},{5... | collective-permute-start | bytes 2555912 | tf_op jit(solution)/shard_map/ppermute | solution.py:29
  383.5 7.3 %collective-permute-start.42 = (bf16[256,8064]{1,0:T(8,128)(2,1)}, bf16[256,8064]{1,0:T(8,128)(2,1)S(1)}, u32[]{:S(2)}, u32[]{:S(2)}) collective-permute-start(bf16[256,8064]{1,0:T(8,128)(2,1)} %get-tuple-element.173), channel_id=1, source_target_pairs={{0,4},{4,0},{8,12},{12,8},{16,20},{20,16},{24,28},{28,24},{1,5},{5... | collective-permute-start | bytes 12386312 | tf_op jit(solution)/shard_map/ppermute | solution.py:29
  399.2 14.1 %collective-permute-start.43 = (bf16[32,8064]{1,0:T(8,128)(2,1)}, bf16[32,8064]{1,0:T(8,128)(2,1)S(1)}, u32[]{:S(2)}, u32[]{:S(2)}) collective-permute-start(bf16[32,8064]{1,0:T(8,128)(2,1)} %get-tuple-element.177), channel_id=1, source_target_pairs={{0,8},{4,12},{8,0},{12,4},{16,24},{20,28},{24,16},{28,20},{1,9},{5... | collective-permute-start | bytes 1548296 | tf_op jit(solution)/shard_map/ppermute | solution.py:29
  400.7 13.7 %collective-permute-start.44 = (bf16[32,8064]{1,0:T(8,128)(2,1)}, bf16[32,8064]{1,0:T(8,128)(2,1)S(1)}, u32[]{:S(2)}, u32[]{:S(2)}) collective-permute-start(bf16[32,8064]{1,0:T(8,128)(2,1)} %get-tuple-element.179), channel_id=1, source_target_pairs={{0,16},{4,20},{8,24},{12,28},{16,0},{20,4},{24,8},{28,12},{1,17},{... | collective-permute-start | bytes 1548296 | tf_op jit(solution)/shard_map/ppermute | solution.py:29
  419.0 24.1 %collective-permute-start.45 = (bf16[64,8064]{1,0:T(8,128)(2,1)}, bf16[64,8064]{1,0:T(8,128)(2,1)}, u32[]{:S(2)}, u32[]{:S(2)}) collective-permute-start(bf16[64,8064]{1,0:T(8,128)(2,1)} %get-tuple-element.180), channel_id=1, source_target_pairs={{0,16},{4,20},{8,24},{12,28},{16,0},{20,4},{24,8},{28,12},{1,17},{... | collective-permute-start | bytes 3096584 | tf_op jit(solution)/shard_map/ppermute | solution.py:29
  419.9 13.8 %collective-permute-start.46 = (bf16[64,1664]{1,0:T(8,128)(2,1)S(1)}, bf16[64,1664]{1,0:T(8,128)(2,1)S(1)}, u32[]{:S(2)}, u32[]{:S(2)}) collective-permute-start(bf16[64,1664]{1,0:T(8,128)(2,1)S(1)} %get-tuple-element.310), channel_id=1, source_target_pairs={{0,1},{1,2},{2,3},{3,0},{4,5},{5,6},{6,7},{7,4},{8,9},{9,10},{10,1... | collective-permute-start | bytes 638984 | tf_op jit(solution)/shard_map/ppermute | solution.py:33
  422.4 19.1 %collective-permute-start.47 = (bf16[64,1664]{1,0:T(8,128)(2,1)S(1)}, bf16[64,1664]{1,0:T(8,128)(2,1)}, u32[]{:S(2)}, u32[]{:S(2)}) collective-permute-start(bf16[64,1664]{1,0:T(8,128)(2,1)S(1)} %get-tuple-element.309), channel_id=1, source_target_pairs={{0,2},{1,3},{2,0},{3,1},{4,6},{5,7},{6,4},{7,5},{8,10},{9,11},{10,... | collective-permute-start | bytes 638984 | tf_op jit(solution)/shard_map/ppermute | solution.py:33
  424.2 17.3 %collective-permute-start.48 = (bf16[64,1664]{1,0:T(8,128)(2,1)S(1)}, bf16[64,1664]{1,0:T(8,128)(2,1)}, u32[]{:S(2)}, u32[]{:S(2)}) collective-permute-start(bf16[64,1664]{1,0:T(8,128)(2,1)S(1)} %get-tuple-element.308), channel_id=1, source_target_pairs={{0,3},{1,0},{2,1},{3,2},{4,7},{5,4},{6,5},{7,6},{8,11},{9,8},{10,9... | collective-permute-start | bytes 638984 | tf_op jit(solution)/shard_map/ppermute | solution.py:33
  425.4 24.6 %collective-permute-start.49 = (bf16[64,8064]{1,0:T(8,128)(2,1)}, bf16[64,8064]{1,0:T(8,128)(2,1)}, u32[]{:S(2)}, u32[]{:S(2)}) collective-permute-start(bf16[64,8064]{1,0:T(8,128)(2,1)} %get-tuple-element.188), channel_id=1, source_target_pairs={{0,8},{4,12},{8,0},{12,4},{16,24},{20,28},{24,16},{28,20},{1,9},{5... | collective-permute-start | bytes 3096584 | tf_op jit(solution)/shard_map/ppermute | solution.py:29
  457.3 3.7 collective-permute-start.51
  460.9 3.7 collective-permute-start.52
  464.6 6.9 %collective-permute-start.53 = (f32[9,128]{1,0:T(8,128)S(1)}, f32[9,128]{1,0:T(8,128)S(1)}, u32[]{:S(2)}, u32[]{:S(2)}) collective-permute-start(f32[9,128]{1,0:T(8,128)S(1)} %add.238), channel_id=1, source_target_pairs={{0,1},{1,2},{2,3},{3,0},{4,5},{5,6},{6,7},{7,4},{8,9},{9,10},{10,1... | collective-permute-start | bytes 13832 | tf_op jit(solution)/shard_map/ppermute | solution.py:33
  468.0 4.5 collective-permute-start.54
  469.4 3.7 collective-permute-start.55
  491.0 3.7 collective-permute-start.57
  494.7 3.7 collective-permute-start.58
  498.5 5.7 %collective-permute-start.59 = (f32[25,128]{1,0:T(8,128)S(1)}, f32[25,128]{1,0:T(8,128)S(1)}, u32[]{:S(2)}, u32[]{:S(2)}) collective-permute-start(f32[25,128]{1,0:T(8,128)S(1)} %add.250), channel_id=1, source_target_pairs={{0,1},{1,2},{2,3},{3,0},{4,5},{5,6},{6,7},{7,4},{8,9},{9,10},{10,1... | collective-permute-start | bytes 38408 | tf_op jit(solution)/shard_map/ppermute | solution.py:33
  498.6 5.6 %collective-permute-start.60 = (f32[25,128]{1,0:T(8,128)S(1)}, f32[25,128]{1,0:T(8,128)S(1)}, u32[]{:S(2)}, u32[]{:S(2)}) collective-permute-start(f32[25,128]{1,0:T(8,128)S(1)} %add.250), channel_id=1, source_target_pairs={{0,2},{1,3},{2,0},{3,1},{4,6},{5,7},{6,4},{7,5},{8,10},{9,11},{10,... | collective-permute-start | bytes 38408 | tf_op jit(solution)/shard_map/ppermute | solution.py:33
  501.7 3.7 collective-permute-start.61
  (49 other events, 536.6 us)
Sparse Core Ops, SparseCore 0:
  43.3 51.8 all-gather.4
  97.6 54.3 all-gather.6
  276.4 74.8 reduce-scatter.2
  401.4 31.2 reduce-scatter.4

commit v5 on v4

--- a/solution.py
+++ b/solution.py
@@ -159,7 +159,7 @@
 
 def lookup(ids, table_parts):
     rows, vocab = ids.shape[0], table_parts[0].shape[1]
-    tile = 1024
+    tile = 2048
     return pl.pallas_call(
         functools.partial(lookup_kernel, vocab, tile),
         out_shape=[
@@ -177,7 +177,7 @@
 
 def pick(ids, table_rows, waits):
     rows, vocab = ids.shape[0], table_rows.shape[0]
-    tile = 1024
+    tile = 2048
     return pl.pallas_call(
         ordered(functools.partial(pick_kernel, vocab, tile), 2, waits),
         out_shape=jax.ShapeDtypeStruct((rows, D), BF),
@@ -210,7 +210,7 @@
         out_ref[...] = acc_ref[...].astype(BF)
 
 
-def spread_kernel(tile, ids_ref, rows_ref, *refs):
+def spread_kernel(tile, first, ids_ref, rows_ref, *refs):
     step = pl.program_id(0)
     turned_ref = refs[-1]
 
@@ -218,7 +218,7 @@
     def _():
         turned_ref[...] = rows_ref[...].T
 
-    place = step * tile + lax.broadcasted_iota(jnp.int32, (1, tile), 1)
+    place = (first + step) * tile + lax.broadcasted_iota(jnp.int32, (1, tile), 1)
     hit = (ids_ref[...] == place).astype(BF)
     total = jnp.dot(turned_ref[...], hit, preferred_element_type=F32)
     if len(refs) == 4:
@@ -235,9 +235,12 @@
         send_ref[...] = total[D // 2 :].astype(BF)
 
 
-def spread(ids, rows_low, columns, final_t=None, slope=None, base=None, waits=()):
+SPREAD_TILE = 1024
+
+
+def spread(ids, rows_low, columns, final_t=None, slope=None, base=None, first=0, waits=()):
     rows = ids.shape[0]
-    tile = 1024
+    tile = SPREAD_TILE
     if base is None:
         shapes = [((D, columns), F32)]
         more = [final_t, slope]
@@ -245,15 +248,15 @@
     else:
         shapes = [((D // 8, columns), F32)] * 4 + [((D // 2, columns), BF)]
         more = [base]
-        specs = [pl.BlockSpec((D, tile), lambda i: (0, i))]
+        specs = [pl.BlockSpec((D, tile), lambda i: (0, i + first))]
     return pl.pallas_call(
-        ordered(functools.partial(spread_kernel, tile), 2 + len(more), waits),
+        ordered(functools.partial(spread_kernel, tile, first), 2 + len(more), waits),
         out_shape=[jax.ShapeDtypeStruct(*shape) for shape in shapes],
         grid=(pl.cdiv(columns, tile),),
         in_specs=[fixed((rows, 1)), fixed((rows, D))] + specs + [ANYWHERE] * len(waits),
         out_specs=[pl.BlockSpec((shape[0][0], tile), lambda i: (0, i)) for shape in shapes],
         scratch_shapes=[pltpu.VMEM((D, rows), BF)],
-        cost_estimate=cost(18),
+        cost_estimate=cost(18 if base is None else 9),
         compiler_params=pltpu.CompilerParams(vmem_limit_bytes=VMEM_LIMIT),
     )(ids.reshape(rows, 1), rows_low, *more, *waits)
 
@@ -363,7 +366,7 @@
             )
             self.pieces = [dp_swap(d_low, 2, dp), dp_swap(d_high, 4, dp)]
 
-    def near(self, tile):
+    def near(self, tile, waits=()):
         dp = self.dp
         self.last = self.ready = ()
         if dp == 8:
@@ -375,11 +378,12 @@
                 [(rows, BF)] * 2,
                 columns,
                 tile,
+                waits=waits,
             )
             self.ready = [y_sum, x_sum]
             self.last = [dp_swap(y_sum, 4, dp), dp_swap(x_sum, 2, dp)]
 
-    def result(self, tile, columns=None):
+    def result(self, tile, columns=None, waits=()):
         dp = self.dp
         if dp != 8:
             total = jnp.concatenate(
@@ -406,18 +410,25 @@
         kernel = functools.partial(last_sums_kernel, len(self.groups), columns, tile)
         sums = [] if columns is None else [(8, 128)]
         rows = self.groups[0][0].shape[0]
-        return sums_call(kernel, inputs, [(rows, F32)], columns or wide, tile, sums)
+        return sums_call(kernel, inputs, [(rows, F32)], columns or wide, tile, sums, waits)
 
 
 def sums_call(kernel, inputs, outputs, columns, tile, sums=(), waits=()):
     if tile is not None:
         return column_call(kernel, inputs, outputs, tile, sums, columns, waits)
+    everything = pl.BlockSpec(memory_space=pltpu.VMEM)
     return pl.pallas_call(
-        kernel,
+        ordered(kernel, len(inputs), waits),
+        in_specs=[everything] * len(inputs) + [ANYWHERE] * len(waits),
         out_shape=[jax.ShapeDtypeStruct((rows, columns), dtype) for rows, dtype in outputs],
         cost_estimate=cost(5),
         compiler_params=pltpu.CompilerParams(vmem_limit_bytes=VMEM_LIMIT),
-    )(*inputs)
+    )(*inputs, *waits)
+
+
+HALF = 0.5 * 1.4426950408889634
+CHUNKS = 4
+BACK_CHUNKS = 1
 
 
 def logits_kernel(vocab, tile, final_ref, label_ref, teacher_ref, table_ref, out_ref, *stats):
@@ -433,17 +444,26 @@
             ref[...] = jnp.zeros_like(ref)
 
     def work(valid):
-        logits = jnp.dot(table_ref[...], final_ref[...], preferred_element_type=F32)
+        for chunk in range(CHUNKS):
+            if chunk * part < valid:
+                work_part(chunk * part, min(valid - chunk * part, part))
+
+    part = tile // CHUNKS
+
+    def work_part(start, valid):
+        logits = jnp.dot(
+            table_ref[start : start + part], final_ref[...], preferred_element_type=F32
+        )
         tokens = logits.shape[1]
 
         def folded(value):
-            return value.reshape(tile // 8, 8, tokens)
+            return (value * HALF).reshape(part // 8, 8, tokens)
 
         student = folded(logits)
-        teacher = folded(teacher_ref[...].astype(F32))
-        place = 8 * lax.broadcasted_iota(jnp.int32, (tile // 8, 8, 1), 0)
-        place = place + lax.broadcasted_iota(jnp.int32, (tile // 8, 8, 1), 1)
-        if valid < tile:
+        teacher = folded(teacher_ref[start : start + part].astype(F32))
+        place = 8 * lax.broadcasted_iota(jnp.int32, (part // 8, 8, 1), 0)
+        place = place + lax.broadcasted_iota(jnp.int32, (part // 8, 8, 1), 1)
+        if valid < part:
             student = jnp.where(place < valid, student, -1e30)
             teacher = jnp.where(place < valid, teacher, -1e30)
         old_s, old_t = top_s[...], top_t[...]
@@ -451,15 +471,15 @@
         new_t = jnp.maximum(old_t, jnp.max(teacher, 0))
         top_s[...] = new_s
         top_t[...] = new_t
-        scale_s = jnp.exp((old_s - new_s) * 0.5)
-        scale_t = jnp.exp((old_t - new_t) * 0.5)
-        e = jnp.exp((student - new_s[None]) * 0.5)
+        scale_s = jnp.exp2(old_s - new_s)
+        scale_t = jnp.exp2(old_t - new_t)
+        e = jnp.exp2(student - new_s[None])
         half[...] = half[...] * scale_s + jnp.sum(e, 0)
         one[...] = one[...] * (scale_s * scale_s) + jnp.sum(e * e, 0)
-        e = jnp.exp((teacher - new_t[None]) * 0.5)
+        e = jnp.exp2(teacher - new_t[None])
         teach[...] = teach[...] * scale_t + jnp.sum(e, 0)
         cross[...] = cross[...] * scale_t + jnp.sum(e * (teacher - student), 0)
-        labels = (label_ref[...] - step * tile)[None]
+        labels = (label_ref[...] - (step * tile + start))[None]
         label[...] += jnp.sum(jnp.where(labels == place, student, 0.0), 0)
 
     rest = vocab - (pl.cdiv(vocab, tile) - 1) * tile
@@ -479,19 +499,19 @@
     def _():
         peak_s = jnp.max(top_s[...], 0, keepdims=True)
         peak_t = jnp.max(top_t[...], 0, keepdims=True)
-        by_s = jnp.exp((top_s[...] - peak_s) * 0.5)
-        by_t = jnp.exp((top_t[...] - peak_t) * 0.5)
+        by_s = jnp.exp2(top_s[...] - peak_s)
+        by_t = jnp.exp2(top_t[...] - peak_t)
 
         def total(value):
             return jnp.sum(value, 0, keepdims=True)
 
-        out_ref[0:1] = peak_s
-        out_ref[1:2] = peak_t
+        out_ref[0:1] = peak_s * (1.0 / HALF)
+        out_ref[1:2] = peak_t * (1.0 / HALF)
         out_ref[2:3] = total(one[...] * (by_s * by_s))
         out_ref[3:4] = total(half[...] * by_s)
         out_ref[4:5] = total(teach[...] * by_t)
-        out_ref[5:6] = total(cross[...] * by_t) * 0.5
-        out_ref[6:7] = total(label[...])
+        out_ref[5:6] = total(cross[...] * by_t) * (0.5 / HALF)
+        out_ref[6:7] = total(label[...]) * (1.0 / HALF)
         out_ref[7:8] = jnp.zeros_like(peak_s)
 
 
@@ -524,24 +544,33 @@
     def _():
         acc_ref[...] = jnp.zeros_like(acc_ref)
 
-    good = lax.broadcasted_iota(jnp.int32, (1, tile), 1) < vocab - step * tile
-    block = stacked(table_refs)
-    block = jnp.where(good, block, jnp.zeros_like(block))
-    place = lax.broadcasted_iota(jnp.int32, (tile, 1), 0)
-    logits = jnp.dot(rows_ref[...], final_ref[...], preferred_element_type=F32)
-    lse_half = scalar_ref[0:1]
-    lse_teacher = scalar_ref[1:2]
+    log2e = 2.0 * HALF
+    lse_half = scalar_ref[0:1] * log2e
+    lse_teacher = scalar_ref[1:2] * log2e
     soft_one = scalar_ref[2:3]
     soft_half = scalar_ref[3:4]
     weight = scalar_ref[4:5]
-    student = jnp.exp(logits * 0.5 - lse_half)
-    teacher = jnp.exp(teacher_ref[...].astype(F32) * 0.5 - lse_teacher)
-    labels = label_ref[...] - step * tile
-    slope = student * (soft_one * student + soft_half) - soft_half * teacher
-    slope = slope - jnp.where(labels == place, weight, 0.0)
-    slope = jnp.where(place < vocab - step * tile, slope, 0.0).astype(BF)
-    slope_ref[...] = slope
-    acc_ref[...] += jnp.dot(block, slope, preferred_element_type=F32)
+    part = tile // BACK_CHUNKS
+    total = acc_ref[...]
+    for start in range(0, tile, part):
+        left = vocab - step * tile - start
+        good = lax.broadcasted_iota(jnp.int32, (1, part), 1) < left
+        block = jnp.concatenate([ref[:, start : start + part] for ref in table_refs], 0)
+        block = jnp.where(good, block, jnp.zeros_like(block))
+        place = lax.broadcasted_iota(jnp.int32, (part, 1), 0)
+        logits = jnp.dot(
+            rows_ref[start : start + part], final_ref[...], preferred_element_type=F32
+        )
+        student = jnp.exp2(logits * HALF - lse_half)
+        teacher = teacher_ref[start : start + part].astype(F32)
+        teacher = jnp.exp2(teacher * HALF - lse_teacher)
+        labels = label_ref[...] - (step * tile + start)
+        slope = student * (soft_one * student + soft_half) - soft_half * teacher
+        slope = slope - jnp.where(labels == place, weight, 0.0)
+        slope = jnp.where(place < left, slope, 0.0).astype(BF)
+        slope_ref[start : start + part] = slope
+        total = total + jnp.dot(block, slope, preferred_element_type=F32)
+    acc_ref[...] = total
 
     @pl.when(step == last)
     def _():
@@ -588,8 +617,10 @@
     return moment, second, update
 
 
-def lamb_columns_kernel(columns, tile, w, m, v, g, clip, m_out, v_out, u_out, squares):
-    moment, second, update = lamb(w[...], m[...], v[...], g[...], clip[0:1, 0:1])
+def lamb_columns_kernel(columns, tile, left, *refs):
+    w, m, v, g_left, g_right, clip, m_out, v_out, u_out, squares = refs
+    grad = jnp.where(pl.program_id(0) < left, g_left[...], g_right[...])
+    moment, second, update = lamb(w[...], m[...], v[...], grad, clip[0:1, 0:1])
     m_out[...] = moment
     v_out[...] = second
     u_out[...] = update
@@ -599,6 +630,51 @@
         squares[...] = jnp.zeros_like(squares)
 
     squares[...] += lane_sums(inside(columns, tile, update * update))
+
+
+def lamb_columns(state, g_left, g_right, clip, tile):
+    rows, columns = state[0].shape
+    left = g_left.shape[1] // tile
+    spec = pl.BlockSpec((rows, tile), lambda i: (0, i))
+    return pl.pallas_call(
+        functools.partial(lamb_columns_kernel, columns, tile, left),
+        out_shape=[jax.ShapeDtypeStruct((rows, columns), F32)] * 3
+        + [jax.ShapeDtypeStruct((8, 128), F32)],
+        grid=(pl.cdiv(columns, tile),),
+        in_specs=[
+            spec,
+            spec,
+            spec,
+            pl.BlockSpec((rows, tile), lambda i: (0, jnp.minimum(i, left - 1))),
+            pl.BlockSpec((rows, tile), lambda i: (0, jnp.maximum(i - left, 0))),
+            fixed(clip.shape),
+        ],
+        out_specs=[spec, spec, spec, fixed((8, 128))],
+        cost_estimate=cost(8),
+        compiler_params=pltpu.CompilerParams(vmem_limit_bytes=VMEM_LIMIT),
+    )(*state, g_left, g_right, clip)
+
+
+def step_kernel(counts, rates, *refs):
+    groups = len(counts)
+    row = 1
+    for group, count in enumerate(counts):
+        w, u, out = refs[2 * group], refs[2 * group + 1], refs[2 * groups + group]
+        for number in range(count):
+            out[number] = w[number] - rates[row] * u[number]
+            row += 1
+
+
+def step_matrices(rates, pairs):
+    flat = [array for pair in pairs for array in pair]
+    return pl.pallas_call(
+        functools.partial(step_kernel, [pair[0].shape[0] for pair in pairs]),
+        out_shape=[jax.ShapeDtypeStruct(pair[0].shape, F32) for pair in pairs],
+        in_specs=[pl.BlockSpec(memory_space=pltpu.SMEM)]
+        + [pl.BlockSpec(memory_space=pltpu.VMEM)] * len(flat),
+        cost_estimate=cost(3),
+        compiler_params=pltpu.CompilerParams(vmem_limit_bytes=VMEM_LIMIT),
+    )(rates, *flat)
 
 
 def lamb_matrices_kernel(places, clip_ref, *refs):
@@ -1306,17 +1382,30 @@
     far_rows = jnp.concatenate(enc_rows[1:], 0)
     enc_scatter.near(None)
     waits = [dec_done, *enc_scatter.last]
-    *keeps, send = spread(far_ids, far_rows, columns, base=grad_table_t, waits=waits)
-    scatter = ScatterDp(dp)
-    scatter.add(keeps, send)
-    (enc_shard,) = enc_scatter.result(None)
-    scatter.far(4096, [enc_shard])
-    enc_sums = send_heads(enc_shard.astype(BF).reshape(heads, -1, enc_shard.shape[1]))
+    tiles = pl.cdiv(columns, SPREAD_TILE)
+    left = tiles // 4 * 2
+    cut = left * SPREAD_TILE
+    a, b = ScatterDp(dp), ScatterDp(dp)
+    *keeps, send_a = spread(far_ids, far_rows, cut, base=grad_table_t, waits=waits)
+    a.add(keeps, send_a)
+    *keeps, send_b = spread(
+        far_ids, far_rows, columns - cut, base=grad_table_t, first=left, waits=[send_a]
+    )
+    b.add(keeps, send_b)
+    step = 2048
+    a.far(step, [send_b])
+    b.far(step, a.later[:1] if a.pieces else [])
+    a.near(step)
+    (enc_shard,) = enc_scatter.result(None, None, [*b.later[:1], *a.ready[:1]] if b.pieces else [])
+    b.near(step, a.ready[:1])
+    enc_low_shard = after(enc_shard.astype(BF), *a.last)
+    enc_sums = send_heads(enc_low_shard.reshape(heads, -1, enc_shard.shape[1]))
     enc_sums[0] = enc_shard.reshape(heads, -1, enc_shard.shape[1])[0]
-    scatter.near(4096)
-    if scatter.last:
-        scatter.last[0], dec_shard, *enc_sums = tie(scatter.last[0], dec_shard, *enc_sums)
-    g_table, table_squares = scatter.result(4096, vocab_local)
+    g_left, left_squares = a.result(step, cut)
+    if b.last:
+        b.last[0], dec_shard, *enc_sums = tie(b.last[0], dec_shard, *enc_sums)
+    g_right, right_squares = b.result(step, vocab_local - cut, [left_squares])
+    table_squares = left_squares + right_squares
     g_dec = dec_shard.astype(F32)
     g_enc = functools.reduce(jnp.add, [value.astype(F32) for value in enc_sums])
 
@@ -1350,12 +1439,8 @@
     grad_norm = jnp.sqrt(totals[0, matrix_count + 1] + jnp.sum(totals[1:]))
     total_loss = totals[0, matrix_count]
     clip = jnp.full((8, 128), jnp.minimum(1.0, CLIP_NORM / grad_norm))
-    m_table, v_table, u_table, squares_table = column_call(
-        functools.partial(lamb_columns_kernel, vocab_local, 2048),
-        [masters[0], moments[0], seconds[0], g_table, clip],
-        [(embed_t.shape[0], F32)] * 3,
-        2048,
-        sums=[(8, 128)],
+    m_table, v_table, u_table, squares_table = lamb_columns(
+        (masters[0], moments[0], seconds[0]), g_left, g_right, clip, step
     )
 
     def flat9(array):
@@ -1396,19 +1481,18 @@
         ]
     )
     rates = LEARN_RATE * jnp.sqrt(totals[0, :matrix_count]) / (jnp.sqrt(update_squares) + 1e-06)
+    fresh_w = step_matrices(
+        rates, [(group[0], update) for group, update in zip(groups, fresh[2::3], strict=True)]
+    )
+    fresh_w = [
+        embed_t - rates[0] * u_table,
+        *fresh_w,
+        gains - rates[1 + small_count :].reshape(gain_rows, 1) * u_gain,
+    ]
     fresh_m = [m_table] + list(fresh[0::3]) + [m_gain]
     fresh_v = [v_table] + list(fresh[1::3]) + [v_gain]
-    updates = [u_table] + list(fresh[2::3]) + [u_gain]
-    for stack in (fresh_m, fresh_v, updates):
+    for stack in (fresh_w, fresh_m, fresh_v):
         stack[1] = stack[1].reshape(attn_in.shape)
-    shapes = [(1, 1), (3, 3, 1, 1), (3, 1, 1), (2, 1, 1), (2, 1, 1), (gain_rows, 1)]
-    fresh_w, start = [], 0
-    for master, update, shape in zip(masters, updates, shapes, strict=True):
-        count = 1
-        for extent in shape:
-            count *= extent
-        fresh_w.append(master - rates[start : start + count].reshape(shape) * update)
-        start += count
     return (
         total_loss.reshape(1),
         grad_norm.reshape(1),

time: 533 us -> 525 us (0.985)
  waiting for transfers between devices: 132 us -> 121 us
  other arithmetic: 35.2 us -> 26.9 us
  Pallas kernels: 232 us -> 238 us
    pallas_call x5 -> x8, Pallas kernels: 50.7 us -> 64.1 us  [the longest x3 39.9 us: spread(): pl.pallas_call(ordered(functools.partial(spread_kernel, tile, first), 2 +...]
    ppermute x26 -> x31, waiting for transfers between devices: 59.5 us -> 54 us  [dp_swap(): return lax.ppermute(x, 'dp', [(i, i ^ bit) for i in range(dp)])]
    ppermute x36, waiting for transfers between devices: 72.7 us -> 67.3 us  [head_shift(): lax.ppermute(x, 'head', [(i, (i + step) % heads) for i in range(heads)])]
    ppermute x26 -> x31, starting transfers between devices: 18.4 us -> 23.3 us  [dp_swap(): return lax.ppermute(x, 'dp', [(i, i ^ bit) for i in range(dp)])]
    pallas_call x4 -> x6, Pallas kernels: 22.9 us -> 19 us  [column_call(): pl.pallas_call(ordered(kernel, len(inputs), waits), out_shape=out_shape,...]
    unnamed x108 -> x118, local copies, waits for them, and re-layouts: 12.4 us -> 11.8 us
  transfers between devices with their start and end apart: 66 -> 71, of which waited for: 35 -> 34; matrix products, arithmetic and copies ran while one was open for 5% -> 4% of each run, Pallas kernels for 21% -> 25%
where the time goes in v5:
time: 525 us; the launch traced here: 517 us
  Pallas kernels  238 us (45%)
  waiting for transfers between devices  121 us (23%)
  starting transfers between devices  84.8 us (16%)
  other arithmetic  26.9 us (5%)
  local copies, waits for them, and re-layouts  25.2 us (5%)
  between operations  20.5 us (4%)
    pallas_call x5, Pallas kernels, call(): pl.pallas_call(kernel, out_shape=[jax.ShapeDtypeStruct(shape, dtype) for...  83.3 us
    ppermute x36, waiting for transfers between devices, head_shift(): lax.ppermute(x, 'head', [(i, (i + step) % heads) for i in range(heads)])  67.3 us
    ppermute x36, starting transfers between devices, head_shift(): lax.ppermute(x, 'head', [(i, (i + step) % heads) for i in range(heads)])  61.4 us
    ppermute x31, waiting for transfers between devices, dp_swap(): return lax.ppermute(x, 'dp', [(i, i ^ bit) for i in range(dp)])  54 us
    pallas_call x3, Pallas kernels, spread(): pl.pallas_call(ordered(functools.partial(spread_kernel, tile, first), 2 +...  39.9 us
    ppermute x31, starting transfers between devices, dp_swap(): return lax.ppermute(x, 'dp', [(i, i ^ bit) for i in range(dp)])  23.3 us
    pallas_call x1, Pallas kernels, logits_back(): pl.pallas_call(functools.partial(logits_back_kernel, vocab, tile), out_sh...  21 us
    pallas_call x6, Pallas kernels, column_call(): pl.pallas_call(ordered(kernel, len(inputs), waits), out_shape=out_shape,...  19 us
  transfers between devices with their start and end apart: 71, of which 34 were waited for; matrix products, arithmetic and copies ran while one was open for 4% of the time, Pallas kernels for 25%

profile of v5, /device:TPU:0, one launch (start us, length us, event | category | flops | bytes accessed | tf_op | source)
XLA Modules:
  0.0 517.2 jit_solution(4418356185568716530)
XLA Ops:
  10.6 1.9 shard_map.393
  12.5 2.0 shard_map.392
  14.6 3.0 collective-permute-start
  19.2 3.6 collective-permute-start.2
  23.8 4.7 collective-permute-done.2
  28.5 11.8 %collective-permute-done.3 = bf16[64,1664]{1,0:T(8,128)(2,1)S(1)} collective-permute-done((bf16[64,1664]{1,0:T(8,128)(2,1)S(1)}, bf16[64,1664]{1,0:T(8,128)(2,1)S(1)}, u32[]{:S(2)}, u32[]{:S(2)}) %collective-permute-start.3) | collective-permute-done | bytes 213024 | tf_op jit(solution)/shard_map/ppermute | solution.py:33
  46.0 15.5 %collective-permute-done.5.refs_3_.refs_4_ = bf16[32,8032]{1,0:T(8,128)(2,1)} collective-permute-done((bf16[32,8032]{1,0:T(8,128)(2,1)S(1)}, bf16[32,8032]{1,0:T(8,128)(2,1)}, u32[]{:S(2)}, u32[]{:S(2)}) %collective-permute-start.5) | collective-permute-done | bytes 514080 | tf_op jit(solution)/shard_map/ppermute | solution.py:29
  61.5 2.4 collective-permute-done.6.refs_4_.refs_5_
  65.1 3.9 collective-permute-start.18
  69.9 15.2 %shard_map.394 = (bf16[1152,512]{1,0:T(8,128)(2,1)}, bf16[8064,512]{1,0:T(8,128)(2,1)}) custom-call(s32[1152,1]{1,0:T(8,128)} %bitcast.179, bf16[64,8032]{1,0:T(8,128)(2,1)} %copy-done.6, bf16[64,8032]{1,0:T(8,128)(2,1)} %copy-done.14, bf16[64,8032]{1,0:T(8,128)(2,1)} %copy-done.15, bf16[32,8032]{1,0:T(8,128)(2,1)} %collective-permute-done.5.refs_3_.refs_4_, ...), custom_call_target="tpu_custom_call" | custom-call | flops 29899999232 | bytes 96200000 | tf_op jit(solution)/shard_map/pallas_call | solution.py:163
  85.1 6.6 %collective-permute-done.19 = bf16[64,2048]{1,0:T(8,128)(2,1)S(1)} collective-permute-done((bf16[64,2048]{1,0:T(8,128)(2,1)S(1)}, bf16[64,2048]{1,0:T(8,128)(2,1)S(1)}, u32[]{:S(2)}, u32[]{:S(2)}) %collective-permute-start.19) | collective-permute-done | bytes 262176 | tf_op jit(solution)/shard_map/ppermute | solution.py:33
  97.5 2.0 collective-permute-start.13
  99.5 2.8 collective-permute-start.14
  102.3 11.2 %shard_map.395 = bf16[896,512]{1,0:T(8,128)(2,1)} custom-call(s32[896,1]{1,0:T(8,128)} %reshape.421.refs_0_, bf16[8064,512]{1,0:T(8,128)(2,1)} %get-tuple-element.137.refs_1_.table_ref.refs_0_, bf16[1152,512]{1,0:T(8,128)(2,1)} %get-tuple-element.138.refs_2_), custom_call_target="tpu_custom_call" | custom-call | flops 13799999488 | bytes 44400000 | tf_op jit(solution)/shard_map/pallas_call | solution.py:181
  113.6 12.5 %collective-permute-done.13 = bf16[384,512]{1,0:T(8,128)(2,1)S(1)} collective-permute-done((bf16[384,512]{1,0:T(8,128)(2,1)S(1)}, bf16[384,512]{1,0:T(8,128)(2,1)S(1)}, u32[]{:S(2)}, u32[]{:S(2)}) %collective-permute-start.13) | collective-permute-done | bytes 393248 | tf_op jit(solution)/shard_map/ppermute | solution.py:33
  126.1 2.1 fusion.4.x_ref
  128.2 8.3 %collective-permute-start.15 = (bf16[128,512]{1,0:T(8,128)(2,1)S(1)}, bf16[128,512]{1,0:T(8,128)(2,1)S(1)}, u32[]{:S(2)}, u32[]{:S(2)}) collective-permute-start(bf16[128,512]{1,0:T(8,128)(2,1)S(1)} %get-tuple-element.350), channel_id=1, source_target_pairs={{0,1},{1,2},{2,3},{3,0},{4,5},{5,6},{6,7},{7,4},{8,9},{9,10},{10,1... | collective-permute-start | bytes 393224 | tf_op jit(solution)/shard_map/ppermute | solution.py:33
  136.5 2.3 collective-permute-start.16
  141.6 14.1 %shard_map.396 = (bf16[4,384,512]{2,1,0:T(8,128)(2,1)}, f32[384,512]{1,0:T(8,128)}, bf16[4,384,512]{2,1,0:T(8,128)(2,1)}, f32[384,512]{1,0:T(8,128)}, bf16[384,512]{1,0:T(8,128)(2,1)}) custom-call(s32[8]{0:T(128)} %broadcast_xor_fusion.order, s32[1]{0:T(128)} %bitcast.14.head, s32[1]{0:T(128)} %dynamic_slice.19.lens, f32[384,512]{1,0:T(8,128)} %fusion.4.x_ref, ...), custom_call_target="tpu_custom_call" | custom-call | flops 16099999744 | bytes 51800000 | tf_op jit(solution)/shard_map/pallas_call | solution.py:858
  157.2 15.6 %shard_map.397 = (bf16[4,128,512]{2,1,0:T(8,128)(2,1)}, f32[128,512]{1,0:T(8,128)}, bf16[4,128,256]{2,1,0:T(8,128)(2,1)}, bf16[4,384,256]{2,1,0:T(8,128)(2,1)}, ...) custom-call(s32[8]{0:T(128)} %broadcast_xor_fusion.order, ...), custom_call_target="tpu_custom_call" | custom-call | flops 18400000000 | bytes 59200000 | tf_op jit(solution)/shard_map/pallas_call | solution.py:858
  173.9 2.0 collective-permute-start.21
  179.8 8.8 %collective-permute-done.22 = bf16[128,512]{0,1:T(8,128)(2,1)S(1)} collective-permute-done((bf16[128,512]{0,1:T(8,128)(2,1)S(1)}, bf16[128,512]{0,1:T(8,128)(2,1)S(1)}, u32[]{:S(2)}, u32[]{:S(2)}) %collective-permute-start.22) | collective-permute-done | bytes 131104 | tf_op jit(solution)/shard_map/ppermute | solution.py:33
  189.7 16.7 %shard_map.398 = f32[8,512]{1,0:T(8,128)} custom-call(bf16[512,512]{1,0:T(8,128)(2,1)} %dynamic-slice_bitcast_fusion.final_ref.refs_0_, s32[1,512]{1,0:T(1,128)} %and_select_fusion.label_ref, bf16[8032,512]{1,0:T(8,128)(2,1)} %bitcast.238, bf16[8064,512]{1,0:T(8,128)(2,1)} %get-tuple-element.137.refs_1_.table_ref.refs_0_), custom_call_target="tpu_custom_call" | custom-call | flops 19549999104 | bytes 62900000 | tf_op jit(solution)/shard_map/pallas_call | solution.py:521
  207.1 2.0 collective-permute-start.26
  216.1 21.0 %shard_map.399 = (bf16[8064,512]{1,0:T(8,128)(2,1)}, bf16[512,512]{1,0:T(8,128)(2,1)}) custom-call(bf16[512,512]{1,0:T(8,128)(2,1)} %dynamic-slice_bitcast_fusion.final_ref.refs_0_, s32[1,512]{1,0:T(1,128)} %and_select_fusion.label_ref, f32[8,512]{1,0:T(8,128)} %stack.71.scalar_ref, bf16[8032,512]{1,0:T(8,128)(2,1)} %bitcast.239, ...), custom_call_target="tpu_custom_call" | custom-call | flops 25300000768 | bytes 81400000 | tf_op jit(solution)/shard_map/pallas_call | solution.py:583
  239.1 2.0 collective-permute-start.28
  242.6 4.3 collective-permute-done.27
  246.9 3.3 collective-permute-done.28
  250.9 23.9 %shard_map.400 = (bf16[8,4,64,2048]{3,2,1,0:T(8,128)(2,1)}, f32[8,512]{1,0:T(8,128)}, f32[384,512]{1,0:T(8,128)}, bf16[128,512]{1,0:T(8,128)(2,1)}) custom-call(s32[8]{0:T(128)} %broadcast_xor_fusion.order, s32[1]{0:T(128)} %bitcast.14.head, s32[1]{0:T(128)} %dynamic_slice.19.lens, f32[128,512]{1,0:T(8,128)} %fusion.6.refs_0_, ...), custom_call_target="tpu_custom_call" | custom-call | flops 27599998976 | bytes 88800000 | tf_op jit(solution)/shard_map/pallas_call | solution.py:858
  275.7 2.9 collective-permute-start.30
  279.7 13.7 %shard_map.401 = (f32[1,4,64,1024]{3,2,1,0:T(8,128)}, f32[1,4,64,1024]{3,2,1,0:T(8,128)}, f32[1,4,64,1024]{3,2,1,0:T(8,128)}, f32[1,4,64,1024]{3,2,1,0:T(8,128)}...) custom-call(s32[8]{0:T(128)} %broadcast_xor_fusion.order, s32[1]{0:T(128)} %bitcast.14.head, ...), custom_call_target="tpu_custom_call" | custom-call | flops 14949999616 | bytes 48100000 | tf_op jit(solution)/shard_map/pallas_call | solution.py:858
  293.5 16.1 %shard_map.402 = (f32[1,4,64,640]{3,2,1,0:T(8,128)}, f32[1,4,64,640]{3,2,1,0:T(8,128)}, f32[1,4,64,640]{3,2,1,0:T(8,128)}, f32[1,4,64,640]{3,2,1,0:T(8,128)}, bf...) custom-call(s32[8]{0:T(128)} %broadcast_xor_fusion.order, s32[1]{0:T(128)} %bitcast.14.head, ...), custom_call_target="tpu_custom_call" | custom-call | flops 18400000000 | bytes 59200000 | tf_op jit(solution)/shard_map/pallas_call | solution.py:858
  311.0 1.9 collective-permute-done.34.refs_7_.refs_3_
  314.6 5.8 %shard_map.403 = (bf16[128,1664]{1,0:T(8,128)(2,1)}, bf16[128,1664]{1,0:T(8,128)(2,1)}, f32[256,1664]{1,0:T(8,128)}, f32[256,1664]{1,0:T(8,128)}) custom-call(f32[256,1024]{1,0:T(8,128)} %bitcast.253, f32[256,1024]{1,0:T(8,128)} %bitcast.254, f32[256,1024]{1,0:T(8,128)} %bitcast.255, bf16[1024,1024]{1,0:T(8,128)(2,1)} %copy-done.33, f32[256,640]{1,0:T(8,128)} %bitcast.257, ...), custom_call_target="tpu_custom_call" | custom-call | flops 5750000128 | bytes 18500000 | tf_op jit(solution)/shard_map/pallas_call | solution.py:420
  321.0 4.1 collective-permute-start.35
  325.8 7.0 %collective-permute-done.38.got_a = bf16[128,1664]{1,0:T(8,128)(2,1)S(1)} collective-permute-done((bf16[128,1664]{1,0:T(8,128)(2,1)}, bf16[128,1664]{1,0:T(8,128)(2,1)S(1)}, u32[]{:S(2)}, u32[]{:S(2)}) %collective-permute-start.38) | collective-permute-done | bytes 426016 | tf_op jit(solution)/shard_map/ppermute | solution.py:29
  334.3 3.5 shard_map.405
  339.5 18.6 %shard_map.404.refs_2_ = f32[512,8064]{1,0:T(8,128)} custom-call(s32[896,1]{1,0:T(8,128)} %reshape.422.ids_ref, bf16[896,512]{1,0:T(8,128)(2,1)} %copy-done.20, bf16[512,512]{1,0:T(8,128)(2,1)} %dynamic-slice_bitcast_fusion.final_ref.refs_0_, bf16[8064,512]{1,0:T(8,128)(2,1)} %get-tuple-element.180.refs_1_), custom_call_target="tpu_custom_call" | custom-call | flops 20700000256 | bytes 66600000 | tf_op jit(solution)/shard_map/pallas_call | solution.py:252
  359.7 2.7 collective-permute-done.40.refs_4_
  363.7 10.5 %shard_map.406 = (f32[64,4096]{1,0:T(8,128)}, f32[64,4096]{1,0:T(8,128)}, f32[64,4096]{1,0:T(8,128)}, f32[64,4096]{1,0:T(8,128)}, bf16[256,4096]{1,0:T(8,128)(2,1)}) custom-call(s32[1152,1]{1,0:T(8,128)} %bitcast.180, bf16[1152,512]{1,0:T(8,128)(2,1)} %copy-done.17, f32[512,8064]{1,0:T(8,128)} %shard_map.404.refs_2_, bf16[4,64,2048]{2,1,0:T(8,128)(2,1)} %bitcast.177, ...), custom_call_target="tpu_custom_call" | custom-call | flops 10350000128 | bytes 33300000 | tf_op jit(solution)/shard_map/pallas_call | solution.py:252
  374.3 10.8 %shard_map.407 = (f32[64,3968]{1,0:T(8,128)}, f32[64,3968]{1,0:T(8,128)}, f32[64,3968]{1,0:T(8,128)}, f32[64,3968]{1,0:T(8,128)}, bf16[256,3968]{1,0:T(8,128)(2,1)}) custom-call(s32[1152,1]{1,0:T(8,128)} %bitcast.181, bf16[1152,512]{1,0:T(8,128)(2,1)} %copy-done.17, f32[512,8064]{1,0:T(8,128)} %shard_map.404.refs_2_, ...), custom_call_target="tpu_custom_call" | custom-call | flops 10350000128 | bytes 33300000 | tf_op jit(solution)/shard_map/pallas_call | solution.py:252
  388.0 3.7 shard_map.408
  393.7 3.8 shard_map.409
  400.4 1.8 collective-permute-done.47.got_b
  403.0 2.6 shard_map.410
  405.6 4.5 shard_map.412
  413.4 2.5 shard_map.411
  419.2 7.5 %collective-permute-done.50.refs_3_ = bf16[64,4096]{1,0:T(8,128)(2,1)S(1)} collective-permute-done((bf16[64,4096]{1,0:T(8,128)(2,1)S(1)}, bf16[64,4096]{1,0:T(8,128)(2,1)S(1)}, u32[]{:S(2)}, u32[]{:S(2)}) %collective-permute-start.50) | collective-permute-done | bytes 524320 | tf_op jit(solution)/shard_map/ppermute | solution.py:29
  426.7 3.0 collective-permute-start.51
  429.7 1.8 collective-permute-start.52
  432.2 3.1 shard_map.413
  435.5 6.7 %collective-permute-done.52 = bf16[64,1664]{1,0:T(8,128)(2,1)S(1)} collective-permute-done((bf16[64,1664]{1,0:T(8,128)(2,1)S(1)}, bf16[64,1664]{1,0:T(8,128)(2,1)S(1)}, u32[]{:S(2)}, u32[]{:S(2)}) %collective-permute-start.52) | collective-permute-done | bytes 213024 | tf_op jit(solution)/shard_map/ppermute | solution.py:33
  443.6 1.7 multiply_reduce_fusion.1
  448.8 3.2 shard_map.414
  454.7 2.9 collective-permute-done.56
  458.5 2.7 collective-permute-done.57
  461.2 2.8 collective-permute-start.58
  472.3 8.0 %shard_map.415 = (f32[64,8032]{1,0:T(8,128)}, f32[64,8032]{1,0:T(8,128)}, f32[64,8032]{1,0:T(8,128)}, f32[8,128]{1,0:T(8,128)}) custom-call(f32[64,8032]{1,0:T(8,128)} %bitcast.173, f32[64,8032]{1,0:T(8,128)} %bitcast.241, f32[64,8032]{1,0:T(8,128)} %bitcast.242, f32[64,4096]{1,0:T(8,128)} %get-tuple-element.221.refs_3_, ...), custom_call_target="tpu_custom_call" | custom-call | flops 9200000000 | bytes 29600000 | tf_op jit(solution)/shard_map/pallas_call | solution.py:639
  480.3 3.9 shard_map.416
  488.5 2.1 collective-permute-done.62
  491.9 2.5 collective-permute-done.63
  494.7 3.2 collective-permute-start.65
  503.8 3.1 subtract_bitcast_fusion
  506.9 2.4 shard_map.417
  (328 shorter events, 94.1 us)
Async XLA Ops:
  7.2 132.0 %all-gather.5.cloned.1.call-start = ((), (), s32[]{:S(2)}) async-start(), calls=%async_computation.4 | async-start | bytes 7667712 | tf_op jit(solution)/shard_map/all_gather | solution.py:1274
  14.6 25.8 %collective-permute-start = (bf16[64,8032]{1,0:T(8,128)(2,1)S(1)}, bf16[64,8032]{1,0:T(8,128)(2,1)S(1)}, u32[]{:S(2)}, u32[]{:S(2)}) collective-permute-start(bf16[64,8032]{1,0:T(8,128)(2,1)S(1)} %bitcast_convert_fusion.1.refs_0_.refs_1_), channel_id=1, source_target_pairs={{0,16},{4,20},{8,24},{12,28},{16,0},{20,4},{24,8},{28,12},{1,17},{... | collective-permute-start | bytes 3084296 | tf_op jit(solution)/shard_map/ppermute | solution.py:29
  17.7 24.3 %collective-permute-start.1 = (bf16[64,8032]{1,0:T(8,128)(2,1)S(1)}, bf16[64,8032]{1,0:T(8,128)(2,1)S(1)}, u32[]{:S(2)}, u32[]{:S(2)}) collective-permute-start(bf16[64,8032]{1,0:T(8,128)(2,1)S(1)} %bitcast_convert_fusion.1.refs_0_.refs_1_), channel_id=1, source_target_pairs={{0,8},{4,12},{8,0},{12,4},{16,24},{20,28},{24,16},{28,20},{1,9},{5... | collective-permute-start | bytes 3084296 | tf_op jit(solution)/shard_map/ppermute | solution.py:29
  19.2 9.4 %collective-permute-start.2 = (bf16[64,1664]{1,0:T(8,128)(2,1)S(1)}, bf16[64,1664]{1,0:T(8,128)(2,1)S(1)}, u32[]{:S(2)}, u32[]{:S(2)}) collective-permute-start(bf16[64,1664]{1,0:T(8,128)(2,1)S(1)} %copy-done.16), channel_id=1, source_target_pairs={{0,3},{1,0},{2,1},{3,2},{4,7},{5,4},{6,5},{7,6},{8,11},{9,8},{10,9... | collective-permute-start | bytes 638984 | tf_op jit(solution)/shard_map/ppermute | solution.py:33
  22.8 17.5 %collective-permute-start.3 = (bf16[64,1664]{1,0:T(8,128)(2,1)S(1)}, bf16[64,1664]{1,0:T(8,128)(2,1)S(1)}, u32[]{:S(2)}, u32[]{:S(2)}) collective-permute-start(bf16[64,1664]{1,0:T(8,128)(2,1)S(1)} %copy-done.16), channel_id=1, source_target_pairs={{0,2},{1,3},{2,0},{3,1},{4,6},{5,7},{6,4},{7,5},{8,10},{9,11},{10,... | collective-permute-start | bytes 638984 | tf_op jit(solution)/shard_map/ppermute | solution.py:33
  22.8 17.5 %collective-permute-start.4 = (bf16[64,1664]{1,0:T(8,128)(2,1)S(1)}, bf16[64,1664]{1,0:T(8,128)(2,1)S(1)}, u32[]{:S(2)}, u32[]{:S(2)}) collective-permute-start(bf16[64,1664]{1,0:T(8,128)(2,1)S(1)} %copy-done.16), channel_id=1, source_target_pairs={{0,1},{1,2},{2,3},{3,0},{4,5},{5,6},{6,7},{7,4},{8,9},{9,10},{10,1... | collective-permute-start | bytes 638984 | tf_op jit(solution)/shard_map/ppermute | solution.py:33
  43.1 114.2 %all-gather.7.cloned.1.call-start = ((), (), s32[]{:S(2)}) async-start(), calls=%async_computation.5 | async-start | bytes 9437184 | tf_op jit(solution)/shard_map/all_gather | solution.py:1289
  43.1 21.9 %collective-permute-start.7 = (bf16[64,8032]{1,0:T(8,128)(2,1)S(1)}, bf16[64,8032]{1,0:T(8,128)(2,1)}, u32[]{:S(2)}, u32[]{:S(2)}) collective-permute-start(bf16[64,8032]{1,0:T(8,128)(2,1)S(1)} %bitcast_convert_fusion.1.refs_0_.refs_1_), channel_id=1, source_target_pairs={{0,4},{4,0},{8,12},{12,8},{16,20},{20,16},{24,28},{28,24},{1,5},{5... | collective-permute-start | bytes 3084296 | tf_op jit(solution)/shard_map/ppermute | solution.py:29
  43.3 18.2 %collective-permute-start.5 = (bf16[32,8032]{1,0:T(8,128)(2,1)S(1)}, bf16[32,8032]{1,0:T(8,128)(2,1)}, u32[]{:S(2)}, u32[]{:S(2)}) collective-permute-start(bf16[32,8032]{1,0:T(8,128)(2,1)S(1)} %slice.153), channel_id=1, source_target_pairs={{0,8},{4,12},{8,0},{12,4},{16,24},{20,28},{24,16},{28,20},{1,9},{5... | collective-permute-start | bytes 1542152 | tf_op jit(solution)/shard_map/ppermute | solution.py:29
  44.9 19.1 %collective-permute-start.6 = (bf16[32,8032]{1,0:T(8,128)(2,1)S(1)}, bf16[32,8032]{1,0:T(8,128)(2,1)}, u32[]{:S(2)}, u32[]{:S(2)}) collective-permute-start(bf16[32,8032]{1,0:T(8,128)(2,1)S(1)} %slice.154), channel_id=1, source_target_pairs={{0,16},{4,20},{8,24},{12,28},{16,0},{20,4},{24,8},{28,12},{1,17},{... | collective-permute-start | bytes 1542152 | tf_op jit(solution)/shard_map/ppermute | solution.py:29
  45.5 24.3 %collective-permute-start.8 = (bf16[64,8032]{1,0:T(8,128)(2,1)S(1)}, bf16[64,8032]{1,0:T(8,128)(2,1)}, u32[]{:S(2)}, u32[]{:S(2)}) collective-permute-start(bf16[64,8032]{1,0:T(8,128)(2,1)S(1)} %collective-permute-done.refs_1_.refs_2_), channel_id=1, source_target_pairs={{0,4},{4,0},{8,12},{12,8},{16,20},{20,16},{24,28},{28,24},{1,5},{5... | collective-permute-start | bytes 3084296 | tf_op jit(solution)/shard_map/ppermute | solution.py:29
  45.5 24.3 %collective-permute-start.9 = (bf16[64,8032]{1,0:T(8,128)(2,1)S(1)}, bf16[64,8032]{1,0:T(8,128)(2,1)}, u32[]{:S(2)}, u32[]{:S(2)}) collective-permute-start(bf16[64,8032]{1,0:T(8,128)(2,1)S(1)} %collective-permute-done.1.refs_2_.refs_3_), channel_id=1, source_target_pairs={{0,4},{4,0},{8,12},{12,8},{16,20},{20,16},{24,28},{28,24},{1,5},{5... | collective-permute-start | bytes 3084296 | tf_op jit(solution)/shard_map/ppermute | solution.py:29
  61.5 7.4 %collective-permute-start.10 = (bf16[32,8032]{1,0:T(8,128)(2,1)}, bf16[32,8032]{1,0:T(8,128)(2,1)}, u32[]{:S(2)}, u32[]{:S(2)}) collective-permute-start(bf16[32,8032]{1,0:T(8,128)(2,1)} %collective-permute-done.5.refs_3_.refs_4_), channel_id=1, source_target_pairs={{0,4},{4,0},{8,12},{12,8},{16,20},{20,16},{24,28},{28,24},{1,5},{5... | collective-permute-start | bytes 1542152 | tf_op jit(solution)/shard_map/ppermute | solution.py:29
  63.9 5.0 collective-permute-start.11
  65.1 20.0 %collective-permute-start.18 = (bf16[64,2048]{1,0:T(8,128)(2,1)S(1)}, bf16[64,2048]{1,0:T(8,128)(2,1)S(1)}, u32[]{:S(2)}, u32[]{:S(2)}) collective-permute-start(bf16[64,2048]{1,0:T(8,128)(2,1)S(1)} %copy-done.13), channel_id=1, source_target_pairs={{0,3},{1,0},{2,1},{3,2},{4,7},{5,4},{6,5},{7,6},{8,11},{9,8},{10,9... | collective-permute-start | bytes 786440 | tf_op jit(solution)/shard_map/ppermute | solution.py:33
  69.0 22.8 %collective-permute-start.19 = (bf16[64,2048]{1,0:T(8,128)(2,1)S(1)}, bf16[64,2048]{1,0:T(8,128)(2,1)S(1)}, u32[]{:S(2)}, u32[]{:S(2)}) collective-permute-start(bf16[64,2048]{1,0:T(8,128)(2,1)S(1)} %copy-done.13), channel_id=1, source_target_pairs={{0,2},{1,3},{2,0},{3,1},{4,6},{5,7},{6,4},{7,5},{8,10},{9,11},{10,... | collective-permute-start | bytes 786440 | tf_op jit(solution)/shard_map/ppermute | solution.py:33
  69.0 22.8 %collective-permute-start.20 = (bf16[64,2048]{1,0:T(8,128)(2,1)S(1)}, bf16[64,2048]{1,0:T(8,128)(2,1)S(1)}, u32[]{:S(2)}, u32[]{:S(2)}) collective-permute-start(bf16[64,2048]{1,0:T(8,128)(2,1)S(1)} %copy-done.13), channel_id=1, source_target_pairs={{0,1},{1,2},{2,3},{3,0},{4,5},{5,6},{6,7},{7,4},{8,9},{9,10},{10,1... | collective-permute-start | bytes 786440 | tf_op jit(solution)/shard_map/ppermute | solution.py:33
  92.9 269.6 %reduce-scatter.3.cloned.1.call-start = ((), (), s32[]{:S(2)}) async-start(), calls=%async_computation.2 | async-start | bytes 9437184 | tf_op jit(solution)/shard_map/reduce_scatter | solution.py:1356
  96.4 17.1 %collective-permute-start.12 = (bf16[384,512]{1,0:T(8,128)(2,1)S(1)}, bf16[384,512]{1,0:T(8,128)(2,1)S(1)}, u32[]{:S(2)}, u32[]{:S(2)}) collective-permute-start(bf16[384,512]{1,0:T(8,128)(2,1)S(1)} %get-tuple-element.341), channel_id=1, source_target_pairs={{0,1},{1,2},{2,3},{3,0},{4,5},{5,6},{6,7},{7,4},{8,9},{9,10},{10,1... | collective-permute-start | bytes 1179656 | tf_op jit(solution)/shard_map/ppermute | solution.py:33
  97.5 28.6 %collective-permute-start.13 = (bf16[384,512]{1,0:T(8,128)(2,1)S(1)}, bf16[384,512]{1,0:T(8,128)(2,1)S(1)}, u32[]{:S(2)}, u32[]{:S(2)}) collective-permute-start(bf16[384,512]{1,0:T(8,128)(2,1)S(1)} %get-tuple-element.343), channel_id=1, source_target_pairs={{0,2},{1,3},{2,0},{3,1},{4,6},{5,7},{6,4},{7,5},{8,10},{9,11},{10,... | collective-permute-start | bytes 1179656 | tf_op jit(solution)/shard_map/ppermute | solution.py:33
  99.5 26.6 %collective-permute-start.14 = (bf16[384,512]{1,0:T(8,128)(2,1)S(1)}, bf16[384,512]{1,0:T(8,128)(2,1)S(1)}, u32[]{:S(2)}, u32[]{:S(2)}) collective-permute-start(bf16[384,512]{1,0:T(8,128)(2,1)S(1)} %get-tuple-element.342), channel_id=1, source_target_pairs={{0,3},{1,0},{2,1},{3,2},{4,7},{5,4},{6,5},{7,6},{8,11},{9,8},{10,9... | collective-permute-start | bytes 1179656 | tf_op jit(solution)/shard_map/ppermute | solution.py:33
  128.2 28.3 %collective-permute-start.15 = (bf16[128,512]{1,0:T(8,128)(2,1)S(1)}, bf16[128,512]{1,0:T(8,128)(2,1)S(1)}, u32[]{:S(2)}, u32[]{:S(2)}) collective-permute-start(bf16[128,512]{1,0:T(8,128)(2,1)S(1)} %get-tuple-element.350), channel_id=1, source_target_pairs={{0,1},{1,2},{2,3},{3,0},{4,5},{5,6},{6,7},{7,4},{8,9},{9,10},{10,1... | collective-permute-start | bytes 393224 | tf_op jit(solution)/shard_map/ppermute | solution.py:33
  136.5 20.0 %collective-permute-start.16 = (bf16[128,512]{1,0:T(8,128)(2,1)S(1)}, bf16[128,512]{1,0:T(8,128)(2,1)S(1)}, u32[]{:S(2)}, u32[]{:S(2)}) collective-permute-start(bf16[128,512]{1,0:T(8,128)(2,1)S(1)} %get-tuple-element.352), channel_id=1, source_target_pairs={{0,2},{1,3},{2,0},{3,1},{4,6},{5,7},{6,4},{7,5},{8,10},{9,11},{10,... | collective-permute-start | bytes 393224 | tf_op jit(solution)/shard_map/ppermute | solution.py:33
  138.8 17.7 %collective-permute-start.17 = (bf16[128,512]{1,0:T(8,128)(2,1)S(1)}, bf16[128,512]{1,0:T(8,128)(2,1)S(1)}, u32[]{:S(2)}, u32[]{:S(2)}) collective-permute-start(bf16[128,512]{1,0:T(8,128)(2,1)S(1)} %get-tuple-element.351), channel_id=1, source_target_pairs={{0,3},{1,0},{2,1},{3,2},{4,7},{5,4},{6,5},{7,6},{8,11},{9,8},{10,9... | collective-permute-start | bytes 393224 | tf_op jit(solution)/shard_map/ppermute | solution.py:33
  173.9 5.9 %collective-permute-start.21 = (bf16[128,512]{0,1:T(8,128)(2,1)S(1)}, bf16[128,512]{0,1:T(8,128)(2,1)S(1)}, u32[]{:S(2)}, u32[]{:S(2)}) collective-permute-start(bf16[128,512]{0,1:T(8,128)(2,1)S(1)} %copy.131), channel_id=1, source_target_pairs={{0,3},{1,0},{2,1},{3,2},{4,7},{5,4},{6,5},{7,6},{8,11},{9,8},{10,9... | collective-permute-start | bytes 393224 | tf_op jit(solution)/shard_map/ppermute | solution.py:33
  177.1 11.4 %collective-permute-start.22 = (bf16[128,512]{0,1:T(8,128)(2,1)S(1)}, bf16[128,512]{0,1:T(8,128)(2,1)S(1)}, u32[]{:S(2)}, u32[]{:S(2)}) collective-permute-start(bf16[128,512]{0,1:T(8,128)(2,1)S(1)} %copy.131), channel_id=1, source_target_pairs={{0,2},{1,3},{2,0},{3,1},{4,6},{5,7},{6,4},{7,5},{8,10},{9,11},{10,... | collective-permute-start | bytes 393224 | tf_op jit(solution)/shard_map/ppermute | solution.py:33
  178.6 10.1 %collective-permute-start.23 = (bf16[128,512]{0,1:T(8,128)(2,1)S(1)}, bf16[128,512]{0,1:T(8,128)(2,1)S(1)}, u32[]{:S(2)}, u32[]{:S(2)}) collective-permute-start(bf16[128,512]{0,1:T(8,128)(2,1)S(1)} %copy.131), channel_id=1, source_target_pairs={{0,1},{1,2},{2,3},{3,0},{4,5},{5,6},{6,7},{7,4},{8,9},{9,10},{10,1... | collective-permute-start | bytes 393224 | tf_op jit(solution)/shard_map/ppermute | solution.py:33
  206.4 3.9 collective-permute-start.24
  206.4 4.8 collective-permute-start.25
  207.1 5.8 %collective-permute-start.26 = (f32[8,512]{1,0:T(8,128)}, f32[8,512]{1,0:T(8,128)S(1)}, u32[]{:S(2)}, u32[]{:S(2)}) collective-permute-start(f32[8,512]{1,0:T(8,128)} %shard_map.398), channel_id=1, source_target_pairs={{0,1},{1,2},{2,3},{3,0},{4,5},{5,6},{6,7},{7,4},{8,9},{9,10},{10,1... | collective-permute-start | bytes 49160 | tf_op jit(solution)/shard_map/ppermute | solution.py:33
  238.6 8.3 %collective-permute-start.27 = (bf16[128,512]{1,0:T(8,128)(2,1)S(1)}, bf16[128,512]{1,0:T(8,128)(2,1)S(1)}, u32[]{:S(2)}, u32[]{:S(2)}) collective-permute-start(bf16[128,512]{1,0:T(8,128)(2,1)S(1)} %get-tuple-element.347), channel_id=1, source_target_pairs={{0,1},{1,2},{2,3},{3,0},{4,5},{5,6},{6,7},{7,4},{8,9},{9,10},{10,1... | collective-permute-start | bytes 393224 | tf_op jit(solution)/shard_map/ppermute | solution.py:33
  239.1 11.1 %collective-permute-start.28 = (bf16[128,512]{1,0:T(8,128)(2,1)S(1)}, bf16[128,512]{1,0:T(8,128)(2,1)S(1)}, u32[]{:S(2)}, u32[]{:S(2)}) collective-permute-start(bf16[128,512]{1,0:T(8,128)(2,1)S(1)} %get-tuple-element.348), channel_id=1, source_target_pairs={{0,2},{1,3},{2,0},{3,1},{4,6},{5,7},{6,4},{7,5},{8,10},{9,11},{10,... | collective-permute-start | bytes 393224 | tf_op jit(solution)/shard_map/ppermute | solution.py:33
  241.1 9.1 %collective-permute-start.29 = (bf16[128,512]{1,0:T(8,128)(2,1)S(1)}, bf16[128,512]{1,0:T(8,128)(2,1)S(1)}, u32[]{:S(2)}, u32[]{:S(2)}) collective-permute-start(bf16[128,512]{1,0:T(8,128)(2,1)S(1)} %get-tuple-element.349), channel_id=1, source_target_pairs={{0,3},{1,0},{2,1},{3,2},{4,7},{5,4},{6,5},{7,6},{8,11},{9,8},{10,9... | collective-permute-start | bytes 393224 | tf_op jit(solution)/shard_map/ppermute | solution.py:33
  274.8 160.5 %reduce-scatter.5.cloned.1.call-start = ((), (), s32[]{:S(2)}) async-start(), calls=%async_computation.3 | async-start | bytes 1310720 | tf_op jit(solution)/shard_map/reduce_scatter | solution.py:1358
  275.7 17.7 %collective-permute-start.30 = (bf16[128,512]{1,0:T(8,128)(2,1)S(1)}, bf16[128,512]{1,0:T(8,128)(2,1)S(1)}, u32[]{:S(2)}, u32[]{:S(2)}) collective-permute-start(bf16[128,512]{1,0:T(8,128)(2,1)S(1)} %copy-done.18), channel_id=1, source_target_pairs={{0,3},{1,0},{2,1},{3,2},{4,7},{5,4},{6,5},{7,6},{8,11},{9,8},{10,9... | collective-permute-start | bytes 393224 | tf_op jit(solution)/shard_map/ppermute | solution.py:33
  278.6 14.9 %collective-permute-start.31 = (bf16[128,512]{1,0:T(8,128)(2,1)S(1)}, bf16[128,512]{1,0:T(8,128)(2,1)S(1)}, u32[]{:S(2)}, u32[]{:S(2)}) collective-permute-start(bf16[128,512]{1,0:T(8,128)(2,1)S(1)} %copy-done.18), channel_id=1, source_target_pairs={{0,2},{1,3},{2,0},{3,1},{4,6},{5,7},{6,4},{7,5},{8,10},{9,11},{10,... | collective-permute-start | bytes 393224 | tf_op jit(solution)/shard_map/ppermute | solution.py:33
  279.5 13.9 %collective-permute-start.32 = (bf16[128,512]{1,0:T(8,128)(2,1)S(1)}, bf16[128,512]{1,0:T(8,128)(2,1)S(1)}, u32[]{:S(2)}, u32[]{:S(2)}) collective-permute-start(bf16[128,512]{1,0:T(8,128)(2,1)S(1)} %copy-done.18), channel_id=1, source_target_pairs={{0,1},{1,2},{2,3},{3,0},{4,5},{5,6},{6,7},{7,4},{8,9},{9,10},{10,1... | collective-permute-start | bytes 393224 | tf_op jit(solution)/shard_map/ppermute | solution.py:33
  293.4 19.5 %collective-permute-start.33 = (bf16[1024,1024]{1,0:T(8,128)(2,1)}, bf16[1024,1024]{1,0:T(8,128)(2,1)S(1)}, u32[]{:S(2)}, u32[]{:S(2)}) collective-permute-start(bf16[1024,1024]{1,0:T(8,128)(2,1)} %bitcast.240), channel_id=1, source_target_pairs={{0,4},{4,0},{8,12},{12,8},{16,20},{20,16},{24,28},{28,24},{1,5},{5... | collective-permute-start | bytes 6291464 | tf_op jit(solution)/shard_map/ppermute | solution.py:29
  320.5 12.3 %collective-permute-start.38 = (bf16[128,1664]{1,0:T(8,128)(2,1)}, bf16[128,1664]{1,0:T(8,128)(2,1)S(1)}, u32[]{:S(2)}, u32[]{:S(2)}) collective-permute-start(bf16[128,1664]{1,0:T(8,128)(2,1)} %get-tuple-element.183), channel_id=1, source_target_pairs={{0,8},{4,12},{8,0},{12,4},{16,24},{20,28},{24,16},{28,20},{1,9},{5... | collective-permute-start | bytes 1277960 | tf_op jit(solution)/shard_map/ppermute | solution.py:29
  320.5 12.4 %collective-permute-start.39 = (bf16[128,1664]{1,0:T(8,128)(2,1)}, bf16[128,1664]{1,0:T(8,128)(2,1)S(1)}, u32[]{:S(2)}, u32[]{:S(2)}) collective-permute-start(bf16[128,1664]{1,0:T(8,128)(2,1)} %get-tuple-element.185), channel_id=1, source_target_pairs={{0,16},{4,20},{8,24},{12,28},{16,0},{20,4},{24,8},{28,12},{1,17},{... | collective-permute-start | bytes 1277960 | tf_op jit(solution)/shard_map/ppermute | solution.py:29
  321.0 37.1 %collective-permute-start.35 = (bf16[384,512]{1,0:T(8,128)(2,1)S(1)}, bf16[384,512]{1,0:T(8,128)(2,1)S(1)}, u32[]{:S(2)}, u32[]{:S(2)}) collective-permute-start(bf16[384,512]{1,0:T(8,128)(2,1)S(1)} %copy-done.7), channel_id=1, source_target_pairs={{0,3},{1,0},{2,1},{3,2},{4,7},{5,4},{6,5},{7,6},{8,11},{9,8},{10,9... | collective-permute-start | bytes 1179656 | tf_op jit(solution)/shard_map/ppermute | solution.py:33
  325.1 34.5 %collective-permute-start.36 = (bf16[384,512]{1,0:T(8,128)(2,1)S(1)}, bf16[384,512]{1,0:T(8,128)(2,1)S(1)}, u32[]{:S(2)}, u32[]{:S(2)}) collective-permute-start(bf16[384,512]{1,0:T(8,128)(2,1)S(1)} %copy-done.7), channel_id=1, source_target_pairs={{0,2},{1,3},{2,0},{3,1},{4,6},{5,7},{6,4},{7,5},{8,10},{9,11},{10,... | collective-permute-start | bytes 1179656 | tf_op jit(solution)/shard_map/ppermute | solution.py:33
  325.3 34.4 %collective-permute-start.37 = (bf16[384,512]{1,0:T(8,128)(2,1)S(1)}, bf16[384,512]{1,0:T(8,128)(2,1)S(1)}, u32[]{:S(2)}, u32[]{:S(2)}) collective-permute-start(bf16[384,512]{1,0:T(8,128)(2,1)S(1)} %copy-done.7), channel_id=1, source_target_pairs={{0,1},{1,2},{2,3},{3,0},{4,5},{5,6},{6,7},{7,4},{8,9},{9,10},{10,1... | collective-permute-start | bytes 1179656 | tf_op jit(solution)/shard_map/ppermute | solution.py:33
  337.8 24.6 %collective-permute-start.40 = (bf16[256,1664]{1,0:T(8,128)(2,1)}, bf16[256,1664]{1,0:T(8,128)(2,1)S(1)}, u32[]{:S(2)}, u32[]{:S(2)}) collective-permute-start(bf16[256,1664]{1,0:T(8,128)(2,1)} %get-tuple-element.186), channel_id=1, source_target_pairs={{0,16},{4,20},{8,24},{12,28},{16,0},{20,4},{24,8},{28,12},{1,17},{... | collective-permute-start | bytes 2555912 | tf_op jit(solution)/shard_map/ppermute | solution.py:29
  338.9 23.5 %collective-permute-start.41 = (bf16[256,1664]{1,0:T(8,128)(2,1)}, bf16[256,1664]{1,0:T(8,128)(2,1)S(1)}, u32[]{:S(2)}, u32[]{:S(2)}) collective-permute-start(bf16[256,1664]{1,0:T(8,128)(2,1)} %get-tuple-element.187), channel_id=1, source_target_pairs={{0,8},{4,12},{8,0},{12,4},{16,24},{20,28},{24,16},{28,20},{1,9},{5... | collective-permute-start | bytes 2555912 | tf_op jit(solution)/shard_map/ppermute | solution.py:29
  374.2 13.7 %collective-permute-start.43 = (bf16[256,4096]{1,0:T(8,128)(2,1)}, bf16[256,4096]{1,0:T(8,128)(2,1)}, u32[]{:S(2)}, u32[]{:S(2)}) collective-permute-start(bf16[256,4096]{1,0:T(8,128)(2,1)} %get-tuple-element.188.refs_3_), channel_id=1, source_target_pairs={{0,4},{4,0},{8,12},{12,8},{16,20},{20,16},{24,28},{28,24},{1,5},{5... | collective-permute-start | bytes 6291464 | tf_op jit(solution)/shard_map/ppermute | solution.py:29
  385.1 8.7 %collective-permute-start.42 = (bf16[256,3968]{1,0:T(8,128)(2,1)}, bf16[256,3968]{1,0:T(8,128)(2,1)}, u32[]{:S(2)}, u32[]{:S(2)}) collective-permute-start(bf16[256,3968]{1,0:T(8,128)(2,1)} %get-tuple-element.192.refs_4_), channel_id=1, source_target_pairs={{0,4},{4,0},{8,12},{12,8},{16,20},{20,16},{24,28},{28,24},{1,5},{5... | collective-permute-start | bytes 6094856 | tf_op jit(solution)/shard_map/ppermute | solution.py:29
  391.6 8.8 %collective-permute-start.46 = (bf16[32,4096]{1,0:T(8,128)(2,1)}, bf16[32,4096]{1,0:T(8,128)(2,1)S(1)}, u32[]{:S(2)}, u32[]{:S(2)}) collective-permute-start(bf16[32,4096]{1,0:T(8,128)(2,1)} %get-tuple-element.202), channel_id=1, source_target_pairs={{0,8},{4,12},{8,0},{12,4},{16,24},{20,28},{24,16},{28,20},{1,9},{5... | collective-permute-start | bytes 786440 | tf_op jit(solution)/shard_map/ppermute | solution.py:29
  393.3 8.9 %collective-permute-start.47 = (bf16[32,4096]{1,0:T(8,128)(2,1)}, bf16[32,4096]{1,0:T(8,128)(2,1)S(1)}, u32[]{:S(2)}, u32[]{:S(2)}) collective-permute-start(bf16[32,4096]{1,0:T(8,128)(2,1)} %get-tuple-element.203), channel_id=1, source_target_pairs={{0,16},{4,20},{8,24},{12,28},{16,0},{20,4},{24,8},{28,12},{1,17},{... | collective-permute-start | bytes 786440 | tf_op jit(solution)/shard_map/ppermute | solution.py:29
  397.6 15.1 %collective-permute-start.44 = (bf16[32,3968]{1,0:T(8,128)(2,1)}, bf16[32,3968]{1,0:T(8,128)(2,1)S(1)}, u32[]{:S(2)}, u32[]{:S(2)}) collective-permute-start(bf16[32,3968]{1,0:T(8,128)(2,1)} %get-tuple-element.198), channel_id=1, source_target_pairs={{0,8},{4,12},{8,0},{12,4},{16,24},{20,28},{24,16},{28,20},{1,9},{5... | collective-permute-start | bytes 761864 | tf_op jit(solution)/shard_map/ppermute | solution.py:29
  398.8 13.9 %collective-permute-start.45 = (bf16[32,3968]{1,0:T(8,128)(2,1)}, bf16[32,3968]{1,0:T(8,128)(2,1)S(1)}, u32[]{:S(2)}, u32[]{:S(2)}) collective-permute-start(bf16[32,3968]{1,0:T(8,128)(2,1)} %get-tuple-element.200), channel_id=1, source_target_pairs={{0,16},{4,20},{8,24},{12,28},{16,0},{20,4},{24,8},{28,12},{1,17},{... | collective-permute-start | bytes 761864 | tf_op jit(solution)/shard_map/ppermute | solution.py:29
  405.6 13.6 %collective-permute-start.49 = (bf16[64,4096]{1,0:T(8,128)(2,1)}, bf16[64,4096]{1,0:T(8,128)(2,1)S(1)}, u32[]{:S(2)}, u32[]{:S(2)}) collective-permute-start(bf16[64,4096]{1,0:T(8,128)(2,1)} %get-tuple-element.204.refs_4_.refs_7_), channel_id=1, source_target_pairs={{0,16},{4,20},{8,24},{12,28},{16,0},{20,4},{24,8},{28,12},{1,17},{... | collective-permute-start | bytes 1572872 | tf_op jit(solution)/shard_map/ppermute | solution.py:29
  411.7 14.9 %collective-permute-start.50 = (bf16[64,4096]{1,0:T(8,128)(2,1)S(1)}, bf16[64,4096]{1,0:T(8,128)(2,1)S(1)}, u32[]{:S(2)}, u32[]{:S(2)}) collective-permute-start(bf16[64,4096]{1,0:T(8,128)(2,1)S(1)} %copy-done.39), channel_id=1, source_target_pairs={{0,8},{4,12},{8,0},{12,4},{16,24},{20,28},{24,16},{28,20},{1,9},{5... | collective-permute-start | bytes 1572872 | tf_op jit(solution)/shard_map/ppermute | solution.py:29
  416.0 19.4 %collective-permute-start.48 = (bf16[64,3968]{1,0:T(8,128)(2,1)}, bf16[64,3968]{1,0:T(8,128)(2,1)S(1)}, u32[]{:S(2)}, u32[]{:S(2)}) collective-permute-start(bf16[64,3968]{1,0:T(8,128)(2,1)} %get-tuple-element.205), channel_id=1, source_target_pairs={{0,16},{4,20},{8,24},{12,28},{16,0},{20,4},{24,8},{28,12},{1,17},{... | collective-permute-start | bytes 1523720 | tf_op jit(solution)/shard_map/ppermute | solution.py:29
  417.5 30.6 %collective-permute-start.54 = (bf16[64,3968]{1,0:T(8,128)(2,1)}, bf16[64,3968]{1,0:T(8,128)(2,1)S(1)}, u32[]{:S(2)}, u32[]{:S(2)}) collective-permute-start(bf16[64,3968]{1,0:T(8,128)(2,1)} %get-tuple-element.219), channel_id=1, source_target_pairs={{0,8},{4,12},{8,0},{12,4},{16,24},{20,28},{24,16},{28,20},{1,9},{5... | collective-permute-start | bytes 1523720 | tf_op jit(solution)/shard_map/ppermute | solution.py:29
  426.7 8.8 %collective-permute-start.51 = (bf16[64,1664]{1,0:T(8,128)(2,1)S(1)}, bf16[64,1664]{1,0:T(8,128)(2,1)S(1)}, u32[]{:S(2)}, u32[]{:S(2)}) collective-permute-start(bf16[64,1664]{1,0:T(8,128)(2,1)S(1)} %get-tuple-element.346), channel_id=1, source_target_pairs={{0,1},{1,2},{2,3},{3,0},{4,5},{5,6},{6,7},{7,4},{8,9},{9,10},{10,1... | collective-permute-start | bytes 638984 | tf_op jit(solution)/shard_map/ppermute | solution.py:33
  429.7 12.5 %collective-permute-start.52 = (bf16[64,1664]{1,0:T(8,128)(2,1)S(1)}, bf16[64,1664]{1,0:T(8,128)(2,1)S(1)}, u32[]{:S(2)}, u32[]{:S(2)}) collective-permute-start(bf16[64,1664]{1,0:T(8,128)(2,1)S(1)} %get-tuple-element.345), channel_id=1, source_target_pairs={{0,2},{1,3},{2,0},{3,1},{4,6},{5,7},{6,4},{7,5},{8,10},{9,11},{10,... | collective-permute-start | bytes 638984 | tf_op jit(solution)/shard_map/ppermute | solution.py:33
  431.5 10.7 %collective-permute-start.53 = (bf16[64,1664]{1,0:T(8,128)(2,1)S(1)}, bf16[64,1664]{1,0:T(8,128)(2,1)S(1)}, u32[]{:S(2)}, u32[]{:S(2)}) collective-permute-start(bf16[64,1664]{1,0:T(8,128)(2,1)S(1)} %get-tuple-element.344), channel_id=1, source_target_pairs={{0,3},{1,0},{2,1},{3,2},{4,7},{5,4},{6,5},{7,6},{8,11},{9,8},{10,9... | collective-permute-start | bytes 638984 | tf_op jit(solution)/shard_map/ppermute | solution.py:33
  461.2 6.5 %collective-permute-start.58 = (f32[9,128]{1,0:T(8,128)S(1)}, f32[9,128]{1,0:T(8,128)S(1)}, u32[]{:S(2)}, u32[]{:S(2)}) collective-permute-start(f32[9,128]{1,0:T(8,128)S(1)} %add.242), channel_id=1, source_target_pairs={{0,1},{1,2},{2,3},{3,0},{4,5},{5,6},{6,7},{7,4},{8,9},{9,10},{10,1... | collective-permute-start | bytes 13832 | tf_op jit(solution)/shard_map/ppermute | solution.py:33
  464.1 4.5 collective-permute-start.59
  465.3 3.8 collective-permute-start.60
  490.6 3.7 collective-permute-start.63
  494.3 6.0 %collective-permute-start.64 = (f32[25,128]{1,0:T(8,128)S(1)}, f32[25,128]{1,0:T(8,128)S(1)}, u32[]{:S(2)}, u32[]{:S(2)}) collective-permute-start(f32[25,128]{1,0:T(8,128)S(1)} %add.254), channel_id=1, source_target_pairs={{0,1},{1,2},{2,3},{3,0},{4,5},{5,6},{6,7},{7,4},{8,9},{9,10},{10,1... | collective-permute-start | bytes 38408 | tf_op jit(solution)/shard_map/ppermute | solution.py:33
  494.7 5.6 %collective-permute-start.65 = (f32[25,128]{1,0:T(8,128)S(1)}, f32[25,128]{1,0:T(8,128)S(1)}, u32[]{:S(2)}, u32[]{:S(2)}) collective-permute-start(f32[25,128]{1,0:T(8,128)S(1)} %add.254), channel_id=1, source_target_pairs={{0,2},{1,3},{2,0},{3,1},{4,6},{5,7},{6,4},{7,5},{8,10},{9,11},{10,... | collective-permute-start | bytes 38408 | tf_op jit(solution)/shard_map/ppermute | solution.py:33
  (58 other events, 497.3 us)
Sparse Core Ops, SparseCore 0:
  43.2 51.8 all-gather.4
  97.6 54.3 all-gather.6
  274.9 74.4 reduce-scatter.2
  388.1 27.7 reduce-scatter.4
